TPU v7x, 32 devices: a whole 2x2x4 slice. The times are simulated.
32 devices in a mesh: dp: 8 (over y, x, core), tensor: 4 (over z).
Axes of the slice: x: 2, y: 2, z: 4, core: 2. Of those that a mesh axis runs over, the one named last changes fastest.
Arguments:
- tokens: bfloat16 [12288, 1024], P(('dp', 'tensor')), may hold values from -0.19921875 to 0.19921875
- w_query: bfloat16 [1024, 1024], P('dp', 'tensor'), may hold values from -0.1875 to 0.1875
- w_key: bfloat16 [1024, 1024], P('dp', 'tensor'), may hold values from -0.1875 to 0.1875
- w_value: bfloat16 [1024, 1024], P('dp', 'tensor'), may hold values from -0.1875 to 0.1875
- w_out_t: bfloat16 [1024, 1024], P('dp', 'tensor'), may hold values from -0.1875 to 0.1875
- w_up: bfloat16 [1024, 4096], P('dp', 'tensor'), may hold values from -0.1875 to 0.1875
- w_gate: bfloat16 [1024, 4096], P('dp', 'tensor'), may hold values from -0.1875 to 0.1875
- w_down_t: bfloat16 [1024, 4096], P('dp', 'tensor'), may hold values from -0.09375 to 0.09375
- scale_qk: float32 [1024], replicated, may hold values from 0.6 to 1.8
- alpha_attn: float32 [1024], replicated, may hold values from 0.1 to 0.6
- scale_up: float32 [4096], replicated, may hold values from 0.5 to 2
- scale_gate: float32 [4096], replicated, may hold values from 0.5 to 2
- alpha_mlp: float32 [1024], replicated, may hold values from 0.1 to 0.6
- order: int32 [8, 1536], P('dp'), may hold values from 0 to 1535, each once within a row
- lengths: int32 [8, 3], P('dp'), may hold values from 1 to 1024, 1536 in all within a row
- cotangent: bfloat16 [12288, 1024], P(('dp', 'tensor')), may hold values from -6 to 6
Outputs:
- out: bfloat16 [12288, 1024], P(('dp', 'tensor'))
- grad_tokens: float32 [12288, 1024], P(('dp', 'tensor'))
- grad_w_query: float32 [1024, 1024], P('dp', 'tensor')
- grad_w_key: float32 [1024, 1024], P('dp', 'tensor')
- grad_w_value: float32 [1024, 1024], P('dp', 'tensor')
- grad_w_out_t: float32 [1024, 1024], P('dp', 'tensor')
- grad_w_up: float32 [1024, 4096], P('dp', 'tensor')
- grad_w_gate: float32 [1024, 4096], P('dp', 'tensor')
- grad_w_down_t: float32 [1024, 4096], P('dp', 'tensor')
- grad_scale_qk: float32 [1024], replicated
- grad_alpha_attn: float32 [1024], replicated
- grad_scale_up: float32 [4096], replicated
- grad_scale_gate: float32 [4096], replicated
- grad_alpha_mlp: float32 [1024], replicated
Inputs may be any that keep to these rules, and one draw needn't show every extreme that they name: Each row of order holds every place 0 to 1535 once. Each row of lengths sums to 1536, and its largest entry is exactly 1024.
All inputs are finite; a program needn't handle non-finite values.
Results may differ from a plain program's by a relative error of at most 0.017.
Values may be sent and summed in bfloat16 or wider, within the bound.
A program may use at most 192 MiB of HBM per device.

v0:
```python
import math

import jax
import jax.numpy as jnp
from jax import lax
from jax.sharding import PartitionSpec as P

D = 1024
HD = 64


def matmul_ab(first_op, second_op):
    return jnp.dot(first_op, second_op, preferred_element_type=jnp.float32)


def matmul_abt(first_op, second_op):
    return lax.dot_general(
        first_op, second_op, (((1,), (1,)), ((), ())), preferred_element_type=jnp.float32
    )


def matmul_atb(first_op, second_op):
    return lax.dot_general(
        first_op, second_op, (((0,), (0,)), ((), ())), preferred_element_type=jnp.float32
    )


def unit_pair(matrix):
    factor = lax.rsqrt(jnp.sum(matrix * matrix, axis=-1, keepdims=True) + 1e-06)
    return (matrix * factor, factor)


def unit_back(normed, factor, grad_out):
    return factor * (grad_out - normed * jnp.sum(normed * grad_out, axis=-1, keepdims=True))


def rotate(matrix, angles, direction):
    half_width = matrix.shape[-1] // 2
    cosine = jnp.cos(angles)[:, None, :]
    sine_part = direction * jnp.sin(angles)[:, None, :]
    lead_half = matrix[..., :half_width]
    tail_half = matrix[..., half_width:]
    return jnp.concatenate(
        [lead_half * cosine - tail_half * sine_part, tail_half * cosine + lead_half * sine_part],
        axis=-1,
    )


def layout(order_row, length_row):
    group_rows = order_row.shape[0]
    places = jnp.arange(group_rows, dtype=jnp.int32)
    seg_ends = jnp.cumsum(length_row, dtype=jnp.int32)
    seg_starts = seg_ends - length_row
    segment = jnp.sum(
        (places[:, None] >= seg_ends[None, :]).astype(jnp.int32), axis=1, dtype=jnp.int32
    )
    seg_first = jnp.max(
        jnp.where(seg_starts[None, :] <= places[:, None], seg_starts[None, :], 0), axis=1
    )
    half_width = HD // 2
    inv_freq = jnp.exp(
        jnp.arange(half_width, dtype=jnp.float32) * (-math.log(10000.0) / half_width)
    )
    angles = (places - seg_first).astype(jnp.float32)[:, None] * inv_freq[None, :]
    inverse = jnp.zeros((group_rows,), jnp.int32).at[order_row].set(places)
    return (segment, places, angles, inverse)


def on_device(
    tokens,
    w_query,
    w_key,
    w_value,
    w_out_t,
    w_up,
    w_gate,
    w_down_t,
    scale_qk,
    alpha_attn,
    scale_up,
    scale_gate,
    alpha_mlp,
    order,
    lengths,
    cotangent,
):
    tensor_rank = lax.axis_index("tensor")
    head_cols = w_query.shape[1]
    hidden_cols = w_up.shape[1]
    local_heads = head_cols // HD
    qk_gains = lax.dynamic_slice_in_dim(scale_qk, tensor_rank * head_cols, head_cols).reshape(
        local_heads, HD
    )
    up_gains = lax.dynamic_slice_in_dim(scale_up, tensor_rank * hidden_cols, hidden_cols)
    gate_gains = lax.dynamic_slice_in_dim(
        scale_gate, tensor_rank * hidden_cols, hidden_cols
    ) * math.sqrt(D)
    order_row = order[0]
    segment, places, angles, inverse = layout(order_row, lengths[0])
    group_rows = order_row.shape[0]
    block_rows = 512
    block_count = group_rows // block_rows
    score_scale = math.sqrt(HD)
    attn_full = (
        lax.all_gather(w_query, "dp", axis=0, tiled=True),
        lax.all_gather(w_key, "dp", axis=0, tiled=True),
        lax.all_gather(w_value, "dp", axis=0, tiled=True),
        lax.all_gather(w_out_t, "dp", axis=0, tiled=True),
    )
    mlp_full = (
        lax.all_gather(w_up, "dp", axis=0, tiled=True),
        lax.all_gather(w_gate, "dp", axis=0, tiled=True),
        lax.all_gather(w_down_t, "dp", axis=0, tiled=True),
    )
    wq_full, wk_full, wv_full, wo_full = attn_full
    wu_full, wg_full, wd_full = mlp_full
    gathered = lax.all_gather(tokens, "tensor", axis=0, tiled=True)
    packed = gathered[order_row]
    query_n, query_f = unit_pair(matmul_ab(packed, wq_full).reshape(group_rows, local_heads, HD))
    key_n, key_f = unit_pair(matmul_ab(packed, wk_full).reshape(group_rows, local_heads, HD))
    queries = rotate(query_n * qk_gains, angles, 1.0).astype(jnp.bfloat16)
    key_rows = rotate(key_n * qk_gains, angles, 1.0).astype(jnp.bfloat16)
    value_rows = (
        matmul_ab(packed, wv_full).astype(jnp.bfloat16).reshape(group_rows, local_heads, HD)
    )

    def block_scores(start_row):
        query_block = lax.dynamic_slice_in_dim(queries, start_row, block_rows)
        raw_scores = (
            jnp.einsum("qhd,khd->hqk", query_block, key_rows, preferred_element_type=jnp.float32)
            * score_scale
        )
        row_ids = start_row + jnp.arange(block_rows, dtype=jnp.int32)
        seg_block = lax.dynamic_slice_in_dim(segment, start_row, block_rows)
        allowed = (seg_block[:, None] == segment[None, :]) & (places[None, :] <= row_ids[:, None])
        return (query_block, jnp.where(allowed[None], raw_scores, -1e30))

    def forward_block(block_id):
        query_block, masked = block_scores(block_id * block_rows)
        top_score = jnp.max(masked, axis=-1, keepdims=True)
        log_total = top_score + jnp.log(
            jnp.sum(jnp.exp(masked - top_score), axis=-1, keepdims=True)
        )
        probs_b = jnp.exp(masked - log_total).astype(jnp.bfloat16)
        block_out = jnp.einsum(
            "hqk,khd->qhd", probs_b, value_rows, preferred_element_type=jnp.float32
        )
        return (block_out.astype(jnp.bfloat16), log_total)

    attended_blocks, log_totals = lax.map(forward_block, jnp.arange(block_count, dtype=jnp.int32))
    attended = attended_blocks.reshape(group_rows, head_cols)
    attended_mine = lax.all_to_all(
        attended[inverse], "tensor", split_axis=0, concat_axis=1, tiled=True
    )
    wo_every = lax.all_gather(wo_full, "tensor", axis=1, tiled=True)
    branch_a = matmul_abt(attended_mine, wo_every)
    inputs_f = tokens.astype(jnp.float32)
    norm_a, factor_a = unit_pair(branch_a)
    middle, factor_mid = unit_pair(inputs_f + alpha_attn * (norm_a - inputs_f))
    middle_rows = lax.all_gather(middle.astype(jnp.bfloat16), "tensor", axis=0, tiled=True)
    up_raw = matmul_ab(middle_rows, wu_full)
    gate_raw = matmul_ab(middle_rows, wg_full)
    up_proj = up_raw * up_gains
    gate_proj = gate_raw * gate_gains
    sigmoid_g = jax.nn.sigmoid(gate_proj)
    silu_g = jax.nn.silu(gate_proj)
    mixed_b = (up_proj * silu_g).astype(jnp.bfloat16)
    branch_m = lax.psum_scatter(
        matmul_abt(mixed_b, wd_full).astype(jnp.bfloat16), "tensor", scatter_dimension=0, tiled=True
    ).astype(jnp.float32)
    norm_m, factor_m = unit_pair(branch_m)
    outputs, factor_out = unit_pair(middle + alpha_mlp * (norm_m - middle))
    mlp_back = (
        lax.all_gather(w_up, "dp", axis=0, tiled=True),
        lax.all_gather(w_gate, "dp", axis=0, tiled=True),
        lax.all_gather(w_down_t, "dp", axis=0, tiled=True),
    )
    attn_back = (
        lax.all_gather(w_query, "dp", axis=0, tiled=True),
        lax.all_gather(w_key, "dp", axis=0, tiled=True),
        lax.all_gather(w_value, "dp", axis=0, tiled=True),
        lax.all_gather(w_out_t, "dp", axis=0, tiled=True),
    )
    wu_back, wg_back, wd_back = mlp_back
    wq_back, wk_back, wv_back, wo_back = attn_back
    grad_out = cotangent.astype(jnp.float32)
    grad_h2 = unit_back(outputs, factor_out, grad_out)
    grad_alpha_m = jnp.sum(grad_h2 * (norm_m - middle), axis=0)
    grad_bm = unit_back(norm_m, factor_m, alpha_mlp * grad_h2).astype(jnp.bfloat16)
    grad_bm_rows = lax.all_gather(grad_bm, "tensor", axis=0, tiled=True)
    grad_mixed = matmul_ab(grad_bm_rows, wd_back)
    grad_wd = matmul_atb(grad_bm_rows, mixed_b)
    grad_upp = grad_mixed * silu_g
    grad_gatep = grad_mixed * up_proj * sigmoid_g * (1.0 + gate_proj * (1.0 - sigmoid_g))
    grad_su = jnp.sum(grad_upp * up_raw, axis=0)
    grad_sv = jnp.sum(grad_gatep * gate_raw, axis=0) * math.sqrt(D)
    grad_up_b = (grad_upp * up_gains).astype(jnp.bfloat16)
    grad_gate_b = (grad_gatep * gate_gains).astype(jnp.bfloat16)
    grad_wu = matmul_atb(middle_rows, grad_up_b)
    grad_wg = matmul_atb(middle_rows, grad_gate_b)
    back_terms = matmul_abt(grad_up_b, wu_back) + matmul_abt(grad_gate_b, wg_back)
    grad_middle = (1.0 - alpha_mlp) * grad_h2 + lax.psum_scatter(
        back_terms.astype(jnp.bfloat16), "tensor", scatter_dimension=0, tiled=True
    ).astype(jnp.float32)
    grad_h1 = unit_back(middle, factor_mid, grad_middle)
    grad_alpha_a = jnp.sum(grad_h1 * (norm_a - inputs_f), axis=0)
    grad_ba = unit_back(norm_a, factor_a, alpha_attn * grad_h1).astype(jnp.bfloat16)
    grad_ba_rows = lax.all_gather(grad_ba, "tensor", axis=0, tiled=True)[order_row]
    grad_att = matmul_ab(grad_ba_rows, wo_back).astype(jnp.bfloat16)
    grad_wo = matmul_atb(grad_ba_rows, attended)
    grad_att_h = grad_att.reshape(group_rows, local_heads, HD)

    def backward_block(running, block_id):
        grad_keys, grad_vals = running
        start_row = block_id * block_rows
        query_block, masked = block_scores(start_row)
        probs_f = jnp.exp(masked - log_totals[block_id])
        out_grad = lax.dynamic_slice_in_dim(grad_att_h, start_row, block_rows)
        grad_probs = jnp.einsum(
            "qhd,khd->hqk", out_grad, value_rows, preferred_element_type=jnp.float32
        )
        delta_row = jnp.sum(probs_f * grad_probs, axis=-1, keepdims=True)
        grad_scores = (probs_f * (grad_probs - delta_row)).astype(jnp.bfloat16)
        grad_query = (
            jnp.einsum("hqk,khd->qhd", grad_scores, key_rows, preferred_element_type=jnp.float32)
            * score_scale
        )
        grad_keys = (
            grad_keys
            + jnp.einsum(
                "hqk,qhd->khd", grad_scores, query_block, preferred_element_type=jnp.float32
            )
            * score_scale
        )
        grad_vals = grad_vals + jnp.einsum(
            "hqk,qhd->khd",
            probs_f.astype(jnp.bfloat16),
            out_grad,
            preferred_element_type=jnp.float32,
        )
        return ((grad_keys, grad_vals), grad_query)

    zero_heads = jnp.zeros((group_rows, local_heads, HD), jnp.float32)
    (grad_keys, grad_vals), grad_queries = lax.scan(
        backward_block, (zero_heads, zero_heads), jnp.arange(block_count, dtype=jnp.int32)
    )
    grad_queries = grad_queries.reshape(group_rows, local_heads, HD)
    grad_qs = rotate(grad_queries, angles, -1.0)
    grad_ks = rotate(grad_keys, angles, -1.0)
    grad_gain = jnp.sum(grad_qs * query_n + grad_ks * key_n, axis=0).reshape(head_cols)
    grad_qraw = (
        unit_back(query_n, query_f, grad_qs * qk_gains)
        .astype(jnp.bfloat16)
        .reshape(group_rows, head_cols)
    )
    grad_kraw = (
        unit_back(key_n, key_f, grad_ks * qk_gains)
        .astype(jnp.bfloat16)
        .reshape(group_rows, head_cols)
    )
    grad_vraw = grad_vals.astype(jnp.bfloat16).reshape(group_rows, head_cols)
    grad_wq = matmul_atb(packed, grad_qraw)
    grad_wk = matmul_atb(packed, grad_kraw)
    grad_wv = matmul_atb(packed, grad_vraw)
    query_mine, key_mine, value_mine = (
        lax.all_to_all(grad_qraw[inverse], "tensor", split_axis=0, concat_axis=1, tiled=True),
        lax.all_to_all(grad_kraw[inverse], "tensor", split_axis=0, concat_axis=1, tiled=True),
        lax.all_to_all(grad_vraw[inverse], "tensor", split_axis=0, concat_axis=1, tiled=True),
    )
    wq_every, wk_every, wv_every = (
        lax.all_gather(wq_back, "tensor", axis=1, tiled=True),
        lax.all_gather(wk_back, "tensor", axis=1, tiled=True),
        lax.all_gather(wv_back, "tensor", axis=1, tiled=True),
    )
    attn_part = (
        matmul_abt(query_mine, wq_every)
        + matmul_abt(key_mine, wk_every)
        + matmul_abt(value_mine, wv_every)
    )
    grad_tokens = (1.0 - alpha_attn) * grad_h1 + attn_part
    grad_qk_full = lax.dynamic_update_slice_in_dim(
        jnp.zeros(scale_qk.shape, jnp.float32), grad_gain, tensor_rank * head_cols, 0
    )
    grad_su_full = lax.dynamic_update_slice_in_dim(
        jnp.zeros(scale_up.shape, jnp.float32), grad_su, tensor_rank * hidden_cols, 0
    )
    grad_sv_full = lax.dynamic_update_slice_in_dim(
        jnp.zeros(scale_gate.shape, jnp.float32), grad_sv, tensor_rank * hidden_cols, 0
    )
    vector_sums = lax.psum(
        (grad_qk_full, grad_alpha_a, grad_su_full, grad_sv_full, grad_alpha_m), ("dp", "tensor")
    )
    weight_sums = (
        lax.psum_scatter(grad_wq, "dp", scatter_dimension=0, tiled=True),
        lax.psum_scatter(grad_wk, "dp", scatter_dimension=0, tiled=True),
        lax.psum_scatter(grad_wv, "dp", scatter_dimension=0, tiled=True),
        lax.psum_scatter(grad_wo, "dp", scatter_dimension=0, tiled=True),
        lax.psum_scatter(grad_wu, "dp", scatter_dimension=0, tiled=True),
        lax.psum_scatter(grad_wg, "dp", scatter_dimension=0, tiled=True),
        lax.psum_scatter(grad_wd, "dp", scatter_dimension=0, tiled=True),
    )
    return (
        outputs.astype(jnp.bfloat16),
        grad_tokens,
        weight_sums[0],
        weight_sums[1],
        weight_sums[2],
        weight_sums[3],
        weight_sums[4],
        weight_sums[5],
        weight_sums[6],
        vector_sums[0],
        vector_sums[1],
        vector_sums[2],
        vector_sums[3],
        vector_sums[4],
    )


def solution(mesh):
    return jax.shard_map(
        on_device,
        mesh=mesh,
        in_specs=(
            P(("dp", "tensor"), None),
            P("dp", "tensor"),
            P("dp", "tensor"),
            P("dp", "tensor"),
            P("dp", "tensor"),
            P("dp", "tensor"),
            P("dp", "tensor"),
            P("dp", "tensor"),
            P(),
            P(),
            P(),
            P(),
            P(),
            P("dp", None),
            P("dp", None),
            P(("dp", "tensor"), None),
        ),
        out_specs=(
            P(("dp", "tensor"), None),
            P(("dp", "tensor"), None),
            P("dp", "tensor"),
            P("dp", "tensor"),
            P("dp", "tensor"),
            P("dp", "tensor"),
            P("dp", "tensor"),
            P("dp", "tensor"),
            P("dp", "tensor"),
            P(),
            P(),
            P(),
            P(),
            P(),
        ),
        check_vma=False,
    )
```

profile of v0, /device:TPU:0, one launch (start us, length us, event | category | flops | bytes accessed | tf_op | source)
XLA Modules:
  0.0 1065.6 jit_solution(8562368292466010642)
XLA Ops:
  8.0 13.2 %all_gather.56 = bf16[1024,256]{1,0:T(8,128)(2,1)} all-gather(bf16[128,256]{1,0:T(8,128)(2,1)} %param.24), channel_id=1, replica_groups=mesh['dp'=8,'tensor'=4] {'dp'}, dimensions={0}, use_global_device_ids=true | all-gather | bytes 589824 | tf_op jit(solution)/shard_map/all_gather | solution.py:108
  30.8 10.0 all_gather.53
  40.7 10.7 %all_gather.54 = bf16[1024,256]{1,0:T(8,128)(2,1)} all-gather(bf16[128,256]{1,0:T(8,128)(2,1)S(1)} %copy-done.54), channel_id=1, replica_groups=mesh['dp'=8,'tensor'=4] {'dp'}, dimensions={0}, use_global_device_ids=true | all-gather | bytes 589824 | tf_op jit(solution)/shard_map/all_gather | solution.py:106
  51.4 9.9 all_gather.55
  62.8 13.0 %all-gather.12.cloned.1.call-done = bf16[1536,1024]{1,0:T(8,128)(2,1)} async-done(((bf16[384,1024]{1,0:T(8,128)(2,1)}), bf16[1536,1024]{1,0:T(8,128)(2,1)}) %all-gather.12.cloned.1.call-update) | async-done | bytes 3145744 | tf_op jit(solution)/shard_map/all_gather | solution.py:117
  75.8 9.5 gather_fusion
  94.0 54.9 %while.28 = (s32[]{:T(128)}, bf16[3,512,4,64]{1,3,2,0:T(8,128)(2,1)S(1)}, f32[3,4,512,1]{2,1,3,0:T(4,128)S(1)}, s32[3]{0:T(128)S(1)}, s32[1536]{0:T(1024)S(1)}, ...) while((s32[]{:T(128)}, ...), condition=%wide.region_8.9_spmd.clone, body=%wide.region_5.8_spmd.clone.sunk | while | flops 842398208 | bytes 93405416 | solution.py:150
  159.6 20.4 %all-to-all-done = bf16[4,384,256]{1,2,0:T(8,128)(2,1)S(1)} async-done(((bf16[4,384,256]{1,2,0:T(8,128)(2,1)}), bf16[4,384,256]{1,2,0:T(8,128)(2,1)S(1)}, u32[]{:S(2)}, u32[]{:S(2)}) %all-to-all-start) | async-done | bytes 786464 | tf_op jit(solution)/shard_map/all_to_all | solution.py:152
  188.6 59.8 %all-gather.16.cloned.1.call-done = bf16[1536,1024]{1,0:T(8,128)(2,1)} async-done(((bf16[384,1024]{1,0:T(8,128)(2,1)}), bf16[1536,1024]{1,0:T(8,128)(2,1)}) %all-gather.16.cloned.1.call-update) | async-done | bytes 3145744 | tf_op jit(solution)/shard_map/all_gather | solution.py:160
  248.4 8.6 fusion.72
  257.0 19.6 %all-gather.18.cloned.1.call-done = bf16[1024,1024]{1,0:T(8,128)(2,1)} async-done(((bf16[128,1024]{1,0:T(8,128)(2,1)}), bf16[1024,1024]{1,0:T(8,128)(2,1)}) %all-gather.18.cloned.1.call-update) | async-done | bytes 2097168 | tf_op jit(solution)/shard_map/all_gather | solution.py:111
  276.6 12.4 %multiply_convert_fusion.3 = (bf16[1536,1024]{1,0:T(8,128)(2,1)}, f32[1536,1024]{1,0:T(8,128)}) fusion(f32[1024]{0:T(1024)S(1)} %dynamic_slice.35, f32[1536,1024]{1,0:T(8,128)} %fusion.72, f32[1024]{0:T(1024)S(1)} %dynamic-slice_multiply_fusion, bf16[1536,1024]{1,0:T(8,128)(2,1)} %all-gather.16.cloned.1.call-done, ...), kind=kOutput, calls=%fused_computation.61 | convolution fusion | flops 3233808384 | bytes 20979712 | tf_op jit(solution)/shard_map/dot_general | solution.py:13
  289.0 17.2 %all-gather.22.cloned.1.call-done = bf16[1024,1024]{1,0:T(8,128)(2,1)} async-done(((bf16[128,1024]{1,0:T(8,128)(2,1)}), bf16[1024,1024]{1,0:T(8,128)(2,1)}) %all-gather.22.cloned.1.call-update) | async-done | bytes 2097168 | tf_op jit(solution)/shard_map/all_gather | solution.py:113
  314.1 60.3 %reduce-scatter.10.cloned.1.call-done = bf16[384,1024]{1,0:T(8,128)(2,1)} async-done(((bf16[1536,1024]{1,0:T(8,128)(2,1)}), bf16[384,1024]{1,0:T(8,128)(2,1)}) %reduce-scatter.10.cloned.1.call-update) | async-done | bytes 786448 | tf_op jit(solution)/shard_map/reduce_scatter | solution.py:168
  383.0 63.5 %all-gather.24.cloned.1.call-done = bf16[1536,1024]{1,0:T(8,128)(2,1)} async-done(((bf16[384,1024]{1,0:T(8,128)(2,1)}), bf16[1536,1024]{1,0:T(8,128)(2,1)}) %all-gather.24.cloned.1.call-update) | async-done | bytes 3145744 | tf_op jit(solution)/shard_map/all_gather | solution.py:190
  446.4 12.2 %multiply_reduce_fusion.1 = (f32[1024]{0:T(1024)}, f32[1024]{0:T(1024)}, f32[1536,1024]{1,0:T(8,128)S(1)}, bf16[1536,1024]{1,0:T(8,128)(2,1)S(1)}) fusion(f32[1536,1024]{1,0:T(8,128)} %fusion.72, f32[1536,1024]{1,0:T(8,128)} %get-tuple-element.279, f32[1024]{0:T(1024)S(1)} %dynamic-slice_multiply_fusion, f32[1024]{0:T(1024)S(1)} %dynamic_slice.35, ...), kind=kOutput, calls=%fused_computation.55 | convolution fusion | flops 3251107840 | bytes 27279360 | tf_op jit(solution)/shard_map/dot_general | solution.py:13
  467.9 58.7 %reduce-scatter.12.cloned.1.call-done = bf16[384,1024]{1,0:T(8,128)(2,1)} async-done(((bf16[1536,1024]{1,0:T(8,128)(2,1)}), bf16[384,1024]{1,0:T(8,128)(2,1)}) %reduce-scatter.12.cloned.1.call-update) | async-done | bytes 786448 | tf_op jit(solution)/shard_map/reduce_scatter | solution.py:202
  544.3 9.2 fusion.62
  562.2 35.1 %all-gather.26.cloned.1.call-done = bf16[1536,1024]{1,0:T(8,128)(2,1)} async-done(((bf16[384,1024]{1,0:T(8,128)(2,1)}), bf16[1536,1024]{1,0:T(8,128)(2,1)}) %all-gather.26.cloned.1.call-update) | async-done | bytes 3145744 | tf_op jit(solution)/shard_map/all_gather | solution.py:208
  597.3 10.1 gather_fusion.2
  613.4 112.9 %while.29 = (s32[]{:T(128)}, f32[1536,4,64]{0,2,1:T(8,128)}, f32[1536,4,64]{0,2,1:T(8,128)}, f32[3,512,4,64]{1,0,3,2:T(4,128)}, s32[3]{0:T(128)S(1)}, /*index=5*...) while((s32[]{:T(128)}, f32[1536,4,64]{0,2,1:T(8,128)}, ...), condition=%wide.region_22.23_spmd.clone, body=%wide.region_20.22_spmd.clone.sunk | while | flops 2046032384 | bytes 152363440 | solution.py:244
  639.4 11.3 %dynamic_update_slice.35 = f32[3,512,4,64]{1,0,3,2:T(4,128)} dynamic-update-slice(f32[3,512,4,64]{1,0,3,2:T(4,128)} %get-tuple-element.465, f32[1,512,4,64]{1,0,3,2:T(1,128)S(1)} %copy.75, s32[]{:T(128)S(6)} %copy.92, s32[]{:T(128)} %constant.50.clone.1..sunk.1, s32[]{:T(128)} %constant.50.clone.1..sunk.1, s32[]{:T(128)} %constant.50.clone.1..sunk.1) | dynamic-update-slice | bytes 1048580 | tf_op jit(solution)/shard_map/while/body/jit(dynamic_update_index_in_dim)/dynamic_update_slice | solution.py:244
  677.2 11.3 %dynamic_update_slice.35 = f32[3,512,4,64]{1,0,3,2:T(4,128)} dynamic-update-slice(f32[3,512,4,64]{1,0,3,2:T(4,128)} %get-tuple-element.465, f32[1,512,4,64]{1,0,3,2:T(1,128)S(1)} %copy.75, s32[]{:T(128)S(6)} %copy.92, s32[]{:T(128)} %constant.50.clone.1..sunk.1, s32[]{:T(128)} %constant.50.clone.1..sunk.1, s32[]{:T(128)} %constant.50.clone.1..sunk.1) | dynamic-update-slice | bytes 1048580 | tf_op jit(solution)/shard_map/while/body/jit(dynamic_update_index_in_dim)/dynamic_update_slice | solution.py:244
  715.0 11.3 %dynamic_update_slice.35 = f32[3,512,4,64]{1,0,3,2:T(4,128)} dynamic-update-slice(f32[3,512,4,64]{1,0,3,2:T(4,128)} %get-tuple-element.465, f32[1,512,4,64]{1,0,3,2:T(1,128)S(1)} %copy.75, s32[]{:T(128)S(6)} %copy.92, s32[]{:T(128)} %constant.50.clone.1..sunk.1, s32[]{:T(128)} %constant.50.clone.1..sunk.1, s32[]{:T(128)} %constant.50.clone.1..sunk.1) | dynamic-update-slice | bytes 1048580 | tf_op jit(solution)/shard_map/while/body/jit(dynamic_update_index_in_dim)/dynamic_update_slice | solution.py:244
  770.9 9.4 all-to-all-done.1
  792.5 11.6 %all-to-all-done.2 = bf16[4,384,256]{1,2,0:T(8,128)(2,1)} async-done(((bf16[4,384,256]{1,2,0:T(8,128)(2,1)}), bf16[4,384,256]{1,2,0:T(8,128)(2,1)}, u32[]{:S(2)}, u32[]{:S(2)}) %all-to-all-start.2) | async-done | bytes 786464 | tf_op jit(solution)/shard_map/all_to_all | solution.py:267
  812.3 42.4 %all-reduce = (f32[1024]{0:T(1024)}, f32[1024]{0:T(1024)}, f32[4096]{0:T(1024)}, f32[4096]{0:T(1024)}, f32[1024]{0:T(1024)}) all-reduce(f32[1024]{0:T(1024)S(1)} %dynamic_update_slice.21, f32[1024]{0:T(1024)S(1)} %copy-done.58, f32[4096]{0:T(1024)S(1)} %dynamic_update_slice.22, ...), channel_id=1, replica_groups=mesh['dp'=8,'tensor'=4] {'dp','tensor'}, use_global_device_ids=true, to_apply=%region_33.34 | all-reduce | flops 11264 | bytes 90112 | tf_op jit(solution)/shard_map/psum | solution.py:290
  866.9 32.8 %reduce-scatter.22.cloned.1.call-done = f32[128,1024]{1,0:T(8,128)} async-done(((f32[1024,1024]{1,0:T(8,128)}), f32[128,1024]{1,0:T(8,128)}) %reduce-scatter.22.cloned.1.call-update) | async-done | bytes 524304 | tf_op jit(solution)/shard_map/reduce_scatter | solution.py:298
  899.7 39.6 %reduce-scatter.20.cloned.1.call-done = f32[128,256]{1,0:T(8,128)} async-done(((f32[1024,256]{1,0:T(8,128)}), f32[128,256]{1,0:T(8,128)}) %reduce-scatter.20.cloned.1.call-update) | async-done | bytes 131088 | tf_op jit(solution)/shard_map/reduce_scatter | solution.py:297
  939.3 39.6 %reduce-scatter.18.cloned.1.call-done = f32[128,256]{1,0:T(8,128)} async-done(((f32[1024,256]{1,0:T(8,128)}), f32[128,256]{1,0:T(8,128)}) %reduce-scatter.18.cloned.1.call-update) | async-done | bytes 131088 | tf_op jit(solution)/shard_map/reduce_scatter | solution.py:296
  978.9 39.8 %reduce-scatter.16.cloned.1.call-done = f32[128,256]{1,0:T(8,128)} async-done(((f32[1024,256]{1,0:T(8,128)}), f32[128,256]{1,0:T(8,128)}) %reduce-scatter.16.cloned.1.call-update) | async-done | bytes 131088 | tf_op jit(solution)/shard_map/reduce_scatter | solution.py:295
  1018.7 39.6 %reduce-scatter.14.cloned.1.call-done = f32[128,256]{1,0:T(8,128)} async-done(((f32[1024,256]{1,0:T(8,128)}), f32[128,256]{1,0:T(8,128)}) %reduce-scatter.14.cloned.1.call-update) | async-done | bytes 131088 | tf_op jit(solution)/shard_map/reduce_scatter | solution.py:294
  (366 shorter events, 297.6 us)
Async XLA Ops:
  7.2 23.5 %copy-start.53 = (bf16[128,256]{1,0:T(8,128)(2,1)S(1)}, bf16[128,256]{1,0:T(8,128)(2,1)}, u32[]{:S(2)}) copy-start(bf16[128,256]{1,0:T(8,128)(2,1)} %param.21) | copy-start | bytes 196612
  7.2 33.5 %copy-start.54 = (bf16[128,256]{1,0:T(8,128)(2,1)S(1)}, bf16[128,256]{1,0:T(8,128)(2,1)}, u32[]{:S(2)}) copy-start(bf16[128,256]{1,0:T(8,128)(2,1)} %param.22) | copy-start | bytes 196612
  7.2 44.2 %copy-start.55 = (bf16[128,256]{1,0:T(8,128)(2,1)S(1)}, bf16[128,256]{1,0:T(8,128)(2,1)}, u32[]{:S(2)}) copy-start(bf16[128,256]{1,0:T(8,128)(2,1)} %param.23) | copy-start | bytes 196612
  7.2 68.6 %all-gather.12.cloned.1.call-start = ((), (), s32[]{:S(2)}) async-start(), calls=%async_computation.13 | async-start | bytes 3932160 | tf_op jit(solution)/shard_map/all_gather | solution.py:117
  8.0 151.6 %all-gather.14.cloned.1.call-start = ((), (), s32[]{:S(2)}) async-start(), calls=%async_computation.14 | async-start | bytes 2621440 | tf_op jit(solution)/shard_map/all_gather | solution.py:155
  21.3 167.3 %all-gather.20.cloned.1.call-start = ((), (), s32[]{:S(2)}) async-start(), calls=%async_computation.17 | async-start | bytes 2359296 | tf_op jit(solution)/shard_map/all_gather | solution.py:112
  30.7 119.3 %copy-start.46 = (s32[2048]{0:T(1024)}, s32[2048]{0:T(1024)S(1)}, u32[]{:S(2)}) copy-start(s32[2048]{0:T(1024)S(1)} %pad_clamp_fusion) | copy-start | bytes 24580
  62.8 29.4 %copy-start.38 = (f32[1536,32]{0,1:T(8,128)}, f32[1536,32]{0,1:T(8,128)S(1)}, u32[]{:S(2)}) copy-start(f32[1536,32]{0,1:T(8,128)S(1)} %get-tuple-element.269) | copy-start | bytes 589828
  156.0 24.0 %all-to-all-start = ((bf16[4,384,256]{1,2,0:T(8,128)(2,1)}), bf16[4,384,256]{1,2,0:T(8,128)(2,1)S(1)}, u32[]{:S(2)}, u32[]{:S(2)}) async-start(bf16[4,384,256]{1,2,0:T(8,128)(2,1)} %copy.46), calls=%async_computation | async-start | bytes 1572864 | tf_op jit(solution)/shard_map/all_to_all | solution.py:152
  159.5 88.9 %all-gather.16.cloned.1.call-start = ((), (), s32[]{:S(2)}) async-start(), calls=%async_computation.15 | async-start | bytes 3932160 | tf_op jit(solution)/shard_map/all_gather | solution.py:160
  185.6 91.0 %all-gather.18.cloned.1.call-start = ((), (), s32[]{:S(2)}) async-start(), calls=%async_computation.16 | async-start | bytes 2359296 | tf_op jit(solution)/shard_map/all_gather | solution.py:111
  186.2 119.9 %all-gather.22.cloned.1.call-start = ((), (), s32[]{:S(2)}) async-start(), calls=%async_computation.18 | async-start | bytes 2359296 | tf_op jit(solution)/shard_map/all_gather | solution.py:113
  186.7 187.6 %reduce-scatter.10.cloned.1.call-start = ((), (), s32[]{:S(2)}) async-start(), calls=%async_computation.19 | async-start | bytes 3932160 | tf_op jit(solution)/shard_map/reduce_scatter | solution.py:168
  313.8 62.0 %copy-start.50 = (f32[1024]{0:T(1024)S(1)}, f32[1024]{0:T(1024)}, u32[]{:S(2)}) copy-start(f32[1024]{0:T(1024)} %param.32) | copy-start | bytes 12292
  313.8 132.6 %all-gather.24.cloned.1.call-start = ((), (), s32[]{:S(2)}) async-start(), calls=%async_computation.20 | async-start | bytes 3932160 | tf_op jit(solution)/shard_map/all_gather | solution.py:190
  382.9 143.7 %reduce-scatter.12.cloned.1.call-start = ((), (), s32[]{:S(2)}) async-start(), calls=%async_computation.21 | async-start | bytes 3932160 | tf_op jit(solution)/shard_map/reduce_scatter | solution.py:202
  467.4 129.9 %all-gather.26.cloned.1.call-start = ((), (), s32[]{:S(2)}) async-start(), calls=%async_computation.22 | async-start | bytes 3932160 | tf_op jit(solution)/shard_map/all_gather | solution.py:208
  533.8 320.9 %all-gather.28.cloned.1.call-start = ((), (), s32[]{:S(2)}) async-start(), calls=%async_computation.23 | async-start | bytes 2621440 | tf_op jit(solution)/shard_map/all_gather | solution.py:271
  534.5 323.4 %all-gather.30.cloned.1.call-start = ((), (), s32[]{:S(2)}) async-start(), calls=%async_computation.24 | async-start | bytes 2621440 | tf_op jit(solution)/shard_map/all_gather | solution.py:272
  535.1 327.2 %all-gather.32.cloned.1.call-start = ((), (), s32[]{:S(2)}) async-start(), calls=%async_computation.25 | async-start | bytes 2621440 | tf_op jit(solution)/shard_map/all_gather | solution.py:273
  535.8 331.1 %reduce-scatter.26.cloned.1.call-start = ((), (), s32[]{:S(2)}) async-start(), calls=%async_computation.32 | async-start | bytes 4718592 | tf_op jit(solution)/shard_map/reduce_scatter | solution.py:300
  544.3 322.6 %reduce-scatter.24.cloned.1.call-start = ((), (), s32[]{:S(2)}) async-start(), calls=%async_computation.31 | async-start | bytes 4718592 | tf_op jit(solution)/shard_map/reduce_scatter | solution.py:299
  553.5 346.1 %reduce-scatter.22.cloned.1.call-start = ((), (), s32[]{:S(2)}) async-start(), calls=%async_computation.30 | async-start | bytes 4718592 | tf_op jit(solution)/shard_map/reduce_scatter | solution.py:298
  561.9 35.4 %copy-start.48 = (s32[2048]{0:T(1024)S(1)}, s32[2048]{0:T(1024)}, u32[]{:S(2)}) copy-start(s32[2048]{0:T(1024)} %pad_clamp_fusion.1) | copy-start | bytes 24580
  561.9 377.4 %reduce-scatter.20.cloned.1.call-start = ((), (), s32[]{:S(2)}) async-start(), calls=%async_computation.29 | async-start | bytes 1179648 | tf_op jit(solution)/shard_map/reduce_scatter | solution.py:297
  562.2 45.2 %copy-start.37 = (bf16[1024,256]{1,0:T(8,128)(2,1)S(1)}, bf16[1024,256]{1,0:T(8,128)(2,1)}, u32[]{:S(2)}) copy-start(bf16[1024,256]{1,0:T(8,128)(2,1)} %all_gather.56) | copy-start | bytes 1572868
  613.4 365.5 %reduce-scatter.18.cloned.1.call-start = ((), (), s32[]{:S(2)}) async-start(), calls=%async_computation.28 | async-start | bytes 1179648 | tf_op jit(solution)/shard_map/reduce_scatter | solution.py:296
  756.0 24.2 %all-to-all-start.1 = ((bf16[4,384,256]{1,2,0:T(8,128)(2,1)}), bf16[4,384,256]{1,2,0:T(8,128)(2,1)}, u32[]{:S(2)}, u32[]{:S(2)}) async-start(bf16[4,384,256]{1,2,0:T(8,128)(2,1)} %copy.49), calls=%async_computation.3 | async-start | bytes 1572864 | tf_op jit(solution)/shard_map/all_to_all | solution.py:266
  760.2 258.5 %reduce-scatter.16.cloned.1.call-start = ((), (), s32[]{:S(2)}) async-start(), calls=%async_computation.27 | async-start | bytes 1179648 | tf_op jit(solution)/shard_map/reduce_scatter | solution.py:295
  780.2 23.9 %all-to-all-start.2 = ((bf16[4,384,256]{1,2,0:T(8,128)(2,1)}), bf16[4,384,256]{1,2,0:T(8,128)(2,1)}, u32[]{:S(2)}, u32[]{:S(2)}) async-start(bf16[4,384,256]{1,2,0:T(8,128)(2,1)} %copy.51), calls=%async_computation.4 | async-start | bytes 1572864 | tf_op jit(solution)/shard_map/all_to_all | solution.py:267
  804.2 58.2 %all-to-all-start.3 = ((bf16[4,384,256]{1,2,0:T(8,128)(2,1)}), bf16[4,384,256]{1,2,0:T(8,128)(2,1)}, u32[]{:S(2)}, u32[]{:S(2)}) async-start(bf16[4,384,256]{1,2,0:T(8,128)(2,1)} %copy.53), calls=%async_computation.5 | async-start | bytes 1572864 | tf_op jit(solution)/shard_map/all_to_all | solution.py:268
  808.4 249.9 %reduce-scatter.14.cloned.1.call-start = ((), (), s32[]{:S(2)}) async-start(), calls=%async_computation.26 | async-start | bytes 1179648 | tf_op jit(solution)/shard_map/reduce_scatter | solution.py:294
  (74 other events, 332.4 us)
Sparse Core Ops, SparseCore 0:
  9.6 66.1 all-gather.11
  77.4 44.8 all-gather.13
  124.2 26.0 all-gather.19
  185.7 62.6 all-gather.15
  250.1 26.4 all-gather.17
  278.3 27.7 all-gather.21
  314.0 60.3 reduce-scatter.9
  383.0 63.3 all-gather.23
  467.5 59.0 reduce-scatter.11
  533.9 63.3 all-gather.25
  598.9 44.8 all-gather.27
  645.2 44.4 all-gather.29
  691.2 44.4 all-gather.31
  739.5 49.3 reduce-scatter.25
  792.7 51.9 reduce-scatter.23
  848.5 51.1 reduce-scatter.21
  903.3 35.9 reduce-scatter.19
  942.9 35.9 reduce-scatter.17
  982.7 35.9 reduce-scatter.15
  1022.3 35.9 reduce-scatter.13
where the time goes:
time: 1080 us; the launch traced here: 1070 us
  waiting for transfers between devices  564 us (52%)
  matrix products  198 us (18%)
  local copies, waits for them, and re-layouts  116 us (11%)
  blocking collectives  86.2 us (8%)
  other arithmetic  56.6 us (5%)
  starting transfers between devices  18 us (2%)
  between operations  15.6 us (1%)
    all_gather x1, waiting for transfers between devices, on_device(): grad_bm_rows = lax.all_gather(grad_bm, 'tensor', axis=0, tiled=True)  63.5 us
    reduce_scatter x1, waiting for transfers between devices, on_device(): lax.psum_scatter(matmul_abt(mixed_b, wd_full).astype(jnp.bfloat16), 'tens...  60.3 us
    all_gather x1, waiting for transfers between devices, on_device(): lax.all_gather(middle.astype(jnp.bfloat16), 'tensor', axis=0, tiled=True)  59.8 us
    reduce_scatter x1, waiting for transfers between devices, on_device(): lax.psum_scatter(back_terms.astype(jnp.bfloat16), 'tensor', scatter_dimen...  58.7 us
    dot_general x7, matrix products, matmul_ab(): return jnp.dot(first_op, second_op, preferred_element_type=jnp.float32)  42.8 us
    psum x1, blocking collectives, on_device(): lax.psum((grad_qk_full, grad_alpha_a, grad_su_full, grad_sv_full, grad_al...  42.4 us
    reduce_scatter x1, waiting for transfers between devices, on_device(): lax.psum_scatter(grad_wk, 'dp', scatter_dimension=0, tiled=True)  39.8 us
    reduce_scatter x1, waiting for transfers between devices, on_device(): lax.psum_scatter(grad_wv, 'dp', scatter_dimension=0, tiled=True)  39.6 us
  transfers between devices with their start and end apart: 24, of which 16 were waited for; matrix products, arithmetic and copies ran while one was open for 30% of the time, Pallas kernels for 0%

commit v1 on v0

--- a/solution.py
+++ b/solution.py
@@ -3,10 +3,176 @@
 import jax
 import jax.numpy as jnp
 from jax import lax
+from jax.experimental import pallas as pl
+from jax.experimental.pallas import tpu as pltpu
 from jax.sharding import PartitionSpec as P
 
 D = 1024
 HD = 64
+BLK = 256
+LOG2E = 1.4426950408889634
+VMEM_LIMIT = 60 * 1024 * 1024
+
+
+def dot_ab(a, b):
+    return lax.dot_general(a, b, (((1,), (0,)), ((), ())), preferred_element_type=jnp.float32)
+
+
+def dot_abt(a, b):
+    return lax.dot_general(a, b, (((1,), (1,)), ((), ())), preferred_element_type=jnp.float32)
+
+
+def split_heads(block, heads):
+    lane_head = lax.broadcasted_iota(jnp.int32, block.shape, 1) // HD
+    zero = jnp.zeros_like(block)
+    return jnp.concatenate([jnp.where(lane_head == h, block, zero) for h in range(heads)], axis=0)
+
+
+def attn_fwd_body(low_ref, start_ref, q_ref, k_ref, v_ref, out_ref, lse_ref, vt_ref, qs_ref, acc_ref, sum_ref):
+    rows, cols = q_ref.shape
+    heads = cols // HD
+    scale = math.sqrt(HD) * LOG2E
+    for b in range(rows // BLK):
+        vt_ref[:, b * BLK : (b + 1) * BLK] = v_ref[b * BLK : (b + 1) * BLK, :].T
+
+    def one_block(i, _):
+        base = pl.multiple_of(i * BLK, BLK)
+        qs_ref[...] = split_heads(q_ref[pl.ds(base, BLK), :], heads)
+        acc_ref[...] = jnp.zeros_like(acc_ref)
+        sum_ref[...] = jnp.zeros_like(sum_ref)
+        start = jnp.concatenate([start_ref[:, pl.ds(base, BLK)]] * heads, axis=1)
+        own = lax.broadcasted_iota(jnp.int32, (1, heads * BLK), 1) % BLK + base
+
+        def step(j, causal):
+            at = pl.multiple_of(j * BLK, BLK)
+            scores = dot_abt(k_ref[pl.ds(at, BLK), :], qs_ref[...])
+            place = lax.broadcasted_iota(jnp.int32, scores.shape, 0) + at
+            keep = place >= start
+            if causal:
+                keep = keep & (place <= own)
+            probs = jnp.where(keep, jnp.exp2(scores * scale), 0.0)
+            sum_ref[...] += jnp.sum(probs, axis=0, keepdims=True)
+            probs_b = probs.astype(jnp.bfloat16)
+            for h in range(heads):
+                acc_ref[h * HD : (h + 1) * HD, :] += dot_ab(
+                    vt_ref[h * HD : (h + 1) * HD, pl.ds(at, BLK)], probs_b[:, h * BLK : (h + 1) * BLK]
+                )
+
+        lax.fori_loop(low_ref[i], i, lambda j, c: (step(j, False), c)[1], 0)
+        step(i, True)
+        total = sum_ref[...]
+        inv = 1.0 / total
+        logs = jnp.log2(total)
+        for h in range(heads):
+            lse_ref[h : h + 1, pl.ds(base, BLK)] = logs[:, h * BLK : (h + 1) * BLK]
+            acc_ref[h * HD : (h + 1) * HD, :] *= inv[:, h * BLK : (h + 1) * BLK]
+        out_ref[pl.ds(base, BLK), :] = acc_ref[...].T.astype(jnp.bfloat16)
+        return 0
+
+    lax.fori_loop(0, rows // BLK, one_block, 0)
+
+
+def vmem():
+    return pl.BlockSpec(memory_space=pltpu.VMEM)
+
+
+def attn_fwd(low, start, q, k, v):
+    rows, cols = q.shape
+    heads = cols // HD
+    return pl.pallas_call(
+        attn_fwd_body,
+        out_shape=(
+            jax.ShapeDtypeStruct((rows, cols), jnp.bfloat16),
+            jax.ShapeDtypeStruct((8, rows), jnp.float32),
+        ),
+        in_specs=[pl.BlockSpec(memory_space=pltpu.SMEM)] + [vmem()] * 4,
+        out_specs=(vmem(), vmem()),
+        scratch_shapes=[
+            pltpu.VMEM((cols, rows), jnp.bfloat16),
+            pltpu.VMEM((heads * BLK, cols), jnp.bfloat16),
+            pltpu.VMEM((cols, BLK), jnp.float32),
+            pltpu.VMEM((1, heads * BLK), jnp.float32),
+        ],
+        compiler_params=pltpu.CompilerParams(vmem_limit_bytes=VMEM_LIMIT),
+        cost_estimate=pl.CostEstimate(flops=4 * rows * rows * cols, bytes_accessed=8 * rows * cols, transcendentals=rows * rows * heads),
+        name="attn_fwd",
+    )(low, start, q, k, v)
+
+
+def attn_bwd_body(
+    low_ref, start_ref, lse_ref, q_ref, k_ref, v_ref, o_ref, g_ref,
+    dq_ref, dk_ref, dv_ref, kt_ref, qs_ref, gs_ref, dqt_ref, dk_acc, dv_acc,
+):
+    rows, cols = q_ref.shape
+    heads = cols // HD
+    root = math.sqrt(HD)
+    scale = root * LOG2E
+    for b in range(rows // BLK):
+        kt_ref[:, b * BLK : (b + 1) * BLK] = k_ref[b * BLK : (b + 1) * BLK, :].T
+    dk_acc[...] = jnp.zeros_like(dk_acc)
+    dv_acc[...] = jnp.zeros_like(dv_acc)
+
+    def one_block(i, _):
+        base = pl.multiple_of(i * BLK, BLK)
+        qs_ref[...] = split_heads(q_ref[pl.ds(base, BLK), :], heads)
+        grads = g_ref[pl.ds(base, BLK), :]
+        gs_ref[...] = split_heads(grads, heads)
+        dqt_ref[...] = jnp.zeros_like(dqt_ref)
+        start = jnp.concatenate([start_ref[:, pl.ds(base, BLK)]] * heads, axis=1)
+        own = lax.broadcasted_iota(jnp.int32, (1, heads * BLK), 1) % BLK + base
+        prod = (grads.astype(jnp.float32) * o_ref[pl.ds(base, BLK), :].astype(jnp.float32)).T
+        delta = jnp.concatenate(
+            [jnp.sum(prod[h * HD : (h + 1) * HD, :], axis=0, keepdims=True) for h in range(heads)], axis=1
+        )
+        lse = jnp.concatenate([lse_ref[h : h + 1, pl.ds(base, BLK)] for h in range(heads)], axis=1)
+
+        def step(j, causal):
+            at = pl.multiple_of(j * BLK, BLK)
+            scores = dot_abt(k_ref[pl.ds(at, BLK), :], qs_ref[...])
+            dprobs = dot_abt(v_ref[pl.ds(at, BLK), :], gs_ref[...])
+            place = lax.broadcasted_iota(jnp.int32, scores.shape, 0) + at
+            keep = place >= start
+            if causal:
+                keep = keep & (place <= own)
+            probs = jnp.where(keep, jnp.exp2(scores * scale - lse), 0.0)
+            dsc = (probs * (dprobs - delta)).astype(jnp.bfloat16)
+            dv_acc[pl.ds(at, BLK), :] += dot_ab(probs.astype(jnp.bfloat16), gs_ref[...])
+            dk_acc[pl.ds(at, BLK), :] += dot_ab(dsc, qs_ref[...])
+            for h in range(heads):
+                dqt_ref[h * HD : (h + 1) * HD, :] += dot_ab(
+                    kt_ref[h * HD : (h + 1) * HD, pl.ds(at, BLK)], dsc[:, h * BLK : (h + 1) * BLK]
+                )
+
+        lax.fori_loop(low_ref[i], i, lambda j, c: (step(j, False), c)[1], 0)
+        step(i, True)
+        dq_ref[pl.ds(base, BLK), :] = (dqt_ref[...].T * root).astype(dq_ref.dtype)
+        return 0
+
+    lax.fori_loop(0, rows // BLK, one_block, 0)
+    dk_ref[...] = (dk_acc[...] * root).astype(dk_ref.dtype)
+    dv_ref[...] = dv_acc[...].astype(dv_ref.dtype)
+
+
+def attn_bwd(low, start, lse, q, k, v, o, g):
+    rows, cols = q.shape
+    heads = cols // HD
+    return pl.pallas_call(
+        attn_bwd_body,
+        out_shape=(jax.ShapeDtypeStruct((rows, cols), jnp.bfloat16),) * 3,
+        in_specs=[pl.BlockSpec(memory_space=pltpu.SMEM)] + [vmem()] * 7,
+        out_specs=(vmem(),) * 3,
+        scratch_shapes=[
+            pltpu.VMEM((cols, rows), jnp.bfloat16),
+            pltpu.VMEM((heads * BLK, cols), jnp.bfloat16),
+            pltpu.VMEM((heads * BLK, cols), jnp.bfloat16),
+            pltpu.VMEM((cols, BLK), jnp.float32),
+            pltpu.VMEM((rows, cols), jnp.float32),
+            pltpu.VMEM((rows, cols), jnp.float32),
+        ],
+        compiler_params=pltpu.CompilerParams(vmem_limit_bytes=VMEM_LIMIT),
+        cost_estimate=pl.CostEstimate(flops=10 * rows * rows * cols, bytes_accessed=16 * rows * cols, transcendentals=rows * rows * heads),
+        name="attn_bwd",
+    )(low, start, lse, q, k, v, o, g)
 
 
 def matmul_ab(first_op, second_op):
@@ -51,9 +217,6 @@
     places = jnp.arange(group_rows, dtype=jnp.int32)
     seg_ends = jnp.cumsum(length_row, dtype=jnp.int32)
     seg_starts = seg_ends - length_row
-    segment = jnp.sum(
-        (places[:, None] >= seg_ends[None, :]).astype(jnp.int32), axis=1, dtype=jnp.int32
-    )
     seg_first = jnp.max(
         jnp.where(seg_starts[None, :] <= places[:, None], seg_starts[None, :], 0), axis=1
     )
@@ -63,7 +226,7 @@
     )
     angles = (places - seg_first).astype(jnp.float32)[:, None] * inv_freq[None, :]
     inverse = jnp.zeros((group_rows,), jnp.int32).at[order_row].set(places)
-    return (segment, places, angles, inverse)
+    return (seg_first, angles, inverse)
 
 
 def on_device(
@@ -96,11 +259,8 @@
         scale_gate, tensor_rank * hidden_cols, hidden_cols
     ) * math.sqrt(D)
     order_row = order[0]
-    segment, places, angles, inverse = layout(order_row, lengths[0])
+    seg_first, angles, inverse = layout(order_row, lengths[0])
     group_rows = order_row.shape[0]
-    block_rows = 512
-    block_count = group_rows // block_rows
-    score_scale = math.sqrt(HD)
     attn_full = (
         lax.all_gather(w_query, "dp", axis=0, tiled=True),
         lax.all_gather(w_key, "dp", axis=0, tiled=True),
@@ -124,31 +284,12 @@
         matmul_ab(packed, wv_full).astype(jnp.bfloat16).reshape(group_rows, local_heads, HD)
     )
 
-    def block_scores(start_row):
-        query_block = lax.dynamic_slice_in_dim(queries, start_row, block_rows)
-        raw_scores = (
-            jnp.einsum("qhd,khd->hqk", query_block, key_rows, preferred_element_type=jnp.float32)
-            * score_scale
-        )
-        row_ids = start_row + jnp.arange(block_rows, dtype=jnp.int32)
-        seg_block = lax.dynamic_slice_in_dim(segment, start_row, block_rows)
-        allowed = (seg_block[:, None] == segment[None, :]) & (places[None, :] <= row_ids[:, None])
-        return (query_block, jnp.where(allowed[None], raw_scores, -1e30))
-
-    def forward_block(block_id):
-        query_block, masked = block_scores(block_id * block_rows)
-        top_score = jnp.max(masked, axis=-1, keepdims=True)
-        log_total = top_score + jnp.log(
-            jnp.sum(jnp.exp(masked - top_score), axis=-1, keepdims=True)
-        )
-        probs_b = jnp.exp(masked - log_total).astype(jnp.bfloat16)
-        block_out = jnp.einsum(
-            "hqk,khd->qhd", probs_b, value_rows, preferred_element_type=jnp.float32
-        )
-        return (block_out.astype(jnp.bfloat16), log_total)
-
-    attended_blocks, log_totals = lax.map(forward_block, jnp.arange(block_count, dtype=jnp.int32))
-    attended = attended_blocks.reshape(group_rows, head_cols)
+    low = lax.slice(seg_first, (0,), (group_rows,), (BLK,)) // BLK
+    start = seg_first[None, :]
+    queries = queries.reshape(group_rows, head_cols)
+    key_rows = key_rows.reshape(group_rows, head_cols)
+    value_rows = value_rows.reshape(group_rows, head_cols)
+    attended, log_totals = attn_fwd(low, start, queries, key_rows, value_rows)
     attended_mine = lax.all_to_all(
         attended[inverse], "tensor", split_axis=0, concat_axis=1, tiled=True
     )
@@ -208,43 +349,11 @@
     grad_ba_rows = lax.all_gather(grad_ba, "tensor", axis=0, tiled=True)[order_row]
     grad_att = matmul_ab(grad_ba_rows, wo_back).astype(jnp.bfloat16)
     grad_wo = matmul_atb(grad_ba_rows, attended)
-    grad_att_h = grad_att.reshape(group_rows, local_heads, HD)
-
-    def backward_block(running, block_id):
-        grad_keys, grad_vals = running
-        start_row = block_id * block_rows
-        query_block, masked = block_scores(start_row)
-        probs_f = jnp.exp(masked - log_totals[block_id])
-        out_grad = lax.dynamic_slice_in_dim(grad_att_h, start_row, block_rows)
-        grad_probs = jnp.einsum(
-            "qhd,khd->hqk", out_grad, value_rows, preferred_element_type=jnp.float32
-        )
-        delta_row = jnp.sum(probs_f * grad_probs, axis=-1, keepdims=True)
-        grad_scores = (probs_f * (grad_probs - delta_row)).astype(jnp.bfloat16)
-        grad_query = (
-            jnp.einsum("hqk,khd->qhd", grad_scores, key_rows, preferred_element_type=jnp.float32)
-            * score_scale
-        )
-        grad_keys = (
-            grad_keys
-            + jnp.einsum(
-                "hqk,qhd->khd", grad_scores, query_block, preferred_element_type=jnp.float32
-            )
-            * score_scale
-        )
-        grad_vals = grad_vals + jnp.einsum(
-            "hqk,qhd->khd",
-            probs_f.astype(jnp.bfloat16),
-            out_grad,
-            preferred_element_type=jnp.float32,
-        )
-        return ((grad_keys, grad_vals), grad_query)
-
-    zero_heads = jnp.zeros((group_rows, local_heads, HD), jnp.float32)
-    (grad_keys, grad_vals), grad_queries = lax.scan(
-        backward_block, (zero_heads, zero_heads), jnp.arange(block_count, dtype=jnp.int32)
-    )
-    grad_queries = grad_queries.reshape(group_rows, local_heads, HD)
+    grad_queries, grad_keys, grad_vals = attn_bwd(
+        low, start, log_totals, queries, key_rows, value_rows, attended, grad_att
+    )
+    grad_queries = grad_queries.astype(jnp.float32).reshape(group_rows, local_heads, HD)
+    grad_keys = grad_keys.astype(jnp.float32).reshape(group_rows, local_heads, HD)
     grad_qs = rotate(grad_queries, angles, -1.0)
     grad_ks = rotate(grad_keys, angles, -1.0)
     grad_gain = jnp.sum(grad_qs * query_n + grad_ks * key_n, axis=0).reshape(head_cols)
@@ -290,15 +399,15 @@
     vector_sums = lax.psum(
         (grad_qk_full, grad_alpha_a, grad_su_full, grad_sv_full, grad_alpha_m), ("dp", "tensor")
     )
-    weight_sums = (
-        lax.psum_scatter(grad_wq, "dp", scatter_dimension=0, tiled=True),
-        lax.psum_scatter(grad_wk, "dp", scatter_dimension=0, tiled=True),
-        lax.psum_scatter(grad_wv, "dp", scatter_dimension=0, tiled=True),
-        lax.psum_scatter(grad_wo, "dp", scatter_dimension=0, tiled=True),
-        lax.psum_scatter(grad_wu, "dp", scatter_dimension=0, tiled=True),
-        lax.psum_scatter(grad_wg, "dp", scatter_dimension=0, tiled=True),
-        lax.psum_scatter(grad_wd, "dp", scatter_dimension=0, tiled=True),
-    )
+    mlp_sums = lax.psum_scatter(
+        jnp.concatenate([grad_wu, grad_wg, grad_wd], axis=1).astype(jnp.bfloat16), "dp", scatter_dimension=0, tiled=True
+    ).astype(jnp.float32)
+    attn_sums = lax.psum_scatter(
+        jnp.concatenate([grad_wq, grad_wk, grad_wv, grad_wo], axis=1).astype(jnp.bfloat16), "dp", scatter_dimension=0, tiled=True
+    ).astype(jnp.float32)
+    weight_sums = [attn_sums[:, i * head_cols : (i + 1) * head_cols] for i in range(4)] + [
+        mlp_sums[:, i * hidden_cols : (i + 1) * hidden_cols] for i in range(3)
+    ]
     return (
         outputs.astype(jnp.bfloat16),
         grad_tokens,

time: 1080 us -> 851 us (0.79)
  waiting for transfers between devices: 564 us -> 457 us
  matrix products: 198 us -> 96.9 us
  Pallas kernels: 0 us -> 29.1 us
  local copies, waits for them, and re-layouts: 116 us -> 94.6 us
  other arithmetic: 56.6 us -> 38.4 us
    reduce_scatter x7 -> x0, waiting for transfers between devices: 191 us -> none  [the longest x1 39.8 us: on_device(): lax.psum_scatter(grad_wk, 'dp', scatter_dimension=0, tiled=True)]
    dot_general x21 -> x0, matrix products: 88 us -> none  [the longest x6 27 us: block_scores(): jnp.einsum('qhd,khd->hqk', query_block, key_rows, preferred_element_type=...]
    all_gather x1, waiting for transfers between devices: 0.01 us -> 41 us  [on_device(): lax.all_gather(wv_back, 'tensor', axis=1, tiled=True)]
    unnamed x20 -> x17, waiting for transfers between devices: 4.53 us -> 41.8 us
    dynamic_update_slice x6 -> x0, local copies, waits for them, and re-layouts: 35.6 us -> none  [on_device(): lax.scan(backward_block, (zero_heads, zero_heads), jnp.arange(block_count...]
    pallas_call x0 -> x2, Pallas kernels: none -> 29.1 us  [the longest x1 17.8 us: attn_bwd(): pl.pallas_call(attn_bwd_body, out_shape=(jax.ShapeDtypeStruct((rows, cols...]
    unnamed x129 -> x117, local copies, waits for them, and re-layouts: 9.92 us -> 32.3 us
    all_to_all x1, waiting for transfers between devices: 11.6 us -> 29.8 us  [on_device(): lax.all_to_all(grad_kraw[inverse], 'tensor', split_axis=0, concat_axis=1,...]
  transfers between devices with their start and end apart: 24 -> 19, of which waited for: 16 -> 15; matrix products, arithmetic and copies ran while one was open for 30% -> 21% of each run, Pallas kernels for 0% -> 3%
where the time goes in v1:
time: 851 us; the launch traced here: 846 us
  waiting for transfers between devices  457 us (54%)
  matrix products  96.9 us (11%)
  local copies, waits for them, and re-layouts  94.6 us (11%)
  blocking collectives  92.7 us (11%)
  other arithmetic  38.4 us (5%)
  Pallas kernels  29.1 us (3%)
  starting transfers between devices  22.4 us (3%)
  between operations  15.2 us (2%)
    all_gather x1, waiting for transfers between devices, on_device(): lax.all_gather(middle.astype(jnp.bfloat16), 'tensor', axis=0, tiled=True)  65.5 us
    all_gather x1, waiting for transfers between devices, on_device(): grad_bm_rows = lax.all_gather(grad_bm, 'tensor', axis=0, tiled=True)  63.5 us
    reduce_scatter x1, waiting for transfers between devices, on_device(): lax.psum_scatter(matmul_abt(mixed_b, wd_full).astype(jnp.bfloat16), 'tens...  60.1 us
    reduce_scatter x1, waiting for transfers between devices, on_device(): lax.psum_scatter(back_terms.astype(jnp.bfloat16), 'tensor', scatter_dimen...  59.1 us
    psum x1, blocking collectives, on_device(): lax.psum((grad_qk_full, grad_alpha_a, grad_su_full, grad_sv_full, grad_al...  48.9 us
    dot_general x7, matrix products, matmul_ab(): return jnp.dot(first_op, second_op, preferred_element_type=jnp.float32)  43.2 us
    unnamed x17, waiting for transfers between devices  41.8 us
    all_gather x1, waiting for transfers between devices, on_device(): lax.all_gather(wv_back, 'tensor', axis=1, tiled=True)  41 us
  transfers between devices with their start and end apart: 19, of which 15 were waited for; matrix products, arithmetic and copies ran while one was open for 21% of the time, Pallas kernels for 3%

profile of v1, /device:TPU:0, one launch (start us, length us, event | category | flops | bytes accessed | tf_op | source)
XLA Modules:
  0.0 845.9 jit_solution(9022209582868004334)
XLA Ops:
  8.0 13.2 %all_gather.56 = bf16[1024,256]{1,0:T(8,128)(2,1)} all-gather(bf16[128,256]{1,0:T(8,128)(2,1)} %param.20), channel_id=1, replica_groups=mesh['dp'=8,'tensor'=4] {'dp'}, dimensions={0}, use_global_device_ids=true | all-gather | bytes 589824 | tf_op jit(solution)/shard_map/all_gather | solution.py:268
  23.6 10.0 %all_gather.54 = bf16[1024,256]{1,0:T(8,128)(2,1)} all-gather(bf16[128,256]{1,0:T(8,128)(2,1)S(1)} %copy-done.34), channel_id=1, replica_groups=mesh['dp'=8,'tensor'=4] {'dp'}, dimensions={0}, use_global_device_ids=true | all-gather | bytes 589824 | tf_op jit(solution)/shard_map/all_gather | solution.py:266
  35.0 10.7 %all_gather.53 = bf16[1024,256]{1,0:T(8,128)(2,1)} all-gather(bf16[128,256]{1,0:T(8,128)(2,1)S(1)} %copy-done.35), channel_id=1, replica_groups=mesh['dp'=8,'tensor'=4] {'dp'}, dimensions={0}, use_global_device_ids=true | all-gather | bytes 589824 | tf_op jit(solution)/shard_map/all_gather | solution.py:265
  45.7 9.9 %all_gather.55 = bf16[1024,256]{1,0:T(8,128)(2,1)} all-gather(bf16[128,256]{1,0:T(8,128)(2,1)S(1)} %copy-done.36), channel_id=1, replica_groups=mesh['dp'=8,'tensor'=4] {'dp'}, dimensions={0}, use_global_device_ids=true | all-gather | bytes 589824 | tf_op jit(solution)/shard_map/all_gather | solution.py:267
  55.6 6.4 scatter_custom_fusion
  63.4 12.4 %all-gather.12.cloned.1.call-done = bf16[1536,1024]{1,0:T(8,128)(2,1)} async-done(((bf16[384,1024]{1,0:T(8,128)(2,1)}), bf16[1536,1024]{1,0:T(8,128)(2,1)}) %all-gather.12.cloned.1.call-update) | async-done | bytes 3145744 | tf_op jit(solution)/shard_map/all_gather | solution.py:277
  75.8 9.4 %gather_fusion = bf16[1536,1024]{1,0:T(8,128)(2,1)S(1)} fusion(bf16[1536,1024]{1,0:T(8,128)(2,1)} %all-gather.12.cloned.1.call-done, s32[2048]{0:T(1024)S(1)} %pad_clamp_fusion.1), kind=kCustom, calls=%fused_computation | custom fusion | bytes 6297600 | tf_op jit(solution)/shard_map/gather | solution.py:278
  99.4 11.3 %attn_fwd.1 = (bf16[1536,256]{1,0:T(8,128)(2,1)}, f32[8,1536]{1,0:T(8,128)}) custom-call(s32[6]{0:T(128)} %and_select_fusion.low_ref, s32[1,1536]{1,0:T(1,128)} %broadcast_in_dim.17.start_ref, bf16[1536,256]{1,0:T(8,128)(2,1)} %copy.83.q_ref, bf16[1536,256]{1,0:T(8,128)(2,1)} %copy.84.k_ref, bf16[1536,256]{1,0:T(8,128)(2,1)} %convolution_convert_fusion.2.v_ref), custom_call_target="tpu_custom_call" | custom-call | flops 2415919104 | bytes 3145728 | tf_op jit(solution)/shard_map/attn_fwd/pallas_call | solution.py:82
  122.3 18.2 %all-to-all-done = bf16[4,384,256]{1,2,0:T(8,128)(2,1)S(1)} async-done(((bf16[4,384,256]{1,2,0:T(8,128)(2,1)}), bf16[4,384,256]{1,2,0:T(8,128)(2,1)S(1)}, u32[]{:S(2)}, u32[]{:S(2)}) %all-to-all-start) | async-done | bytes 786464 | tf_op jit(solution)/shard_map/all_to_all | solution.py:293
  150.2 65.5 %all-gather.16.cloned.1.call-done = bf16[1536,1024]{1,0:T(8,128)(2,1)} async-done(((bf16[384,1024]{1,0:T(8,128)(2,1)}), bf16[1536,1024]{1,0:T(8,128)(2,1)}) %all-gather.16.cloned.1.call-update) | async-done | bytes 3145744 | tf_op jit(solution)/shard_map/all_gather | solution.py:301
  215.7 8.7 %fusion.35 = f32[1536,1024]{1,0:T(8,128)} fusion(bf16[1536,1024]{1,0:T(8,128)(2,1)} %all-gather.16.cloned.1.call-done, bf16[1024,1024]{1,0:T(8,128)(2,1)} %all-gather.20.cloned.1.call-done), kind=kOutput, calls=%fused_computation.135 | convolution fusion | flops 3221225472 | bytes 11534336 | tf_op jit(solution)/shard_map/dot_general | solution.py:179
  224.3 19.5 %all-gather.18.cloned.1.call-done = bf16[1024,1024]{1,0:T(8,128)(2,1)} async-done(((bf16[128,1024]{1,0:T(8,128)(2,1)}), bf16[1024,1024]{1,0:T(8,128)(2,1)}) %all-gather.18.cloned.1.call-update) | async-done | bytes 2097168 | tf_op jit(solution)/shard_map/all_gather | solution.py:271
  243.8 12.4 %multiply_convert_fusion.2 = (bf16[1536,1024]{1,0:T(8,128)(2,1)}, f32[1536,1024]{1,0:T(8,128)}) fusion(f32[1024]{0:T(1024)S(1)} %dynamic_slice.10, f32[1536,1024]{1,0:T(8,128)} %fusion.35, f32[1024]{0:T(1024)S(1)} %dynamic-slice_multiply_fusion, bf16[1536,1024]{1,0:T(8,128)(2,1)} %all-gather.16.cloned.1.call-done, ...), kind=kOutput, calls=%fused_computation.16 | convolution fusion | flops 3233808384 | bytes 20979712 | tf_op jit(solution)/shard_map/dot_general | solution.py:179
  256.3 17.1 %all-gather.22.cloned.1.call-done = bf16[1024,1024]{1,0:T(8,128)(2,1)} async-done(((bf16[128,1024]{1,0:T(8,128)(2,1)}), bf16[1024,1024]{1,0:T(8,128)(2,1)}) %all-gather.22.cloned.1.call-update) | async-done | bytes 2097168 | tf_op jit(solution)/shard_map/all_gather | solution.py:273
  273.4 7.7 convolution_convert_fusion
  281.6 60.1 %reduce-scatter.9.cloned.1.call-done = bf16[384,1024]{1,0:T(8,128)(2,1)} async-done(((bf16[1536,1024]{1,0:T(8,128)(2,1)}), bf16[384,1024]{1,0:T(8,128)(2,1)}) %reduce-scatter.9.cloned.1.call-update) | async-done | bytes 786448 | tf_op jit(solution)/shard_map/reduce_scatter | solution.py:309
  349.0 63.5 %all-gather.24.cloned.1.call-done = bf16[1536,1024]{1,0:T(8,128)(2,1)} async-done(((bf16[384,1024]{1,0:T(8,128)(2,1)}), bf16[1536,1024]{1,0:T(8,128)(2,1)}) %all-gather.24.cloned.1.call-update) | async-done | bytes 3145744 | tf_op jit(solution)/shard_map/all_gather | solution.py:331
  412.5 12.2 %multiply_reduce_fusion = (f32[1024]{0:T(1024)}, f32[1024]{0:T(1024)}, f32[1536,1024]{1,0:T(8,128)S(1)}, bf16[1536,1024]{1,0:T(8,128)(2,1)S(1)}) fusion(f32[1536,1024]{1,0:T(8,128)} %fusion.35, f32[1536,1024]{1,0:T(8,128)} %get-tuple-element.135, f32[1024]{0:T(1024)S(1)} %dynamic-slice_multiply_fusion, f32[1024]{0:T(1024)S(1)} %dynamic_slice.10, ...), kind=kOutput, calls=%fused_computation.10 | convolution fusion | flops 3251107840 | bytes 27279360 | tf_op jit(solution)/shard_map/dot_general | solution.py:179
  433.5 59.1 %reduce-scatter.11.cloned.1.call-done = bf16[384,1024]{1,0:T(8,128)(2,1)} async-done(((bf16[1536,1024]{1,0:T(8,128)(2,1)}), bf16[384,1024]{1,0:T(8,128)(2,1)}) %reduce-scatter.11.cloned.1.call-update) | async-done | bytes 786448 | tf_op jit(solution)/shard_map/reduce_scatter | solution.py:343
  499.8 6.5 convolution_convert_fusion.3
  510.0 6.5 convolution_convert_fusion.4
  516.6 13.5 %pad_maximum_fusion = bf16[1024,3072]{0,1:T(8,128)(2,1)} fusion(bf16[1024,1024]{0,1:T(8,128)(2,1)S(1)} %convolution_convert_fusion.3, bf16[1024,1024]{0,1:T(8,128)(2,1)S(1)} %convolution_convert_fusion.4, bf16[1024,1024]{0,1:T(8,128)(2,1)S(1)} %convolution_convert_fusion.5), kind=kLoop, calls=%fused_computation.9 | loop fusion | flops 18874368 | bytes 12582912 | tf_op jit(solution)/shard_map/concatenate | solution.py:403
  530.0 8.6 %copy.104 = bf16[1024,3072]{1,0:T(8,128)(2,1)} copy(bf16[1024,3072]{0,1:T(8,128)(2,1)} %pad_maximum_fusion) | data formatting | bytes 12582912
  540.6 22.4 %all-gather.26.cloned.1.call-done = bf16[1536,1024]{1,0:T(8,128)(2,1)} async-done(((bf16[384,1024]{1,0:T(8,128)(2,1)}), bf16[1536,1024]{1,0:T(8,128)(2,1)}) %all-gather.26.cloned.1.call-update) | async-done | bytes 3145744 | tf_op jit(solution)/shard_map/all_gather | solution.py:349
  563.0 9.4 %gather_fusion.2 = bf16[1536,1024]{1,0:T(8,128)(2,1)S(1)} fusion(bf16[1536,1024]{1,0:T(8,128)(2,1)} %all-gather.26.cloned.1.call-done, s32[2048]{0:T(1024)S(1)} %pad_clamp_fusion.1), kind=kCustom, calls=%fused_computation.2 | custom fusion | bytes 6297600 | tf_op jit(solution)/shard_map/gather | solution.py:349
  575.8 17.8 %attn_bwd.1 = (bf16[1536,256]{1,0:T(8,128)(2,1)}, bf16[1536,256]{1,0:T(8,128)(2,1)}, bf16[1536,256]{1,0:T(8,128)(2,1)}) custom-call(s32[6]{0:T(128)} %and_select_fusion.low_ref, s32[1,1536]{1,0:T(1,128)} %broadcast_in_dim.17.start_ref, f32[8,1536]{1,0:T(8,128)} %get-tuple-element.20.lse_ref, bf16[1536,256]{1,0:T(8,128)(2,1)} %copy.83.q_ref, ...), custom_call_target="tpu_custom_call" | custom-call | flops 6039797760 | bytes 6291456 | tf_op jit(solution)/shard_map/attn_bwd/pallas_call | solution.py:159
  603.9 5.3 gather_fusion.3
  647.6 29.8 %all-to-all-done.2 = bf16[4,384,256]{1,2,0:T(8,128)(2,1)S(1)} async-done(((bf16[4,384,256]{1,2,0:T(8,128)(2,1)}), bf16[4,384,256]{1,2,0:T(8,128)(2,1)S(1)}, u32[]{:S(2)}, u32[]{:S(2)}) %all-to-all-start.2) | async-done | bytes 786464 | tf_op jit(solution)/shard_map/all_to_all | solution.py:376
  678.2 7.9 all-to-all-start.3
  691.3 48.9 %all-reduce = (f32[1024]{0:T(1024)}, f32[1024]{0:T(1024)}, f32[4096]{0:T(1024)}, f32[4096]{0:T(1024)}, f32[1024]{0:T(1024)}) all-reduce(f32[1024]{0:T(1024)S(1)} %dynamic_update_slice.9, f32[1024]{0:T(1024)S(1)} %copy-done.39, f32[4096]{0:T(1024)S(1)} %dynamic_update_slice.10, ...), channel_id=1, replica_groups=mesh['dp'=8,'tensor'=4] {'dp','tensor'}, use_global_device_ids=true, to_apply=%region_20.21 | all-reduce | flops 11264 | bytes 90112 | tf_op jit(solution)/shard_map/psum | solution.py:399
  751.2 41.0 %all-gather.32.cloned.1.call-done = bf16[1024,1024]{1,0:T(8,128)(2,1)} async-done(((bf16[1024,256]{1,0:T(8,128)(2,1)}), bf16[1024,1024]{1,0:T(8,128)(2,1)}) %all-gather.32.cloned.1.call-update) | async-done | bytes 2097168 | tf_op jit(solution)/shard_map/all_gather | solution.py:382
  797.0 37.7 %reduce-scatter.13.cloned.1.call-done = bf16[128,1024]{1,0:T(8,128)(2,1)} async-done(((bf16[1024,1024]{1,0:T(8,128)(2,1)}), bf16[128,1024]{1,0:T(8,128)(2,1)}) %reduce-scatter.13.cloned.1.call-update) | async-done | bytes 262160
  (238 shorter events, 148.2 us)
Async XLA Ops:
  7.2 14.8 %copy-start.49 = (s32[1,3]{1,0:T(1,128)S(1)}, s32[1,3]{1,0:T(1,128)}, u32[]{:S(2)}) copy-start(s32[1,3]{1,0:T(1,128)} %param.30) | copy-start | bytes 40
  7.2 16.3 %copy-start.43 = (s32[1,1536]{1,0:T(1,128)S(1)}, s32[1,1536]{1,0:T(1,128)}, u32[]{:S(2)}) copy-start(s32[1,1536]{1,0:T(1,128)} %param.29) | copy-start | bytes 18436
  7.2 16.4 %copy-start.34 = (bf16[128,256]{1,0:T(8,128)(2,1)S(1)}, bf16[128,256]{1,0:T(8,128)(2,1)}, u32[]{:S(2)}) copy-start(bf16[128,256]{1,0:T(8,128)(2,1)} %param.18) | copy-start | bytes 196612
  7.2 27.8 %copy-start.35 = (bf16[128,256]{1,0:T(8,128)(2,1)S(1)}, bf16[128,256]{1,0:T(8,128)(2,1)}, u32[]{:S(2)}) copy-start(bf16[128,256]{1,0:T(8,128)(2,1)} %param.17) | copy-start | bytes 196612
  7.2 38.4 %copy-start.36 = (bf16[128,256]{1,0:T(8,128)(2,1)S(1)}, bf16[128,256]{1,0:T(8,128)(2,1)}, u32[]{:S(2)}) copy-start(bf16[128,256]{1,0:T(8,128)(2,1)} %param.19) | copy-start | bytes 196612
  7.2 68.6 %all-gather.12.cloned.1.call-start = ((), (), s32[]{:S(2)}) async-start(), calls=%async_computation.8 | async-start | bytes 3932160 | tf_op jit(solution)/shard_map/all_gather | solution.py:277
  8.0 114.3 %all-gather.14.cloned.1.call-start = ((), (), s32[]{:S(2)}) async-start(), calls=%async_computation.9 | async-start | bytes 2621440 | tf_op jit(solution)/shard_map/all_gather | solution.py:296
  21.3 128.9 %all-gather.20.cloned.1.call-start = ((), (), s32[]{:S(2)}) async-start(), calls=%async_computation.12 | async-start | bytes 2359296 | tf_op jit(solution)/shard_map/all_gather | solution.py:272
  34.3 21.3 %copy-start.41 = (f32[256]{0:T(256)}, f32[256]{0:T(256)S(1)}, u32[]{:S(2)}) copy-start(f32[256]{0:T(256)S(1)} %dynamic_slice.9) | copy-start | bytes 3076
  85.2 11.3 %copy-start.2 = (bf16[1536,1024]{1,0:T(8,128)(2,1)}, bf16[1536,1024]{1,0:T(8,128)(2,1)S(1)}, u32[]{:S(2)}) copy-start(bf16[1536,1024]{1,0:T(8,128)(2,1)S(1)} %gather_fusion) | copy-start | bytes 9437188
  116.8 23.7 %all-to-all-start = ((bf16[4,384,256]{1,2,0:T(8,128)(2,1)}), bf16[4,384,256]{1,2,0:T(8,128)(2,1)S(1)}, u32[]{:S(2)}, u32[]{:S(2)}) async-start(bf16[4,384,256]{1,2,0:T(8,128)(2,1)} %copy.85), calls=%async_computation | async-start | bytes 1572864 | tf_op jit(solution)/shard_map/all_to_all | solution.py:293
  120.3 95.4 %all-gather.16.cloned.1.call-start = ((), (), s32[]{:S(2)}) async-start(), calls=%async_computation.10 | async-start | bytes 3932160 | tf_op jit(solution)/shard_map/all_gather | solution.py:301
  146.1 97.7 %all-gather.18.cloned.1.call-start = ((), (), s32[]{:S(2)}) async-start(), calls=%async_computation.11 | async-start | bytes 2359296 | tf_op jit(solution)/shard_map/all_gather | solution.py:271
  146.7 126.7 %all-gather.22.cloned.1.call-start = ((), (), s32[]{:S(2)}) async-start(), calls=%async_computation.13 | async-start | bytes 2359296 | tf_op jit(solution)/shard_map/all_gather | solution.py:273
  147.3 194.4 %reduce-scatter.9.cloned.1.call-start = ((), (), s32[]{:S(2)}) async-start(), calls=%async_computation.14 | async-start | bytes 3932160 | tf_op jit(solution)/shard_map/reduce_scatter | solution.py:309
  281.1 62.0 %copy-start.31 = (f32[1024]{0:T(1024)S(1)}, f32[1024]{0:T(1024)}, u32[]{:S(2)}) copy-start(f32[1024]{0:T(1024)} %param.28) | copy-start | bytes 12292
  281.1 131.3 %all-gather.24.cloned.1.call-start = ((), (), s32[]{:S(2)}) async-start(), calls=%async_computation.15 | async-start | bytes 3932160 | tf_op jit(solution)/shard_map/all_gather | solution.py:331
  349.0 143.7 %reduce-scatter.11.cloned.1.call-start = ((), (), s32[]{:S(2)}) async-start(), calls=%async_computation.16 | async-start | bytes 3932160 | tf_op jit(solution)/shard_map/reduce_scatter | solution.py:343
  412.5 12.2 %copy-start.48 = (bf16[1024,1024]{1,0:T(8,128)(2,1)S(1)}, bf16[1024,1024]{1,0:T(8,128)(2,1)}, u32[]{:S(2)}) copy-start(bf16[1024,1024]{1,0:T(8,128)(2,1)} %all-gather.18.cloned.1.call-done) | copy-start | bytes 6291460
  433.4 129.6 %all-gather.26.cloned.1.call-start = ((), (), s32[]{:S(2)}) async-start(), calls=%async_computation.17 | async-start | bytes 3932160 | tf_op jit(solution)/shard_map/all_gather | solution.py:349
  499.5 187.0 %reduce-scatter.15.cloned.1.call-start = ((), (), s32[]{:S(2)}) async-start(), calls=%async_computation.22 | async-start | bytes 7077888
  538.7 201.5 %all-gather.28.cloned.1.call-start = ((), (), s32[]{:S(2)}) async-start(), calls=%async_computation.18 | async-start | bytes 2621440 | tf_op jit(solution)/shard_map/all_gather | solution.py:380
  539.3 208.0 %all-gather.30.cloned.1.call-start = ((), (), s32[]{:S(2)}) async-start(), calls=%async_computation.19 | async-start | bytes 2621440 | tf_op jit(solution)/shard_map/all_gather | solution.py:381
  540.0 252.3 %all-gather.32.cloned.1.call-start = ((), (), s32[]{:S(2)}) async-start(), calls=%async_computation.20 | async-start | bytes 2621440 | tf_op jit(solution)/shard_map/all_gather | solution.py:382
  611.7 24.9 %all-to-all-start.1 = ((bf16[4,384,256]{1,2,0:T(8,128)(2,1)}), bf16[4,384,256]{1,2,0:T(8,128)(2,1)}, u32[]{:S(2)}, u32[]{:S(2)}) async-start(bf16[4,384,256]{1,2,0:T(8,128)(2,1)} %copy.90), calls=%async_computation.3 | async-start | bytes 1572864 | tf_op jit(solution)/shard_map/all_to_all | solution.py:375
  615.9 218.9 %reduce-scatter.13.cloned.1.call-start = ((), (), s32[]{:S(2)}) async-start(), calls=%async_computation.21 | async-start | bytes 2359296
  636.6 40.7 %all-to-all-start.2 = ((bf16[4,384,256]{1,2,0:T(8,128)(2,1)}), bf16[4,384,256]{1,2,0:T(8,128)(2,1)S(1)}, u32[]{:S(2)}, u32[]{:S(2)}) async-start(bf16[4,384,256]{1,2,0:T(8,128)(2,1)} %copy.93), calls=%async_computation.4 | async-start | bytes 1572864 | tf_op jit(solution)/shard_map/all_to_all | solution.py:376
  646.4 39.8 %copy-start.33 = (f32[1024]{0:T(1024)S(1)}, f32[1024]{0:T(1024)}, u32[]{:S(2)}) copy-start(f32[1024]{0:T(1024)} %param.25) | copy-start | bytes 12292
  646.4 39.8 %copy-start.45 = (f32[1024]{0:T(1024)S(1)}, f32[1024]{0:T(1024)}, u32[]{:S(2)}) copy-start(f32[1024]{0:T(1024)} %get-tuple-element.81) | copy-start | bytes 12292
  646.4 40.1 %copy-start.44 = (f32[1024]{0:T(1024)S(1)}, f32[1024]{0:T(1024)}, u32[]{:S(2)}) copy-start(f32[1024]{0:T(1024)} %get-tuple-element.80) | copy-start | bytes 12292
  678.2 114.0 %all-to-all-start.3 = ((bf16[4,384,256]{1,2,0:T(8,128)(2,1)}), bf16[4,384,256]{1,2,0:T(8,128)(2,1)S(1)}, u32[]{:S(2)}, u32[]{:S(2)}) async-start(bf16[4,384,256]{1,2,0:T(8,128)(2,1)} %copy.94), calls=%async_computation.5 | async-start | bytes 1572864 | tf_op jit(solution)/shard_map/all_to_all | solution.py:377
  747.2 45.0 %copy-start.13 = (f32[384,1024]{1,0:T(8,128)S(1)}, f32[384,1024]{1,0:T(8,128)}, u32[]{:S(2)}) copy-start(f32[384,1024]{1,0:T(8,128)} %copy-done.12) | copy-start | bytes 4718596
  (40 other events, 100.7 us)
Sparse Core Ops, SparseCore 0:
  9.6 66.1 all-gather.11
  77.4 44.8 all-gather.13
  124.2 25.9 all-gather.19
  152.2 63.4 all-gather.15
  217.4 26.4 all-gather.17
  245.6 27.7 all-gather.21
  281.3 60.3 reduce-scatter.8
  349.1 63.3 all-gather.23
  433.5 59.0 reduce-scatter.10
  499.6 63.3 all-gather.25
  566.4 60.3 reduce-scatter.14
  628.2 68.6 all-gather.27
  698.5 48.6 all-gather.29
  748.7 43.5 all-gather.31
  795.4 39.2 reduce-scatter.12

commit v2 on v1

--- a/solution.py
+++ b/solution.py
@@ -173,6 +173,473 @@
         cost_estimate=pl.CostEstimate(flops=10 * rows * rows * cols, bytes_accessed=16 * rows * cols, transcendentals=rows * rows * heads),
         name="attn_bwd",
     )(low, start, lse, q, k, v, o, g)
+
+
+MESH_ID = pl.DeviceIdType.MESH
+EPS = 1e-06
+TILE = 256
+STRIP = 64
+
+
+def flip1(index):
+    return index + 1 - 2 * lax.rem(index, 2)
+
+
+def flip2(index):
+    return index + 2 - 4 * (index // 2)
+
+
+def over(count, body):
+    lax.fori_loop(0, count, lambda i, carry: (body(i), carry)[1], 0)
+
+
+def tile_at(index, size):
+    return pl.ds(pl.multiple_of(index * size, size), size)
+
+
+def row_sum(value):
+    return jnp.sum(value, axis=-1, keepdims=True)
+
+
+def middle_body(
+    att_ref, wo_hbm, w_hbm, tok_hbm, cot_hbm, aa_ref, am_ref, su_ref, sg_ref,
+    out_ref, datt_ref, gw_hbm, gwo_hbm, dh1_ref, gaa_ref, gam_ref, gsu_ref, gsg_ref,
+    wo, wall, tok, cot, parts, mids, dbms, mid_t, dbm_t, ups, gates, mixed,
+    middle, branch, dh2, own_part, send_a, recv_a, send_d, recv_d, send_z, recv_z,
+    gw, gwo, dparts, load_sems, store_sems, hop_send, hop_recv, a2a_send, a2a_recv, d2a_send, d2a_recv, part_send, part_recv,
+):
+    d = lax.axis_index("dp")
+    t = lax.axis_index("tensor")
+    rows, width = tok.shape
+    heads_w = att_ref.shape[1]
+    hid = wall.shape[2]
+    nq = w_hbm.shape[0]
+    qrows = w_hbm.shape[2]
+    chunks = hop_send.shape[0] // 6
+    crow = rows // chunks
+    core_peer = (flip1(d), t)
+    z_peer = (d, flip1(t))
+    line = [t, flip1(t), flip2(t), 3 - t]
+
+    barrier = pltpu.get_barrier_semaphore()
+    for peer in [core_peer] + [(d, line[k]) for k in (1, 2, 3)]:
+        pl.semaphore_signal(barrier, inc=1, device_id=peer, device_id_type=MESH_ID)
+    pl.semaphore_wait(barrier, 4)
+
+    def remote(src, dst, ssem, rsem, peer):
+        return pltpu.make_async_remote_copy(
+            src_ref=src, dst_ref=dst, send_sem=ssem, recv_sem=rsem, device_id=peer, device_id_type=MESH_ID
+        )
+
+    a2a = [
+        remote(att_ref.at[tile_at(line[k], rows), :], parts.at[k - 1], a2a_send.at[k - 1], a2a_recv.at[k - 1], (d, line[k]))
+        for k in (1, 2, 3)
+    ]
+    for copy in a2a:
+        copy.start()
+    loads = [
+        pltpu.make_async_copy(wo_hbm, wo, load_sems.at[0]),
+        pltpu.make_async_copy(tok_hbm, tok, load_sems.at[1]),
+        pltpu.make_async_copy(cot_hbm, cot, load_sems.at[2]),
+    ]
+    wloads = [
+        [
+            pltpu.make_async_copy(w_hbm.at[q, m], wall.at[m, pl.ds(q * qrows, qrows), :], load_sems.at[3 + m * nq + q])
+            for q in range(nq)
+        ]
+        for m in range(3)
+    ]
+    for copy in loads + wloads[0] + wloads[1] + wloads[2]:
+        copy.start()
+
+    gsu_ref[...] = jnp.zeros_like(gsu_ref)
+    gsg_ref[...] = jnp.zeros_like(gsg_ref)
+    gam_ref[...] = jnp.zeros_like(gam_ref)
+    gaa_ref[...] = jnp.zeros_like(gaa_ref)
+
+    loads[0].wait()
+    for copy in a2a:
+        copy.wait_recv()
+
+    def project(n):
+        cols = tile_at(n, TILE)
+        total = dot_abt(att_ref[tile_at(t, rows), :], wo[cols, tile_at(t, heads_w)])
+        for k in (1, 2, 3):
+            total += dot_abt(parts[k - 1], wo[cols, tile_at(line[k], heads_w)])
+        branch[:, cols] = total
+
+    over(width // TILE, project)
+    loads[1].wait()
+
+    def hop(buf, phase, ch, kind):
+        part = pl.ds(ch * crow, crow)
+        index = (phase * chunks + ch) * 3 + kind
+        src, dst, peer = ((0, 2, z_peer), (0, 1, core_peer), (2, 3, core_peer))[kind]
+        return remote(buf.at[src, part, :], buf.at[dst, part, :], hop_send.at[index], hop_recv.at[index], peer)
+
+    def strips(ch, body):
+        over(crow // STRIP, lambda i: body(tile_at(i + ch * (crow // STRIP), STRIP)))
+
+    def unit_of(value):
+        factor = lax.rsqrt(row_sum(value * value) + EPS)
+        return value * factor, factor
+
+    def make_middle(at):
+        inputs = tok[at, :].astype(jnp.float32)
+        norm_a, factor_a = unit_of(branch[at, :])
+        mid, factor_mid = unit_of(inputs + aa_ref[...] * (norm_a - inputs))
+        return inputs, norm_a, factor_a, mid, factor_mid
+
+    def first(at):
+        mid = make_middle(at)[3]
+        middle[at, :] = mid
+        mids[0, at, :] = mid.astype(jnp.bfloat16)
+
+    for ch in range(chunks):
+        strips(ch, first)
+        hop(mids, 0, ch, 0).start()
+        hop(mids, 0, ch, 1).start()
+
+    for m in range(3):
+        for copy in wloads[m]:
+            copy.wait()
+
+    def forward_rows(slot, at, store, ready):
+        base = slot * rows
+
+        def hidden(n):
+            cols = tile_at(n, TILE)
+            x = mids[slot, at, :]
+            up = dot_ab(x, wall[0, :, cols])
+            gate_raw = dot_ab(x, wall[1, :, cols])
+            gate = gate_raw * sg_ref[:, cols]
+            silu = gate / (1.0 + jnp.exp(-gate))
+            where = pl.ds(base + at.start, at.size)
+            ups[where, cols] = up.astype(jnp.bfloat16)
+            gates[where, cols] = gate_raw.astype(jnp.bfloat16)
+            mixed[where, cols] = (up * su_ref[:, cols] * silu).astype(jnp.bfloat16)
+
+        over(hid // TILE, hidden)
+        ready()
+
+        def down(n):
+            cols = tile_at(n, TILE)
+            store(at, cols, dot_abt(mixed[pl.ds(base + at.start, at.size), :], wall[2, cols, :]))
+
+        over(width // TILE, down)
+
+    def backward_rows(slot, at, store, ready):
+        base = slot * rows
+        where = pl.ds(base + at.start, at.size)
+
+        def hidden(n):
+            cols = tile_at(n, TILE)
+            dmix = dot_ab(dbms[slot, at, :], wall[2, :, cols])
+            up_raw = ups[where, cols].astype(jnp.float32)
+            gate_raw = gates[where, cols].astype(jnp.float32)
+            gate = gate_raw * sg_ref[:, cols]
+            sig = 1.0 / (1.0 + jnp.exp(-gate))
+            d_up = dmix * (gate * sig)
+            d_gate = dmix * (up_raw * su_ref[:, cols]) * (sig * (1.0 + gate * (1.0 - sig)))
+            gsu_ref[:, cols] += jnp.sum(d_up * up_raw, axis=0, keepdims=True)
+            gsg_ref[:, cols] += jnp.sum(d_gate * gate_raw, axis=0, keepdims=True)
+            ups[where, cols] = (d_up * su_ref[:, cols]).astype(jnp.bfloat16)
+            gates[where, cols] = (d_gate * sg_ref[:, cols]).astype(jnp.bfloat16)
+
+        over(hid // TILE, hidden)
+        ready()
+
+        def down(n):
+            cols = tile_at(n, TILE)
+            store(at, cols, dot_abt(ups[where, :], wall[0, cols, :]) + dot_abt(gates[where, :], wall[1, cols, :]))
+
+        over(width // TILE, down)
+
+    def part_copy(phase, kind, ch):
+        part = pl.ds(ch * crow, crow)
+        index = (phase * 3 + kind) * chunks + ch
+        src, dst, peer = ((send_a, recv_a, core_peer), (send_d, recv_d, core_peer), (send_z, recv_z, z_peer))[kind]
+        return remote(src.at[part, :], dst.at[part, :], part_send.at[index], part_recv.at[index], peer)
+
+    everything = pl.ds(0, rows)
+
+    def nothing():
+        pass
+
+    def tensor_pass(phase, buf, rows_fn, fillers):
+        def keep_own(at, cols, value):
+            own_part[at, cols] = value
+
+        def to(ref):
+            def store(at, cols, value):
+                ref[at, cols] = value.astype(jnp.bfloat16)
+
+            return store
+
+        def to_z(at, cols, value):
+            send_z[at, cols] = (value + recv_d[at, cols].astype(jnp.float32)).astype(jnp.bfloat16)
+
+        rows_fn(0, everything, keep_own, nothing)
+        for ch in range(chunks):
+            hop(buf, phase, ch, 1).wait_recv()
+        if phase == 1:
+            for ch in range(chunks):
+                part_copy(0, 0, ch).wait_send()
+        rows_fn(1, everything, to(send_a), nothing)
+        for ch in range(chunks):
+            part_copy(phase, 0, ch).start()
+        fillers[0]()
+        for ch in range(chunks):
+            hop(buf, phase, ch, 0).wait_recv()
+            hop(buf, phase, ch, 2).start()
+            at = pl.ds(ch * crow, crow)
+            hop(buf, phase, ch, 2).wait_recv()
+            if phase == 1:
+                part_copy(0, 1, ch).wait_send()
+            rows_fn(3, at, to(send_d), nothing)
+            part_copy(phase, 1, ch).start()
+
+            def ready():
+                part_copy(phase, 1, ch).wait_recv()
+                if phase == 1:
+                    part_copy(0, 2, ch).wait_send()
+
+            rows_fn(2, at, to_z, ready)
+            part_copy(phase, 2, ch).start()
+        fillers[1]()
+
+    def transpose_into(dst, buf, slots):
+        for slot in slots:
+            for b in range(rows // 128):
+                for n in range(width // TILE):
+                    dst[n * TILE : (n + 1) * TILE, slot * rows + b * 128 : slot * rows + (b + 1) * 128] = buf[
+                        slot, b * 128 : (b + 1) * 128, n * TILE : (n + 1) * TILE
+                    ].T
+
+    tensor_pass(
+        0, mids, forward_rows,
+        [lambda: transpose_into(mid_t, mids, (0, 1)), lambda: transpose_into(mid_t, mids, (2, 3))],
+    )
+
+    loads[2].wait()
+
+    def turn(at):
+        mid = middle[at, :]
+        branch_m = own_part[at, :] + recv_a[at, :].astype(jnp.float32) + recv_z[at, :].astype(jnp.float32)
+        norm_m, factor_m = unit_of(branch_m)
+        alpha = am_ref[...]
+        y, factor_y = unit_of(mid + alpha * (norm_m - mid))
+        out_ref[at, :] = y.astype(jnp.bfloat16)
+        dy = cot[at, :].astype(jnp.float32)
+        grad = factor_y * (dy - y * row_sum(y * dy))
+        gam_ref[...] += jnp.sum(grad * (norm_m - mid), axis=0, keepdims=True)
+        back = alpha * grad
+        dbms[0, at, :] = (factor_m * (back - norm_m * row_sum(norm_m * back))).astype(jnp.bfloat16)
+        dh2[at, :] = grad - back
+
+    for ch in range(chunks):
+        part_copy(0, 0, ch).wait_recv()
+        part_copy(0, 2, ch).wait_recv()
+        strips(ch, turn)
+        hop(dbms, 1, ch, 0).start()
+        hop(dbms, 1, ch, 1).start()
+
+    def weight_grads():
+        transpose_into(dbm_t, dbms, (2, 3))
+        for m, (lhs, rhs) in enumerate(((mid_t, ups), (mid_t, gates), (dbm_t, mixed))):
+
+            def block(i):
+                q = i // (hid // TILE)
+                cols = tile_at(lax.rem(i, hid // TILE), TILE)
+                value = dot_ab(lhs[tile_at(q, TILE), :], rhs[:, cols])
+                gw[m, tile_at(q, TILE), cols] = value.astype(jnp.bfloat16)
+
+            over((width // TILE) * (hid // TILE), block)
+            for q in range(nq):
+                grad_store(m, q).start()
+
+    def grad_store(m, q):
+        return pltpu.make_async_copy(gw.at[m, pl.ds(q * qrows, qrows), :], gw_hbm.at[q, m], store_sems.at[m * nq + q])
+
+    tensor_pass(1, dbms, backward_rows, [lambda: transpose_into(dbm_t, dbms, (0, 1)), weight_grads])
+
+    def last(at):
+        inputs, norm_a, factor_a, mid, factor_mid = make_middle(at)
+        grad_mid = dh2[at, :] + own_part[at, :] + recv_a[at, :].astype(jnp.float32) + recv_z[at, :].astype(jnp.float32)
+        grad = factor_mid * (grad_mid - mid * row_sum(mid * grad_mid))
+        gaa_ref[...] += jnp.sum(grad * (norm_a - inputs), axis=0, keepdims=True)
+        back = aa_ref[...] * grad
+        dh1_ref[at, :] = grad - back
+        mids[0, at, :] = (factor_a * (back - norm_a * row_sum(norm_a * back))).astype(jnp.bfloat16)
+
+    for ch in range(chunks):
+        hop(mids, 0, ch, 0).wait_send()
+        hop(mids, 0, ch, 1).wait_send()
+        part_copy(1, 0, ch).wait_recv()
+        part_copy(1, 2, ch).wait_recv()
+        strips(ch, last)
+
+    dback = [
+        remote(dparts.at[k], datt_ref.at[tile_at(t, rows), :], d2a_send.at[k - 1], d2a_recv.at[k - 1], (d, line[k]))
+        for k in (1, 2, 3)
+    ]
+    for k in (3, 2, 1, 0):
+        value = dot_ab(mids[0], wo[:, tile_at(line[k], heads_w)]).astype(jnp.bfloat16)
+        if k:
+            dparts[k] = value
+            dback[k - 1].start()
+        else:
+            datt_ref[tile_at(t, rows), :] = value
+
+    for b in range(rows // 128):
+        for n in range(width // TILE):
+            mid_t[n * TILE : (n + 1) * TILE, b * 128 : (b + 1) * 128] = mids[
+                0, b * 128 : (b + 1) * 128, n * TILE : (n + 1) * TILE
+            ].T
+
+    def out_grad(n):
+        at = tile_at(n, TILE)
+        lhs = mid_t[at, 0:rows]
+        gwo[at, tile_at(t, heads_w)] = dot_ab(lhs, att_ref[tile_at(t, rows), :]).astype(jnp.bfloat16)
+        for k in (1, 2, 3):
+            gwo[at, tile_at(line[k], heads_w)] = dot_ab(lhs, parts[k - 1]).astype(jnp.bfloat16)
+
+    over(width // TILE, out_grad)
+    wo_store = pltpu.make_async_copy(gwo, gwo_hbm, store_sems.at[3 * nq])
+    wo_store.start()
+
+    for k in (1, 2, 3):
+        remote(
+            dparts.at[k], datt_ref.at[tile_at(line[k], rows), :], d2a_send.at[k - 1], d2a_recv.at[k - 1], (d, line[k])
+        ).wait()
+    for copy in a2a:
+        copy.wait_send()
+    for ch in range(chunks):
+        hop(mids, 0, ch, 2).wait_send()
+        for kind in range(3):
+            hop(dbms, 1, ch, kind).wait_send()
+            part_copy(1, kind, ch).wait_send()
+    for m in range(3):
+        for q in range(nq):
+            grad_store(m, q).wait()
+    wo_store.wait()
+
+
+def middle_call(chunks, attended, wo, w_parts, tokens, cotangent, alpha_a, alpha_m, su, sg):
+    rows, width = tokens.shape
+    group, heads_w = attended.shape
+    nq, _, qrows, hid = w_parts.shape
+    bf, f32 = jnp.bfloat16, jnp.float32
+    anywhere = pl.BlockSpec(memory_space=pl.ANY)
+    dma = pltpu.SemaphoreType.DMA
+    return pl.pallas_call(
+        middle_body,
+        out_shape=(
+            jax.ShapeDtypeStruct((rows, width), bf),
+            jax.ShapeDtypeStruct((group, heads_w), bf),
+            jax.ShapeDtypeStruct((nq, 3, qrows, hid), bf),
+            jax.ShapeDtypeStruct((width, width), bf),
+            jax.ShapeDtypeStruct((rows, width), f32),
+            jax.ShapeDtypeStruct((1, width), f32),
+            jax.ShapeDtypeStruct((1, width), f32),
+            jax.ShapeDtypeStruct((1, hid), f32),
+            jax.ShapeDtypeStruct((1, hid), f32),
+        ),
+        in_specs=[vmem(), anywhere, anywhere, anywhere, anywhere] + [vmem()] * 4,
+        out_specs=(vmem(), vmem(), anywhere, anywhere) + (vmem(),) * 5,
+        scratch_shapes=[
+            pltpu.VMEM((width, width), bf),
+            pltpu.VMEM((3, width, hid), bf),
+            pltpu.VMEM((rows, width), bf),
+            pltpu.VMEM((rows, width), bf),
+            pltpu.VMEM((3, rows, heads_w), bf),
+            pltpu.VMEM((4, rows, width), bf),
+            pltpu.VMEM((4, rows, width), bf),
+            pltpu.VMEM((width, 4 * rows), bf),
+            pltpu.VMEM((width, 4 * rows), bf),
+            pltpu.VMEM((4 * rows, hid), bf),
+            pltpu.VMEM((4 * rows, hid), bf),
+            pltpu.VMEM((4 * rows, hid), bf),
+            pltpu.VMEM((rows, width), f32),
+            pltpu.VMEM((rows, width), f32),
+            pltpu.VMEM((rows, width), f32),
+            pltpu.VMEM((rows, width), f32),
+        ]
+        + [pltpu.VMEM((rows, width), bf)] * 6
+        + [
+            pltpu.VMEM((3, width, hid), bf),
+            pltpu.VMEM((width, width), bf),
+            pltpu.VMEM((4, rows, heads_w), bf),
+            dma((3 + 3 * nq,)),
+            dma((3 * nq + 1,)),
+            dma((6 * chunks,)),
+            dma((6 * chunks,)),
+            dma((3,)),
+            dma((3,)),
+            dma((3,)),
+            dma((3,)),
+            dma((6 * chunks,)),
+            dma((6 * chunks,)),
+        ],
+        compiler_params=pltpu.CompilerParams(vmem_limit_bytes=67000000, collective_id=1, has_side_effects=True),
+        cost_estimate=pl.CostEstimate(flops=10**11, bytes_accessed=10**8, transcendentals=10**6),
+        name="middle",
+    )(attended, wo, w_parts, tokens, cotangent, alpha_a, alpha_m, su, sg)
+
+
+def flat(dp_index, tensor_index, tensor_count):
+    return dp_index * tensor_count + tensor_index
+
+
+def hidden_routes(dp_count, tensor_count):
+    near, far = [], []
+    for d in range(dp_count):
+        for t in range(tensor_count):
+            own = flat(d, t, tensor_count)
+            if d % 2 != t // 2:
+                near.append((own, flat(d ^ 1, t, tensor_count)))
+                far.append((own, flat(d ^ 1, t ^ 2, tensor_count)))
+            else:
+                near.append((own, flat(d, t ^ 2, tensor_count)))
+    return near, far
+
+
+def same_core_groups(dp_count):
+    return [list(range(parity, dp_count, 2)) for parity in range(2)]
+
+
+def gather_hidden(own, dp_count, tensor_count):
+    near, far = hidden_routes(dp_count, tensor_count)
+    axes = ("dp", "tensor")
+    core = lax.rem(lax.axis_index("dp"), 2)
+    home = core == lax.axis_index("tensor") // 2
+    first = lax.ppermute(own, axes, near)
+    second = lax.ppermute(own, axes, far)
+    mine = jnp.where(home, own, first)
+    other = jnp.where(home, first, second)
+    pair = jnp.where(core == 0, jnp.stack([mine, other], 1), jnp.stack([other, mine], 1))
+    kinds, _, rows, cols = pair.shape
+    return lax.all_gather(
+        pair.reshape(kinds, 2 * rows, cols), "dp", axis=0, tiled=False, axis_index_groups=same_core_groups(dp_count)
+    )
+
+
+def scatter_hidden(parts, dp_count, tensor_count):
+    near, far = hidden_routes(dp_count, tensor_count)
+    axes = ("dp", "tensor")
+    core = lax.rem(lax.axis_index("dp"), 2)
+    home = core == lax.axis_index("tensor") // 2
+    summed = lax.psum_scatter(
+        parts, "dp", scatter_dimension=0, tiled=False, axis_index_groups=same_core_groups(dp_count)
+    )
+    kinds, rows, cols = summed.shape
+    halves = summed.reshape(kinds, 2, rows // 2, cols)
+    mine = jnp.where(core == 0, halves[:, 0], halves[:, 1])
+    other = jnp.where(core == 0, halves[:, 1], halves[:, 0])
+    first = lax.ppermute(jnp.where(home, other, mine), axes, [(b, a) for a, b in near])
+    second = lax.ppermute(other, axes, [(b, a) for a, b in far])
+    f32 = jnp.float32
+    return jnp.where(home, mine.astype(f32), second.astype(f32)) + first.astype(f32)
 
 
 def matmul_ab(first_op, second_op):
@@ -254,10 +721,12 @@
     qk_gains = lax.dynamic_slice_in_dim(scale_qk, tensor_rank * head_cols, head_cols).reshape(
         local_heads, HD
     )
-    up_gains = lax.dynamic_slice_in_dim(scale_up, tensor_rank * hidden_cols, hidden_cols)
+    dp_count, tensor_count = lax.axis_size("dp"), lax.axis_size("tensor")
+    hidden_rank = lax.rem(tensor_rank, 2) + 2 * lax.rem(lax.axis_index("dp"), 2)
+    up_gains = lax.dynamic_slice_in_dim(scale_up, hidden_rank * hidden_cols, hidden_cols)[None, :]
     gate_gains = lax.dynamic_slice_in_dim(
-        scale_gate, tensor_rank * hidden_cols, hidden_cols
-    ) * math.sqrt(D)
+        scale_gate, hidden_rank * hidden_cols, hidden_cols
+    )[None, :] * math.sqrt(D)
     order_row = order[0]
     seg_first, angles, inverse = layout(order_row, lengths[0])
     group_rows = order_row.shape[0]
@@ -267,13 +736,8 @@
         lax.all_gather(w_value, "dp", axis=0, tiled=True),
         lax.all_gather(w_out_t, "dp", axis=0, tiled=True),
     )
-    mlp_full = (
-        lax.all_gather(w_up, "dp", axis=0, tiled=True),
-        lax.all_gather(w_gate, "dp", axis=0, tiled=True),
-        lax.all_gather(w_down_t, "dp", axis=0, tiled=True),
-    )
     wq_full, wk_full, wv_full, wo_full = attn_full
-    wu_full, wg_full, wd_full = mlp_full
+    mlp_parts = gather_hidden(jnp.stack([w_up, w_gate, w_down_t]), dp_count, tensor_count)
     gathered = lax.all_gather(tokens, "tensor", axis=0, tiled=True)
     packed = gathered[order_row]
     query_n, query_f = unit_pair(matmul_ab(packed, wq_full).reshape(group_rows, local_heads, HD))
@@ -290,65 +754,20 @@
     key_rows = key_rows.reshape(group_rows, head_cols)
     value_rows = value_rows.reshape(group_rows, head_cols)
     attended, log_totals = attn_fwd(low, start, queries, key_rows, value_rows)
-    attended_mine = lax.all_to_all(
-        attended[inverse], "tensor", split_axis=0, concat_axis=1, tiled=True
-    )
     wo_every = lax.all_gather(wo_full, "tensor", axis=1, tiled=True)
-    branch_a = matmul_abt(attended_mine, wo_every)
-    inputs_f = tokens.astype(jnp.float32)
-    norm_a, factor_a = unit_pair(branch_a)
-    middle, factor_mid = unit_pair(inputs_f + alpha_attn * (norm_a - inputs_f))
-    middle_rows = lax.all_gather(middle.astype(jnp.bfloat16), "tensor", axis=0, tiled=True)
-    up_raw = matmul_ab(middle_rows, wu_full)
-    gate_raw = matmul_ab(middle_rows, wg_full)
-    up_proj = up_raw * up_gains
-    gate_proj = gate_raw * gate_gains
-    sigmoid_g = jax.nn.sigmoid(gate_proj)
-    silu_g = jax.nn.silu(gate_proj)
-    mixed_b = (up_proj * silu_g).astype(jnp.bfloat16)
-    branch_m = lax.psum_scatter(
-        matmul_abt(mixed_b, wd_full).astype(jnp.bfloat16), "tensor", scatter_dimension=0, tiled=True
-    ).astype(jnp.float32)
-    norm_m, factor_m = unit_pair(branch_m)
-    outputs, factor_out = unit_pair(middle + alpha_mlp * (norm_m - middle))
-    mlp_back = (
-        lax.all_gather(w_up, "dp", axis=0, tiled=True),
-        lax.all_gather(w_gate, "dp", axis=0, tiled=True),
-        lax.all_gather(w_down_t, "dp", axis=0, tiled=True),
-    )
-    attn_back = (
-        lax.all_gather(w_query, "dp", axis=0, tiled=True),
-        lax.all_gather(w_key, "dp", axis=0, tiled=True),
-        lax.all_gather(w_value, "dp", axis=0, tiled=True),
-        lax.all_gather(w_out_t, "dp", axis=0, tiled=True),
-    )
-    wu_back, wg_back, wd_back = mlp_back
-    wq_back, wk_back, wv_back, wo_back = attn_back
-    grad_out = cotangent.astype(jnp.float32)
-    grad_h2 = unit_back(outputs, factor_out, grad_out)
-    grad_alpha_m = jnp.sum(grad_h2 * (norm_m - middle), axis=0)
-    grad_bm = unit_back(norm_m, factor_m, alpha_mlp * grad_h2).astype(jnp.bfloat16)
-    grad_bm_rows = lax.all_gather(grad_bm, "tensor", axis=0, tiled=True)
-    grad_mixed = matmul_ab(grad_bm_rows, wd_back)
-    grad_wd = matmul_atb(grad_bm_rows, mixed_b)
-    grad_upp = grad_mixed * silu_g
-    grad_gatep = grad_mixed * up_proj * sigmoid_g * (1.0 + gate_proj * (1.0 - sigmoid_g))
-    grad_su = jnp.sum(grad_upp * up_raw, axis=0)
-    grad_sv = jnp.sum(grad_gatep * gate_raw, axis=0) * math.sqrt(D)
-    grad_up_b = (grad_upp * up_gains).astype(jnp.bfloat16)
-    grad_gate_b = (grad_gatep * gate_gains).astype(jnp.bfloat16)
-    grad_wu = matmul_atb(middle_rows, grad_up_b)
-    grad_wg = matmul_atb(middle_rows, grad_gate_b)
-    back_terms = matmul_abt(grad_up_b, wu_back) + matmul_abt(grad_gate_b, wg_back)
-    grad_middle = (1.0 - alpha_mlp) * grad_h2 + lax.psum_scatter(
-        back_terms.astype(jnp.bfloat16), "tensor", scatter_dimension=0, tiled=True
-    ).astype(jnp.float32)
-    grad_h1 = unit_back(middle, factor_mid, grad_middle)
-    grad_alpha_a = jnp.sum(grad_h1 * (norm_a - inputs_f), axis=0)
-    grad_ba = unit_back(norm_a, factor_a, alpha_attn * grad_h1).astype(jnp.bfloat16)
-    grad_ba_rows = lax.all_gather(grad_ba, "tensor", axis=0, tiled=True)[order_row]
-    grad_att = matmul_ab(grad_ba_rows, wo_back).astype(jnp.bfloat16)
-    grad_wo = matmul_atb(grad_ba_rows, attended)
+    out_rows, grad_att_rows, mlp_grads, wo_grads, grad_h1_kept, grad_alpha_a, grad_alpha_m, grad_su, grad_sv = middle_call(
+        2,
+        attended[inverse],
+        wo_every,
+        mlp_parts,
+        tokens,
+        cotangent,
+        alpha_attn[None, :],
+        alpha_mlp[None, :],
+        up_gains,
+        gate_gains,
+    )
+    grad_att = grad_att_rows[order_row]
     grad_queries, grad_keys, grad_vals = attn_bwd(
         low, start, log_totals, queries, key_rows, value_rows, attended, grad_att
     )
@@ -371,45 +790,34 @@
     grad_wq = matmul_atb(packed, grad_qraw)
     grad_wk = matmul_atb(packed, grad_kraw)
     grad_wv = matmul_atb(packed, grad_vraw)
-    query_mine, key_mine, value_mine = (
-        lax.all_to_all(grad_qraw[inverse], "tensor", split_axis=0, concat_axis=1, tiled=True),
-        lax.all_to_all(grad_kraw[inverse], "tensor", split_axis=0, concat_axis=1, tiled=True),
-        lax.all_to_all(grad_vraw[inverse], "tensor", split_axis=0, concat_axis=1, tiled=True),
-    )
-    wq_every, wk_every, wv_every = (
-        lax.all_gather(wq_back, "tensor", axis=1, tiled=True),
-        lax.all_gather(wk_back, "tensor", axis=1, tiled=True),
-        lax.all_gather(wv_back, "tensor", axis=1, tiled=True),
-    )
-    attn_part = (
-        matmul_abt(query_mine, wq_every)
-        + matmul_abt(key_mine, wk_every)
-        + matmul_abt(value_mine, wv_every)
-    )
-    grad_tokens = (1.0 - alpha_attn) * grad_h1 + attn_part
+    back_rows = jnp.concatenate([grad_qraw, grad_kraw, grad_vraw], axis=1)[inverse]
+    back_weights = jnp.concatenate([wq_full, wk_full, wv_full], axis=1)
+    attn_part = lax.psum_scatter(
+        matmul_abt(back_rows, back_weights).astype(jnp.bfloat16), "tensor", scatter_dimension=0, tiled=True
+    ).astype(jnp.float32)
+    grad_tokens = grad_h1_kept + attn_part
     grad_qk_full = lax.dynamic_update_slice_in_dim(
         jnp.zeros(scale_qk.shape, jnp.float32), grad_gain, tensor_rank * head_cols, 0
     )
     grad_su_full = lax.dynamic_update_slice_in_dim(
-        jnp.zeros(scale_up.shape, jnp.float32), grad_su, tensor_rank * hidden_cols, 0
+        jnp.zeros(scale_up.shape, jnp.float32), grad_su[0], hidden_rank * hidden_cols, 0
     )
     grad_sv_full = lax.dynamic_update_slice_in_dim(
-        jnp.zeros(scale_gate.shape, jnp.float32), grad_sv, tensor_rank * hidden_cols, 0
+        jnp.zeros(scale_gate.shape, jnp.float32), grad_sv[0] * math.sqrt(D), hidden_rank * hidden_cols, 0
     )
     vector_sums = lax.psum(
-        (grad_qk_full, grad_alpha_a, grad_su_full, grad_sv_full, grad_alpha_m), ("dp", "tensor")
-    )
-    mlp_sums = lax.psum_scatter(
-        jnp.concatenate([grad_wu, grad_wg, grad_wd], axis=1).astype(jnp.bfloat16), "dp", scatter_dimension=0, tiled=True
+        (grad_qk_full, grad_alpha_a[0], grad_su_full, grad_sv_full, grad_alpha_m[0]), ("dp", "tensor")
+    )
+    mlp_sums = scatter_hidden(mlp_grads, dp_count, tensor_count)
+    attn_sums = lax.psum_scatter(
+        jnp.concatenate([grad_wq, grad_wk, grad_wv], axis=1).astype(jnp.bfloat16), "dp", scatter_dimension=0, tiled=True
     ).astype(jnp.float32)
-    attn_sums = lax.psum_scatter(
-        jnp.concatenate([grad_wq, grad_wk, grad_wv, grad_wo], axis=1).astype(jnp.bfloat16), "dp", scatter_dimension=0, tiled=True
+    wo_sums = lax.psum_scatter(
+        lax.psum_scatter(wo_grads, "dp", scatter_dimension=0, tiled=True), "tensor", scatter_dimension=1, tiled=True
     ).astype(jnp.float32)
-    weight_sums = [attn_sums[:, i * head_cols : (i + 1) * head_cols] for i in range(4)] + [
-        mlp_sums[:, i * hidden_cols : (i + 1) * hidden_cols] for i in range(3)
-    ]
+    weight_sums = [attn_sums[:, i * head_cols : (i + 1) * head_cols] for i in range(3)] + [wo_sums, *mlp_sums]
     return (
-        outputs.astype(jnp.bfloat16),
+        out_rows,
         grad_tokens,
         weight_sums[0],
         weight_sums[1],

time: 851 us -> 618 us (0.73)
  waiting for transfers between devices: 457 us -> 156 us
  Pallas kernels: 29.1 us -> 164 us
  matrix products: 96.9 us -> 15.7 us
  blocking collectives: 92.7 us -> 141 us
  starting transfers between devices: 22.4 us -> 8.48 us
  local copies, waits for them, and re-layouts: 94.6 us -> 81.3 us
    all_gather x9 -> x1, waiting for transfers between devices: 233 us -> 37.4 us  [gather_hidden(): lax.all_gather(pair.reshape(kinds, 2 * rows, cols), 'dp', axis=0, tiled=F...]
    pallas_call x0 -> x1, Pallas kernels: none -> 135 us  [middle_call(): pl.pallas_call(middle_body, out_shape=(jax.ShapeDtypeStruct((rows, width)...]
    reduce_scatter x2 -> x3, waiting for transfers between devices: 119 us -> 55.4 us  [the longest x1 55.4 us: on_device(): lax.psum_scatter(matmul_abt(back_rows, back_weights).astype(jnp.bfloat16)...]
    all_to_all x4 -> x0, waiting for transfers between devices: 47.9 us -> none  [the longest x1 29.8 us: on_device(): lax.all_to_all(grad_kraw[inverse], 'tensor', split_axis=0, concat_axis=1,...]
    all_gather x1, blocking collectives: 9.95 us -> 52.8 us  [on_device(): lax.all_gather(w_key, 'dp', axis=0, tiled=True)]
    dot_general x7 -> x3, matrix products: 43.2 us -> 6.48 us  [matmul_ab(): return jnp.dot(first_op, second_op, preferred_element_type=jnp.float32)]
    ppermute x0 -> x4, waiting for transfers between devices: none -> 33.7 us  [the longest x1 33.7 us: gather_hidden(): first = lax.ppermute(own, axes, near)]
    dot_general x7 -> x1, matrix products: 31.7 us -> 6.11 us  [matmul_abt(): lax.dot_general(first_op, second_op, (((1,), (1,)), ((), ())), preferred_...]
  transfers between devices with their start and end apart: 19 -> 12, of which waited for: 15 -> 4; matrix products, arithmetic and copies ran while one was open for 21% -> 20% of each run, Pallas kernels for 3% -> 5%
where the time goes in v2:
time: 618 us; the launch traced here: 611 us
  Pallas kernels  164 us (27%)
  waiting for transfers between devices  156 us (25%)
  blocking collectives  141 us (23%)
  local copies, waits for them, and re-layouts  81.3 us (13%)
  other arithmetic  30.5 us (5%)
  matrix products  15.7 us (3%)
  between operations  14.9 us (2%)
  starting transfers between devices  8.48 us (1%)
    pallas_call x1, Pallas kernels, middle_call(): pl.pallas_call(middle_body, out_shape=(jax.ShapeDtypeStruct((rows, width)...  135 us
    reduce_scatter x1, waiting for transfers between devices, on_device(): lax.psum_scatter(matmul_abt(back_rows, back_weights).astype(jnp.bfloat16)...  55.4 us
    psum x1, blocking collectives, on_device(): lax.psum((grad_qk_full, grad_alpha_a[0], grad_su_full, grad_sv_full, grad...  54.5 us
    all_gather x1, blocking collectives, on_device(): lax.all_gather(w_key, 'dp', axis=0, tiled=True)  52.8 us
    all_gather x1, waiting for transfers between devices, gather_hidden(): lax.all_gather(pair.reshape(kinds, 2 * rows, cols), 'dp', axis=0, tiled=F...  37.4 us
    ppermute x1, waiting for transfers between devices, gather_hidden(): first = lax.ppermute(own, axes, near)  33.7 us
    unnamed x10, waiting for transfers between devices  29.4 us
    pallas_call x1, Pallas kernels, attn_bwd(): pl.pallas_call(attn_bwd_body, out_shape=(jax.ShapeDtypeStruct((rows, cols...  17.3 us
  transfers between devices with their start and end apart: 12, of which 4 were waited for; matrix products, arithmetic and copies ran while one was open for 20% of the time, Pallas kernels for 5%

profile of v2, /device:TPU:0, one launch (start us, length us, event | category | flops | bytes accessed | tf_op | source)
XLA Modules:
  0.0 611.5 jit_solution(11087620495503572062)
XLA Ops:
  8.0 13.2 %all_gather.25 = bf16[1024,256]{1,0:T(8,128)(2,1)} all-gather(bf16[128,256]{1,0:T(8,128)(2,1)} %param.20), channel_id=1, replica_groups=mesh['dp'=8,'tensor'=4] {'dp'}, dimensions={0}, use_global_device_ids=true | all-gather | bytes 589824 | tf_op jit(solution)/shard_map/all_gather | solution.py:737
  21.4 2.7 collective-permute-start
  24.8 33.7 %collective-permute-done = bf16[3,128,1024]{2,1,0:T(8,128)(2,1)S(1)} collective-permute-done((bf16[3,128,1024]{2,1,0:T(8,128)(2,1)S(1)}, bf16[3,128,1024]{2,1,0:T(8,128)(2,1)S(1)}, u32[]{:S(2)}, u32[]{:S(2)}) %collective-permute-start) | collective-permute-done | bytes 786464 | tf_op jit(solution)/shard_map/ppermute | solution.py:616
  63.3 6.2 %scatter_custom_fusion = s32[1536]{0:T(1024)S(1)} fusion(s32[1536]{0:T(1024)S(1)} %fusion.17, s32[1536]{0:T(1024)S(1)} %iota.17, s32[]{:T(128)} %constant.49.clone.1), kind=kCustom, calls=%fused_computation.78 | custom fusion | bytes 6148 | tf_op jit(solution)/shard_map/scatter | solution.py:695
  72.1 52.8 %all_gather.23 = bf16[1024,256]{1,0:T(8,128)(2,1)} all-gather(bf16[128,256]{1,0:T(8,128)(2,1)S(1)} %copy-done.34), channel_id=1, replica_groups=mesh['dp'=8,'tensor'=4] {'dp'}, dimensions={0}, use_global_device_ids=true | all-gather | bytes 589824 | tf_op jit(solution)/shard_map/all_gather | solution.py:735
  124.9 9.9 %all_gather.22 = bf16[1024,256]{1,0:T(8,128)(2,1)} all-gather(bf16[128,256]{1,0:T(8,128)(2,1)S(1)} %copy-done.35), channel_id=1, replica_groups=mesh['dp'=8,'tensor'=4] {'dp'}, dimensions={0}, use_global_device_ids=true | all-gather | bytes 589824 | tf_op jit(solution)/shard_map/all_gather | solution.py:734
  134.9 10.7 %all_gather.24 = bf16[1024,256]{1,0:T(8,128)(2,1)} all-gather(bf16[128,256]{1,0:T(8,128)(2,1)S(1)} %copy-done.36), channel_id=1, replica_groups=mesh['dp'=8,'tensor'=4] {'dp'}, dimensions={0}, use_global_device_ids=true | all-gather | bytes 589824 | tf_op jit(solution)/shard_map/all_gather | solution.py:736
  147.5 9.7 %gather_fusion = bf16[1536,1024]{1,0:T(8,128)(2,1)S(1)} fusion(bf16[1536,1024]{1,0:T(8,128)(2,1)} %all-gather.4.cloned.1.call-done, s32[2048]{0:T(1024)S(1)} %pad_clamp_fusion.1), kind=kCustom, calls=%fused_computation | custom fusion | bytes 6297600 | tf_op jit(solution)/shard_map/gather | solution.py:742
  157.3 2.5 multiply_reduce_fusion.2
  168.7 2.9 convolution_convert_fusion.1.v_ref
  171.6 11.3 %attn_fwd.1 = (bf16[1536,256]{1,0:T(8,128)(2,1)}, f32[8,1536]{1,0:T(8,128)}) custom-call(s32[6]{0:T(128)} %and_select_fusion.low_ref, s32[1,1536]{1,0:T(1,128)} %broadcast_in_dim.23.start_ref, bf16[1536,256]{1,0:T(8,128)(2,1)} %copy.88.q_ref, bf16[1536,256]{1,0:T(8,128)(2,1)} %copy.89.k_ref, bf16[1536,256]{1,0:T(8,128)(2,1)} %convolution_convert_fusion.1.v_ref), custom_call_target="tpu_custom_call" | custom-call | flops 2415919104 | bytes 3145728 | tf_op jit(solution)/shard_map/attn_fwd/pallas_call | solution.py:82
  182.9 5.7 gather_fusion.1
  188.7 37.4 %all-gather.8.cloned.1.call-done.w_hbm = bf16[4,3,256,1024]{3,2,1,0:T(8,128)(2,1)} async-done(((bf16[1,3,256,1024]{3,2,1,0:T(8,128)(2,1)}), bf16[4,3,256,1024]{3,2,1,0:T(8,128)(2,1)}) %all-gather.8.cloned.1.call-update) | async-done | bytes 6291472 | tf_op jit(solution)/shard_map/all_gather | solution.py:622
  226.1 134.9 %middle.1 = (bf16[384,1024]{1,0:T(8,128)(2,1)}, bf16[1536,256]{1,0:T(8,128)(2,1)}, bf16[4,3,256,1024]{3,2,1,0:T(8,128)(2,1)}, bf16[1024,1024]{1,0:T(8,128)(2,1)}...) custom-call(bf16[1536,256]{1,0:T(8,128)(2,1)} %gather_fusion.1, ...), custom_call_target="tpu_custom_call" | custom-call | flops 99999997952 | bytes 100000000 | tf_op jit(solution)/shard_map/middle/pallas_call | solution.py:535
  369.0 3.3 copy.98
  372.3 5.5 gather_fusion.2
  377.8 17.3 %attn_bwd.1 = (bf16[1536,256]{1,0:T(8,128)(2,1)}, bf16[1536,256]{1,0:T(8,128)(2,1)}, bf16[1536,256]{1,0:T(8,128)(2,1)}) custom-call(s32[6]{0:T(128)} %and_select_fusion.low_ref, s32[1,1536]{1,0:T(1,128)} %broadcast_in_dim.23.start_ref, f32[8,1536]{1,0:T(8,128)} %get-tuple-element.31.lse_ref, bf16[1536,256]{1,0:T(8,128)(2,1)} %copy.88.q_ref, ...), custom_call_target="tpu_custom_call" | custom-call | flops 6039797760 | bytes 6291456 | tf_op jit(solution)/shard_map/attn_bwd/pallas_call | solution.py:159
  395.1 2.6 copy.93
  399.2 3.7 multiply_subtract_fusion.1
  404.4 3.1 copy.103
  407.5 2.9 fusion.1
  410.4 3.3 copy.97
  415.0 3.1 copy.94
  419.8 5.5 add_reduce_fusion
  433.2 5.6 gather_fusion.3
  439.2 6.1 convolution_convert_fusion
  445.3 28.1 %reduce-scatter.18.cloned.1.call-done = bf16[1,3,256,1024]{3,2,1,0:T(8,128)(2,1)} async-done(((bf16[4,3,256,1024]{3,2,1,0:T(8,128)(2,1)}), bf16[1,3,256,1024]{3,2,1,0:T(8,128)(2,1)}) %reduce-scatter.18.cloned.1.call-update) | async-done | bytes 1572880
  473.4 2.6 bitcast_select_fusion
  476.8 3.8 collective-permute-start.3
  481.4 54.5 %all-reduce.1 = (f32[1024]{0:T(1024)}, f32[1024]{0:T(1024)}, f32[4096]{0:T(1024)}, f32[4096]{0:T(1024)}, f32[1024]{0:T(1024)}) all-reduce(f32[1024]{0:T(1024)S(1)} %dynamic_update_slice.9, f32[1024]{0:T(1024)S(1)} %bitcast.113, f32[4096]{0:T(1024)S(1)} %dynamic_update_slice.10, ...), channel_id=1, replica_groups=mesh['dp'=8,'tensor'=4] {'dp','tensor'}, use_global_device_ids=true, to_apply=%region_13.14 | all-reduce | flops 11264 | bytes 90112 | tf_op jit(solution)/shard_map/psum | solution.py:808
  543.4 55.4 %reduce-scatter.10.cloned.1.call-done = bf16[384,1024]{1,0:T(8,128)(2,1)} async-done(((bf16[1536,1024]{1,0:T(8,128)(2,1)}), bf16[384,1024]{1,0:T(8,128)(2,1)}) %reduce-scatter.10.cloned.1.call-update) | async-done | bytes 786448 | tf_op jit(solution)/shard_map/reduce_scatter | solution.py:795
  598.8 2.6 convert_add_fusion.1
  (182 shorter events, 53.8 us)
Async XLA Ops:
  7.2 14.1 %copy-start.23 = (bf16[128,1024]{1,0:T(8,128)(2,1)S(1)}, bf16[128,1024]{1,0:T(8,128)(2,1)}, u32[]{:S(2)}) copy-start(bf16[128,1024]{1,0:T(8,128)(2,1)} %param.21) | copy-start | bytes 786436
  7.2 14.1 %copy-start.22 = (bf16[128,1024]{1,0:T(8,128)(2,1)S(1)}, bf16[128,1024]{1,0:T(8,128)(2,1)}, u32[]{:S(2)}) copy-start(bf16[128,1024]{1,0:T(8,128)(2,1)} %param.22) | copy-start | bytes 786436
  7.2 14.1 %copy-start.21 = (bf16[128,1024]{1,0:T(8,128)(2,1)S(1)}, bf16[128,1024]{1,0:T(8,128)(2,1)}, u32[]{:S(2)}) copy-start(bf16[128,1024]{1,0:T(8,128)(2,1)} %param.23) | copy-start | bytes 786436
  7.2 140.3 %all-gather.4.cloned.1.call-start = ((), (), s32[]{:S(2)}) async-start(), calls=%async_computation.5 | async-start | bytes 3932160 | tf_op jit(solution)/shard_map/all_gather | solution.py:741
  7.9 180.8 %all-gather.6.cloned.1.call-start = ((), (), s32[]{:S(2)}) async-start(), calls=%async_computation.6 | async-start | bytes 2621440 | tf_op jit(solution)/shard_map/all_gather | solution.py:757
  21.2 204.9 %all-gather.8.cloned.1.call-start = ((), (), s32[]{:S(2)}) async-start(), calls=%async_computation.7 | async-start | bytes 7864320 | tf_op jit(solution)/shard_map/all_gather | solution.py:622
  21.4 37.1 %collective-permute-start = (bf16[3,128,1024]{2,1,0:T(8,128)(2,1)S(1)}, bf16[3,128,1024]{2,1,0:T(8,128)(2,1)S(1)}, u32[]{:S(2)}, u32[]{:S(2)}) collective-permute-start(bf16[3,128,1024]{2,1,0:T(8,128)(2,1)S(1)} %pad_maximum_fusion.6), channel_id=1, source_target_pairs={{0,2},{1,3},{2,6},{3,7},{4,0},{5,1},{6,4},{7,5},{8,10},{9,11},{10,... | collective-permute-start | bytes 2359304 | tf_op jit(solution)/shard_map/ppermute | solution.py:616
  24.1 34.5 %collective-permute-start.1 = (bf16[3,128,1024]{2,1,0:T(8,128)(2,1)S(1)}, bf16[3,128,1024]{2,1,0:T(8,128)(2,1)S(1)}, u32[]{:S(2)}, u32[]{:S(2)}) collective-permute-start(bf16[3,128,1024]{2,1,0:T(8,128)(2,1)S(1)} %pad_maximum_fusion.6), channel_id=1, source_target_pairs={{2,4},{3,5},{4,2},{5,3},{10,12},{11,13},{12,10},{13,11},{18,20},{1... | collective-permute-start | bytes 2359304 | tf_op jit(solution)/shard_map/ppermute | solution.py:617
  60.2 11.9 %copy-start.34 = (bf16[128,256]{1,0:T(8,128)(2,1)S(1)}, bf16[128,256]{1,0:T(8,128)(2,1)}, u32[]{:S(2)}) copy-start(bf16[128,256]{1,0:T(8,128)(2,1)} %param.18) | copy-start | bytes 196612
  60.2 64.7 %copy-start.35 = (bf16[128,256]{1,0:T(8,128)(2,1)S(1)}, bf16[128,256]{1,0:T(8,128)(2,1)}, u32[]{:S(2)}) copy-start(bf16[128,256]{1,0:T(8,128)(2,1)} %param.17) | copy-start | bytes 196612
  60.2 74.6 %copy-start.36 = (bf16[128,256]{1,0:T(8,128)(2,1)S(1)}, bf16[128,256]{1,0:T(8,128)(2,1)}, u32[]{:S(2)}) copy-start(bf16[128,256]{1,0:T(8,128)(2,1)} %param.19) | copy-start | bytes 196612
  60.3 378.6 %reduce-scatter.12.cloned.1.call-start = ((), (), s32[]{:S(2)}) async-start(), calls=%async_computation.9 | async-start | bytes 2359296 | tf_op jit(solution)/shard_map/reduce_scatter | solution.py:816
  147.5 14.6 %copy-start.18 = (f32[1536,32]{0,1:T(8,128)}, f32[1536,32]{0,1:T(8,128)S(1)}, u32[]{:S(2)}) copy-start(f32[1536,32]{0,1:T(8,128)S(1)} %get-tuple-element.130) | copy-start | bytes 589828
  157.3 11.4 %copy-start.1 = (bf16[1536,1024]{1,0:T(8,128)(2,1)}, bf16[1536,1024]{1,0:T(8,128)(2,1)S(1)}, u32[]{:S(2)}) copy-start(bf16[1536,1024]{1,0:T(8,128)(2,1)S(1)} %gather_fusion) | copy-start | bytes 9437188
  361.1 112.3 %reduce-scatter.18.cloned.1.call-start = ((), (), s32[]{:S(2)}) async-start(), calls=%async_computation.12 | async-start | bytes 7864320
  361.7 174.3 %reduce-scatter.16.cloned.1.call-start = ((), (), s32[]{:S(2)}) async-start(), calls=%async_computation.11 | async-start | bytes 1769472
  369.0 3.3 copy-start
  399.1 3.7 copy-start.7
  399.2 3.7 copy-start.33
  399.2 3.7 copy-start.38
  419.8 5.5 copy-start.2
  430.5 111.4 %reduce-scatter.14.cloned.1.call-start = ((), (), s32[]{:S(2)}) async-start(), calls=%async_computation.10 | async-start | bytes 327680 | tf_op jit(solution)/shard_map/reduce_scatter | solution.py:815
  433.2 6.0 copy-start.15
  433.2 6.0 copy-start.17
  438.9 159.9 %reduce-scatter.10.cloned.1.call-start = ((), (), s32[]{:S(2)}) async-start(), calls=%async_computation.8 | async-start | bytes 3932160 | tf_op jit(solution)/shard_map/reduce_scatter | solution.py:795
  473.4 7.4 %copy-start.43 = (f32[1,1024]{1,0:T(1,128)S(1)}, f32[1,1024]{1,0:T(1,128)}, u32[]{:S(2)}) copy-start(f32[1,1024]{1,0:T(1,128)} %get-tuple-element.40) | copy-start | bytes 12292
  473.4 7.7 %copy-start.42 = (f32[1,1024]{1,0:T(1,128)S(1)}, f32[1,1024]{1,0:T(1,128)}, u32[]{:S(2)}) copy-start(f32[1,1024]{1,0:T(1,128)} %get-tuple-element.39) | copy-start | bytes 12292
  473.4 8.0 %copy-start.44 = (f32[1,1024]{1,0:T(1,128)S(1)}, f32[1,1024]{1,0:T(1,128)}, u32[]{:S(2)}) copy-start(f32[1,1024]{1,0:T(1,128)} %get-tuple-element.38) | copy-start | bytes 12292
  473.4 8.0 %copy-start.45 = (f32[1,1024]{1,0:T(1,128)S(1)}, f32[1,1024]{1,0:T(1,128)}, u32[]{:S(2)}) copy-start(f32[1,1024]{1,0:T(1,128)} %get-tuple-element.41) | copy-start | bytes 12292
  476.0 122.8 %copy-start.20 = (f32[384,1024]{1,0:T(8,128)S(1)}, f32[384,1024]{1,0:T(8,128)}, u32[]{:S(2)}) copy-start(f32[384,1024]{1,0:T(8,128)} %get-tuple-element.30) | copy-start | bytes 4718596
  476.0 125.4 %collective-permute-start.2 = (bf16[3,128,1024]{2,1,0:T(8,128)(2,1)}, bf16[3,128,1024]{2,1,0:T(8,128)(2,1)S(1)}, u32[]{:S(2)}, u32[]{:S(2)}) collective-permute-start(bf16[3,128,1024]{2,1,0:T(8,128)(2,1)} %get-tuple-element.104), channel_id=1, source_target_pairs={{4,2},{5,3},{2,4},{3,5},{12,10},{13,11},{10,12},{11,13},{20,18},{2... | collective-permute-start | bytes 2359304 | tf_op jit(solution)/shard_map/ppermute | solution.py:640
  476.8 124.6 %collective-permute-start.3 = (bf16[3,128,1024]{2,1,0:T(8,128)(2,1)}, bf16[3,128,1024]{2,1,0:T(8,128)(2,1)S(1)}, u32[]{:S(2)}, u32[]{:S(2)}) collective-permute-start(bf16[3,128,1024]{2,1,0:T(8,128)(2,1)} %get-tuple-element.103), channel_id=1, source_target_pairs={{2,0},{3,1},{6,2},{7,3},{0,4},{1,5},{4,6},{5,7},{10,8},{11,9},{14,... | collective-permute-start | bytes 2359304 | tf_op jit(solution)/shard_map/ppermute | solution.py:639
  (27 other events, 47.2 us)
Sparse Core Ops, SparseCore 0:
  9.6 99.3 all-gather.3
  110.6 44.8 all-gather.5
  157.9 68.2 all-gather.7
  361.2 39.2 reduce-scatter.11
  403.3 70.0 reduce-scatter.17
  477.1 38.3 reduce-scatter.15
  517.8 19.9 reduce-scatter.13
  540.1 58.6 reduce-scatter.9

commit v3 on v2

--- a/solution.py
+++ b/solution.py
@@ -1,3 +1,4 @@
+import functools
 import math
 
 import jax
@@ -28,7 +29,9 @@
     return jnp.concatenate([jnp.where(lane_head == h, block, zero) for h in range(heads)], axis=0)
 
 
-def attn_fwd_body(low_ref, start_ref, q_ref, k_ref, v_ref, out_ref, lse_ref, vt_ref, qs_ref, acc_ref, sum_ref):
+def attn_fwd_body(
+    low_ref, start_ref, order_row, q_ref, k_ref, v_ref, out_ref, lse_ref, plain_ref, vt_ref, qs_ref, acc_ref, sum_ref
+):
     rows, cols = q_ref.shape
     heads = cols // HD
     scale = math.sqrt(HD) * LOG2E
@@ -70,13 +73,30 @@
         return 0
 
     lax.fori_loop(0, rows // BLK, one_block, 0)
+    over(rows // BLK, lambda b: to_token_order(b, order_row, out_ref, plain_ref))
+
+
+def to_token_order(b, order_row, src, dst):
+    at = pl.ds(pl.multiple_of(b * BLK, BLK), BLK)
+    hot = lax.broadcasted_iota(jnp.int32, (BLK, src.shape[0]), 0) + b * BLK == order_row[...]
+    dst[at, :] = dot_ab(hot.astype(jnp.float32).astype(jnp.bfloat16), src[...]).astype(dst.dtype)
+
+
+def to_packed_order(b, order_col, src, dst):
+    at = pl.ds(pl.multiple_of(b * BLK, BLK), BLK)
+    hot = lax.broadcasted_iota(jnp.int32, (BLK, src.shape[0]), 1) == order_col[at, :]
+    dst[at, :] = dot_ab(hot.astype(jnp.float32).astype(jnp.bfloat16), src[...]).astype(dst.dtype)
+
+
+def over(count, body):
+    lax.fori_loop(0, count, lambda i, carry: (body(i), carry)[1], 0)
 
 
 def vmem():
     return pl.BlockSpec(memory_space=pltpu.VMEM)
 
 
-def attn_fwd(low, start, q, k, v):
+def attn_fwd(low, start, order_row, q, k, v):
     rows, cols = q.shape
     heads = cols // HD
     return pl.pallas_call(
@@ -84,9 +104,10 @@
         out_shape=(
             jax.ShapeDtypeStruct((rows, cols), jnp.bfloat16),
             jax.ShapeDtypeStruct((8, rows), jnp.float32),
+            jax.ShapeDtypeStruct((rows, cols), jnp.bfloat16),
         ),
-        in_specs=[pl.BlockSpec(memory_space=pltpu.SMEM)] + [vmem()] * 4,
-        out_specs=(vmem(), vmem()),
+        in_specs=[pl.BlockSpec(memory_space=pltpu.SMEM)] + [vmem()] * 5,
+        out_specs=(vmem(),) * 3,
         scratch_shapes=[
             pltpu.VMEM((cols, rows), jnp.bfloat16),
             pltpu.VMEM((heads * BLK, cols), jnp.bfloat16),
@@ -96,12 +117,12 @@
         compiler_params=pltpu.CompilerParams(vmem_limit_bytes=VMEM_LIMIT),
         cost_estimate=pl.CostEstimate(flops=4 * rows * rows * cols, bytes_accessed=8 * rows * cols, transcendentals=rows * rows * heads),
         name="attn_fwd",
-    )(low, start, q, k, v)
+    )(low, start, order_row, q, k, v)
 
 
 def attn_bwd_body(
-    low_ref, start_ref, lse_ref, q_ref, k_ref, v_ref, o_ref, g_ref,
-    dq_ref, dk_ref, dv_ref, kt_ref, qs_ref, gs_ref, dqt_ref, dk_acc, dv_acc,
+    low_ref, start_ref, order_row, order_col, lse_ref, q_ref, k_ref, v_ref, o_ref, grad_ref,
+    plain_ref, kt_ref, qs_ref, gs_ref, dqt_ref, dk_acc, dv_acc, g_ref, packed,
 ):
     rows, cols = q_ref.shape
     heads = cols // HD
@@ -109,6 +130,7 @@
     scale = root * LOG2E
     for b in range(rows // BLK):
         kt_ref[:, b * BLK : (b + 1) * BLK] = k_ref[b * BLK : (b + 1) * BLK, :].T
+    over(rows // BLK, lambda b: to_packed_order(b, order_col, grad_ref, g_ref))
     dk_acc[...] = jnp.zeros_like(dk_acc)
     dv_acc[...] = jnp.zeros_like(dv_acc)
 
@@ -145,22 +167,23 @@
 
         lax.fori_loop(low_ref[i], i, lambda j, c: (step(j, False), c)[1], 0)
         step(i, True)
-        dq_ref[pl.ds(base, BLK), :] = (dqt_ref[...].T * root).astype(dq_ref.dtype)
+        packed[pl.ds(base, BLK), 0:cols] = (dqt_ref[...].T * root).astype(packed.dtype)
         return 0
 
     lax.fori_loop(0, rows // BLK, one_block, 0)
-    dk_ref[...] = (dk_acc[...] * root).astype(dk_ref.dtype)
-    dv_ref[...] = dv_acc[...].astype(dv_ref.dtype)
-
-
-def attn_bwd(low, start, lse, q, k, v, o, g):
+    packed[:, cols : 2 * cols] = (dk_acc[...] * root).astype(packed.dtype)
+    packed[:, 2 * cols : 3 * cols] = dv_acc[...].astype(packed.dtype)
+    over(rows // BLK, lambda b: to_token_order(b, order_row, packed, plain_ref))
+
+
+def attn_bwd(low, start, order_row, order_col, lse, q, k, v, o, g):
     rows, cols = q.shape
     heads = cols // HD
     return pl.pallas_call(
         attn_bwd_body,
-        out_shape=(jax.ShapeDtypeStruct((rows, cols), jnp.bfloat16),) * 3,
-        in_specs=[pl.BlockSpec(memory_space=pltpu.SMEM)] + [vmem()] * 7,
-        out_specs=(vmem(),) * 3,
+        out_shape=jax.ShapeDtypeStruct((rows, 3 * cols), jnp.bfloat16),
+        in_specs=[pl.BlockSpec(memory_space=pltpu.SMEM)] + [vmem()] * 9,
+        out_specs=vmem(),
         scratch_shapes=[
             pltpu.VMEM((cols, rows), jnp.bfloat16),
             pltpu.VMEM((heads * BLK, cols), jnp.bfloat16),
@@ -168,11 +191,13 @@
             pltpu.VMEM((cols, BLK), jnp.float32),
             pltpu.VMEM((rows, cols), jnp.float32),
             pltpu.VMEM((rows, cols), jnp.float32),
+            pltpu.VMEM((rows, cols), jnp.bfloat16),
+            pltpu.VMEM((rows, 3 * cols), jnp.bfloat16),
         ],
         compiler_params=pltpu.CompilerParams(vmem_limit_bytes=VMEM_LIMIT),
         cost_estimate=pl.CostEstimate(flops=10 * rows * rows * cols, bytes_accessed=16 * rows * cols, transcendentals=rows * rows * heads),
         name="attn_bwd",
-    )(low, start, lse, q, k, v, o, g)
+    )(low, start, order_row, order_col, lse, q, k, v, o, g)
 
 
 MESH_ID = pl.DeviceIdType.MESH
@@ -187,10 +212,6 @@
 
 def flip2(index):
     return index + 2 - 4 * (index // 2)
-
-
-def over(count, body):
-    lax.fori_loop(0, count, lambda i, carry: (body(i), carry)[1], 0)
 
 
 def tile_at(index, size):
@@ -587,6 +608,319 @@
     )(attended, wo, w_parts, tokens, cotangent, alpha_a, alpha_m, su, sg)
 
 
+def remote_copy(src, dst, send_sem, recv_sem, peer):
+    return pltpu.make_async_remote_copy(
+        src_ref=src, dst_ref=dst, send_sem=send_sem, recv_sem=recv_sem, device_id=peer, device_id_type=MESH_ID
+    )
+
+
+def greet(peers):
+    barrier = pltpu.get_barrier_semaphore()
+    for peer in peers:
+        pl.semaphore_signal(barrier, inc=1, device_id=peer, device_id_type=MESH_ID)
+    pl.semaphore_wait(barrier, len(peers))
+
+
+def spread_body(
+    count, tok, w_up, w_gate, w_down, wq, wk, wv, wo, pair, tok2, wqkv, wo_all,
+    own_mlp, own_att, wo_rows, load_sem, keep_sem, a_send, a_recv, b_send, b_recv, tok_send, tok_recv,
+    qkv_send, qkv_recv, oz_send, oz_recv, oq_send, oq_recv, oc_send, oc_recv,
+):
+    d = lax.axis_index("dp")
+    t = lax.axis_index("tensor")
+    core = lax.rem(d, 2)
+    home = core == t // 2
+    far = (d - core + t // 2, flip2(t))
+    wrows, wcols = wq.shape
+    half = count // 2
+    mlp = (w_up, w_gate, w_down)
+    att = (wq, wk, wv)
+    mine = tile_at(d, wrows)
+    side = tile_at(core, wrows)
+    other_side = tile_at(1 - core, wrows)
+
+    barrier = pltpu.get_barrier_semaphore()
+
+    def dp_peer(i):
+        return lax.rem(d + 1 + i, count)
+
+    def hello(i):
+        pl.semaphore_signal(barrier, inc=1, device_id=(dp_peer(i), t), device_id_type=MESH_ID)
+
+    over(count - 1, hello)
+    for k in (1, 2, 3):
+        pl.semaphore_signal(barrier, inc=1, device_id=(d, lax.rem(t + k, 4)), device_id_type=MESH_ID)
+    pl.semaphore_signal(barrier, inc=1, device_id=(flip1(d), flip2(t)), device_id_type=MESH_ID)
+    pl.semaphore_wait(barrier, count + 3)
+
+    def b_copy(m):
+        return remote_copy(mlp[m], pair.at[m, side, :], b_send.at[m], b_recv.at[core * 3 + m], far)
+
+    def a_copy(m):
+        return remote_copy(mlp[m], pair.at[m, side, :], a_send.at[m], a_recv.at[m], (flip1(d), t))
+
+    tok_copy = remote_copy(tok, tok2, tok_send, tok_recv, (d, flip1(t)))
+    for m in range(3):
+        b_copy(m).start()
+    tok_copy.start()
+
+    def oz_copy(k):
+        return remote_copy(wo, wo_rows.at[:, tile_at(t, wcols)], oz_send.at[k - 1], oz_recv.at[k - 1], (d, lax.rem(t + k, 4)))
+
+    for k in (1, 2, 3):
+        oz_copy(k).start()
+    load_o = pltpu.make_async_copy(wo, wo_rows.at[:, tile_at(t, wcols)], load_sem.at[0])
+    load_o.start()
+
+    def qkv_copy(i, m):
+        return remote_copy(
+            att[m], wqkv.at[mine, pl.ds(m * wcols, wcols)], qkv_send.at[i, m], qkv_recv.at[i, m], (dp_peer(i), t)
+        )
+
+    def qkv_start(i):
+        for m in range(3):
+            qkv_copy(i, m).start()
+
+    over(count - 1, qkv_start)
+
+    @pl.when(jnp.logical_not(home))
+    def _():
+        for m in range(3):
+            a_copy(m).start()
+
+    loads = [pltpu.make_async_copy(mlp[m], own_mlp.at[m], load_sem.at[1 + m]) for m in range(3)]
+    loads += [pltpu.make_async_copy(att[m], own_att.at[m], load_sem.at[4 + m]) for m in range(3)]
+    for copy in loads:
+        copy.start()
+    for copy in loads:
+        copy.wait()
+    keeps = [
+        pltpu.make_async_copy(own_att.at[m], wqkv.at[mine, pl.ds(m * wcols, wcols)], keep_sem.at[m]) for m in range(3)
+    ]
+    for copy in keeps:
+        copy.start()
+    pair_keeps = [pltpu.make_async_copy(own_mlp.at[m], pair.at[m, side, :], keep_sem.at[3 + m]) for m in range(3)]
+
+    @pl.when(home)
+    def _():
+        for copy in pair_keeps:
+            copy.start()
+
+    load_o.wait()
+    for k in (1, 2, 3):
+        oz_copy(k).wait_recv()
+    keep_o = pltpu.make_async_copy(wo_rows, wo_all.at[mine, :], keep_sem.at[6])
+    keep_o.start()
+
+    def oq_copy(j):
+        return remote_copy(wo_rows, wo_all.at[mine, :], oq_send.at[j], oq_recv.at[j], (lax.rem(d + 2 + 2 * j, count), t))
+
+    def oc_own():
+        return remote_copy(wo_rows, wo_all.at[mine, :], oc_send.at[half - 1], oc_recv.at[half - 1], (flip1(d), t))
+
+    def oc_copy(j):
+        rows = tile_at(lax.rem(d + count - 2 - 2 * j, count), wrows)
+        return remote_copy(wo_all.at[rows, :], wo_all.at[rows, :], oc_send.at[j], oc_recv.at[j], (flip1(d), t))
+
+    over(half - 1, lambda j: oq_copy(j).start())
+    oc_own().start()
+
+    def oq_next(j):
+        oq_copy(j).wait_recv()
+        oc_copy(j).start()
+
+    over(half - 1, oq_next)
+
+    def qkv_wait(i):
+        for m in range(3):
+            qkv_copy(i, m).wait()
+
+    over(count - 1, qkv_wait)
+    over(half - 1, lambda j: oq_copy(j).wait_send())
+    over(half - 1, lambda j: oc_copy(j).wait())
+    oc_own().wait()
+    for k in (1, 2, 3):
+        oz_copy(k).wait_send()
+    keep_o.wait()
+    for copy in keeps:
+        copy.wait()
+    tok_copy.wait()
+    for m in range(3):
+        b_copy(m).wait_send()
+
+    @pl.when(home)
+    def _():
+        for m in range(3):
+            pair_keeps[m].wait()
+            remote_copy(mlp[m], pair.at[m, other_side, :], a_send.at[m], a_recv.at[m], (flip1(d), t)).wait_recv()
+
+    @pl.when(jnp.logical_not(home))
+    def _():
+        for m in range(3):
+            a_copy(m).wait_send()
+            for c in range(2):
+                remote_copy(
+                    mlp[m], pair.at[m, pl.ds(c * wrows, wrows), :], b_send.at[m], b_recv.at[c * 3 + m], far
+                ).wait_recv()
+
+
+def spread_call(count, tokens, w_up, w_gate, w_down, wq, wk, wv, wo):
+    rows, width = tokens.shape
+    wrows, wcols = wq.shape
+    hid = w_up.shape[1]
+    bf = jnp.bfloat16
+    anywhere = pl.BlockSpec(memory_space=pl.ANY)
+    dma = pltpu.SemaphoreType.DMA
+    return pl.pallas_call(
+        functools.partial(spread_body, count),
+        out_shape=(
+            jax.ShapeDtypeStruct((3, 2 * wrows, hid), bf),
+            jax.ShapeDtypeStruct((rows, width), bf),
+            jax.ShapeDtypeStruct((width, 3 * wcols), bf),
+            jax.ShapeDtypeStruct((width, width), bf),
+        ),
+        in_specs=[anywhere] * 8,
+        out_specs=(anywhere,) * 4,
+        scratch_shapes=[
+            pltpu.VMEM((3, wrows, hid), bf),
+            pltpu.VMEM((3, wrows, wcols), bf),
+            pltpu.VMEM((wrows, width), bf),
+            dma((7,)), dma((7,)), dma((3,)), dma((3,)), dma((3,)), dma((6,)), dma, dma,
+            dma((count - 1, 3)), dma((count - 1, 3)), dma((3,)), dma((3,)),
+            dma((count // 2,)), dma((count // 2,)), dma((count // 2,)), dma((count // 2,)),
+        ],
+        compiler_params=pltpu.CompilerParams(vmem_limit_bytes=VMEM_LIMIT, collective_id=2, has_side_effects=True),
+        name="spread",
+    )(tokens, w_up, w_gate, w_down, wq, wk, wv, wo)
+
+
+def head_sums(value):
+    width = value.shape[1]
+    same = (
+        lax.broadcasted_iota(jnp.int32, (width, width), 0) // HD == lax.broadcasted_iota(jnp.int32, (width, width), 1) // HD
+    )
+    ones = jnp.where(same, 1.0, 0.0).astype(jnp.bfloat16)
+    high = value.astype(jnp.bfloat16)
+    low = (value - high.astype(jnp.float32)).astype(jnp.bfloat16)
+    return dot_ab(high, ones) + dot_ab(low, ones)
+
+
+def swap_halves(value):
+    width = value.shape[1]
+    lane = lax.broadcasted_iota(jnp.int32, value.shape, 1) % HD
+    return jnp.where(lane < HD // 2, pltpu.roll(value, width - HD // 2, 1), pltpu.roll(value, HD // 2, 1))
+
+
+def project_body(
+    tok, tok2, wqkv, cos_ref, sin_ref, order_col, gain_ref, q_ref, k_ref, v_ref, raw_ref, x_hbm,
+    xs, plain, load_sem, keep_sem, mid_send, recv, on_send,
+):
+    t = lax.axis_index("tensor")
+    d = lax.axis_index("dp")
+    _, rows, width = xs.shape
+    group, cols = q_ref.shape
+    near = flip1(t)
+    across = 3 - t
+    inner = (t + 1) // 2 == 1
+    arrive = (2 - t // 2, 3 - 3 * (t // 2))
+    part = rows // 2
+    greet([(d, near), (d, across)])
+
+    def mid_copy(k):
+        src = (tok, tok2)[k // 2].at[pl.ds((k % 2) * part, part), :]
+        dst = xs.at[(t, near)[k // 2], pl.ds((k % 2) * part, part), :]
+        return remote_copy(src, dst, mid_send.at[k], recv.at[k], (d, across))
+
+    def on_copy(k):
+        ref = xs.at[arrive[k // 2], pl.ds((k % 2) * part, part), :]
+        return remote_copy(ref, ref, on_send.at[k], recv.at[k], (d, near))
+
+    @pl.when(inner)
+    def _():
+        for k in range(4):
+            mid_copy(k).start()
+
+    loads = [
+        pltpu.make_async_copy(tok, xs.at[t], load_sem.at[0]),
+        pltpu.make_async_copy(tok2, xs.at[near], load_sem.at[1]),
+    ]
+    for copy in loads:
+        copy.start()
+
+    def keep(index, slot):
+        return pltpu.make_async_copy(xs.at[slot], x_hbm.at[tile_at(slot, rows), :], keep_sem.at[index])
+
+    def work(index, slot):
+        keep(index, slot).start()
+        at = tile_at(slot, rows)
+        x = xs[slot]
+        cos = jnp.concatenate([cos_ref[at, :]] * (cols // cos_ref.shape[1]), axis=1)
+        sin = jnp.concatenate([sin_ref[at, :]] * (cols // sin_ref.shape[1]), axis=1)
+        for m in range(2):
+            raw = dot_ab(x, wqkv[:, m * cols : (m + 1) * cols])
+            raw_ref[at, m * cols : (m + 1) * cols] = raw.astype(jnp.bfloat16)
+            normed = raw * lax.rsqrt(head_sums(raw * raw) + EPS) * gain_ref[...]
+            plain[at, m * cols : (m + 1) * cols] = (normed * cos + swap_halves(normed) * sin).astype(jnp.bfloat16)
+        plain[at, 2 * cols : 3 * cols] = dot_ab(x, wqkv[:, 2 * cols : 3 * cols]).astype(jnp.bfloat16)
+
+    loads[0].wait()
+    work(0, t)
+    loads[1].wait()
+    work(1, near)
+    for k in range(4):
+        slot = arrive[k // 2]
+        ref = xs.at[slot, pl.ds((k % 2) * part, part), :]
+        remote_copy(ref, ref, on_send.at[k], recv.at[k], (d, near)).wait_recv()
+
+        @pl.when(inner)
+        def _():
+            on_copy(k).start()
+
+        if k % 2:
+            work(2 + k // 2, slot)
+
+    def permute(b):
+        at = tile_at(b, BLK)
+        hot = (lax.broadcasted_iota(jnp.int32, (BLK, group), 1) == order_col[at, :]).astype(jnp.float32)
+        value = dot_ab(hot.astype(jnp.bfloat16), plain[...])
+        for m, ref in enumerate((q_ref, k_ref, v_ref)):
+            ref[at, :] = value[:, m * cols : (m + 1) * cols].astype(jnp.bfloat16)
+
+    over(group // BLK, permute)
+    for index, slot in enumerate((t, near, *arrive)):
+        keep(index, slot).wait()
+
+    @pl.when(inner)
+    def _():
+        for k in range(4):
+            mid_copy(k).wait_send()
+            on_copy(k).wait_send()
+
+
+def project_call(tokens, tok2, wqkv, cos, sin, order_col, gains):
+    rows, width = tokens.shape
+    group = order_col.shape[0]
+    cols = wqkv.shape[1] // 3
+    bf = jnp.bfloat16
+    anywhere = pl.BlockSpec(memory_space=pl.ANY)
+    dma = pltpu.SemaphoreType.DMA
+    return pl.pallas_call(
+        project_body,
+        out_shape=(jax.ShapeDtypeStruct((group, cols), bf),) * 3
+        + (jax.ShapeDtypeStruct((group, 2 * cols), bf), jax.ShapeDtypeStruct((group, width), bf)),
+        in_specs=[anywhere, anywhere] + [vmem()] * 5,
+        out_specs=(vmem(),) * 4 + (anywhere,),
+        scratch_shapes=[
+            pltpu.VMEM((group // rows, rows, width), bf),
+            pltpu.VMEM((group, 3 * cols), bf),
+            dma((2,)), dma((4,)), dma((4,)), dma((4,)), dma((4,)),
+        ],
+        compiler_params=pltpu.CompilerParams(vmem_limit_bytes=VMEM_LIMIT, collective_id=3, has_side_effects=True),
+        cost_estimate=pl.CostEstimate(flops=6 * 10**10, bytes_accessed=10**7, transcendentals=10**6),
+        name="project",
+    )(tokens, tok2, wqkv, cos, sin, order_col, gains)
+
+
 def flat(dp_index, tensor_index, tensor_count):
     return dp_index * tensor_count + tensor_index
 
@@ -608,22 +942,6 @@
     return [list(range(parity, dp_count, 2)) for parity in range(2)]
 
 
-def gather_hidden(own, dp_count, tensor_count):
-    near, far = hidden_routes(dp_count, tensor_count)
-    axes = ("dp", "tensor")
-    core = lax.rem(lax.axis_index("dp"), 2)
-    home = core == lax.axis_index("tensor") // 2
-    first = lax.ppermute(own, axes, near)
-    second = lax.ppermute(own, axes, far)
-    mine = jnp.where(home, own, first)
-    other = jnp.where(home, first, second)
-    pair = jnp.where(core == 0, jnp.stack([mine, other], 1), jnp.stack([other, mine], 1))
-    kinds, _, rows, cols = pair.shape
-    return lax.all_gather(
-        pair.reshape(kinds, 2 * rows, cols), "dp", axis=0, tiled=False, axis_index_groups=same_core_groups(dp_count)
-    )
-
-
 def scatter_hidden(parts, dp_count, tensor_count):
     near, far = hidden_routes(dp_count, tensor_count)
     axes = ("dp", "tensor")
@@ -642,14 +960,8 @@
     return jnp.where(home, mine.astype(f32), second.astype(f32)) + first.astype(f32)
 
 
-def matmul_ab(first_op, second_op):
-    return jnp.dot(first_op, second_op, preferred_element_type=jnp.float32)
-
-
 def matmul_abt(first_op, second_op):
-    return lax.dot_general(
-        first_op, second_op, (((1,), (1,)), ((), ())), preferred_element_type=jnp.float32
-    )
+    return dot_abt(first_op, second_op)
 
 
 def matmul_atb(first_op, second_op):
@@ -667,10 +979,10 @@
     return factor * (grad_out - normed * jnp.sum(normed * grad_out, axis=-1, keepdims=True))
 
 
-def rotate(matrix, angles, direction):
+def rotate_back(matrix, angles):
     half_width = matrix.shape[-1] // 2
     cosine = jnp.cos(angles)[:, None, :]
-    sine_part = direction * jnp.sin(angles)[:, None, :]
+    sine_part = -jnp.sin(angles)[:, None, :]
     lead_half = matrix[..., :half_width]
     tail_half = matrix[..., half_width:]
     return jnp.concatenate(
@@ -691,9 +1003,11 @@
     inv_freq = jnp.exp(
         jnp.arange(half_width, dtype=jnp.float32) * (-math.log(10000.0) / half_width)
     )
-    angles = (places - seg_first).astype(jnp.float32)[:, None] * inv_freq[None, :]
-    inverse = jnp.zeros((group_rows,), jnp.int32).at[order_row].set(places)
-    return (seg_first, angles, inverse)
+    depth = jnp.sum(
+        jnp.where(order_row[None, :] == places[:, None], (places - seg_first)[None, :], 0), axis=1, dtype=jnp.int32
+    )
+    angles = depth.astype(jnp.float32)[:, None] * inv_freq[None, :]
+    return (seg_first, angles)
 
 
 def on_device(
@@ -718,9 +1032,7 @@
     head_cols = w_query.shape[1]
     hidden_cols = w_up.shape[1]
     local_heads = head_cols // HD
-    qk_gains = lax.dynamic_slice_in_dim(scale_qk, tensor_rank * head_cols, head_cols).reshape(
-        local_heads, HD
-    )
+    qk_gains = lax.dynamic_slice_in_dim(scale_qk, tensor_rank * head_cols, head_cols)
     dp_count, tensor_count = lax.axis_size("dp"), lax.axis_size("tensor")
     hidden_rank = lax.rem(tensor_rank, 2) + 2 * lax.rem(lax.axis_index("dp"), 2)
     up_gains = lax.dynamic_slice_in_dim(scale_up, hidden_rank * hidden_cols, hidden_cols)[None, :]
@@ -728,36 +1040,28 @@
         scale_gate, hidden_rank * hidden_cols, hidden_cols
     )[None, :] * math.sqrt(D)
     order_row = order[0]
-    seg_first, angles, inverse = layout(order_row, lengths[0])
+    seg_first, angles = layout(order_row, lengths[0])
     group_rows = order_row.shape[0]
-    attn_full = (
-        lax.all_gather(w_query, "dp", axis=0, tiled=True),
-        lax.all_gather(w_key, "dp", axis=0, tiled=True),
-        lax.all_gather(w_value, "dp", axis=0, tiled=True),
-        lax.all_gather(w_out_t, "dp", axis=0, tiled=True),
-    )
-    wq_full, wk_full, wv_full, wo_full = attn_full
-    mlp_parts = gather_hidden(jnp.stack([w_up, w_gate, w_down_t]), dp_count, tensor_count)
-    gathered = lax.all_gather(tokens, "tensor", axis=0, tiled=True)
-    packed = gathered[order_row]
-    query_n, query_f = unit_pair(matmul_ab(packed, wq_full).reshape(group_rows, local_heads, HD))
-    key_n, key_f = unit_pair(matmul_ab(packed, wk_full).reshape(group_rows, local_heads, HD))
-    queries = rotate(query_n * qk_gains, angles, 1.0).astype(jnp.bfloat16)
-    key_rows = rotate(key_n * qk_gains, angles, 1.0).astype(jnp.bfloat16)
-    value_rows = (
-        matmul_ab(packed, wv_full).astype(jnp.bfloat16).reshape(group_rows, local_heads, HD)
-    )
-
     low = lax.slice(seg_first, (0,), (group_rows,), (BLK,)) // BLK
     start = seg_first[None, :]
-    queries = queries.reshape(group_rows, head_cols)
-    key_rows = key_rows.reshape(group_rows, head_cols)
-    value_rows = value_rows.reshape(group_rows, head_cols)
-    attended, log_totals = attn_fwd(low, start, queries, key_rows, value_rows)
-    wo_every = lax.all_gather(wo_full, "tensor", axis=1, tiled=True)
+    order_col = order_row[:, None]
+    cosine, sine = jnp.cos(angles), jnp.sin(angles)
+    cos_table = jnp.concatenate([cosine] * 4, axis=1)
+    sin_table = jnp.concatenate([-sine, sine] * 2, axis=1)
+
+    pair, near_tokens, wqkv, wo_every = spread_call(
+        dp_count, tokens, w_up, w_gate, w_down_t, w_query, w_key, w_value, w_out_t
+    )
+    mlp_parts = lax.all_gather(
+        pair, "dp", axis=0, tiled=False, axis_index_groups=same_core_groups(dp_count)
+    )
+    queries, key_rows, value_rows, raw, all_tokens = project_call(
+        tokens, near_tokens, wqkv, cos_table, sin_table, order_col, qk_gains[None, :]
+    )
+    attended, log_totals, attended_plain = attn_fwd(low, start, order, queries, key_rows, value_rows)
     out_rows, grad_att_rows, mlp_grads, wo_grads, grad_h1_kept, grad_alpha_a, grad_alpha_m, grad_su, grad_sv = middle_call(
         2,
-        attended[inverse],
+        attended_plain,
         wo_every,
         mlp_parts,
         tokens,
@@ -767,33 +1071,21 @@
         up_gains,
         gate_gains,
     )
-    grad_att = grad_att_rows[order_row]
-    grad_queries, grad_keys, grad_vals = attn_bwd(
-        low, start, log_totals, queries, key_rows, value_rows, attended, grad_att
-    )
-    grad_queries = grad_queries.astype(jnp.float32).reshape(group_rows, local_heads, HD)
-    grad_keys = grad_keys.astype(jnp.float32).reshape(group_rows, local_heads, HD)
-    grad_qs = rotate(grad_queries, angles, -1.0)
-    grad_ks = rotate(grad_keys, angles, -1.0)
-    grad_gain = jnp.sum(grad_qs * query_n + grad_ks * key_n, axis=0).reshape(head_cols)
-    grad_qraw = (
-        unit_back(query_n, query_f, grad_qs * qk_gains)
-        .astype(jnp.bfloat16)
-        .reshape(group_rows, head_cols)
-    )
-    grad_kraw = (
-        unit_back(key_n, key_f, grad_ks * qk_gains)
-        .astype(jnp.bfloat16)
-        .reshape(group_rows, head_cols)
-    )
-    grad_vraw = grad_vals.astype(jnp.bfloat16).reshape(group_rows, head_cols)
-    grad_wq = matmul_atb(packed, grad_qraw)
-    grad_wk = matmul_atb(packed, grad_kraw)
-    grad_wv = matmul_atb(packed, grad_vraw)
-    back_rows = jnp.concatenate([grad_qraw, grad_kraw, grad_vraw], axis=1)[inverse]
-    back_weights = jnp.concatenate([wq_full, wk_full, wv_full], axis=1)
+    grad_qkv = attn_bwd(
+        low, start, order, order_col, log_totals, queries, key_rows, value_rows, attended, grad_att_rows
+    )
+    gains = qk_gains.reshape(local_heads, HD)
+    parts = []
+    grad_gain = 0.0
+    for m in range(2):
+        cols = slice(m * head_cols, (m + 1) * head_cols)
+        normed, factor = unit_pair(raw[:, cols].astype(jnp.float32).reshape(group_rows, local_heads, HD))
+        grad = rotate_back(grad_qkv[:, cols].astype(jnp.float32).reshape(group_rows, local_heads, HD), angles)
+        grad_gain = grad_gain + jnp.sum(grad * normed, axis=0).reshape(head_cols)
+        parts.append(unit_back(normed, factor, grad * gains).astype(jnp.bfloat16).reshape(group_rows, head_cols))
+    grad_raw = jnp.concatenate(parts + [grad_qkv[:, 2 * head_cols :]], axis=1)
     attn_part = lax.psum_scatter(
-        matmul_abt(back_rows, back_weights).astype(jnp.bfloat16), "tensor", scatter_dimension=0, tiled=True
+        matmul_abt(grad_raw, wqkv).astype(jnp.bfloat16), "tensor", scatter_dimension=0, tiled=True
     ).astype(jnp.float32)
     grad_tokens = grad_h1_kept + attn_part
     grad_qk_full = lax.dynamic_update_slice_in_dim(
@@ -810,7 +1102,7 @@
     )
     mlp_sums = scatter_hidden(mlp_grads, dp_count, tensor_count)
     attn_sums = lax.psum_scatter(
-        jnp.concatenate([grad_wq, grad_wk, grad_wv], axis=1).astype(jnp.bfloat16), "dp", scatter_dimension=0, tiled=True
+        matmul_atb(all_tokens, grad_raw).astype(jnp.bfloat16), "dp", scatter_dimension=0, tiled=True
     ).astype(jnp.float32)
     wo_sums = lax.psum_scatter(
         lax.psum_scatter(wo_grads, "dp", scatter_dimension=0, tiled=True), "tensor", scatter_dimension=1, tiled=True

time: 618 us -> 550 us (0.89)
  Pallas kernels: 164 us -> 295 us
  blocking collectives: 141 us -> 56.9 us
  waiting for transfers between devices: 156 us -> 83.9 us
  local copies, waits for them, and re-layouts: 81.3 us -> 40.7 us
  other arithmetic: 30.5 us -> 39.4 us
  starting transfers between devices: 8.48 us -> 1.15 us
  matrix products: 15.7 us -> 9.33 us
    pallas_call x1 -> x3, Pallas kernels: 17.3 us -> 147 us  [the longest x1 60.9 us: spread_call(): pl.pallas_call(functools.partial(spread_body, count), out_shape=(jax.Shap...]
    all_gather x4 -> x0, blocking collectives: 86.7 us -> none  [the longest x1 52.8 us: on_device(): lax.all_gather(w_key, 'dp', axis=0, tiled=True)]
    all_gather x3 -> x1, waiting for transfers between devices: 37.4 us -> 0.01 us  [on_device(): lax.all_gather(pair, 'dp', axis=0, tiled=False, axis_index_groups=same_co...]
    ppermute x2 -> x0, waiting for transfers between devices: 33.7 us -> none  [the longest x1 33.7 us: gather_hidden(): first = lax.ppermute(own, axes, near)]
    gather x4 -> x0, local copies, waits for them, and re-layouts: 26.7 us -> none  [the longest x1 9.75 us: on_device(): packed = gathered[order_row]]
    dot_general x4 -> x1, matrix products: 12.6 us -> 5.48 us  [dot_abt(): lax.dot_general(a, b, (((1,), (1,)), ((), ())), preferred_element_type=jn...]
    unnamed x100 -> x63, local copies, waits for them, and re-layouts: 11.5 us -> 5.03 us
    scatter x1 -> x0, local copies, waits for them, and re-layouts: 6.18 us -> none  [layout(): inverse = jnp.zeros((group_rows,), jnp.int32).at[order_row].set(places)]
  transfers between devices with their start and end apart: 12 -> 8, of which waited for: 4 -> 3; matrix products, arithmetic and copies ran while one was open for 20% -> 15% of each run, Pallas kernels for 5% -> 18%
where the time goes in v3:
time: 550 us; the launch traced here: 541 us
  Pallas kernels  295 us (54%)
  waiting for transfers between devices  83.9 us (15%)
  blocking collectives  56.9 us (10%)
  local copies, waits for them, and re-layouts  40.7 us (7%)
  other arithmetic  39.4 us (7%)
  between operations  14.7 us (3%)
  matrix products  9.33 us (2%)
    pallas_call x1, Pallas kernels, middle_call(): pl.pallas_call(middle_body, out_shape=(jax.ShapeDtypeStruct((rows, width)...  135 us
    pallas_call x1, Pallas kernels, spread_call(): pl.pallas_call(functools.partial(spread_body, count), out_shape=(jax.Shap...  60.9 us
    pallas_call x1, Pallas kernels, project_call(): pl.pallas_call(project_body, out_shape=(jax.ShapeDtypeStruct((group, cols...  60.2 us
    reduce_scatter x1, waiting for transfers between devices, on_device(): lax.psum_scatter(matmul_abt(grad_raw, wqkv).astype(jnp.bfloat16), 'tensor...  59.3 us
    psum x1, blocking collectives, on_device(): lax.psum((grad_qk_full, grad_alpha_a[0], grad_su_full, grad_sv_full, grad...  56.9 us
    pallas_call x1, Pallas kernels, attn_bwd(): pl.pallas_call(attn_bwd_body, out_shape=jax.ShapeDtypeStruct((rows, 3 * c...  25.4 us
    unnamed x7, waiting for transfers between devices  23.3 us
    pallas_call x1, Pallas kernels, attn_fwd(): pl.pallas_call(attn_fwd_body, out_shape=(jax.ShapeDtypeStruct((rows, cols...  13.6 us
  transfers between devices with their start and end apart: 8, of which 3 were waited for; matrix products, arithmetic and copies ran while one was open for 15% of the time, Pallas kernels for 18%

profile of v3, /device:TPU:0, one launch (start us, length us, event | category | flops | bytes accessed | tf_op | source)
XLA Modules:
  0.0 541.0 jit_solution(1128322325330220602)
XLA Ops:
  7.2 60.9 %spread.1 = (bf16[3,256,1024]{2,1,0:T(8,128)(2,1)}, bf16[384,1024]{1,0:T(8,128)(2,1)}, bf16[1024,768]{1,0:T(8,128)(2,1)}, bf16[1024,1024]{1,0:T(8,128)(2,1)}) custom-call(bf16[384,1024]{1,0:T(8,128)(2,1)} %tok_hbm.1, bf16[128,1024]{1,0:T(8,128)(2,1)} %w_up.1, bf16[128,1024]{1,0:T(8,128)(2,1)} %w_gate.1, bf16[128,1024]{1,0:T(8,128)(2,1)} %w_down.1, ...), custom_call_target="tpu_custom_call" | custom-call | tf_op jit(solution)/shard_map/spread/pallas_call | solution.py:774
  76.0 2.8 fusion.12
  78.8 2.4 pad_maximum_fusion.5
  81.3 60.2 %project.1 = (bf16[1536,256]{1,0:T(8,128)(2,1)}, bf16[1536,256]{1,0:T(8,128)(2,1)}, bf16[1536,256]{1,0:T(8,128)(2,1)}, bf16[1536,512]{1,0:T(8,128)(2,1)}, bf16[1536,1024]{1,0:T(8,128)(2,1)}) custom-call(bf16[384,1024]{1,0:T(8,128)(2,1)} %tok_hbm.1, bf16[384,1024]{1,0:T(8,128)(2,1)} %get-tuple-element.35.tok2, bf16[1024,768]{1,0:T(8,128)(2,1)} %get-tuple-element.36.wqkv, ...), custom_call_target="tpu_custom_call" | custom-call | flops 60000002048 | bytes 10000000 | tf_op jit(solution)/shard_map/project/pallas_call | solution.py:907
  141.5 13.6 %attn_fwd.1 = (bf16[1536,256]{1,0:T(8,128)(2,1)}, f32[8,1536]{1,0:T(8,128)}, bf16[1536,256]{1,0:T(8,128)(2,1)}) custom-call(s32[6]{0:T(128)} %and_select_fusion.low_ref, s32[1,1536]{1,0:T(1,128)} %broadcast_in_dim.35.start_ref, s32[1,1536]{1,0:T(1,128)} %order_row.3, bf16[1536,256]{1,0:T(8,128)(2,1)} %get-tuple-element.37.q_ref, ...), custom_call_target="tpu_custom_call" | custom-call | flops 2415919104 | bytes 3145728 | tf_op jit(solution)/shard_map/attn_fwd/pallas_call | solution.py:102
  155.1 134.7 %middle.1 = (bf16[384,1024]{1,0:T(8,128)(2,1)}, bf16[1536,256]{1,0:T(8,128)(2,1)}, bf16[4,3,256,1024]{3,2,1,0:T(8,128)(2,1)}, bf16[1024,1024]{1,0:T(8,128)(2,1)}...) custom-call(bf16[1536,256]{1,0:T(8,128)(2,1)} %get-tuple-element.40., ...), custom_call_target="tpu_custom_call" | custom-call | flops 99999997952 | bytes 100000000 | tf_op jit(solution)/shard_map/middle/pallas_call | solution.py:556
  291.4 2.8 slice_convert_fusion.3
  295.7 1.6 copy.102
  297.3 1.9 copy.103
  301.4 3.1 copy.108
  304.5 25.4 %attn_bwd.1 = bf16[1536,768]{1,0:T(8,128)(2,1)} custom-call(s32[6]{0:T(128)} %and_select_fusion.low_ref, s32[1,1536]{1,0:T(1,128)} %broadcast_in_dim.35.start_ref, s32[1,1536]{1,0:T(1,128)} %order_row.3, s32[1536,1]{1,0:T(8,128)} %copy.93.order_col, f32[8,1536]{1,0:T(8,128)} %get-tuple-element.46.lse_ref, bf16[1536,256]{1,0:T(8,128)(2,1)} %get-tuple-element.37.q_ref, ...), custom_call_target="tpu_custom_call" | custom-call | flops 6039797760 | bytes 6291456 | tf_op jit(solution)/shard_map/attn_bwd/pallas_call | solution.py:182
  329.9 3.7 slice_convert_fusion.1
  333.6 3.0 copy.96
  336.6 3.0 copy.104
  339.7 3.8 multiply_subtract_fusion.1
  345.2 3.1 copy.99
  348.3 2.6 pad_maximum_fusion.2
  350.9 3.1 copy.105
  354.0 2.9 fusion.1
  356.9 3.1 copy.101
  360.1 1.5 fusion
  361.6 3.2 copy.107
  364.8 4.4 multiply_reduce_fusion
  370.4 3.8 convolution_convert_fusion.1
  375.6 5.5 %convolution_convert_fusion = bf16[1536,1024]{1,0:T(8,128)(2,1)} fusion(bf16[1024,768]{1,0:T(8,128)(2,1)S(1)} %copy-done.28, bf16[1536,256]{1,0:T(8,128)(2,1)S(1)} %copy-done.13, bf16[1536,256]{1,0:T(8,128)(2,1)} %copy-done.17, bf16[1536,256]{1,0:T(8,128)(2,1)S(1)} %copy-done.16), kind=kOutput, calls=%fused_computation.4 | convolution fusion | flops 2424569856 | bytes 7077888 | tf_op jit(solution)/shard_map/dot_general | solution.py:23
  381.1 22.1 %reduce-scatter.16.cloned.1.call-done = bf16[1,3,256,1024]{3,2,1,0:T(8,128)(2,1)} async-done(((bf16[4,3,256,1024]{3,2,1,0:T(8,128)(2,1)}), bf16[1,3,256,1024]{3,2,1,0:T(8,128)(2,1)}) %reduce-scatter.16.cloned.1.call-update) | async-done | bytes 1572880
  403.3 2.7 bitcast_select_fusion
  407.7 56.9 %all-reduce.1 = (f32[1024]{0:T(1024)}, f32[1024]{0:T(1024)}, f32[4096]{0:T(1024)}, f32[4096]{0:T(1024)}, f32[1024]{0:T(1024)}) all-reduce(f32[1024]{0:T(1024)S(1)} %add_dynamic-update-slice_fusion, f32[1024]{0:T(1024)S(1)} %bitcast.83, f32[4096]{0:T(1024)S(1)} %dynamic_update_slice.10, ...), channel_id=1, replica_groups=mesh['dp'=8,'tensor'=4] {'dp','tensor'}, use_global_device_ids=true, to_apply=%region_14.15 | all-reduce | flops 11264 | bytes 90112 | tf_op jit(solution)/shard_map/psum | solution.py:1100
  464.6 1.7 fusion.15
  467.5 1.5 convert_element_type.56
  469.0 59.3 %reduce-scatter.8.cloned.1.call-done = bf16[384,1024]{1,0:T(8,128)(2,1)} async-done(((bf16[1536,1024]{1,0:T(8,128)(2,1)}), bf16[384,1024]{1,0:T(8,128)(2,1)}) %reduce-scatter.8.cloned.1.call-update) | async-done | bytes 786448 | tf_op jit(solution)/shard_map/reduce_scatter | solution.py:1087
  528.3 2.6 convert_add_fusion.1
  (118 shorter events, 23.0 us)
Async XLA Ops:
  7.2 61.1 %copy-start.29 = (s32[1,3]{1,0:T(1,128)S(1)}, s32[1,3]{1,0:T(1,128)}, u32[]{:S(2)}) copy-start(s32[1,3]{1,0:T(1,128)} %param.30) | copy-start | bytes 40
  7.2 62.0 %copy-start.22 = (s32[1,1536]{1,0:T(1,128)S(1)}, s32[1,1536]{1,0:T(1,128)}, u32[]{:S(2)}) copy-start(s32[1,1536]{1,0:T(1,128)} %order_row.3) | copy-start | bytes 18436
  7.2 147.9 %all-gather.3.cloned.1.call-start = ((), (), s32[]{:S(2)}) async-start(), calls=%async_computation.9 | async-start | bytes 7864320 | tf_op jit(solution)/shard_map/all_gather | solution.py:1055
  68.2 306.1 %reduce-scatter.12.cloned.1.call-start = ((), (), s32[]{:S(2)}) async-start(), calls=%async_computation.7 | async-start | bytes 2359296 | tf_op jit(solution)/shard_map/reduce_scatter | solution.py:1108
  78.8 2.4 copy-start.4
  78.8 2.4 copy-start.6
  289.8 113.5 %reduce-scatter.16.cloned.1.call-start = ((), (), s32[]{:S(2)}) async-start(), calls=%async_computation.10 | async-start | bytes 7864320
  289.8 1.4 copy-start.5
  290.5 174.1 %reduce-scatter.10.cloned.1.call-start = ((), (), s32[]{:S(2)}) async-start(), calls=%async_computation.6 | async-start | bytes 1769472 | tf_op jit(solution)/shard_map/reduce_scatter | solution.py:1104
  343.5 1.4 copy-start.2
  343.5 1.7 copy-start.3
  350.9 3.1 copy-start.19
  356.9 3.1 copy-start
  356.9 3.1 copy-start.1
  356.9 3.1 copy-start.21
  361.6 3.2 copy-start.9
  361.6 3.2 copy-start.10
  364.8 5.6 %copy-start.12 = (bf16[1536,256]{1,0:T(8,128)(2,1)S(1)}, bf16[1536,256]{1,0:T(8,128)(2,1)}, u32[]{:S(2)}) copy-start(bf16[1536,256]{1,0:T(8,128)(2,1)} %get-tuple-element.68) | copy-start | bytes 2359300
  364.8 5.6 %copy-start.30 = (bf16[1536,1024]{1,0:T(8,128)(2,1)S(1)}, bf16[1536,1024]{1,0:T(8,128)(2,1)}, u32[]{:S(2)}) copy-start(bf16[1536,1024]{1,0:T(8,128)(2,1)} %get-tuple-element.49) | copy-start | bytes 9437188
  370.4 4.5 copy-start.28
  374.2 1.4 copy-start.16
  374.3 93.2 %reduce-scatter.14.cloned.1.call-start = ((), (), s32[]{:S(2)}) async-start(), calls=%async_computation.8 | async-start | bytes 327680 | tf_op jit(solution)/shard_map/reduce_scatter | solution.py:1107
  374.9 153.5 %reduce-scatter.8.cloned.1.call-start = ((), (), s32[]{:S(2)}) async-start(), calls=%async_computation.5 | async-start | bytes 3932160 | tf_op jit(solution)/shard_map/reduce_scatter | solution.py:1087
  403.2 3.7 copy-start.25
  403.2 3.7 copy-start.24
  403.2 4.4 copy-start.26
  403.2 4.4 copy-start.27
  403.3 125.1 %copy-start.11 = (f32[384,1024]{1,0:T(8,128)S(1)}, f32[384,1024]{1,0:T(8,128)}, u32[]{:S(2)}) copy-start(f32[384,1024]{1,0:T(8,128)} %get-tuple-element.44) | copy-start | bytes 4718596
  406.0 124.9 %collective-permute-start.1 = (bf16[3,128,1024]{2,1,0:T(8,128)(2,1)}, bf16[3,128,1024]{2,1,0:T(8,128)(2,1)S(1)}, u32[]{:S(2)}, u32[]{:S(2)}) collective-permute-start(bf16[3,128,1024]{2,1,0:T(8,128)(2,1)} %get-tuple-element.63), channel_id=1, source_target_pairs={{2,0},{3,1},{6,2},{7,3},{0,4},{1,5},{4,6},{5,7},{10,8},{11,9},{14,... | collective-permute-start | bytes 2359304 | tf_op jit(solution)/shard_map/ppermute | solution.py:957
  406.2 124.7 %collective-permute-start = (bf16[3,128,1024]{2,1,0:T(8,128)(2,1)}, bf16[3,128,1024]{2,1,0:T(8,128)(2,1)S(1)}, u32[]{:S(2)}, u32[]{:S(2)}) collective-permute-start(bf16[3,128,1024]{2,1,0:T(8,128)(2,1)} %get-tuple-element.64), channel_id=1, source_target_pairs={{4,2},{5,3},{2,4},{3,5},{12,10},{13,11},{10,12},{11,13},{20,18},{2... | collective-permute-start | bytes 2359304 | tf_op jit(solution)/shard_map/ppermute | solution.py:958
  528.3 2.6 copy-start.8
  531.5 1.6 copy-start.14
  (7 other events, 6.2 us)
Sparse Core Ops, SparseCore 0:
  68.3 70.3 all-gather.2
  289.9 40.2 reduce-scatter.11
  333.2 70.0 reduce-scatter.15
  407.0 38.3 reduce-scatter.9
  447.5 19.9 reduce-scatter.13
  469.6 58.6 reduce-scatter.7

commit v4 on v3

--- a/solution.py
+++ b/solution.py
@@ -921,6 +921,300 @@
     )(tokens, tok2, wqkv, cos, sin, order_col, gains)
 
 
+def tail_body(
+    count, grad_ref, raw_ref, cos_ref, sin_ref, wqkv, x_hbm, gwo_hbm, kept_ref, gain_ref, gaa_ref, gam_ref, gsu_ref, gsg_ref,
+    tok_out, qkv_out, wo_out, gain_out, aa_out, am_out, su_out, sg_out,
+    xs, x_t, draw, part_far, part_mid, part_near, own_part, from_a, from_b, from_c, from_d, from_e, from_f,
+    gq, got_q, got_w, wo_mid, got_z, vec, got_v, vec_mid, got_s, load_sem,
+    hop_send, hop_recv, q_send, q_recv, w_send, w_recv, z_send, z_recv, v_send, v_recv, s_send, s_recv,
+):
+    d = lax.axis_index("dp")
+    t = lax.axis_index("tensor")
+    rows, width = tok_out.shape
+    group = draw.shape[0]
+    cols = draw.shape[1] // 3
+    wrows = qkv_out.shape[0]
+    near = flip1(t)
+    inner = (t + 1) // 2 == 1
+    outer = jnp.logical_not(inner)
+    far, mid = 3 - 3 * (t // 2), 2 - t // 2
+    chunk = rows // 2
+
+    def dp_peer(i):
+        return lax.rem(d + 1 + i, count)
+
+    def line_peer(k):
+        return lax.rem(t + k, 4)
+
+    barrier = pltpu.get_barrier_semaphore()
+    over(
+        count - 1,
+        lambda i: pl.semaphore_signal(barrier, inc=1, device_id=(dp_peer(i), t), device_id_type=MESH_ID),
+    )
+    for k in (1, 2, 3):
+        pl.semaphore_signal(barrier, inc=1, device_id=(d, line_peer(k)), device_id_type=MESH_ID)
+    pl.semaphore_wait(barrier, count + 2)
+
+    def w_copy(i):
+        return remote_copy(
+            gwo_hbm.at[tile_at(dp_peer(i), wrows), :], got_w.at[d], w_send.at[i], w_recv.at[i], (dp_peer(i), t)
+        )
+
+    over(count - 1, lambda i: w_copy(i).start())
+    load_w = pltpu.make_async_copy(gwo_hbm.at[tile_at(d, wrows), :], got_w.at[d], load_sem.at[0])
+    load_x = pltpu.make_async_copy(x_hbm, xs, load_sem.at[1])
+    load_w.start()
+    load_x.start()
+
+    def hop(kind, ch):
+        src, dst, to = (
+            (part_far, from_a, near),
+            (part_mid, from_b, near),
+            (part_near, from_c, near),
+            (part_far, from_d, 3 - t),
+            (part_mid, from_e, 3 - t),
+            (part_near, from_f, near),
+        )[kind]
+        part = pl.ds(ch * chunk, chunk)
+        return remote_copy(src.at[part, :], dst.at[part, :], hop_send.at[kind, ch], hop_recv.at[kind, ch], (d, to))
+
+    vec[...] = jnp.zeros_like(vec)
+
+    def work(slot, store):
+        at = tile_at(slot, rows)
+        cos = jnp.concatenate([cos_ref[at, :]] * (cols // cos_ref.shape[1]), axis=1)
+        sin = jnp.concatenate([sin_ref[at, :]] * (cols // sin_ref.shape[1]), axis=1)
+        gain = gain_ref[...]
+        for m in range(2):
+            grad = grad_ref[at, m * cols : (m + 1) * cols].astype(jnp.float32)
+            raw = raw_ref[at, m * cols : (m + 1) * cols].astype(jnp.float32)
+            back = grad * cos - swap_halves(grad) * sin
+            factor = lax.rsqrt(head_sums(raw * raw) + EPS)
+            normed = raw * factor
+            vec[4:5, 0:cols] += jnp.sum(back * normed, axis=0, keepdims=True)
+            scaled = back * gain
+            draw[at, m * cols : (m + 1) * cols] = (factor * (scaled - normed * head_sums(normed * scaled))).astype(
+                jnp.bfloat16
+            )
+        draw[at, 2 * cols : 3 * cols] = grad_ref[at, 2 * cols : 3 * cols]
+
+        def product(n):
+            tile = tile_at(n, TILE)
+            store(tile, dot_abt(draw[at, :], wqkv[tile, :]))
+
+        over(width // TILE, product)
+
+    def into(ref):
+        def store(tile, value):
+            ref[:, tile] = value.astype(ref.dtype)
+
+        return store
+
+    for kind, (slot, ref) in enumerate(((far, part_far), (mid, part_mid), (near, part_near))):
+        work(slot, into(ref))
+
+        @pl.when(outer)
+        def _():
+            for ch in range(2):
+                hop(kind, ch).start()
+
+    work(t, into(own_part))
+
+    for row, ref in enumerate((gaa_ref, gam_ref, gsu_ref, gsg_ref)):
+        vec[row : row + 1, :] = ref[...]
+    got_v[d] = vec[...]
+
+    def v_copy(i):
+        return remote_copy(vec, got_v.at[d], v_send.at[i], v_recv.at[i], (dp_peer(i), t))
+
+    over(count - 1, lambda i: v_copy(i).start())
+
+    def pass_on(kind, ch, own, got, then):
+        @pl.when(inner)
+        def _():
+            part = pl.ds(ch * chunk, chunk)
+            hop(kind, ch).wait_recv()
+            own[part, :] = (own[part, :].astype(jnp.float32) + got[part, :].astype(jnp.float32)).astype(jnp.bfloat16)
+            hop(then, ch).start()
+
+    pass_on(0, 0, part_far, from_a, 3)
+    pass_on(0, 1, part_far, from_a, 3)
+
+    load_x.wait()
+
+    def flip_block(b):
+        at = tile_at(b, 128)
+        for n in range(width // TILE):
+            x_t[n * TILE : (n + 1) * TILE, at] = xs[at, n * TILE : (n + 1) * TILE].T
+
+    over(group // 128, flip_block)
+    pass_on(3, 0, part_near, from_d, 5)
+
+    def weight_grad(n):
+        tile = tile_at(n, TILE)
+        gq[tile, :] = dot_ab(x_t[tile, :], draw[...]).astype(jnp.bfloat16)
+
+    over(width // TILE, weight_grad)
+
+    def q_copy(i):
+        return remote_copy(gq.at[tile_at(dp_peer(i), wrows), :], got_q.at[d], q_send.at[i], q_recv.at[i], (dp_peer(i), t))
+
+    over(count - 1, lambda i: q_copy(i).start())
+    got_q[d] = gq[tile_at(d, wrows), :]
+    pass_on(1, 0, part_mid, from_b, 4)
+    pass_on(3, 1, part_near, from_d, 5)
+    pass_on(1, 1, part_mid, from_b, 4)
+
+    load_w.wait()
+    over(count - 1, lambda i: w_copy(i).wait_recv())
+    wo_mid[...] = lax.fori_loop(
+        1, count, lambda i, total: total + got_w[i].astype(jnp.float32), got_w[0].astype(jnp.float32)
+    ).astype(jnp.bfloat16)
+
+    def z_copy(k):
+        return remote_copy(
+            wo_mid.at[:, tile_at(line_peer(k), cols)], got_z.at[t], z_send.at[k - 1], z_recv.at[k - 1], (d, line_peer(k))
+        )
+
+    for k in (1, 2, 3):
+        z_copy(k).start()
+    got_z[t] = wo_mid[:, tile_at(t, cols)]
+
+    over(count - 1, lambda i: v_copy(i).wait_recv())
+    even, odd = lax.fori_loop(
+        1, count // 2, lambda i, total: (total[0] + got_v[2 * i], total[1] + got_v[2 * i + 1]), (got_v[0], got_v[1])
+    )
+    both = even + odd
+    vec_mid[...] = jnp.concatenate([both[0:2], even[2:3], odd[2:3], even[3:4], odd[3:4], both[4:5], both[4:5]], axis=0)
+
+    def s_copy(k):
+        return remote_copy(vec_mid, got_s.at[t], s_send.at[k - 1], s_recv.at[k - 1], (d, line_peer(k)))
+
+    for k in (1, 2, 3):
+        s_copy(k).start()
+    got_s[t] = vec_mid[...]
+
+    over(count - 1, lambda i: q_copy(i).wait_recv())
+    qkv_out[...] = lax.fori_loop(
+        1, count, lambda i, total: total + got_q[i].astype(jnp.float32), got_q[0].astype(jnp.float32)
+    )
+
+    for k in (1, 2, 3):
+        z_copy(k).wait_recv()
+        s_copy(k).wait_recv()
+    wo_out[...] = (
+        got_z[0].astype(jnp.float32)
+        + got_z[1].astype(jnp.float32)
+        + got_z[2].astype(jnp.float32)
+        + got_z[3].astype(jnp.float32)
+    )
+    shared = got_s[0] + got_s[1] + got_s[2] + got_s[3]
+    aa_out[...] = shared[0:1]
+    am_out[...] = shared[1:2]
+    pairs = (got_s[0] + got_s[2], got_s[1] + got_s[3])
+    for s in range(4):
+        su_out[s : s + 1, :] = pairs[s % 2][2 + s // 2 : 3 + s // 2]
+        sg_out[s : s + 1, :] = pairs[s % 2][4 + s // 2 : 5 + s // 2] * math.sqrt(D)
+        gain_out[s : s + 1, :] = got_s[s][6:7, 0:cols]
+
+    for ch in range(2):
+        part = pl.ds(ch * chunk, chunk)
+
+        @pl.when(inner)
+        def _():
+            hop(2, ch).wait_recv()
+            hop(4, ch).wait_recv()
+            tok_out[part, :] = (
+                kept_ref[part, :]
+                + own_part[part, :]
+                + from_c[part, :].astype(jnp.float32)
+                + from_e[part, :].astype(jnp.float32)
+            )
+
+        @pl.when(outer)
+        def _():
+            hop(5, ch).wait_recv()
+            tok_out[part, :] = kept_ref[part, :] + own_part[part, :] + from_f[part, :].astype(jnp.float32)
+
+    for ch in range(2):
+
+        @pl.when(inner)
+        def _():
+            for kind in (3, 4, 5):
+                hop(kind, ch).wait_send()
+
+        @pl.when(outer)
+        def _():
+            for kind in (0, 1, 2):
+                hop(kind, ch).wait_send()
+
+    def drain(i):
+        w_copy(i).wait_send()
+        v_copy(i).wait_send()
+        q_copy(i).wait_send()
+
+    over(count - 1, drain)
+    for k in (1, 2, 3):
+        z_copy(k).wait_send()
+        s_copy(k).wait_send()
+
+
+def tail_call(count, grad_qkv, raw, cos, sin, wqkv, all_tokens, wo_grads, kept, gains, gaa, gam, gsu, gsg):
+    rows, width = kept.shape
+    group, three = grad_qkv.shape
+    cols = three // 3
+    wrows = width // count
+    bf, f32 = jnp.bfloat16, jnp.float32
+    anywhere = pl.BlockSpec(memory_space=pl.ANY)
+    dma = pltpu.SemaphoreType.DMA
+    shape = jax.ShapeDtypeStruct
+    return pl.pallas_call(
+        functools.partial(tail_body, count),
+        out_shape=(
+            shape((rows, width), f32),
+            shape((wrows, three), f32),
+            shape((wrows, cols), f32),
+            shape((4, cols), f32),
+            shape((1, width), f32),
+            shape((1, width), f32),
+            shape((4, width), f32),
+            shape((4, width), f32),
+        ),
+        in_specs=[vmem()] * 5 + [anywhere, anywhere] + [vmem()] * 6,
+        out_specs=(vmem(),) * 8,
+        scratch_shapes=[
+            pltpu.VMEM((group, width), bf),
+            pltpu.VMEM((width, group), bf),
+            pltpu.VMEM((group, three), bf),
+            pltpu.VMEM((rows, width), bf),
+            pltpu.VMEM((rows, width), bf),
+            pltpu.VMEM((rows, width), bf),
+            pltpu.VMEM((rows, width), f32),
+        ]
+        + [pltpu.VMEM((rows, width), bf)] * 6
+        + [
+            pltpu.VMEM((width, three), bf),
+            pltpu.VMEM((count, wrows, three), bf),
+            pltpu.VMEM((count, wrows, width), bf),
+            pltpu.VMEM((wrows, width), bf),
+            pltpu.VMEM((4, wrows, cols), bf),
+            pltpu.VMEM((8, width), f32),
+            pltpu.VMEM((count, 8, width), f32),
+            pltpu.VMEM((8, width), f32),
+            pltpu.VMEM((4, 8, width), f32),
+            dma((2,)),
+            dma((6, 2)), dma((6, 2)),
+            dma((count - 1,)), dma((count - 1,)), dma((count - 1,)), dma((count - 1,)),
+            dma((3,)), dma((3,)),
+            dma((count - 1,)), dma((count - 1,)),
+            dma((3,)), dma((3,)),
+        ],
+        compiler_params=pltpu.CompilerParams(vmem_limit_bytes=VMEM_LIMIT, collective_id=4, has_side_effects=True),
+        cost_estimate=pl.CostEstimate(flops=6 * 10**10, bytes_accessed=10**7, transcendentals=10**6),
+        name="tail",
+    )(grad_qkv, raw, cos, sin, wqkv, all_tokens, wo_grads, kept, gains, gaa, gam, gsu, gsg)
+
+
 def flat(dp_index, tensor_index, tensor_count):
     return dp_index * tensor_count + tensor_index
 
@@ -958,37 +1252,6 @@
     second = lax.ppermute(other, axes, [(b, a) for a, b in far])
     f32 = jnp.float32
     return jnp.where(home, mine.astype(f32), second.astype(f32)) + first.astype(f32)
-
-
-def matmul_abt(first_op, second_op):
-    return dot_abt(first_op, second_op)
-
-
-def matmul_atb(first_op, second_op):
-    return lax.dot_general(
-        first_op, second_op, (((0,), (0,)), ((), ())), preferred_element_type=jnp.float32
-    )
-
-
-def unit_pair(matrix):
-    factor = lax.rsqrt(jnp.sum(matrix * matrix, axis=-1, keepdims=True) + 1e-06)
-    return (matrix * factor, factor)
-
-
-def unit_back(normed, factor, grad_out):
-    return factor * (grad_out - normed * jnp.sum(normed * grad_out, axis=-1, keepdims=True))
-
-
-def rotate_back(matrix, angles):
-    half_width = matrix.shape[-1] // 2
-    cosine = jnp.cos(angles)[:, None, :]
-    sine_part = -jnp.sin(angles)[:, None, :]
-    lead_half = matrix[..., :half_width]
-    tail_half = matrix[..., half_width:]
-    return jnp.concatenate(
-        [lead_half * cosine - tail_half * sine_part, tail_half * cosine + lead_half * sine_part],
-        axis=-1,
-    )
 
 
 def layout(order_row, length_row):
@@ -1031,7 +1294,6 @@
     tensor_rank = lax.axis_index("tensor")
     head_cols = w_query.shape[1]
     hidden_cols = w_up.shape[1]
-    local_heads = head_cols // HD
     qk_gains = lax.dynamic_slice_in_dim(scale_qk, tensor_rank * head_cols, head_cols)
     dp_count, tensor_count = lax.axis_size("dp"), lax.axis_size("tensor")
     hidden_rank = lax.rem(tensor_rank, 2) + 2 * lax.rem(lax.axis_index("dp"), 2)
@@ -1074,40 +1336,24 @@
     grad_qkv = attn_bwd(
         low, start, order, order_col, log_totals, queries, key_rows, value_rows, attended, grad_att_rows
     )
-    gains = qk_gains.reshape(local_heads, HD)
-    parts = []
-    grad_gain = 0.0
-    for m in range(2):
-        cols = slice(m * head_cols, (m + 1) * head_cols)
-        normed, factor = unit_pair(raw[:, cols].astype(jnp.float32).reshape(group_rows, local_heads, HD))
-        grad = rotate_back(grad_qkv[:, cols].astype(jnp.float32).reshape(group_rows, local_heads, HD), angles)
-        grad_gain = grad_gain + jnp.sum(grad * normed, axis=0).reshape(head_cols)
-        parts.append(unit_back(normed, factor, grad * gains).astype(jnp.bfloat16).reshape(group_rows, head_cols))
-    grad_raw = jnp.concatenate(parts + [grad_qkv[:, 2 * head_cols :]], axis=1)
-    attn_part = lax.psum_scatter(
-        matmul_abt(grad_raw, wqkv).astype(jnp.bfloat16), "tensor", scatter_dimension=0, tiled=True
-    ).astype(jnp.float32)
-    grad_tokens = grad_h1_kept + attn_part
-    grad_qk_full = lax.dynamic_update_slice_in_dim(
-        jnp.zeros(scale_qk.shape, jnp.float32), grad_gain, tensor_rank * head_cols, 0
-    )
-    grad_su_full = lax.dynamic_update_slice_in_dim(
-        jnp.zeros(scale_up.shape, jnp.float32), grad_su[0], hidden_rank * hidden_cols, 0
-    )
-    grad_sv_full = lax.dynamic_update_slice_in_dim(
-        jnp.zeros(scale_gate.shape, jnp.float32), grad_sv[0] * math.sqrt(D), hidden_rank * hidden_cols, 0
-    )
-    vector_sums = lax.psum(
-        (grad_qk_full, grad_alpha_a[0], grad_su_full, grad_sv_full, grad_alpha_m[0]), ("dp", "tensor")
+    grad_tokens, qkv_sums, wo_sums, grad_gain, sum_aa, sum_am, sum_su, sum_sv = tail_call(
+        dp_count,
+        grad_qkv,
+        raw,
+        cos_table,
+        sin_table,
+        wqkv,
+        all_tokens,
+        wo_grads,
+        grad_h1_kept,
+        qk_gains[None, :],
+        grad_alpha_a,
+        grad_alpha_m,
+        grad_su,
+        grad_sv,
     )
     mlp_sums = scatter_hidden(mlp_grads, dp_count, tensor_count)
-    attn_sums = lax.psum_scatter(
-        matmul_atb(all_tokens, grad_raw).astype(jnp.bfloat16), "dp", scatter_dimension=0, tiled=True
-    ).astype(jnp.float32)
-    wo_sums = lax.psum_scatter(
-        lax.psum_scatter(wo_grads, "dp", scatter_dimension=0, tiled=True), "tensor", scatter_dimension=1, tiled=True
-    ).astype(jnp.float32)
-    weight_sums = [attn_sums[:, i * head_cols : (i + 1) * head_cols] for i in range(3)] + [wo_sums, *mlp_sums]
+    weight_sums = [qkv_sums[:, i * head_cols : (i + 1) * head_cols] for i in range(3)] + [wo_sums, *mlp_sums]
     return (
         out_rows,
         grad_tokens,
@@ -1118,11 +1364,11 @@
         weight_sums[4],
         weight_sums[5],
         weight_sums[6],
-        vector_sums[0],
-        vector_sums[1],
-        vector_sums[2],
-        vector_sums[3],
-        vector_sums[4],
+        grad_gain.reshape(-1),
+        sum_aa.reshape(-1),
+        sum_su.reshape(-1),
+        sum_sv.reshape(-1),
+        sum_am.reshape(-1),
     )
 
 

time: 550 us -> 471 us (0.86)
  Pallas kernels: 295 us -> 375 us
  blocking collectives: 56.9 us -> 0 us
  waiting for transfers between devices: 83.9 us -> 43.7 us
  other arithmetic: 39.4 us -> 11.3 us
  local copies, waits for them, and re-layouts: 40.7 us -> 16.1 us
  matrix products: 9.33 us -> 0 us
    pallas_call x0 -> x1, Pallas kernels: none -> 82.6 us  [tail_call(): pl.pallas_call(functools.partial(tail_body, count), out_shape=(shape((row...]
    reduce_scatter x4 -> x0, waiting for transfers between devices: 60.6 us -> none  [the longest x1 59.3 us: on_device(): lax.psum_scatter(matmul_abt(grad_raw, wqkv).astype(jnp.bfloat16), 'tensor...]
    psum x1 -> x0, blocking collectives: 56.9 us -> none  [on_device(): lax.psum((grad_qk_full, grad_alpha_a[0], grad_su_full, grad_sv_full, grad...]
    unnamed x7 -> x3, waiting for transfers between devices: 23.3 us -> 43.7 us
    mul x7 -> x0, local copies, waits for them, and re-layouts: 12.6 us -> none  [the longest x2 6.32 us: unit_back(): normed * jnp.sum(normed * grad_out, axis=-1, keepdims=True)]
    dot_general x2 -> x0, matrix products: 9.33 us -> none  [the longest x1 5.48 us: dot_abt(): lax.dot_general(a, b, (((1,), (1,)), ((), ())), preferred_element_type=jn...]
    concatenate x2 -> x0, local copies, waits for them, and re-layouts: 6.2 us -> none  [rotate_back(): jnp.concatenate([lead_half * cosine - tail_half * sine_part, tail_half *...]
    reshape x2 -> x0, local copies, waits for them, and re-layouts: 6.04 us -> none  [on_device(): grad_qkv[:, cols].astype(jnp.float32).reshape(group_rows, local_heads, HD)]
  transfers between devices with their start and end apart: 8 -> 4, of which waited for: 3 -> 1; matrix products, arithmetic and copies ran while one was open for 15% -> 4% of each run, Pallas kernels for 18% -> 39%
where the time goes in v4:
time: 471 us; the launch traced here: 462 us
  Pallas kernels  375 us (80%)
  waiting for transfers between devices  43.7 us (9%)
  local copies, waits for them, and re-layouts  16.1 us (3%)
  between operations  14.7 us (3%)
  other arithmetic  11.3 us (2%)
    pallas_call x1, Pallas kernels, middle_call(): pl.pallas_call(middle_body, out_shape=(jax.ShapeDtypeStruct((rows, width)...  133 us
    pallas_call x1, Pallas kernels, tail_call(): pl.pallas_call(functools.partial(tail_body, count), out_shape=(shape((row...  82.6 us
    pallas_call x1, Pallas kernels, spread_call(): pl.pallas_call(functools.partial(spread_body, count), out_shape=(jax.Shap...  60.9 us
    pallas_call x1, Pallas kernels, project_call(): pl.pallas_call(project_body, out_shape=(jax.ShapeDtypeStruct((group, cols...  60.2 us
    unnamed x3, waiting for transfers between devices  43.7 us
    pallas_call x1, Pallas kernels, attn_bwd(): pl.pallas_call(attn_bwd_body, out_shape=jax.ShapeDtypeStruct((rows, 3 * c...  25.2 us
    pallas_call x1, Pallas kernels, attn_fwd(): pl.pallas_call(attn_fwd_body, out_shape=(jax.ShapeDtypeStruct((rows, cols...  13.6 us
  transfers between devices with their start and end apart: 4, of which 1 were waited for; matrix products, arithmetic and copies ran while one was open for 4% of the time, Pallas kernels for 39%

profile of v4, /device:TPU:0, one launch (start us, length us, event | category | flops | bytes accessed | tf_op | source)
XLA Modules:
  0.0 461.8 jit_solution(16313145716152575693)
XLA Ops:
  7.2 60.9 %spread.1 = (bf16[3,256,1024]{2,1,0:T(8,128)(2,1)}, bf16[384,1024]{1,0:T(8,128)(2,1)}, bf16[1024,768]{1,0:T(8,128)(2,1)}, bf16[1024,1024]{1,0:T(8,128)(2,1)}) custom-call(bf16[384,1024]{1,0:T(8,128)(2,1)} %tok_hbm.1, bf16[128,1024]{1,0:T(8,128)(2,1)} %w_up.1, bf16[128,1024]{1,0:T(8,128)(2,1)} %w_gate.1, bf16[128,1024]{1,0:T(8,128)(2,1)} %w_down.1, ...), custom_call_target="tpu_custom_call" | custom-call | tf_op jit(solution)/shard_map/spread/pallas_call | solution.py:774
  68.3 0.2 reduce-window_clone.1
  68.6 0.6 broadcast_in_dim.47.start_ref
  69.3 1.0 select_reduce_fusion
  70.3 1.3 copy.45.order_col
  71.6 1.3 dynamic_slice.9
  72.9 1.3 dynamic_slice.10
  74.2 1.3 dynamic-slice_multiply_fusion
  75.5 0.5 and_select_fusion.low_ref
  76.0 2.8 fusion
  78.8 2.4 pad_maximum_fusion
  81.2 60.2 %project.1 = (bf16[1536,256]{1,0:T(8,128)(2,1)}, bf16[1536,256]{1,0:T(8,128)(2,1)}, bf16[1536,256]{1,0:T(8,128)(2,1)}, bf16[1536,512]{1,0:T(8,128)(2,1)}, bf16[1536,1024]{1,0:T(8,128)(2,1)}) custom-call(bf16[384,1024]{1,0:T(8,128)(2,1)} %tok_hbm.1, bf16[384,1024]{1,0:T(8,128)(2,1)} %get-tuple-element.43.tok2, bf16[1024,768]{1,0:T(8,128)(2,1)} %get-tuple-element.44.wqkv, ...), custom_call_target="tpu_custom_call" | custom-call | flops 60000002048 | bytes 10000000 | tf_op jit(solution)/shard_map/project/pallas_call | solution.py:907
  141.5 13.6 %attn_fwd.1 = (bf16[1536,256]{1,0:T(8,128)(2,1)}, f32[8,1536]{1,0:T(8,128)}, bf16[1536,256]{1,0:T(8,128)(2,1)}) custom-call(s32[6]{0:T(128)} %and_select_fusion.low_ref, s32[1,1536]{1,0:T(1,128)} %broadcast_in_dim.47.start_ref, s32[1,1536]{1,0:T(1,128)} %order_row.3, bf16[1536,256]{1,0:T(8,128)(2,1)} %get-tuple-element.45.q_ref, ...), custom_call_target="tpu_custom_call" | custom-call | flops 2415919104 | bytes 3145728 | tf_op jit(solution)/shard_map/attn_fwd/pallas_call | solution.py:102
  155.0 132.8 %middle.1 = (bf16[384,1024]{1,0:T(8,128)(2,1)}, bf16[1536,256]{1,0:T(8,128)(2,1)}, bf16[4,3,256,1024]{3,2,1,0:T(8,128)(2,1)}, bf16[1024,1024]{1,0:T(8,128)(2,1)}...) custom-call(bf16[1536,256]{1,0:T(8,128)(2,1)} %get-tuple-element.48., ...), custom_call_target="tpu_custom_call" | custom-call | flops 99999997952 | bytes 100000000 | tf_op jit(solution)/shard_map/middle/pallas_call | solution.py:556
  287.9 25.2 %attn_bwd.1.grad_ref = bf16[1536,768]{1,0:T(8,128)(2,1)} custom-call(s32[6]{0:T(128)} %and_select_fusion.low_ref, s32[1,1536]{1,0:T(1,128)} %broadcast_in_dim.47.start_ref, s32[1,1536]{1,0:T(1,128)} %order_row.3, s32[1536,1]{1,0:T(8,128)} %copy.45.order_col, f32[8,1536]{1,0:T(8,128)} %get-tuple-element.52.lse_ref, ...), custom_call_target="tpu_custom_call" | custom-call | flops 6039797760 | bytes 6291456 | tf_op jit(solution)/shard_map/attn_bwd/pallas_call | solution.py:182
  313.1 43.6 %reduce-scatter.4.cloned.1.call-done = bf16[1,3,256,1024]{3,2,1,0:T(8,128)(2,1)} async-done(((bf16[4,3,256,1024]{3,2,1,0:T(8,128)(2,1)}), bf16[1,3,256,1024]{3,2,1,0:T(8,128)(2,1)}) %reduce-scatter.4.cloned.1.call-update) | async-done | bytes 1572880
  356.7 2.4 bitcast_select_fusion
  359.0 0.7 collective-permute-start
  359.8 82.6 %tail.1 = (f32[384,1024]{1,0:T(8,128)}, f32[128,768]{1,0:T(8,128)}, f32[128,256]{1,0:T(8,128)}, f32[4,256]{1,0:T(4,128)}, f32[1,1024]{1,0:T(1,128)}, /*index=5*/...) custom-call(bf16[1536,768]{1,0:T(8,128)(2,1)} %attn_bwd.1.grad_ref, bf16[1536,512]{1,0:T(8,128)(2,1)} %get-tuple-element.55.raw_ref, ...), custom_call_target="tpu_custom_call" | custom-call | flops 60000002048 | bytes 10000000 | tf_op jit(solution)/shard_map/tail/pallas_call | solution.py:1171
  442.4 1.3 copy.51
  443.6 1.3 copy.57
  445.0 1.3 copy.56
  446.3 1.8 fusion.1
  448.1 0.6 convert_add_fusion
  448.7 1.2 slice_bitcast_fusion.2
  449.8 0.4 copy-done.2
  450.2 0.9 copy.63
  451.1 0.4 copy-done.1
  451.5 1.1 copy.64
  452.7 0.7 copy.65
  453.3 0.6 copy.66
  453.9 0.6 copy.67
  (29 shorter events, 0.4 us)
Async XLA Ops:
  7.2 61.1 %copy-start.7 = (s32[1,3]{1,0:T(1,128)S(1)}, s32[1,3]{1,0:T(1,128)}, u32[]{:S(2)}) copy-start(s32[1,3]{1,0:T(1,128)} %param.30) | copy-start | bytes 40
  7.2 62.0 %copy-start.4 = (s32[1,1536]{1,0:T(1,128)S(1)}, s32[1,1536]{1,0:T(1,128)}, u32[]{:S(2)}) copy-start(s32[1,1536]{1,0:T(1,128)} %order_row.3) | copy-start | bytes 18436
  7.2 147.8 %all-gather.3.cloned.1.call-start = ((), (), s32[]{:S(2)}) async-start(), calls=%async_computation.1 | async-start | bytes 7864320 | tf_op jit(solution)/shard_map/all_gather | solution.py:1317
  68.2 288.5 %reduce-scatter.4.cloned.1.call-start = ((), (), s32[]{:S(2)}) async-start(), calls=%async_computation.2 | async-start | bytes 7864320
  359.0 89.0 %collective-permute-start.1 = (bf16[3,128,1024]{2,1,0:T(8,128)(2,1)}, bf16[3,128,1024]{2,1,0:T(8,128)(2,1)S(1)}, u32[]{:S(2)}, u32[]{:S(2)}) collective-permute-start(bf16[3,128,1024]{2,1,0:T(8,128)(2,1)} %get-tuple-element.72), channel_id=1, source_target_pairs={{2,0},{3,1},{6,2},{7,3},{0,4},{1,5},{4,6},{5,7},{10,8},{11,9},{14,... | collective-permute-start | bytes 2359304 | tf_op jit(solution)/shard_map/ppermute | solution.py:1251
  359.0 89.0 %collective-permute-start = (bf16[3,128,1024]{2,1,0:T(8,128)(2,1)S(1)}, bf16[3,128,1024]{2,1,0:T(8,128)(2,1)S(1)}, u32[]{:S(2)}, u32[]{:S(2)}) collective-permute-start(bf16[3,128,1024]{2,1,0:T(8,128)(2,1)S(1)} %get-tuple-element.73), channel_id=1, source_target_pairs={{4,2},{5,3},{2,4},{3,5},{12,10},{13,11},{10,12},{11,13},{20,18},{2... | collective-permute-start | bytes 2359304 | tf_op jit(solution)/shard_map/ppermute | solution.py:1252
  359.8 88.3 %copy-start = (bf16[1,3,256,1024]{3,2,1,0:T(8,128)(2,1)S(1)}, bf16[1,3,256,1024]{3,2,1,0:T(8,128)(2,1)}, u32[]{:S(2)}) copy-start(bf16[1,3,256,1024]{3,2,1,0:T(8,128)(2,1)} %reduce-scatter.4.cloned.1.call-done) | copy-start | bytes 4718596
  448.7 1.6 copy-start.2
  449.8 1.7 copy-start.1
  451.5 1.2 copy-start.3
  451.5 1.8 copy-start.6
  451.5 2.4 copy-start.5
Sparse Core Ops, SparseCore 0:
  68.3 70.3 all-gather.2
  288.0 68.6 reduce-scatter.3

commit v5 on v4

--- a/solution.py
+++ b/solution.py
@@ -204,6 +204,7 @@
 EPS = 1e-06
 TILE = 256
 STRIP = 64
+WIDE_STRIP = 192
 
 
 def flip1(index):
@@ -215,6 +216,8 @@
 
 
 def tile_at(index, size):
+    if isinstance(index, int):
+        return pl.ds(index * size, size)
     return pl.ds(pl.multiple_of(index * size, size), size)
 
 
@@ -293,7 +296,7 @@
     loads[1].wait()
 
     def hop(buf, phase, ch, kind):
-        part = pl.ds(ch * crow, crow)
+        part = tile_at(ch, crow)
         index = (phase * chunks + ch) * 3 + kind
         src, dst, peer = ((0, 2, z_peer), (0, 1, core_peer), (2, 3, core_peer))[kind]
         return remote(buf.at[src, part, :], buf.at[dst, part, :], hop_send.at[index], hop_recv.at[index], peer)
@@ -325,8 +328,11 @@
         for copy in wloads[m]:
             copy.wait()
 
+    def within(slot, at):
+        return pl.ds(pl.multiple_of(slot * rows + at.start, STRIP), at.size)
+
     def forward_rows(slot, at, store, ready):
-        base = slot * rows
+        where = within(slot, at)
 
         def hidden(n):
             cols = tile_at(n, TILE)
@@ -335,7 +341,6 @@
             gate_raw = dot_ab(x, wall[1, :, cols])
             gate = gate_raw * sg_ref[:, cols]
             silu = gate / (1.0 + jnp.exp(-gate))
-            where = pl.ds(base + at.start, at.size)
             ups[where, cols] = up.astype(jnp.bfloat16)
             gates[where, cols] = gate_raw.astype(jnp.bfloat16)
             mixed[where, cols] = (up * su_ref[:, cols] * silu).astype(jnp.bfloat16)
@@ -345,13 +350,12 @@
 
         def down(n):
             cols = tile_at(n, TILE)
-            store(at, cols, dot_abt(mixed[pl.ds(base + at.start, at.size), :], wall[2, cols, :]))
+            store(at, cols, dot_abt(mixed[where, :], wall[2, cols, :]))
 
         over(width // TILE, down)
 
     def backward_rows(slot, at, store, ready):
-        base = slot * rows
-        where = pl.ds(base + at.start, at.size)
+        where = within(slot, at)
 
         def hidden(n):
             cols = tile_at(n, TILE)
@@ -377,13 +381,11 @@
         over(width // TILE, down)
 
     def part_copy(phase, kind, ch):
-        part = pl.ds(ch * crow, crow)
+        part = tile_at(ch, crow)
         index = (phase * 3 + kind) * chunks + ch
         src, dst, peer = ((send_a, recv_a, core_peer), (send_d, recv_d, core_peer), (send_z, recv_z, z_peer))[kind]
         return remote(src.at[part, :], dst.at[part, :], part_send.at[index], part_recv.at[index], peer)
 
-    everything = pl.ds(0, rows)
-
     def nothing():
         pass
 
@@ -400,20 +402,20 @@
         def to_z(at, cols, value):
             send_z[at, cols] = (value + recv_d[at, cols].astype(jnp.float32)).astype(jnp.bfloat16)
 
-        rows_fn(0, everything, keep_own, nothing)
+        over(chunks, lambda i: rows_fn(0, tile_at(i, crow), keep_own, nothing))
         for ch in range(chunks):
             hop(buf, phase, ch, 1).wait_recv()
         if phase == 1:
             for ch in range(chunks):
                 part_copy(0, 0, ch).wait_send()
-        rows_fn(1, everything, to(send_a), nothing)
+        over(chunks, lambda i: rows_fn(1, tile_at(i, crow), to(send_a), nothing))
         for ch in range(chunks):
             part_copy(phase, 0, ch).start()
         fillers[0]()
-        for ch in range(chunks):
+        def chunk(ch):
             hop(buf, phase, ch, 0).wait_recv()
             hop(buf, phase, ch, 2).start()
-            at = pl.ds(ch * crow, crow)
+            at = tile_at(ch, crow)
             hop(buf, phase, ch, 2).wait_recv()
             if phase == 1:
                 part_copy(0, 1, ch).wait_send()
@@ -427,15 +429,21 @@
 
             rows_fn(2, at, to_z, ready)
             part_copy(phase, 2, ch).start()
+
+        over(chunks, chunk)
         fillers[1]()
 
     def transpose_into(dst, buf, slots):
-        for slot in slots:
-            for b in range(rows // 128):
-                for n in range(width // TILE):
-                    dst[n * TILE : (n + 1) * TILE, slot * rows + b * 128 : slot * rows + (b + 1) * 128] = buf[
-                        slot, b * 128 : (b + 1) * 128, n * TILE : (n + 1) * TILE
-                    ].T
+        per_slot = rows // 128
+
+        def one(i):
+            slot = slots[0] + i // per_slot
+            at = tile_at(lax.rem(i, per_slot), 128)
+            to = tile_at(slots[0] * per_slot + i, 128)
+            for n in range(width // TILE):
+                dst[n * TILE : (n + 1) * TILE, to] = buf[slot, at, n * TILE : (n + 1) * TILE].T
+
+        over(len(slots) * per_slot, one)
 
     tensor_pass(
         0, mids, forward_rows,
@@ -512,11 +520,7 @@
         else:
             datt_ref[tile_at(t, rows), :] = value
 
-    for b in range(rows // 128):
-        for n in range(width // TILE):
-            mid_t[n * TILE : (n + 1) * TILE, b * 128 : (b + 1) * 128] = mids[
-                0, b * 128 : (b + 1) * 128, n * TILE : (n + 1) * TILE
-            ].T
+    transpose_into(mid_t, mids, (0,))
 
     def out_grad(n):
         at = tile_at(n, TILE)
@@ -852,16 +856,20 @@
 
     def work(index, slot):
         keep(index, slot).start()
-        at = tile_at(slot, rows)
-        x = xs[slot]
-        cos = jnp.concatenate([cos_ref[at, :]] * (cols // cos_ref.shape[1]), axis=1)
-        sin = jnp.concatenate([sin_ref[at, :]] * (cols // sin_ref.shape[1]), axis=1)
-        for m in range(2):
-            raw = dot_ab(x, wqkv[:, m * cols : (m + 1) * cols])
-            raw_ref[at, m * cols : (m + 1) * cols] = raw.astype(jnp.bfloat16)
-            normed = raw * lax.rsqrt(head_sums(raw * raw) + EPS) * gain_ref[...]
-            plain[at, m * cols : (m + 1) * cols] = (normed * cos + swap_halves(normed) * sin).astype(jnp.bfloat16)
-        plain[at, 2 * cols : 3 * cols] = dot_ab(x, wqkv[:, 2 * cols : 3 * cols]).astype(jnp.bfloat16)
+
+        def strip(i):
+            at = tile_at(slot * (rows // WIDE_STRIP) + i, WIDE_STRIP)
+            x = xs[slot, tile_at(i, WIDE_STRIP), :]
+            cos = jnp.concatenate([cos_ref[at, :]] * (cols // cos_ref.shape[1]), axis=1)
+            sin = jnp.concatenate([sin_ref[at, :]] * (cols // sin_ref.shape[1]), axis=1)
+            for m in range(2):
+                raw = dot_ab(x, wqkv[:, m * cols : (m + 1) * cols])
+                raw_ref[at, m * cols : (m + 1) * cols] = raw.astype(jnp.bfloat16)
+                normed = raw * lax.rsqrt(head_sums(raw * raw) + EPS) * gain_ref[...]
+                plain[at, m * cols : (m + 1) * cols] = (normed * cos + swap_halves(normed) * sin).astype(jnp.bfloat16)
+            plain[at, 2 * cols : 3 * cols] = dot_ab(x, wqkv[:, 2 * cols : 3 * cols]).astype(jnp.bfloat16)
+
+        over(rows // WIDE_STRIP, strip)
 
     loads[0].wait()
     work(0, t)
@@ -922,48 +930,22 @@
 
 
 def tail_body(
-    count, grad_ref, raw_ref, cos_ref, sin_ref, wqkv, x_hbm, gwo_hbm, kept_ref, gain_ref, gaa_ref, gam_ref, gsu_ref, gsg_ref,
-    tok_out, qkv_out, wo_out, gain_out, aa_out, am_out, su_out, sg_out,
+    grad_ref, raw_ref, cos_ref, sin_ref, wqkv, x_hbm, kept_ref, gain_ref, tok_out, gq, gain_sum,
     xs, x_t, draw, part_far, part_mid, part_near, own_part, from_a, from_b, from_c, from_d, from_e, from_f,
-    gq, got_q, got_w, wo_mid, got_z, vec, got_v, vec_mid, got_s, load_sem,
-    hop_send, hop_recv, q_send, q_recv, w_send, w_recv, z_send, z_recv, v_send, v_recv, s_send, s_recv,
+    load_sem, hop_send, hop_recv,
 ):
     d = lax.axis_index("dp")
     t = lax.axis_index("tensor")
     rows, width = tok_out.shape
     group = draw.shape[0]
     cols = draw.shape[1] // 3
-    wrows = qkv_out.shape[0]
     near = flip1(t)
     inner = (t + 1) // 2 == 1
     outer = jnp.logical_not(inner)
     far, mid = 3 - 3 * (t // 2), 2 - t // 2
     chunk = rows // 2
-
-    def dp_peer(i):
-        return lax.rem(d + 1 + i, count)
-
-    def line_peer(k):
-        return lax.rem(t + k, 4)
-
-    barrier = pltpu.get_barrier_semaphore()
-    over(
-        count - 1,
-        lambda i: pl.semaphore_signal(barrier, inc=1, device_id=(dp_peer(i), t), device_id_type=MESH_ID),
-    )
-    for k in (1, 2, 3):
-        pl.semaphore_signal(barrier, inc=1, device_id=(d, line_peer(k)), device_id_type=MESH_ID)
-    pl.semaphore_wait(barrier, count + 2)
-
-    def w_copy(i):
-        return remote_copy(
-            gwo_hbm.at[tile_at(dp_peer(i), wrows), :], got_w.at[d], w_send.at[i], w_recv.at[i], (dp_peer(i), t)
-        )
-
-    over(count - 1, lambda i: w_copy(i).start())
-    load_w = pltpu.make_async_copy(gwo_hbm.at[tile_at(d, wrows), :], got_w.at[d], load_sem.at[0])
-    load_x = pltpu.make_async_copy(x_hbm, xs, load_sem.at[1])
-    load_w.start()
+    greet([(d, near), (d, 3 - t)])
+    load_x = pltpu.make_async_copy(x_hbm, xs, load_sem)
     load_x.start()
 
     def hop(kind, ch):
@@ -978,29 +960,33 @@
         part = pl.ds(ch * chunk, chunk)
         return remote_copy(src.at[part, :], dst.at[part, :], hop_send.at[kind, ch], hop_recv.at[kind, ch], (d, to))
 
-    vec[...] = jnp.zeros_like(vec)
+    gain_sum[...] = jnp.zeros_like(gain_sum)
 
     def work(slot, store):
-        at = tile_at(slot, rows)
-        cos = jnp.concatenate([cos_ref[at, :]] * (cols // cos_ref.shape[1]), axis=1)
-        sin = jnp.concatenate([sin_ref[at, :]] * (cols // sin_ref.shape[1]), axis=1)
-        gain = gain_ref[...]
-        for m in range(2):
-            grad = grad_ref[at, m * cols : (m + 1) * cols].astype(jnp.float32)
-            raw = raw_ref[at, m * cols : (m + 1) * cols].astype(jnp.float32)
-            back = grad * cos - swap_halves(grad) * sin
-            factor = lax.rsqrt(head_sums(raw * raw) + EPS)
-            normed = raw * factor
-            vec[4:5, 0:cols] += jnp.sum(back * normed, axis=0, keepdims=True)
-            scaled = back * gain
-            draw[at, m * cols : (m + 1) * cols] = (factor * (scaled - normed * head_sums(normed * scaled))).astype(
-                jnp.bfloat16
-            )
-        draw[at, 2 * cols : 3 * cols] = grad_ref[at, 2 * cols : 3 * cols]
+        def strip(i):
+            at = tile_at(slot * (rows // WIDE_STRIP) + i, WIDE_STRIP)
+            cos = jnp.concatenate([cos_ref[at, :]] * (cols // cos_ref.shape[1]), axis=1)
+            sin = jnp.concatenate([sin_ref[at, :]] * (cols // sin_ref.shape[1]), axis=1)
+            gain = gain_ref[...]
+            for m in range(2):
+                grad = grad_ref[at, m * cols : (m + 1) * cols].astype(jnp.float32)
+                raw = raw_ref[at, m * cols : (m + 1) * cols].astype(jnp.float32)
+                back = grad * cos - swap_halves(grad) * sin
+                factor = lax.rsqrt(head_sums(raw * raw) + EPS)
+                normed = raw * factor
+                gain_sum[...] += jnp.sum(back * normed, axis=0, keepdims=True)
+                scaled = back * gain
+                draw[at, m * cols : (m + 1) * cols] = (
+                    factor * (scaled - normed * head_sums(normed * scaled))
+                ).astype(jnp.bfloat16)
+            draw[at, 2 * cols : 3 * cols] = grad_ref[at, 2 * cols : 3 * cols]
+
+        over(rows // WIDE_STRIP, strip)
+        everything = tile_at(slot, rows)
 
         def product(n):
             tile = tile_at(n, TILE)
-            store(tile, dot_abt(draw[at, :], wqkv[tile, :]))
+            store(tile, dot_abt(draw[everything, :], wqkv[tile, :]))
 
         over(width // TILE, product)
 
@@ -1019,15 +1005,6 @@
                 hop(kind, ch).start()
 
     work(t, into(own_part))
-
-    for row, ref in enumerate((gaa_ref, gam_ref, gsu_ref, gsg_ref)):
-        vec[row : row + 1, :] = ref[...]
-    got_v[d] = vec[...]
-
-    def v_copy(i):
-        return remote_copy(vec, got_v.at[d], v_send.at[i], v_recv.at[i], (dp_peer(i), t))
-
-    over(count - 1, lambda i: v_copy(i).start())
 
     def pass_on(kind, ch, own, got, then):
         @pl.when(inner)
@@ -1055,67 +1032,9 @@
         gq[tile, :] = dot_ab(x_t[tile, :], draw[...]).astype(jnp.bfloat16)
 
     over(width // TILE, weight_grad)
-
-    def q_copy(i):
-        return remote_copy(gq.at[tile_at(dp_peer(i), wrows), :], got_q.at[d], q_send.at[i], q_recv.at[i], (dp_peer(i), t))
-
-    over(count - 1, lambda i: q_copy(i).start())
-    got_q[d] = gq[tile_at(d, wrows), :]
     pass_on(1, 0, part_mid, from_b, 4)
     pass_on(3, 1, part_near, from_d, 5)
     pass_on(1, 1, part_mid, from_b, 4)
-
-    load_w.wait()
-    over(count - 1, lambda i: w_copy(i).wait_recv())
-    wo_mid[...] = lax.fori_loop(
-        1, count, lambda i, total: total + got_w[i].astype(jnp.float32), got_w[0].astype(jnp.float32)
-    ).astype(jnp.bfloat16)
-
-    def z_copy(k):
-        return remote_copy(
-            wo_mid.at[:, tile_at(line_peer(k), cols)], got_z.at[t], z_send.at[k - 1], z_recv.at[k - 1], (d, line_peer(k))
-        )
-
-    for k in (1, 2, 3):
-        z_copy(k).start()
-    got_z[t] = wo_mid[:, tile_at(t, cols)]
-
-    over(count - 1, lambda i: v_copy(i).wait_recv())
-    even, odd = lax.fori_loop(
-        1, count // 2, lambda i, total: (total[0] + got_v[2 * i], total[1] + got_v[2 * i + 1]), (got_v[0], got_v[1])
-    )
-    both = even + odd
-    vec_mid[...] = jnp.concatenate([both[0:2], even[2:3], odd[2:3], even[3:4], odd[3:4], both[4:5], both[4:5]], axis=0)
-
-    def s_copy(k):
-        return remote_copy(vec_mid, got_s.at[t], s_send.at[k - 1], s_recv.at[k - 1], (d, line_peer(k)))
-
-    for k in (1, 2, 3):
-        s_copy(k).start()
-    got_s[t] = vec_mid[...]
-
-    over(count - 1, lambda i: q_copy(i).wait_recv())
-    qkv_out[...] = lax.fori_loop(
-        1, count, lambda i, total: total + got_q[i].astype(jnp.float32), got_q[0].astype(jnp.float32)
-    )
-
-    for k in (1, 2, 3):
-        z_copy(k).wait_recv()
-        s_copy(k).wait_recv()
-    wo_out[...] = (
-        got_z[0].astype(jnp.float32)
-        + got_z[1].astype(jnp.float32)
-        + got_z[2].astype(jnp.float32)
-        + got_z[3].astype(jnp.float32)
-    )
-    shared = got_s[0] + got_s[1] + got_s[2] + got_s[3]
-    aa_out[...] = shared[0:1]
-    am_out[...] = shared[1:2]
-    pairs = (got_s[0] + got_s[2], got_s[1] + got_s[3])
-    for s in range(4):
-        su_out[s : s + 1, :] = pairs[s % 2][2 + s // 2 : 3 + s // 2]
-        sg_out[s : s + 1, :] = pairs[s % 2][4 + s // 2 : 5 + s // 2] * math.sqrt(D)
-        gain_out[s : s + 1, :] = got_s[s][6:7, 0:cols]
 
     for ch in range(2):
         part = pl.ds(ch * chunk, chunk)
@@ -1148,40 +1067,19 @@
             for kind in (0, 1, 2):
                 hop(kind, ch).wait_send()
 
-    def drain(i):
-        w_copy(i).wait_send()
-        v_copy(i).wait_send()
-        q_copy(i).wait_send()
-
-    over(count - 1, drain)
-    for k in (1, 2, 3):
-        z_copy(k).wait_send()
-        s_copy(k).wait_send()
-
-
-def tail_call(count, grad_qkv, raw, cos, sin, wqkv, all_tokens, wo_grads, kept, gains, gaa, gam, gsu, gsg):
+
+def tail_call(grad_qkv, raw, cos, sin, wqkv, all_tokens, kept, gains):
     rows, width = kept.shape
     group, three = grad_qkv.shape
-    cols = three // 3
-    wrows = width // count
     bf, f32 = jnp.bfloat16, jnp.float32
     anywhere = pl.BlockSpec(memory_space=pl.ANY)
     dma = pltpu.SemaphoreType.DMA
     shape = jax.ShapeDtypeStruct
     return pl.pallas_call(
-        functools.partial(tail_body, count),
-        out_shape=(
-            shape((rows, width), f32),
-            shape((wrows, three), f32),
-            shape((wrows, cols), f32),
-            shape((4, cols), f32),
-            shape((1, width), f32),
-            shape((1, width), f32),
-            shape((4, width), f32),
-            shape((4, width), f32),
-        ),
-        in_specs=[vmem()] * 5 + [anywhere, anywhere] + [vmem()] * 6,
-        out_specs=(vmem(),) * 8,
+        tail_body,
+        out_shape=(shape((rows, width), f32), shape((width, three), bf), shape((1, three // 3), f32)),
+        in_specs=[vmem()] * 5 + [anywhere] + [vmem()] * 2,
+        out_specs=(vmem(),) * 3,
         scratch_shapes=[
             pltpu.VMEM((group, width), bf),
             pltpu.VMEM((width, group), bf),
@@ -1192,66 +1090,241 @@
             pltpu.VMEM((rows, width), f32),
         ]
         + [pltpu.VMEM((rows, width), bf)] * 6
+        + [dma, dma((6, 2)), dma((6, 2))],
+        compiler_params=pltpu.CompilerParams(vmem_limit_bytes=VMEM_LIMIT, collective_id=4, has_side_effects=True),
+        cost_estimate=pl.CostEstimate(flops=6 * 10**10, bytes_accessed=10**7, transcendentals=10**6),
+        name="tail",
+    )(grad_qkv, raw, cos, sin, wqkv, all_tokens, kept, gains)
+
+
+def settle_body(
+    count, gq_hbm, gwo_hbm, mlp_hbm, gain_ref, gaa_ref, gam_ref, gsu_ref, gsg_ref,
+    q_out, k_out, v_out, wo_out, up_out, gate_out, down_out, gain_out, aa_out, am_out, su_out, sg_out,
+    own_q, core_q, got_q, own_w, core_w, got_w, wo_mid, got_z, near_mlp, far_mlp, vec, got_v, vec_mid, got_s,
+    load_sem, core_send, core_recv, q_send, q_recv, w_send, w_recv, z_send, z_recv, v_send, v_recv, s_send, s_recv,
+    mlp_send, mlp_recv,
+):
+    d = lax.axis_index("dp")
+    t = lax.axis_index("tensor")
+    half, wrows, three = got_q.shape
+    cols = three // 3
+    width = gaa_ref.shape[1]
+    chip, core = d // 2, lax.rem(d, 2)
+    home = core == t // 2
+    away = jnp.logical_not(home)
+    f32, bf = jnp.float32, jnp.bfloat16
+
+    def dp_peer(i):
+        return lax.rem(d + 1 + i, count)
+
+    def line_peer(k):
+        return lax.rem(t + k, 4)
+
+    def chip_peer(i):
+        return lax.rem(chip + 1 + i, half)
+
+    barrier = pltpu.get_barrier_semaphore()
+    over(
+        count - 1,
+        lambda i: pl.semaphore_signal(barrier, inc=1, device_id=(dp_peer(i), t), device_id_type=MESH_ID),
+    )
+    for k in (1, 2, 3):
+        pl.semaphore_signal(barrier, inc=1, device_id=(d, line_peer(k)), device_id_type=MESH_ID)
+    pl.semaphore_signal(barrier, inc=1, device_id=(flip1(d), flip2(t)), device_id_type=MESH_ID)
+    pl.semaphore_wait(barrier, count + 3)
+
+    near_copy = remote_copy(mlp_hbm.at[:, 1 - core], near_mlp, mlp_send.at[0], mlp_recv.at[0], (flip1(d), t))
+    far_same = remote_copy(mlp_hbm.at[:, core], far_mlp, mlp_send.at[1], mlp_recv.at[1], (d, flip2(t)))
+    far_cross = remote_copy(mlp_hbm.at[:, 1 - core], far_mlp, mlp_send.at[2], mlp_recv.at[1], (flip1(d), flip2(t)))
+    keep_mlp = pltpu.make_async_copy(mlp_hbm.at[:, core], near_mlp, load_sem.at[0])
+
+    @pl.when(home)
+    def _():
+        near_copy.start()
+        keep_mlp.start()
+
+    @pl.when(away)
+    def _():
+        far_same.start()
+        far_cross.start()
+
+    core_w_copy = remote_copy(gwo_hbm.at[:, 1 - core], core_w, core_send.at[0], core_recv.at[0], (flip1(d), t))
+    core_q_copy = remote_copy(gq_hbm.at[:, 1 - core], core_q, core_send.at[1], core_recv.at[1], (flip1(d), t))
+    load_w = pltpu.make_async_copy(gwo_hbm.at[:, core], own_w, load_sem.at[1])
+    load_q = pltpu.make_async_copy(gq_hbm.at[:, core], own_q, load_sem.at[2])
+    core_w_copy.start()
+    core_q_copy.start()
+    load_w.start()
+    load_q.start()
+
+    vec[...] = jnp.zeros_like(vec)
+    for row, ref in enumerate((gaa_ref, gam_ref, gsu_ref, gsg_ref)):
+        vec[row : row + 1, :] = ref[...]
+    vec[4:5, 0:cols] = gain_ref[...]
+    got_v[d] = vec[...]
+
+    def v_copy(i):
+        return remote_copy(vec, got_v.at[d], v_send.at[i], v_recv.at[i], (dp_peer(i), t))
+
+    over(count - 1, lambda i: v_copy(i).start())
+
+    def chip_copy(own, got, sends, recvs, i):
+        return remote_copy(own.at[chip_peer(i)], got.at[chip], sends.at[i], recvs.at[i], (2 * chip_peer(i) + core, t))
+
+    def w_copy(i):
+        return chip_copy(own_w, got_w, w_send, w_recv, i)
+
+    def q_copy(i):
+        return chip_copy(own_q, got_q, q_send, q_recv, i)
+
+    def join(own, other, got):
+        def one(e):
+            own[e] = (own[e].astype(f32) + other[e].astype(f32)).astype(bf)
+
+        over(half, one)
+        got[chip] = own[chip]
+
+    load_w.wait()
+    core_w_copy.wait_recv()
+    join(own_w, core_w, got_w)
+    over(half - 1, lambda i: w_copy(i).start())
+    load_q.wait()
+    core_q_copy.wait_recv()
+    join(own_q, core_q, got_q)
+    over(half - 1, lambda i: q_copy(i).start())
+
+    def total_of(got):
+        return lax.fori_loop(1, half, lambda i, total: total + got[i].astype(f32), got[0].astype(f32))
+
+    over(half - 1, lambda i: w_copy(i).wait_recv())
+    wo_mid[...] = total_of(got_w).astype(bf)
+
+    def z_copy(k):
+        return remote_copy(
+            wo_mid.at[:, tile_at(line_peer(k), cols)], got_z.at[t], z_send.at[k - 1], z_recv.at[k - 1], (d, line_peer(k))
+        )
+
+    for k in (1, 2, 3):
+        z_copy(k).start()
+    got_z[t] = wo_mid[:, tile_at(t, cols)]
+
+    over(count - 1, lambda i: v_copy(i).wait_recv())
+    even, odd = lax.fori_loop(
+        1, half, lambda i, total: (total[0] + got_v[2 * i], total[1] + got_v[2 * i + 1]), (got_v[0], got_v[1])
+    )
+    both = even + odd
+    vec_mid[...] = jnp.concatenate([both[0:2], even[2:3], odd[2:3], even[3:4], odd[3:4], both[4:5], both[4:5]], axis=0)
+
+    def s_copy(k):
+        return remote_copy(vec_mid, got_s.at[t], s_send.at[k - 1], s_recv.at[k - 1], (d, line_peer(k)))
+
+    for k in (1, 2, 3):
+        s_copy(k).start()
+    got_s[t] = vec_mid[...]
+
+    over(half - 1, lambda i: q_copy(i).wait_recv())
+    total = total_of(got_q)
+    for m, ref in enumerate((q_out, k_out, v_out)):
+        ref[...] = total[:, m * cols : (m + 1) * cols]
+
+    for k in (1, 2, 3):
+        z_copy(k).wait_recv()
+        s_copy(k).wait_recv()
+    wo_out[...] = got_z[0].astype(f32) + got_z[1].astype(f32) + got_z[2].astype(f32) + got_z[3].astype(f32)
+    shared = got_s[0] + got_s[1] + got_s[2] + got_s[3]
+    aa_out[...] = shared[0:1]
+    am_out[...] = shared[1:2]
+    pairs = (got_s[0] + got_s[2], got_s[1] + got_s[3])
+    for s in range(4):
+        su_out[:, s * width : (s + 1) * width] = pairs[s % 2][2 + s // 2 : 3 + s // 2]
+        sg_out[:, s * width : (s + 1) * width] = pairs[s % 2][4 + s // 2 : 5 + s // 2] * math.sqrt(D)
+        gain_out[:, s * cols : (s + 1) * cols] = got_s[s][6:7, 0:cols]
+
+    far_same.wait_recv()
+
+    @pl.when(home)
+    def _():
+        keep_mlp.wait()
+        near_copy.wait_send()
+
+    @pl.when(away)
+    def _():
+        near_copy.wait_recv()
+        far_same.wait_send()
+        far_cross.wait_send()
+
+    for m, ref in enumerate((up_out, gate_out, down_out)):
+        ref[...] = near_mlp[m].astype(f32) + far_mlp[m].astype(f32)
+
+    core_w_copy.wait_send()
+    core_q_copy.wait_send()
+    over(count - 1, lambda i: v_copy(i).wait_send())
+
+    def drain(i):
+        w_copy(i).wait_send()
+        q_copy(i).wait_send()
+
+    over(half - 1, drain)
+    for k in (1, 2, 3):
+        z_copy(k).wait_send()
+        s_copy(k).wait_send()
+
+
+def settle_call(count, gq, gwo, mlp, gain_sum, gaa, gam, gsu, gsg):
+    width, three = gq.shape
+    half = count // 2
+    cols = three // 3
+    wrows = width // count
+    hid = mlp.shape[2]
+    bf, f32 = jnp.bfloat16, jnp.float32
+    anywhere = pl.BlockSpec(memory_space=pl.ANY)
+    dma = pltpu.SemaphoreType.DMA
+    shape = jax.ShapeDtypeStruct
+    return pl.pallas_call(
+        functools.partial(settle_body, count),
+        out_shape=(shape((wrows, cols), f32),) * 4
+        + (shape((wrows, hid), f32),) * 3
+        + (
+            shape((1, 4 * cols), f32),
+            shape((1, width), f32),
+            shape((1, width), f32),
+            shape((1, 4 * hid), f32),
+            shape((1, 4 * hid), f32),
+        ),
+        in_specs=[anywhere] * 3 + [vmem()] * 5,
+        out_specs=(vmem(),) * 12,
+        scratch_shapes=[pltpu.VMEM((half, wrows, three), bf)] * 3
+        + [pltpu.VMEM((half, wrows, width), bf)] * 3
         + [
-            pltpu.VMEM((width, three), bf),
-            pltpu.VMEM((count, wrows, three), bf),
-            pltpu.VMEM((count, wrows, width), bf),
             pltpu.VMEM((wrows, width), bf),
             pltpu.VMEM((4, wrows, cols), bf),
+            pltpu.VMEM((3, wrows, hid), bf),
+            pltpu.VMEM((3, wrows, hid), bf),
             pltpu.VMEM((8, width), f32),
             pltpu.VMEM((count, 8, width), f32),
             pltpu.VMEM((8, width), f32),
             pltpu.VMEM((4, 8, width), f32),
-            dma((2,)),
-            dma((6, 2)), dma((6, 2)),
-            dma((count - 1,)), dma((count - 1,)), dma((count - 1,)), dma((count - 1,)),
+            dma((3,)),
+            dma((2,)), dma((2,)),
+            dma((half - 1,)), dma((half - 1,)), dma((half - 1,)), dma((half - 1,)),
             dma((3,)), dma((3,)),
             dma((count - 1,)), dma((count - 1,)),
             dma((3,)), dma((3,)),
+            dma((3,)), dma((2,)),
         ],
-        compiler_params=pltpu.CompilerParams(vmem_limit_bytes=VMEM_LIMIT, collective_id=4, has_side_effects=True),
-        cost_estimate=pl.CostEstimate(flops=6 * 10**10, bytes_accessed=10**7, transcendentals=10**6),
-        name="tail",
-    )(grad_qkv, raw, cos, sin, wqkv, all_tokens, wo_grads, kept, gains, gaa, gam, gsu, gsg)
-
-
-def flat(dp_index, tensor_index, tensor_count):
-    return dp_index * tensor_count + tensor_index
-
-
-def hidden_routes(dp_count, tensor_count):
-    near, far = [], []
-    for d in range(dp_count):
-        for t in range(tensor_count):
-            own = flat(d, t, tensor_count)
-            if d % 2 != t // 2:
-                near.append((own, flat(d ^ 1, t, tensor_count)))
-                far.append((own, flat(d ^ 1, t ^ 2, tensor_count)))
-            else:
-                near.append((own, flat(d, t ^ 2, tensor_count)))
-    return near, far
+        compiler_params=pltpu.CompilerParams(vmem_limit_bytes=VMEM_LIMIT, collective_id=5, has_side_effects=True),
+        cost_estimate=pl.CostEstimate(flops=10**9, bytes_accessed=10**7, transcendentals=0),
+        name="settle",
+    )(
+        gq.reshape(half, 2, wrows, three),
+        gwo.reshape(half, 2, wrows, width),
+        mlp.reshape(3, 2, wrows, hid),
+        gain_sum, gaa, gam, gsu, gsg,
+    )
 
 
 def same_core_groups(dp_count):
     return [list(range(parity, dp_count, 2)) for parity in range(2)]
-
-
-def scatter_hidden(parts, dp_count, tensor_count):
-    near, far = hidden_routes(dp_count, tensor_count)
-    axes = ("dp", "tensor")
-    core = lax.rem(lax.axis_index("dp"), 2)
-    home = core == lax.axis_index("tensor") // 2
-    summed = lax.psum_scatter(
-        parts, "dp", scatter_dimension=0, tiled=False, axis_index_groups=same_core_groups(dp_count)
-    )
-    kinds, rows, cols = summed.shape
-    halves = summed.reshape(kinds, 2, rows // 2, cols)
-    mine = jnp.where(core == 0, halves[:, 0], halves[:, 1])
-    other = jnp.where(core == 0, halves[:, 1], halves[:, 0])
-    first = lax.ppermute(jnp.where(home, other, mine), axes, [(b, a) for a, b in near])
-    second = lax.ppermute(other, axes, [(b, a) for a, b in far])
-    f32 = jnp.float32
-    return jnp.where(home, mine.astype(f32), second.astype(f32)) + first.astype(f32)
 
 
 def layout(order_row, length_row):
@@ -1336,40 +1409,18 @@
     grad_qkv = attn_bwd(
         low, start, order, order_col, log_totals, queries, key_rows, value_rows, attended, grad_att_rows
     )
-    grad_tokens, qkv_sums, wo_sums, grad_gain, sum_aa, sum_am, sum_su, sum_sv = tail_call(
-        dp_count,
-        grad_qkv,
-        raw,
-        cos_table,
-        sin_table,
-        wqkv,
-        all_tokens,
-        wo_grads,
-        grad_h1_kept,
-        qk_gains[None, :],
-        grad_alpha_a,
-        grad_alpha_m,
-        grad_su,
-        grad_sv,
-    )
-    mlp_sums = scatter_hidden(mlp_grads, dp_count, tensor_count)
-    weight_sums = [qkv_sums[:, i * head_cols : (i + 1) * head_cols] for i in range(3)] + [wo_sums, *mlp_sums]
-    return (
-        out_rows,
-        grad_tokens,
-        weight_sums[0],
-        weight_sums[1],
-        weight_sums[2],
-        weight_sums[3],
-        weight_sums[4],
-        weight_sums[5],
-        weight_sums[6],
-        grad_gain.reshape(-1),
-        sum_aa.reshape(-1),
-        sum_su.reshape(-1),
-        sum_sv.reshape(-1),
-        sum_am.reshape(-1),
-    )
+    mlp_sums = lax.psum_scatter(
+        mlp_grads, "dp", scatter_dimension=0, tiled=False, axis_index_groups=same_core_groups(dp_count)
+    )
+    grad_tokens, grad_q, gain_sum = tail_call(
+        grad_qkv, raw, cos_table, sin_table, wqkv, all_tokens, grad_h1_kept, qk_gains[None, :]
+    )
+    settled = settle_call(
+        dp_count, grad_q, wo_grads, mlp_sums, gain_sum, grad_alpha_a, grad_alpha_m, grad_su, grad_sv
+    )
+    weights, vectors = settled[:7], [v.reshape(-1) for v in settled[7:]]
+    grad_gain, sum_aa, sum_am, sum_su, sum_sv = vectors
+    return (out_rows, grad_tokens, *weights, grad_gain, sum_aa, sum_su, sum_sv, sum_am)
 
 
 def solution(mesh):

time: 471 us -> 451 us (0.958); the launches traced: 462 us -> 449 us
  waiting for transfers between devices: 43.7 us -> 0.06 us
  Pallas kernels: 375 us -> 412 us
    unnamed x3, waiting for transfers between devices: 43.7 us -> 0.06 us
    pallas_call x1 -> x2, Pallas kernels: 82.6 us -> 112 us  [the longest x1 61.1 us: tail_call(): pl.pallas_call(tail_body, out_shape=(shape((rows, width), f32), shape((wi...]
    pallas_call x1, Pallas kernels: 133 us -> 139 us  [middle_call(): pl.pallas_call(middle_body, out_shape=(jax.ShapeDtypeStruct((rows, width)...]
    unnamed x24 -> x46, local copies, waits for them, and re-layouts: 8.61 us -> 10.1 us
  transfers between devices with their start and end apart: 4 -> 2, of which waited for: 1 -> 0; matrix products, arithmetic and copies ran while one was open for 4% -> 3% of each run, Pallas kernels for 39% -> 36%
where the time goes in v5:
time: 451 us; the launch traced here: 449 us
  Pallas kernels  412 us (91%)
  local copies, waits for them, and re-layouts  14.6 us (3%)
  between operations  14.3 us (3%)
  other arithmetic  8.39 us (2%)
    pallas_call x1, Pallas kernels, middle_call(): pl.pallas_call(middle_body, out_shape=(jax.ShapeDtypeStruct((rows, width)...  139 us
    pallas_call x1, Pallas kernels, tail_call(): pl.pallas_call(tail_body, out_shape=(shape((rows, width), f32), shape((wi...  61.1 us
    pallas_call x1, Pallas kernels, spread_call(): pl.pallas_call(functools.partial(spread_body, count), out_shape=(jax.Shap...  60.9 us
    pallas_call x1, Pallas kernels, project_call(): pl.pallas_call(project_body, out_shape=(jax.ShapeDtypeStruct((group, cols...  60.5 us
    pallas_call x1, Pallas kernels, settle_call(): pl.pallas_call(functools.partial(settle_body, count), out_shape=(shape((w...  51.3 us
    pallas_call x1, Pallas kernels, attn_bwd(): pl.pallas_call(attn_bwd_body, out_shape=jax.ShapeDtypeStruct((rows, 3 * c...  25.3 us
    pallas_call x1, Pallas kernels, attn_fwd(): pl.pallas_call(attn_fwd_body, out_shape=(jax.ShapeDtypeStruct((rows, cols...  13.6 us
    unnamed x46, local copies, waits for them, and re-layouts  10.1 us
  transfers between devices with their start and end apart: 2, of which 0 were waited for; matrix products, arithmetic and copies ran while one was open for 3% of the time, Pallas kernels for 36%

profile of v5, /device:TPU:0, one launch (start us, length us, event | category | flops | bytes accessed | tf_op | source)
XLA Modules:
  0.0 449.1 jit_solution(6843499910374489544)
XLA Ops:
  7.3 60.9 %spread.1 = (bf16[3,256,1024]{2,1,0:T(8,128)(2,1)}, bf16[384,1024]{1,0:T(8,128)(2,1)}, bf16[1024,768]{1,0:T(8,128)(2,1)}, bf16[1024,1024]{1,0:T(8,128)(2,1)}) custom-call(bf16[384,1024]{1,0:T(8,128)(2,1)} %tok_hbm.1, bf16[128,1024]{1,0:T(8,128)(2,1)} %w_up.1, bf16[128,1024]{1,0:T(8,128)(2,1)} %w_gate.1, bf16[128,1024]{1,0:T(8,128)(2,1)} %w_down.1, ...), custom_call_target="tpu_custom_call" | custom-call | tf_op jit(solution)/shard_map/spread/pallas_call | solution.py:778
  68.3 0.2 reduce-window_clone.1
  68.4 0.1 select_reduce_fusion.1
  68.6 0.6 broadcast_in_dim.47.start_ref
  69.3 1.0 select_reduce_fusion
  70.3 1.3 copy.37.order_col
  71.6 1.3 dynamic_slice.9
  72.9 1.3 dynamic_slice.10
  74.2 1.3 dynamic-slice_multiply_fusion
  75.5 0.5 and_select_fusion.low_ref
  76.0 2.8 fusion
  78.8 2.4 pad_maximum_fusion
  81.2 60.5 %project.1 = (bf16[1536,256]{1,0:T(8,128)(2,1)}, bf16[1536,256]{1,0:T(8,128)(2,1)}, bf16[1536,256]{1,0:T(8,128)(2,1)}, bf16[1536,512]{1,0:T(8,128)(2,1)}, bf16[1536,1024]{1,0:T(8,128)(2,1)}) custom-call(bf16[384,1024]{1,0:T(8,128)(2,1)} %tok_hbm.1, bf16[384,1024]{1,0:T(8,128)(2,1)} %get-tuple-element.50.tok2, bf16[1024,768]{1,0:T(8,128)(2,1)} %get-tuple-element.51.wqkv, ...), custom_call_target="tpu_custom_call" | custom-call | flops 60000002048 | bytes 10000000 | tf_op jit(solution)/shard_map/project/pallas_call | solution.py:915
  141.7 13.6 %attn_fwd.1 = (bf16[1536,256]{1,0:T(8,128)(2,1)}, f32[8,1536]{1,0:T(8,128)}, bf16[1536,256]{1,0:T(8,128)(2,1)}) custom-call(s32[6]{0:T(128)} %and_select_fusion.low_ref, s32[1,1536]{1,0:T(1,128)} %broadcast_in_dim.47.start_ref, s32[1,1536]{1,0:T(1,128)} %order_row.3, bf16[1536,256]{1,0:T(8,128)(2,1)} %get-tuple-element.52.q_ref, ...), custom_call_target="tpu_custom_call" | custom-call | flops 2415919104 | bytes 3145728 | tf_op jit(solution)/shard_map/attn_fwd/pallas_call | solution.py:102
  155.3 139.0 %middle.1 = (bf16[384,1024]{1,0:T(8,128)(2,1)}, bf16[1536,256]{1,0:T(8,128)(2,1)}, bf16[4,3,256,1024]{3,2,1,0:T(8,128)(2,1)}, bf16[1024,1024]{1,0:T(8,128)(2,1)}...) custom-call(bf16[1536,256]{1,0:T(8,128)(2,1)} %get-tuple-element.55., ...), custom_call_target="tpu_custom_call" | custom-call | flops 99999997952 | bytes 100000000 | tf_op jit(solution)/shard_map/middle/pallas_call | solution.py:560
  294.4 25.3 %attn_bwd.1.grad_ref = bf16[1536,768]{1,0:T(8,128)(2,1)} custom-call(s32[6]{0:T(128)} %and_select_fusion.low_ref, s32[1,1536]{1,0:T(1,128)} %broadcast_in_dim.47.start_ref, s32[1,1536]{1,0:T(1,128)} %order_row.3, s32[1536,1]{1,0:T(8,128)} %copy.37.order_col, f32[8,1536]{1,0:T(8,128)} %get-tuple-element.59.lse_ref, ...), custom_call_target="tpu_custom_call" | custom-call | flops 6039797760 | bytes 6291456 | tf_op jit(solution)/shard_map/attn_bwd/pallas_call | solution.py:182
  319.6 61.1 %tail.1 = (f32[384,1024]{1,0:T(8,128)}, bf16[1024,768]{1,0:T(8,128)(2,1)}, f32[1,256]{1,0:T(1,128)}) custom-call(bf16[1536,768]{1,0:T(8,128)(2,1)} %attn_bwd.1.grad_ref, bf16[1536,512]{1,0:T(8,128)(2,1)} %get-tuple-element.62.raw_ref, f32[1536,128]{1,0:T(8,128)} %get-tuple-element.89.cos_ref, f32[1536,128]{1,0:T(8,128)} %get-tuple-element.90.sin_ref, ...), custom_call_target="tpu_custom_call" | custom-call | flops 60000002048 | bytes 10000000 | tf_op jit(solution)/shard_map/tail/pallas_call | solution.py:1078
  380.8 51.3 %settle.1 = (f32[128,256]{1,0:T(8,128)}, f32[128,256]{1,0:T(8,128)}, f32[128,256]{1,0:T(8,128)}, f32[128,256]{1,0:T(8,128)}, f32[128,1024]{1,0:T(8,128)}, /*inde...) custom-call(bf16[4,2,128,768]{3,2,1,0:T(8,128)(2,1)} %bitcast.20, ...), custom_call_target="tpu_custom_call" | custom-call | flops 1000000000 | bytes 10000000 | tf_op jit(solution)/shard_map/settle/pallas_call | solution.py:1283
  432.1 0.9 copy.53
  433.0 1.1 copy.54
  434.2 0.7 copy.55
  434.8 0.7 copy.56
  435.5 0.7 copy.57
  436.2 0.7 copy.58
  436.8 0.8 copy.59
  437.6 0.8 copy.60
  438.4 0.8 copy.61
  439.2 0.6 copy.62
  439.8 0.6 copy.63
  440.4 0.6 copy.64
  441.0 0.6 copy.65
  441.6 0.6 copy.66
  (44 shorter events, 0.3 us)
Async XLA Ops:
  7.2 61.1 %copy-start.15 = (s32[1,3]{1,0:T(1,128)S(1)}, s32[1,3]{1,0:T(1,128)}, u32[]{:S(2)}) copy-start(s32[1,3]{1,0:T(1,128)} %param.30) | copy-start | bytes 40
  7.2 62.0 %copy-start.9 = (s32[1,1536]{1,0:T(1,128)S(1)}, s32[1,1536]{1,0:T(1,128)}, u32[]{:S(2)}) copy-start(s32[1,1536]{1,0:T(1,128)} %order_row.3) | copy-start | bytes 18436
  7.2 148.1 %all-gather.3.cloned.1.call-start = ((), (), s32[]{:S(2)}) async-start(), calls=%async_computation.1 | async-start | bytes 7864320 | tf_op jit(solution)/shard_map/all_gather | solution.py:1390
  68.2 312.6 %reduce-scatter.4.cloned.1.call-start = ((), (), s32[]{:S(2)}) async-start(), calls=%async_computation.2 | async-start | bytes 7864320
  380.8 51.3 %copy-start.1 = (bf16[384,1024]{1,0:T(8,128)(2,1)S(1)}, bf16[384,1024]{1,0:T(8,128)(2,1)}, u32[]{:S(2)}) copy-start(bf16[384,1024]{1,0:T(8,128)(2,1)} %get-tuple-element.105) | copy-start | bytes 2359300
  380.8 52.2 %copy-start = (f32[384,1024]{1,0:T(8,128)S(1)}, f32[384,1024]{1,0:T(8,128)}, u32[]{:S(2)}) copy-start(f32[384,1024]{1,0:T(8,128)} %get-tuple-element.106) | copy-start | bytes 4718596
  432.1 2.1 copy-start.8
  432.1 2.8 copy-start.7
  432.1 3.4 copy-start.6
  432.1 4.1 copy-start.5
  433.0 3.8 copy-start.4
  433.0 4.6 %copy-start.3 = (f32[128,1024]{1,0:T(8,128)S(1)}, f32[128,1024]{1,0:T(8,128)}, u32[]{:S(2)}) copy-start(f32[128,1024]{1,0:T(8,128)} %get-tuple-element.112) | copy-start | bytes 1572868
  433.0 5.4 %copy-start.2 = (f32[128,1024]{1,0:T(8,128)S(1)}, f32[128,1024]{1,0:T(8,128)}, u32[]{:S(2)}) copy-start(f32[128,1024]{1,0:T(8,128)} %get-tuple-element.113) | copy-start | bytes 1572868
  434.2 5.1 %copy-start.14 = (f32[1,1024]{1,0:T(1,128)S(1)}, f32[1,1024]{1,0:T(1,128)}, u32[]{:S(2)}) copy-start(f32[1,1024]{1,0:T(1,128)} %get-tuple-element.81) | copy-start | bytes 12292
  434.2 5.6 %copy-start.13 = (f32[1,1024]{1,0:T(1,128)S(1)}, f32[1,1024]{1,0:T(1,128)}, u32[]{:S(2)}) copy-start(f32[1,1024]{1,0:T(1,128)} %get-tuple-element.82) | copy-start | bytes 12292
  434.2 6.2 %copy-start.11 = (f32[1,4096]{1,0:T(1,128)S(1)}, f32[1,4096]{1,0:T(1,128)}, u32[]{:S(2)}) copy-start(f32[1,4096]{1,0:T(1,128)} %get-tuple-element.83) | copy-start | bytes 49156
  434.2 6.8 %copy-start.10 = (f32[1,4096]{1,0:T(1,128)S(1)}, f32[1,4096]{1,0:T(1,128)}, u32[]{:S(2)}) copy-start(f32[1,4096]{1,0:T(1,128)} %get-tuple-element.84) | copy-start | bytes 49156
  434.2 7.4 %copy-start.12 = (f32[1,1024]{1,0:T(1,128)S(1)}, f32[1,1024]{1,0:T(1,128)}, u32[]{:S(2)}) copy-start(f32[1,1024]{1,0:T(1,128)} %get-tuple-element.85) | copy-start | bytes 12292
Sparse Core Ops, SparseCore 0:
  68.3 70.3 all-gather.2
  294.5 69.1 reduce-scatter.3

commit v6 on v5

--- a/solution.py
+++ b/solution.py
@@ -226,11 +226,11 @@
 
 
 def middle_body(
-    att_ref, wo_hbm, w_hbm, tok_hbm, cot_hbm, aa_ref, am_ref, su_ref, sg_ref,
+    att_ref, wo_hbm, w_hbm, tok_hbm, cot_hbm, aa_ref, am_ref, su_all, sg_all,
     out_ref, datt_ref, gw_hbm, gwo_hbm, dh1_ref, gaa_ref, gam_ref, gsu_ref, gsg_ref,
     wo, wall, tok, cot, parts, mids, dbms, mid_t, dbm_t, ups, gates, mixed,
     middle, branch, dh2, own_part, send_a, recv_a, send_d, recv_d, send_z, recv_z,
-    gw, gwo, dparts, load_sems, store_sems, hop_send, hop_recv, a2a_send, a2a_recv, d2a_send, d2a_recv, part_send, part_recv,
+    gw, gwo, dparts, su_ref, sg_ref, load_sems, store_sems, hop_send, hop_recv, a2a_send, a2a_recv, d2a_send, d2a_recv, part_send, part_recv,
 ):
     d = lax.axis_index("dp")
     t = lax.axis_index("tensor")
@@ -276,6 +276,9 @@
     for copy in loads + wloads[0] + wloads[1] + wloads[2]:
         copy.start()
 
+    shard = lax.rem(t, 2) + 2 * lax.rem(d, 2)
+    su_ref[...] = su_all[:, tile_at(shard, hid)]
+    sg_ref[...] = sg_all[:, tile_at(shard, hid)] * math.sqrt(D)
     gsu_ref[...] = jnp.zeros_like(gsu_ref)
     gsg_ref[...] = jnp.zeros_like(gsg_ref)
     gam_ref[...] = jnp.zeros_like(gam_ref)
@@ -402,13 +405,13 @@
         def to_z(at, cols, value):
             send_z[at, cols] = (value + recv_d[at, cols].astype(jnp.float32)).astype(jnp.bfloat16)
 
-        over(chunks, lambda i: rows_fn(0, tile_at(i, crow), keep_own, nothing))
+        rows_fn(0, tile_at(0, rows), keep_own, nothing)
         for ch in range(chunks):
             hop(buf, phase, ch, 1).wait_recv()
         if phase == 1:
             for ch in range(chunks):
                 part_copy(0, 0, ch).wait_send()
-        over(chunks, lambda i: rows_fn(1, tile_at(i, crow), to(send_a), nothing))
+        rows_fn(1, tile_at(0, rows), to(send_a), nothing)
         for ch in range(chunks):
             part_copy(phase, 0, ch).start()
         fillers[0]()
@@ -595,6 +598,8 @@
             pltpu.VMEM((3, width, hid), bf),
             pltpu.VMEM((width, width), bf),
             pltpu.VMEM((4, rows, heads_w), bf),
+            pltpu.VMEM((1, hid), f32),
+            pltpu.VMEM((1, hid), f32),
             dma((3 + 3 * nq,)),
             dma((3 * nq + 1,)),
             dma((6 * chunks,)),
@@ -625,8 +630,38 @@
     pl.semaphore_wait(barrier, len(peers))
 
 
+def rope_tables(order_ref, length_ref, cos_out, sin_out, col_out, start_out):
+    group = order_ref.shape[1]
+    lanes = cos_out.shape[1]
+    places = lax.broadcasted_iota(jnp.int32, (1, group), 1)
+    first = jnp.zeros((1, group), jnp.int32)
+    begin = jnp.int32(0)
+    for s in range(1, length_ref.shape[1]):
+        begin = begin + length_ref[0, s - 1]
+        first = jnp.where(places >= begin, begin, first)
+    start_out[...] = first
+    depth = (places - first).astype(jnp.float32)
+    order = order_ref[...]
+    order_f = order.astype(jnp.float32)
+    lane = lax.broadcasted_iota(jnp.int32, (1, lanes), 1)
+    half_width = HD // 2
+    freq = jnp.exp((lane % half_width).astype(jnp.float32) * (-math.log(10000.0) / half_width))
+    sign = jnp.where(lane % HD < half_width, -1.0, 1.0)
+
+    def block(b):
+        at = tile_at(b, 128)
+        own = lax.broadcasted_iota(jnp.int32, (128, group), 0) + b * 128
+        col_out[at, :] = row_sum(jnp.where(own == places, order_f, 0.0)).astype(jnp.int32)
+        angles = row_sum(jnp.where(own == order, depth, 0.0)) * freq
+        cos_out[at, :] = jnp.cos(angles)
+        sin_out[at, :] = jnp.sin(angles) * sign
+
+    over(group // 128, block)
+
+
 def spread_body(
-    count, tok, w_up, w_gate, w_down, wq, wk, wv, wo, pair, tok2, wqkv, wo_all,
+    count, tok, w_up, w_gate, w_down, wq, wk, wv, wo, order_ref, length_ref,
+    pair, tok2, wqkv, wo_all, cos_out, sin_out, col_out, start_out,
     own_mlp, own_att, wo_rows, load_sem, keep_sem, a_send, a_recv, b_send, b_recv, tok_send, tok_recv,
     qkv_send, qkv_recv, oz_send, oz_recv, oq_send, oq_recv, oc_send, oc_recv,
 ):
@@ -664,15 +699,14 @@
         return remote_copy(mlp[m], pair.at[m, side, :], a_send.at[m], a_recv.at[m], (flip1(d), t))
 
     tok_copy = remote_copy(tok, tok2, tok_send, tok_recv, (d, flip1(t)))
+    def oz_copy(k):
+        return remote_copy(wo, wo_rows.at[:, tile_at(t, wcols)], oz_send.at[k - 1], oz_recv.at[k - 1], (d, lax.rem(t + k, 4)))
+
+    for k in (1, 2, 3):
+        oz_copy(k).start()
     for m in range(3):
         b_copy(m).start()
     tok_copy.start()
-
-    def oz_copy(k):
-        return remote_copy(wo, wo_rows.at[:, tile_at(t, wcols)], oz_send.at[k - 1], oz_recv.at[k - 1], (d, lax.rem(t + k, 4)))
-
-    for k in (1, 2, 3):
-        oz_copy(k).start()
     load_o = pltpu.make_async_copy(wo, wo_rows.at[:, tile_at(t, wcols)], load_sem.at[0])
     load_o.start()
 
@@ -728,6 +762,7 @@
 
     over(half - 1, lambda j: oq_copy(j).start())
     oc_own().start()
+    rope_tables(order_ref, length_ref, cos_out, sin_out, col_out, start_out)
 
     def oq_next(j):
         oq_copy(j).wait_recv()
@@ -768,8 +803,9 @@
                 ).wait_recv()
 
 
-def spread_call(count, tokens, w_up, w_gate, w_down, wq, wk, wv, wo):
+def spread_call(count, tokens, w_up, w_gate, w_down, wq, wk, wv, wo, order, lengths):
     rows, width = tokens.shape
+    group = order.shape[1]
     wrows, wcols = wq.shape
     hid = w_up.shape[1]
     bf = jnp.bfloat16
@@ -782,9 +818,13 @@
             jax.ShapeDtypeStruct((rows, width), bf),
             jax.ShapeDtypeStruct((width, 3 * wcols), bf),
             jax.ShapeDtypeStruct((width, width), bf),
+            jax.ShapeDtypeStruct((group, 2 * HD), jnp.float32),
+            jax.ShapeDtypeStruct((group, 2 * HD), jnp.float32),
+            jax.ShapeDtypeStruct((group, 1), jnp.int32),
+            jax.ShapeDtypeStruct((1, group), jnp.int32),
         ),
-        in_specs=[anywhere] * 8,
-        out_specs=(anywhere,) * 4,
+        in_specs=[anywhere] * 8 + [vmem(), pl.BlockSpec(memory_space=pltpu.SMEM)],
+        out_specs=(anywhere,) * 4 + (vmem(),) * 4,
         scratch_shapes=[
             pltpu.VMEM((3, wrows, hid), bf),
             pltpu.VMEM((3, wrows, wcols), bf),
@@ -795,7 +835,7 @@
         ],
         compiler_params=pltpu.CompilerParams(vmem_limit_bytes=VMEM_LIMIT, collective_id=2, has_side_effects=True),
         name="spread",
-    )(tokens, w_up, w_gate, w_down, wq, wk, wv, wo)
+    )(tokens, w_up, w_gate, w_down, wq, wk, wv, wo, order, lengths)
 
 
 def head_sums(value):
@@ -865,7 +905,7 @@
             for m in range(2):
                 raw = dot_ab(x, wqkv[:, m * cols : (m + 1) * cols])
                 raw_ref[at, m * cols : (m + 1) * cols] = raw.astype(jnp.bfloat16)
-                normed = raw * lax.rsqrt(head_sums(raw * raw) + EPS) * gain_ref[...]
+                normed = raw * lax.rsqrt(head_sums(raw * raw) + EPS) * gain_ref[:, tile_at(t, cols)]
                 plain[at, m * cols : (m + 1) * cols] = (normed * cos + swap_halves(normed) * sin).astype(jnp.bfloat16)
             plain[at, 2 * cols : 3 * cols] = dot_ab(x, wqkv[:, 2 * cols : 3 * cols]).astype(jnp.bfloat16)
 
@@ -967,7 +1007,7 @@
             at = tile_at(slot * (rows // WIDE_STRIP) + i, WIDE_STRIP)
             cos = jnp.concatenate([cos_ref[at, :]] * (cols // cos_ref.shape[1]), axis=1)
             sin = jnp.concatenate([sin_ref[at, :]] * (cols // sin_ref.shape[1]), axis=1)
-            gain = gain_ref[...]
+            gain = gain_ref[:, tile_at(t, cols)]
             for m in range(2):
                 grad = grad_ref[at, m * cols : (m + 1) * cols].astype(jnp.float32)
                 raw = raw_ref[at, m * cols : (m + 1) * cols].astype(jnp.float32)
@@ -1099,10 +1139,10 @@
 
 def settle_body(
     count, gq_hbm, gwo_hbm, mlp_hbm, gain_ref, gaa_ref, gam_ref, gsu_ref, gsg_ref,
-    q_out, k_out, v_out, wo_out, up_out, gate_out, down_out, gain_out, aa_out, am_out, su_out, sg_out,
+    q_out, k_out, v_out, wo_out, up_out, gate_out, down_out, gain_out, aa_out, su_out, sg_out, am_out,
     own_q, core_q, got_q, own_w, core_w, got_w, wo_mid, got_z, near_mlp, far_mlp, vec, got_v, vec_mid, got_s,
     load_sem, core_send, core_recv, q_send, q_recv, w_send, w_recv, z_send, z_recv, v_send, v_recv, s_send, s_recv,
-    mlp_send, mlp_recv,
+    near_send, near_recv, mlp_send, mlp_recv,
 ):
     d = lax.axis_index("dp")
     t = lax.axis_index("tensor")
@@ -1133,20 +1173,30 @@
     pl.semaphore_signal(barrier, inc=1, device_id=(flip1(d), flip2(t)), device_id_type=MESH_ID)
     pl.semaphore_wait(barrier, count + 3)
 
-    near_copy = remote_copy(mlp_hbm.at[:, 1 - core], near_mlp, mlp_send.at[0], mlp_recv.at[0], (flip1(d), t))
-    far_same = remote_copy(mlp_hbm.at[:, core], far_mlp, mlp_send.at[1], mlp_recv.at[1], (d, flip2(t)))
-    far_cross = remote_copy(mlp_hbm.at[:, 1 - core], far_mlp, mlp_send.at[2], mlp_recv.at[1], (flip1(d), flip2(t)))
+    near_copy = remote_copy(mlp_hbm.at[:, 1 - core], near_mlp, near_send, near_recv, (flip1(d), t))
     keep_mlp = pltpu.make_async_copy(mlp_hbm.at[:, core], near_mlp, load_sem.at[0])
+
+    def far_same(m):
+        return remote_copy(mlp_hbm.at[m, core], far_mlp.at[m], mlp_send.at[m], mlp_recv.at[m], (d, flip2(t)))
+
+    def far_cross(m):
+        return remote_copy(
+            mlp_hbm.at[m, 1 - core], far_mlp.at[m], mlp_send.at[3 + m], mlp_recv.at[m], (flip1(d), flip2(t))
+        )
+
+    def far_start(m):
+        @pl.when(away)
+        def _():
+            far_same(m).start()
+            far_cross(m).start()
 
     @pl.when(home)
     def _():
         near_copy.start()
         keep_mlp.start()
 
-    @pl.when(away)
-    def _():
-        far_same.start()
-        far_cross.start()
+    far_start(0)
+    far_start(1)
 
     core_w_copy = remote_copy(gwo_hbm.at[:, 1 - core], core_w, core_send.at[0], core_recv.at[0], (flip1(d), t))
     core_q_copy = remote_copy(gq_hbm.at[:, 1 - core], core_q, core_send.at[1], core_recv.at[1], (flip1(d), t))
@@ -1221,6 +1271,7 @@
     for k in (1, 2, 3):
         s_copy(k).start()
     got_s[t] = vec_mid[...]
+    far_start(2)
 
     over(half - 1, lambda i: q_copy(i).wait_recv())
     total = total_of(got_q)
@@ -1240,8 +1291,6 @@
         sg_out[:, s * width : (s + 1) * width] = pairs[s % 2][4 + s // 2 : 5 + s // 2] * math.sqrt(D)
         gain_out[:, s * cols : (s + 1) * cols] = got_s[s][6:7, 0:cols]
 
-    far_same.wait_recv()
-
     @pl.when(home)
     def _():
         keep_mlp.wait()
@@ -1250,11 +1299,16 @@
     @pl.when(away)
     def _():
         near_copy.wait_recv()
-        far_same.wait_send()
-        far_cross.wait_send()
 
     for m, ref in enumerate((up_out, gate_out, down_out)):
+        far_same(m).wait_recv()
         ref[...] = near_mlp[m].astype(f32) + far_mlp[m].astype(f32)
+
+    @pl.when(away)
+    def _():
+        for m in range(3):
+            far_same(m).wait_send()
+            far_cross(m).wait_send()
 
     core_w_copy.wait_send()
     core_q_copy.wait_send()
@@ -1287,9 +1341,9 @@
         + (
             shape((1, 4 * cols), f32),
             shape((1, width), f32),
-            shape((1, width), f32),
             shape((1, 4 * hid), f32),
             shape((1, 4 * hid), f32),
+            shape((1, width), f32),
         ),
         in_specs=[anywhere] * 3 + [vmem()] * 5,
         out_specs=(vmem(),) * 12,
@@ -1310,7 +1364,7 @@
             dma((3,)), dma((3,)),
             dma((count - 1,)), dma((count - 1,)),
             dma((3,)), dma((3,)),
-            dma((3,)), dma((2,)),
+            dma, dma, dma((6,)), dma((3,)),
         ],
         compiler_params=pltpu.CompilerParams(vmem_limit_bytes=VMEM_LIMIT, collective_id=5, has_side_effects=True),
         cost_estimate=pl.CostEstimate(flops=10**9, bytes_accessed=10**7, transcendentals=0),
@@ -1323,27 +1377,39 @@
     )
 
 
+def deliver_body(count, total, *refs):
+    ins, outs, rest = refs[:total], refs[total : 2 * total], refs[2 * total :]
+    held, load_sem, store_sem = rest[:count], rest[count], rest[count + 1]
+    loads = [pltpu.make_async_copy(ins[i], held[i], load_sem.at[i]) for i in range(count)]
+    stores = [pltpu.make_async_copy(held[i], outs[i], store_sem.at[i]) for i in range(count)]
+    for copy in loads:
+        copy.start()
+    for i in range(count, total):
+        outs[i][...] = ins[i][0, :]
+    for load, store in zip(loads, stores):
+        load.wait()
+        store.start()
+    for copy in stores:
+        copy.wait()
+
+
+def deliver_call(arrays, vectors):
+    total = len(arrays) + len(vectors)
+    specs = [pl.BlockSpec(memory_space=pl.ANY)] * len(arrays) + [vmem()] * len(vectors)
+    return pl.pallas_call(
+        functools.partial(deliver_body, len(arrays), total),
+        out_shape=tuple(jax.ShapeDtypeStruct(a.shape, a.dtype) for a in arrays)
+        + tuple(jax.ShapeDtypeStruct((v.shape[1],), v.dtype) for v in vectors),
+        in_specs=specs,
+        out_specs=tuple(specs),
+        scratch_shapes=[pltpu.VMEM(a.shape, a.dtype) for a in arrays] + [pltpu.SemaphoreType.DMA((len(arrays),))] * 2,
+        compiler_params=pltpu.CompilerParams(vmem_limit_bytes=VMEM_LIMIT),
+        name="deliver",
+    )(*arrays, *vectors)
+
+
 def same_core_groups(dp_count):
     return [list(range(parity, dp_count, 2)) for parity in range(2)]
-
-
-def layout(order_row, length_row):
-    group_rows = order_row.shape[0]
-    places = jnp.arange(group_rows, dtype=jnp.int32)
-    seg_ends = jnp.cumsum(length_row, dtype=jnp.int32)
-    seg_starts = seg_ends - length_row
-    seg_first = jnp.max(
-        jnp.where(seg_starts[None, :] <= places[:, None], seg_starts[None, :], 0), axis=1
-    )
-    half_width = HD // 2
-    inv_freq = jnp.exp(
-        jnp.arange(half_width, dtype=jnp.float32) * (-math.log(10000.0) / half_width)
-    )
-    depth = jnp.sum(
-        jnp.where(order_row[None, :] == places[:, None], (places - seg_first)[None, :], 0), axis=1, dtype=jnp.int32
-    )
-    angles = depth.astype(jnp.float32)[:, None] * inv_freq[None, :]
-    return (seg_first, angles)
 
 
 def on_device(
@@ -1364,34 +1430,16 @@
     lengths,
     cotangent,
 ):
-    tensor_rank = lax.axis_index("tensor")
-    head_cols = w_query.shape[1]
-    hidden_cols = w_up.shape[1]
-    qk_gains = lax.dynamic_slice_in_dim(scale_qk, tensor_rank * head_cols, head_cols)
-    dp_count, tensor_count = lax.axis_size("dp"), lax.axis_size("tensor")
-    hidden_rank = lax.rem(tensor_rank, 2) + 2 * lax.rem(lax.axis_index("dp"), 2)
-    up_gains = lax.dynamic_slice_in_dim(scale_up, hidden_rank * hidden_cols, hidden_cols)[None, :]
-    gate_gains = lax.dynamic_slice_in_dim(
-        scale_gate, hidden_rank * hidden_cols, hidden_cols
-    )[None, :] * math.sqrt(D)
-    order_row = order[0]
-    seg_first, angles = layout(order_row, lengths[0])
-    group_rows = order_row.shape[0]
-    low = lax.slice(seg_first, (0,), (group_rows,), (BLK,)) // BLK
-    start = seg_first[None, :]
-    order_col = order_row[:, None]
-    cosine, sine = jnp.cos(angles), jnp.sin(angles)
-    cos_table = jnp.concatenate([cosine] * 4, axis=1)
-    sin_table = jnp.concatenate([-sine, sine] * 2, axis=1)
-
-    pair, near_tokens, wqkv, wo_every = spread_call(
-        dp_count, tokens, w_up, w_gate, w_down_t, w_query, w_key, w_value, w_out_t
+    dp_count = lax.axis_size("dp")
+    pair, near_tokens, wqkv, wo_every, cos_table, sin_table, order_col, start = spread_call(
+        dp_count, tokens, w_up, w_gate, w_down_t, w_query, w_key, w_value, w_out_t, order, lengths
     )
+    low = lax.slice(start[0], (0,), (start.shape[1],), (BLK,)) // BLK
     mlp_parts = lax.all_gather(
         pair, "dp", axis=0, tiled=False, axis_index_groups=same_core_groups(dp_count)
     )
     queries, key_rows, value_rows, raw, all_tokens = project_call(
-        tokens, near_tokens, wqkv, cos_table, sin_table, order_col, qk_gains[None, :]
+        tokens, near_tokens, wqkv, cos_table, sin_table, order_col, scale_qk[None, :]
     )
     attended, log_totals, attended_plain = attn_fwd(low, start, order, queries, key_rows, value_rows)
     out_rows, grad_att_rows, mlp_grads, wo_grads, grad_h1_kept, grad_alpha_a, grad_alpha_m, grad_su, grad_sv = middle_call(
@@ -1403,8 +1451,8 @@
         cotangent,
         alpha_attn[None, :],
         alpha_mlp[None, :],
-        up_gains,
-        gate_gains,
+        scale_up[None, :],
+        scale_gate[None, :],
     )
     grad_qkv = attn_bwd(
         low, start, order, order_col, log_totals, queries, key_rows, value_rows, attended, grad_att_rows
@@ -1413,14 +1461,12 @@
         mlp_grads, "dp", scatter_dimension=0, tiled=False, axis_index_groups=same_core_groups(dp_count)
     )
     grad_tokens, grad_q, gain_sum = tail_call(
-        grad_qkv, raw, cos_table, sin_table, wqkv, all_tokens, grad_h1_kept, qk_gains[None, :]
+        grad_qkv, raw, cos_table, sin_table, wqkv, all_tokens, grad_h1_kept, scale_qk[None, :]
     )
     settled = settle_call(
         dp_count, grad_q, wo_grads, mlp_sums, gain_sum, grad_alpha_a, grad_alpha_m, grad_su, grad_sv
     )
-    weights, vectors = settled[:7], [v.reshape(-1) for v in settled[7:]]
-    grad_gain, sum_aa, sum_am, sum_su, sum_sv = vectors
-    return (out_rows, grad_tokens, *weights, grad_gain, sum_aa, sum_su, sum_sv, sum_am)
+    return deliver_call([out_rows, grad_tokens, *settled[:7]], settled[7:])
 
 
 def solution(mesh):

time: 451 us -> 416 us (0.922)
  Pallas kernels: 412 us -> 396 us
  local copies, waits for them, and re-layouts: 14.6 us -> 0.7 us
  other arithmetic: 8.39 us -> 0.55 us
    pallas_call x1, Pallas kernels: 60.9 us -> 46.6 us  [spread_call(): pl.pallas_call(functools.partial(spread_body, count), out_shape=(jax.Shap...]
    unnamed x46 -> x2, local copies, waits for them, and re-layouts: 10.1 us -> 0.61 us
    pallas_call x0 -> x1, Pallas kernels: none -> 5.03 us  [deliver_call(): pl.pallas_call(functools.partial(deliver_body, len(arrays), total), out_s...]
  transfers between devices with their start and end apart: 2 -> 2, of which waited for: 0 -> 0; matrix products, arithmetic and copies ran while one was open for 3% -> 0% of each run, Pallas kernels for 36% -> 39%
where the time goes in v6:
time: 416 us; the launch traced here: 411 us
  Pallas kernels  396 us (95%)
  between operations  14.1 us (3%)
    pallas_call x1, Pallas kernels, middle_call(): pl.pallas_call(middle_body, out_shape=(jax.ShapeDtypeStruct((rows, width)...  137 us
    pallas_call x1, Pallas kernels, tail_call(): pl.pallas_call(tail_body, out_shape=(shape((rows, width), f32), shape((wi...  60.6 us
    pallas_call x1, Pallas kernels, project_call(): pl.pallas_call(project_body, out_shape=(jax.ShapeDtypeStruct((group, cols...  59.4 us
    pallas_call x1, Pallas kernels, settle_call(): pl.pallas_call(functools.partial(settle_body, count), out_shape=(shape((w...  48.4 us
    pallas_call x1, Pallas kernels, spread_call(): pl.pallas_call(functools.partial(spread_body, count), out_shape=(jax.Shap...  46.6 us
    pallas_call x1, Pallas kernels, attn_bwd(): pl.pallas_call(attn_bwd_body, out_shape=jax.ShapeDtypeStruct((rows, 3 * c...  25.2 us
    pallas_call x1, Pallas kernels, attn_fwd(): pl.pallas_call(attn_fwd_body, out_shape=(jax.ShapeDtypeStruct((rows, cols...  13.6 us
  transfers between devices with their start and end apart: 2, of which 0 were waited for; matrix products, arithmetic and copies ran while one was open for 0% of the time, Pallas kernels for 39%

profile of v6, /device:TPU:0, one launch (start us, length us, event | category | flops | bytes accessed | tf_op | source)
XLA Modules:
  0.0 411.4 jit_solution(213098701363290796)
XLA Ops:
  7.2 0.0 all-gather.3.cloned.1.call-start
  7.2 46.6 %spread.1 = (bf16[3,256,1024]{2,1,0:T(8,128)(2,1)}, bf16[384,1024]{1,0:T(8,128)(2,1)}, bf16[1024,768]{1,0:T(8,128)(2,1)}, bf16[1024,1024]{1,0:T(8,128)(2,1)}, f3...) custom-call(bf16[384,1024]{1,0:T(8,128)(2,1)} %tok_hbm.1, ...), custom_call_target="tpu_custom_call" | custom-call | tf_op jit(solution)/shard_map/spread/pallas_call | solution.py:814
  53.8 0.0 copy-start
  53.8 0.0 all-gather.3.cloned.1.call-update
  53.9 0.0 reduce-scatter.4.cloned.1.call-start
  53.9 0.6 copy-done
  54.5 0.1 slice.3
  54.6 0.5 and_select_fusion.low_ref
  55.2 59.4 %project.1 = (bf16[1536,256]{1,0:T(8,128)(2,1)}, bf16[1536,256]{1,0:T(8,128)(2,1)}, bf16[1536,256]{1,0:T(8,128)(2,1)}, bf16[1536,512]{1,0:T(8,128)(2,1)}, bf16[1536,1024]{1,0:T(8,128)(2,1)}) custom-call(bf16[384,1024]{1,0:T(8,128)(2,1)} %tok_hbm.1, bf16[384,1024]{1,0:T(8,128)(2,1)} %get-tuple-element.55.tok2, bf16[1024,768]{1,0:T(8,128)(2,1)} %get-tuple-element.56.wqkv, ...), custom_call_target="tpu_custom_call" | custom-call | flops 60000002048 | bytes 10000000 | tf_op jit(solution)/shard_map/project/pallas_call | solution.py:955
  114.5 13.6 %attn_fwd.1 = (bf16[1536,256]{1,0:T(8,128)(2,1)}, f32[8,1536]{1,0:T(8,128)}, bf16[1536,256]{1,0:T(8,128)(2,1)}) custom-call(s32[6]{0:T(128)} %and_select_fusion.low_ref, s32[1,1536]{1,0:T(1,128)} %get-tuple-element.54.start_ref, s32[1,1536]{1,0:T(1,128)} %order_row.3, bf16[1536,256]{1,0:T(8,128)(2,1)} %get-tuple-element.60.q_ref, ...), custom_call_target="tpu_custom_call" | custom-call | flops 2415919104 | bytes 3145728 | tf_op jit(solution)/shard_map/attn_fwd/pallas_call | solution.py:102
  128.1 0.0 all-gather.3.cloned.1.call-done
  128.1 137.1 %middle.1 = (bf16[384,1024]{1,0:T(8,128)(2,1)}, bf16[1536,256]{1,0:T(8,128)(2,1)}, bf16[4,3,256,1024]{3,2,1,0:T(8,128)(2,1)}, bf16[1024,1024]{1,0:T(8,128)(2,1)}...) custom-call(bf16[1536,256]{1,0:T(8,128)(2,1)} %get-tuple-element.63., ...), custom_call_target="tpu_custom_call" | custom-call | flops 99999997952 | bytes 100000000 | tf_op jit(solution)/shard_map/middle/pallas_call | solution.py:563
  265.2 0.0 reduce-scatter.4.cloned.1.call-update
  265.2 25.2 %attn_bwd.1.grad_ref = bf16[1536,768]{1,0:T(8,128)(2,1)} custom-call(s32[6]{0:T(128)} %and_select_fusion.low_ref, s32[1,1536]{1,0:T(1,128)} %get-tuple-element.54.start_ref, s32[1,1536]{1,0:T(1,128)} %order_row.3, s32[1536,1]{1,0:T(8,128)} %get-tuple-element.59.order_col, f32[8,1536]{1,0:T(8,128)} %get-tuple-element.67.lse_ref, ...), custom_call_target="tpu_custom_call" | custom-call | flops 6039797760 | bytes 6291456 | tf_op jit(solution)/shard_map/attn_bwd/pallas_call | solution.py:182
  290.5 60.6 %tail.1 = (f32[384,1024]{1,0:T(8,128)}, bf16[1024,768]{1,0:T(8,128)(2,1)}, f32[1,256]{1,0:T(1,128)}) custom-call(bf16[1536,768]{1,0:T(8,128)(2,1)} %attn_bwd.1.grad_ref, bf16[1536,512]{1,0:T(8,128)(2,1)} %get-tuple-element.70.raw_ref, f32[1536,128]{1,0:T(8,128)} %get-tuple-element.57.cos_ref, f32[1536,128]{1,0:T(8,128)} %get-tuple-element.58.sin_ref, ...), custom_call_target="tpu_custom_call" | custom-call | flops 60000002048 | bytes 10000000 | tf_op jit(solution)/shard_map/tail/pallas_call | solution.py:1118
  351.1 0.0 reduce-scatter.4.cloned.1.call-done
  351.1 48.4 %settle.1 = (f32[128,256]{1,0:T(8,128)}, f32[128,256]{1,0:T(8,128)}, f32[128,256]{1,0:T(8,128)}, f32[128,256]{1,0:T(8,128)}, f32[128,1024]{1,0:T(8,128)}, /*inde...) custom-call(bf16[4,2,128,768]{3,2,1,0:T(8,128)(2,1)} %bitcast.12, ...), custom_call_target="tpu_custom_call" | custom-call | flops 1000000000 | bytes 10000000 | tf_op jit(solution)/shard_map/settle/pallas_call | solution.py:1337
  399.5 5.0 %deliver.1 = (bf16[384,1024]{1,0:T(8,128)(2,1)}, f32[384,1024]{1,0:T(8,128)}, f32[128,256]{1,0:T(8,128)}, f32[128,256]{1,0:T(8,128)}, f32[128,256]{1,0:T(8,128)}...) custom-call(bf16[384,1024]{1,0:T(8,128)(2,1)} %get-tuple-element.66., ...), custom_call_target="tpu_custom_call" | custom-call | tf_op jit(solution)/shard_map/deliver/pallas_call | solution.py:1399
  (1 shorter events, 0.0 us)
Async XLA Ops:
  7.2 120.9 %all-gather.3.cloned.1.call-start = ((), (), s32[]{:S(2)}) async-start(), calls=%async_computation.1 | async-start | bytes 7864320 | tf_op jit(solution)/shard_map/all_gather | solution.py:1438
  53.8 0.7 copy-start
  53.9 297.2 %reduce-scatter.4.cloned.1.call-start = ((), (), s32[]{:S(2)}) async-start(), calls=%async_computation.2 | async-start | bytes 7864320
Sparse Core Ops, SparseCore 0:
  54.0 73.0 all-gather.2
  265.3 67.4 reduce-scatter.3

commit v7 on v6

--- a/solution.py
+++ b/solution.py
@@ -227,7 +227,7 @@
 
 def middle_body(
     att_ref, wo_hbm, w_hbm, tok_hbm, cot_hbm, aa_ref, am_ref, su_all, sg_all,
-    out_ref, datt_ref, gw_hbm, gwo_hbm, dh1_ref, gaa_ref, gam_ref, gsu_ref, gsg_ref,
+    out_ref, datt_ref, gwu_hbm, gwd_hbm, gwo_hbm, dh1_ref, gaa_ref, gam_ref, gsu_ref, gsg_ref,
     wo, wall, tok, cot, parts, mids, dbms, mid_t, dbm_t, ups, gates, mixed,
     middle, branch, dh2, own_part, send_a, recv_a, send_d, recv_d, send_z, recv_z,
     gw, gwo, dparts, su_ref, sg_ref, load_sems, store_sems, hop_send, hop_recv, a2a_send, a2a_recv, d2a_send, d2a_recv, part_send, part_recv,
@@ -476,24 +476,28 @@
         hop(dbms, 1, ch, 0).start()
         hop(dbms, 1, ch, 1).start()
 
-    def weight_grads():
+    def grad_store(m, q):
+        dst = gwd_hbm.at[q] if m == 2 else gwu_hbm.at[q, m]
+        return pltpu.make_async_copy(gw.at[m, pl.ds(q * qrows, qrows), :], dst, store_sems.at[m * nq + q])
+
+    def weight_grad(m):
+        lhs, rhs = ((mid_t, ups), (mid_t, gates), (dbm_t, mixed))[m]
+
+        def block(i):
+            q = i // (hid // TILE)
+            cols = tile_at(lax.rem(i, hid // TILE), TILE)
+            value = dot_ab(lhs[tile_at(q, TILE), :], rhs[:, cols])
+            gw[m, tile_at(q, TILE), cols] = value.astype(jnp.bfloat16)
+
+        over((width // TILE) * (hid // TILE), block)
+        for q in range(nq):
+            grad_store(m, q).start()
+
+    def down_grad():
         transpose_into(dbm_t, dbms, (2, 3))
-        for m, (lhs, rhs) in enumerate(((mid_t, ups), (mid_t, gates), (dbm_t, mixed))):
-
-            def block(i):
-                q = i // (hid // TILE)
-                cols = tile_at(lax.rem(i, hid // TILE), TILE)
-                value = dot_ab(lhs[tile_at(q, TILE), :], rhs[:, cols])
-                gw[m, tile_at(q, TILE), cols] = value.astype(jnp.bfloat16)
-
-            over((width // TILE) * (hid // TILE), block)
-            for q in range(nq):
-                grad_store(m, q).start()
-
-    def grad_store(m, q):
-        return pltpu.make_async_copy(gw.at[m, pl.ds(q * qrows, qrows), :], gw_hbm.at[q, m], store_sems.at[m * nq + q])
-
-    tensor_pass(1, dbms, backward_rows, [lambda: transpose_into(dbm_t, dbms, (0, 1)), weight_grads])
+        weight_grad(2)
+
+    tensor_pass(1, dbms, backward_rows, [lambda: transpose_into(dbm_t, dbms, (0, 1)), down_grad])
 
     def last(at):
         inputs, norm_a, factor_a, mid, factor_mid = make_middle(at)
@@ -523,11 +527,13 @@
         else:
             datt_ref[tile_at(t, rows), :] = value
 
-    transpose_into(mid_t, mids, (0,))
+    weight_grad(0)
+    weight_grad(1)
+    transpose_into(dbm_t, mids, (0,))
 
     def out_grad(n):
         at = tile_at(n, TILE)
-        lhs = mid_t[at, 0:rows]
+        lhs = dbm_t[at, 0:rows]
         gwo[at, tile_at(t, heads_w)] = dot_ab(lhs, att_ref[tile_at(t, rows), :]).astype(jnp.bfloat16)
         for k in (1, 2, 3):
             gwo[at, tile_at(line[k], heads_w)] = dot_ab(lhs, parts[k - 1]).astype(jnp.bfloat16)
@@ -565,7 +571,8 @@
         out_shape=(
             jax.ShapeDtypeStruct((rows, width), bf),
             jax.ShapeDtypeStruct((group, heads_w), bf),
-            jax.ShapeDtypeStruct((nq, 3, qrows, hid), bf),
+            jax.ShapeDtypeStruct((nq, 2, qrows, hid), bf),
+            jax.ShapeDtypeStruct((nq, qrows, hid), bf),
             jax.ShapeDtypeStruct((width, width), bf),
             jax.ShapeDtypeStruct((rows, width), f32),
             jax.ShapeDtypeStruct((1, width), f32),
@@ -574,7 +581,7 @@
             jax.ShapeDtypeStruct((1, hid), f32),
         ),
         in_specs=[vmem(), anywhere, anywhere, anywhere, anywhere] + [vmem()] * 4,
-        out_specs=(vmem(), vmem(), anywhere, anywhere) + (vmem(),) * 5,
+        out_specs=(vmem(), vmem(), anywhere, anywhere, anywhere) + (vmem(),) * 5,
         scratch_shapes=[
             pltpu.VMEM((width, width), bf),
             pltpu.VMEM((3, width, hid), bf),
@@ -704,9 +711,9 @@
 
     for k in (1, 2, 3):
         oz_copy(k).start()
+    tok_copy.start()
     for m in range(3):
         b_copy(m).start()
-    tok_copy.start()
     load_o = pltpu.make_async_copy(wo, wo_rows.at[:, tile_at(t, wcols)], load_sem.at[0])
     load_o.start()
 
@@ -970,9 +977,9 @@
 
 
 def tail_body(
-    grad_ref, raw_ref, cos_ref, sin_ref, wqkv, x_hbm, kept_ref, gain_ref, tok_out, gq, gain_sum,
+    grad_ref, raw_ref, cos_ref, sin_ref, wqkv, x_hbm, down_hbm, kept_ref, gain_ref, tok_out, gq, gain_sum, down_out,
     xs, x_t, draw, part_far, part_mid, part_near, own_part, from_a, from_b, from_c, from_d, from_e, from_f,
-    load_sem, hop_send, hop_recv,
+    near_mlp, far_mlp, load_sem, hop_send, hop_recv, keep_sem, near_send, near_recv, far_send, far_recv,
 ):
     d = lax.axis_index("dp")
     t = lax.axis_index("tensor")
@@ -984,7 +991,26 @@
     outer = jnp.logical_not(inner)
     far, mid = 3 - 3 * (t // 2), 2 - t // 2
     chunk = rows // 2
-    greet([(d, near), (d, 3 - t)])
+    greet([(d, near), (d, 3 - t), (d, flip2(t)), (flip1(d), t), (flip1(d), flip2(t))])
+
+    core = lax.rem(d, 2)
+    home = core == t // 2
+    away = jnp.logical_not(home)
+    near_copy = remote_copy(down_hbm.at[1 - core], near_mlp, near_send, near_recv, (flip1(d), t))
+    far_same = remote_copy(down_hbm.at[core], far_mlp, far_send.at[0], far_recv, (d, flip2(t)))
+    far_cross = remote_copy(down_hbm.at[1 - core], far_mlp, far_send.at[1], far_recv, (flip1(d), flip2(t)))
+    keep_mlp = pltpu.make_async_copy(down_hbm.at[core], near_mlp, keep_sem)
+
+    @pl.when(home)
+    def _():
+        near_copy.start()
+        keep_mlp.start()
+
+    @pl.when(away)
+    def _():
+        far_same.start()
+        far_cross.start()
+
     load_x = pltpu.make_async_copy(x_hbm, xs, load_sem)
     load_x.start()
 
@@ -997,54 +1023,50 @@
             (part_mid, from_e, 3 - t),
             (part_near, from_f, near),
         )[kind]
-        part = pl.ds(ch * chunk, chunk)
+        part = tile_at(ch, chunk)
         return remote_copy(src.at[part, :], dst.at[part, :], hop_send.at[kind, ch], hop_recv.at[kind, ch], (d, to))
 
     gain_sum[...] = jnp.zeros_like(gain_sum)
 
-    def work(slot, store):
-        def strip(i):
-            at = tile_at(slot * (rows // WIDE_STRIP) + i, WIDE_STRIP)
-            cos = jnp.concatenate([cos_ref[at, :]] * (cols // cos_ref.shape[1]), axis=1)
-            sin = jnp.concatenate([sin_ref[at, :]] * (cols // sin_ref.shape[1]), axis=1)
-            gain = gain_ref[:, tile_at(t, cols)]
-            for m in range(2):
-                grad = grad_ref[at, m * cols : (m + 1) * cols].astype(jnp.float32)
-                raw = raw_ref[at, m * cols : (m + 1) * cols].astype(jnp.float32)
-                back = grad * cos - swap_halves(grad) * sin
-                factor = lax.rsqrt(head_sums(raw * raw) + EPS)
-                normed = raw * factor
-                gain_sum[...] += jnp.sum(back * normed, axis=0, keepdims=True)
-                scaled = back * gain
-                draw[at, m * cols : (m + 1) * cols] = (
-                    factor * (scaled - normed * head_sums(normed * scaled))
-                ).astype(jnp.bfloat16)
-            draw[at, 2 * cols : 3 * cols] = grad_ref[at, 2 * cols : 3 * cols]
-
-        over(rows // WIDE_STRIP, strip)
-        everything = tile_at(slot, rows)
+    def work(slot, ch, ref):
+        at = tile_at(2 * slot + ch, chunk)
+        to = tile_at(ch, chunk)
+        cos = jnp.concatenate([cos_ref[at, :]] * (cols // cos_ref.shape[1]), axis=1)
+        sin = jnp.concatenate([sin_ref[at, :]] * (cols // sin_ref.shape[1]), axis=1)
+        gain = gain_ref[:, tile_at(t, cols)]
+        for m in range(2):
+            grad = grad_ref[at, m * cols : (m + 1) * cols].astype(jnp.float32)
+            raw = raw_ref[at, m * cols : (m + 1) * cols].astype(jnp.float32)
+            back = grad * cos - swap_halves(grad) * sin
+            factor = lax.rsqrt(head_sums(raw * raw) + EPS)
+            normed = raw * factor
+            gain_sum[...] += jnp.sum(back * normed, axis=0, keepdims=True)
+            scaled = back * gain
+            draw[at, m * cols : (m + 1) * cols] = (factor * (scaled - normed * head_sums(normed * scaled))).astype(
+                jnp.bfloat16
+            )
+        draw[at, 2 * cols : 3 * cols] = grad_ref[at, 2 * cols : 3 * cols]
 
         def product(n):
             tile = tile_at(n, TILE)
-            store(tile, dot_abt(draw[everything, :], wqkv[tile, :]))
+            ref[to, tile] = dot_abt(draw[at, :], wqkv[tile, :]).astype(ref.dtype)
 
         over(width // TILE, product)
 
-    def into(ref):
-        def store(tile, value):
-            ref[:, tile] = value.astype(ref.dtype)
-
-        return store
-
-    for kind, (slot, ref) in enumerate(((far, part_far), (mid, part_mid), (near, part_near))):
-        work(slot, into(ref))
-
-        @pl.when(outer)
-        def _():
-            for ch in range(2):
+    def send_part(kind, slot, ref):
+        def one(ch):
+            work(slot, ch, ref)
+
+            @pl.when(outer)
+            def _():
                 hop(kind, ch).start()
 
-    work(t, into(own_part))
+        over(2, one)
+
+    send_part(0, far, part_far)
+    send_part(1, mid, part_mid)
+    send_part(2, near, part_near)
+    over(2, lambda ch: work(t, ch, own_part))
 
     def pass_on(kind, ch, own, got, then):
         @pl.when(inner)
@@ -1075,6 +1097,23 @@
     pass_on(1, 0, part_mid, from_b, 4)
     pass_on(3, 1, part_near, from_d, 5)
     pass_on(1, 1, part_mid, from_b, 4)
+
+    @pl.when(home)
+    def _():
+        keep_mlp.wait()
+        near_copy.wait_send()
+
+    @pl.when(away)
+    def _():
+        near_copy.wait_recv()
+
+    far_same.wait_recv()
+    down_out[...] = near_mlp[...].astype(jnp.float32) + far_mlp[...].astype(jnp.float32)
+
+    @pl.when(away)
+    def _():
+        far_same.wait_send()
+        far_cross.wait_send()
 
     for ch in range(2):
         part = pl.ds(ch * chunk, chunk)
@@ -1108,8 +1147,9 @@
                 hop(kind, ch).wait_send()
 
 
-def tail_call(grad_qkv, raw, cos, sin, wqkv, all_tokens, kept, gains):
+def tail_call(count, grad_qkv, raw, cos, sin, wqkv, all_tokens, down, kept, gains):
     rows, width = kept.shape
+    wrows, hid = width // count, down.shape[1]
     group, three = grad_qkv.shape
     bf, f32 = jnp.bfloat16, jnp.float32
     anywhere = pl.BlockSpec(memory_space=pl.ANY)
@@ -1117,9 +1157,14 @@
     shape = jax.ShapeDtypeStruct
     return pl.pallas_call(
         tail_body,
-        out_shape=(shape((rows, width), f32), shape((width, three), bf), shape((1, three // 3), f32)),
-        in_specs=[vmem()] * 5 + [anywhere] + [vmem()] * 2,
-        out_specs=(vmem(),) * 3,
+        out_shape=(
+            shape((rows, width), f32),
+            shape((width, three), bf),
+            shape((1, three // 3), f32),
+            shape((wrows, hid), f32),
+        ),
+        in_specs=[vmem()] * 5 + [anywhere] * 2 + [vmem()] * 2,
+        out_specs=(vmem(),) * 4,
         scratch_shapes=[
             pltpu.VMEM((group, width), bf),
             pltpu.VMEM((width, group), bf),
@@ -1130,16 +1175,17 @@
             pltpu.VMEM((rows, width), f32),
         ]
         + [pltpu.VMEM((rows, width), bf)] * 6
-        + [dma, dma((6, 2)), dma((6, 2))],
+        + [pltpu.VMEM((wrows, hid), bf)] * 2
+        + [dma, dma((6, 2)), dma((6, 2)), dma, dma, dma, dma((2,)), dma],
         compiler_params=pltpu.CompilerParams(vmem_limit_bytes=VMEM_LIMIT, collective_id=4, has_side_effects=True),
         cost_estimate=pl.CostEstimate(flops=6 * 10**10, bytes_accessed=10**7, transcendentals=10**6),
         name="tail",
-    )(grad_qkv, raw, cos, sin, wqkv, all_tokens, kept, gains)
+    )(grad_qkv, raw, cos, sin, wqkv, all_tokens, down.reshape(2, wrows, hid), kept, gains)
 
 
 def settle_body(
     count, gq_hbm, gwo_hbm, mlp_hbm, gain_ref, gaa_ref, gam_ref, gsu_ref, gsg_ref,
-    q_out, k_out, v_out, wo_out, up_out, gate_out, down_out, gain_out, aa_out, su_out, sg_out, am_out,
+    q_out, k_out, v_out, wo_out, up_out, gate_out, gain_out, aa_out, su_out, sg_out, am_out,
     own_q, core_q, got_q, own_w, core_w, got_w, wo_mid, got_z, near_mlp, far_mlp, vec, got_v, vec_mid, got_s,
     load_sem, core_send, core_recv, q_send, q_recv, w_send, w_recv, z_send, z_recv, v_send, v_recv, s_send, s_recv,
     near_send, near_recv, mlp_send, mlp_recv,
@@ -1176,27 +1222,34 @@
     near_copy = remote_copy(mlp_hbm.at[:, 1 - core], near_mlp, near_send, near_recv, (flip1(d), t))
     keep_mlp = pltpu.make_async_copy(mlp_hbm.at[:, core], near_mlp, load_sem.at[0])
 
-    def far_same(m):
-        return remote_copy(mlp_hbm.at[m, core], far_mlp.at[m], mlp_send.at[m], mlp_recv.at[m], (d, flip2(t)))
-
-    def far_cross(m):
+    hid = near_mlp.shape[2]
+
+    def far_same(u):
+        m, part = u // 2, tile_at(u % 2, hid // 2)
         return remote_copy(
-            mlp_hbm.at[m, 1 - core], far_mlp.at[m], mlp_send.at[3 + m], mlp_recv.at[m], (flip1(d), flip2(t))
+            mlp_hbm.at[m, core, :, part], far_mlp.at[m, :, part], mlp_send.at[u], mlp_recv.at[u], (d, flip2(t))
         )
 
-    def far_start(m):
+    def far_cross(u):
+        m, part = u // 2, tile_at(u % 2, hid // 2)
+        return remote_copy(
+            mlp_hbm.at[m, 1 - core, :, part], far_mlp.at[m, :, part], mlp_send.at[4 + u], mlp_recv.at[u],
+            (flip1(d), flip2(t)),
+        )
+
+    def far_start(u):
         @pl.when(away)
         def _():
-            far_same(m).start()
-            far_cross(m).start()
+            far_same(u).start()
+            far_cross(u).start()
 
     @pl.when(home)
     def _():
         near_copy.start()
         keep_mlp.start()
 
-    far_start(0)
-    far_start(1)
+    for u in range(3):
+        far_start(u)
 
     core_w_copy = remote_copy(gwo_hbm.at[:, 1 - core], core_w, core_send.at[0], core_recv.at[0], (flip1(d), t))
     core_q_copy = remote_copy(gq_hbm.at[:, 1 - core], core_q, core_send.at[1], core_recv.at[1], (flip1(d), t))
@@ -1271,7 +1324,7 @@
     for k in (1, 2, 3):
         s_copy(k).start()
     got_s[t] = vec_mid[...]
-    far_start(2)
+    far_start(3)
 
     over(half - 1, lambda i: q_copy(i).wait_recv())
     total = total_of(got_q)
@@ -1300,15 +1353,16 @@
     def _():
         near_copy.wait_recv()
 
-    for m, ref in enumerate((up_out, gate_out, down_out)):
-        far_same(m).wait_recv()
+    for m, ref in enumerate((up_out, gate_out)):
+        far_same(2 * m).wait_recv()
+        far_same(2 * m + 1).wait_recv()
         ref[...] = near_mlp[m].astype(f32) + far_mlp[m].astype(f32)
 
     @pl.when(away)
     def _():
-        for m in range(3):
-            far_same(m).wait_send()
-            far_cross(m).wait_send()
+        for u in range(4):
+            far_same(u).wait_send()
+            far_cross(u).wait_send()
 
     core_w_copy.wait_send()
     core_q_copy.wait_send()
@@ -1337,7 +1391,7 @@
     return pl.pallas_call(
         functools.partial(settle_body, count),
         out_shape=(shape((wrows, cols), f32),) * 4
-        + (shape((wrows, hid), f32),) * 3
+        + (shape((wrows, hid), f32),) * 2
         + (
             shape((1, 4 * cols), f32),
             shape((1, width), f32),
@@ -1346,14 +1400,14 @@
             shape((1, width), f32),
         ),
         in_specs=[anywhere] * 3 + [vmem()] * 5,
-        out_specs=(vmem(),) * 12,
+        out_specs=(vmem(),) * 11,
         scratch_shapes=[pltpu.VMEM((half, wrows, three), bf)] * 3
         + [pltpu.VMEM((half, wrows, width), bf)] * 3
         + [
             pltpu.VMEM((wrows, width), bf),
             pltpu.VMEM((4, wrows, cols), bf),
-            pltpu.VMEM((3, wrows, hid), bf),
-            pltpu.VMEM((3, wrows, hid), bf),
+            pltpu.VMEM((2, wrows, hid), bf),
+            pltpu.VMEM((2, wrows, hid), bf),
             pltpu.VMEM((8, width), f32),
             pltpu.VMEM((count, 8, width), f32),
             pltpu.VMEM((8, width), f32),
@@ -1364,7 +1418,7 @@
             dma((3,)), dma((3,)),
             dma((count - 1,)), dma((count - 1,)),
             dma((3,)), dma((3,)),
-            dma, dma, dma((6,)), dma((3,)),
+            dma, dma, dma((8,)), dma((4,)),
         ],
         compiler_params=pltpu.CompilerParams(vmem_limit_bytes=VMEM_LIMIT, collective_id=5, has_side_effects=True),
         cost_estimate=pl.CostEstimate(flops=10**9, bytes_accessed=10**7, transcendentals=0),
@@ -1372,7 +1426,7 @@
     )(
         gq.reshape(half, 2, wrows, three),
         gwo.reshape(half, 2, wrows, width),
-        mlp.reshape(3, 2, wrows, hid),
+        mlp.reshape(2, 2, wrows, hid),
         gain_sum, gaa, gam, gsu, gsg,
     )
 
@@ -1442,7 +1496,7 @@
         tokens, near_tokens, wqkv, cos_table, sin_table, order_col, scale_qk[None, :]
     )
     attended, log_totals, attended_plain = attn_fwd(low, start, order, queries, key_rows, value_rows)
-    out_rows, grad_att_rows, mlp_grads, wo_grads, grad_h1_kept, grad_alpha_a, grad_alpha_m, grad_su, grad_sv = middle_call(
+    out_rows, grad_att_rows, up_gate_grads, down_grads, wo_grads, grad_h1_kept, grad_alpha_a, grad_alpha_m, grad_su, grad_sv = middle_call(
         2,
         attended_plain,
         wo_every,
@@ -1457,16 +1511,16 @@
     grad_qkv = attn_bwd(
         low, start, order, order_col, log_totals, queries, key_rows, value_rows, attended, grad_att_rows
     )
-    mlp_sums = lax.psum_scatter(
-        mlp_grads, "dp", scatter_dimension=0, tiled=False, axis_index_groups=same_core_groups(dp_count)
-    )
-    grad_tokens, grad_q, gain_sum = tail_call(
-        grad_qkv, raw, cos_table, sin_table, wqkv, all_tokens, grad_h1_kept, scale_qk[None, :]
+    groups = same_core_groups(dp_count)
+    down_sums = lax.psum_scatter(down_grads, "dp", scatter_dimension=0, tiled=False, axis_index_groups=groups)
+    up_gate_sums = lax.psum_scatter(up_gate_grads, "dp", scatter_dimension=0, tiled=False, axis_index_groups=groups)
+    grad_tokens, grad_q, gain_sum, grad_down = tail_call(
+        dp_count, grad_qkv, raw, cos_table, sin_table, wqkv, all_tokens, down_sums, grad_h1_kept, scale_qk[None, :]
     )
     settled = settle_call(
-        dp_count, grad_q, wo_grads, mlp_sums, gain_sum, grad_alpha_a, grad_alpha_m, grad_su, grad_sv
+        dp_count, grad_q, wo_grads, up_gate_sums, gain_sum, grad_alpha_a, grad_alpha_m, grad_su, grad_sv
     )
-    return deliver_call([out_rows, grad_tokens, *settled[:7]], settled[7:])
+    return deliver_call([out_rows, grad_tokens, *settled[:6], grad_down], settled[6:])
 
 
 def solution(mesh):

time: 416 us -> 403 us (0.969)
  Pallas kernels: 396 us -> 379 us
  waiting for transfers between devices: 0.06 us -> 7.36 us
    pallas_call x1, Pallas kernels: 137 us -> 125 us  [middle_call(): pl.pallas_call(middle_body, out_shape=(jax.ShapeDtypeStruct((rows, width)...]
    unnamed x3 -> x5, waiting for transfers between devices: 0.05 us -> 7.36 us
    pallas_call x1, Pallas kernels: 48.4 us -> 41.3 us  [settle_call(): pl.pallas_call(functools.partial(settle_body, count), out_shape=(shape((w...]
  transfers between devices with their start and end apart: 2 -> 3, of which waited for: 0 -> 1; matrix products, arithmetic and copies ran while one was open for 0% -> 0% of each run, Pallas kernels for 39% -> 40%
where the time goes in v7:
time: 403 us; the launch traced here: 401 us
  Pallas kernels  379 us (94%)
  between operations  13.8 us (3%)
  waiting for transfers between devices  7.36 us (2%)
    pallas_call x1, Pallas kernels, middle_call(): pl.pallas_call(middle_body, out_shape=(jax.ShapeDtypeStruct((rows, width)...  125 us
    pallas_call x1, Pallas kernels, tail_call(): pl.pallas_call(tail_body, out_shape=(shape((rows, width), f32), shape((wi...  62.4 us
    pallas_call x1, Pallas kernels, project_call(): pl.pallas_call(project_body, out_shape=(jax.ShapeDtypeStruct((group, cols...  58.7 us
    pallas_call x1, Pallas kernels, spread_call(): pl.pallas_call(functools.partial(spread_body, count), out_shape=(jax.Shap...  48 us
    pallas_call x1, Pallas kernels, settle_call(): pl.pallas_call(functools.partial(settle_body, count), out_shape=(shape((w...  41.3 us
    pallas_call x1, Pallas kernels, attn_bwd(): pl.pallas_call(attn_bwd_body, out_shape=jax.ShapeDtypeStruct((rows, 3 * c...  25.2 us
    pallas_call x1, Pallas kernels, attn_fwd(): pl.pallas_call(attn_fwd_body, out_shape=(jax.ShapeDtypeStruct((rows, cols...  13.6 us
  transfers between devices with their start and end apart: 3, of which 1 were waited for; matrix products, arithmetic and copies ran while one was open for 0% of the time, Pallas kernels for 40%

profile of v7, /device:TPU:0, one launch (start us, length us, event | category | flops | bytes accessed | tf_op | source)
XLA Modules:
  0.0 401.4 jit_solution(15874670495378762207)
XLA Ops:
  7.2 0.0 all-gather.3.cloned.1.call-start
  7.2 48.0 %spread.1 = (bf16[3,256,1024]{2,1,0:T(8,128)(2,1)}, bf16[384,1024]{1,0:T(8,128)(2,1)}, bf16[1024,768]{1,0:T(8,128)(2,1)}, bf16[1024,1024]{1,0:T(8,128)(2,1)}, f3...) custom-call(bf16[384,1024]{1,0:T(8,128)(2,1)} %tok_hbm.1, ...), custom_call_target="tpu_custom_call" | custom-call | tf_op jit(solution)/shard_map/spread/pallas_call | solution.py:821
  55.2 0.0 all-gather.3.cloned.1.call-update
  55.3 0.0 reduce-scatter.7.cloned.1.call-start
  55.3 0.7 reduce
  56.0 0.1 slice.3
  56.1 0.5 and_select_fusion.low_ref
  56.6 58.7 %project.1 = (bf16[1536,256]{1,0:T(8,128)(2,1)}, bf16[1536,256]{1,0:T(8,128)(2,1)}, bf16[1536,256]{1,0:T(8,128)(2,1)}, bf16[1536,512]{1,0:T(8,128)(2,1)}, bf16[1536,1024]{1,0:T(8,128)(2,1)}) custom-call(bf16[384,1024]{1,0:T(8,128)(2,1)} %tok_hbm.1, bf16[384,1024]{1,0:T(8,128)(2,1)} %get-tuple-element.56.tok2, bf16[1024,768]{1,0:T(8,128)(2,1)} %get-tuple-element.57.wqkv, ...), custom_call_target="tpu_custom_call" | custom-call | flops 60000002048 | bytes 10000000 | tf_op jit(solution)/shard_map/project/pallas_call | solution.py:962
  115.3 13.6 %attn_fwd.1 = (bf16[1536,256]{1,0:T(8,128)(2,1)}, f32[8,1536]{1,0:T(8,128)}, bf16[1536,256]{1,0:T(8,128)(2,1)}) custom-call(s32[6]{0:T(128)} %and_select_fusion.low_ref, s32[1,1536]{1,0:T(1,128)} %get-tuple-element.55.start_ref, s32[1,1536]{1,0:T(1,128)} %order_row.3, bf16[1536,256]{1,0:T(8,128)(2,1)} %get-tuple-element.61.q_ref, ...), custom_call_target="tpu_custom_call" | custom-call | flops 2415919104 | bytes 3145728 | tf_op jit(solution)/shard_map/attn_fwd/pallas_call | solution.py:102
  128.9 0.0 all-gather.3.cloned.1.call-done
  128.9 124.7 %middle.1 = (bf16[384,1024]{1,0:T(8,128)(2,1)}, bf16[1536,256]{1,0:T(8,128)(2,1)}, bf16[4,2,256,1024]{3,2,1,0:T(8,128)(2,1)}, bf16[4,256,1024]{2,1,0:T(8,128)(2,...) custom-call(bf16[1536,256]{1,0:T(8,128)(2,1)} %get-tuple-element.64., ...), custom_call_target="tpu_custom_call" | custom-call | flops 99999997952 | bytes 100000000 | tf_op jit(solution)/shard_map/middle/pallas_call | solution.py:569
  253.5 0.0 reduce-scatter.7.cloned.1.call-update
  253.6 0.0 reduce-scatter.9.cloned.1.call-start
  253.6 0.7 reduce-scatter.9.cloned.1.call-update
  254.3 25.2 %attn_bwd.1.grad_ref = bf16[1536,768]{1,0:T(8,128)(2,1)} custom-call(s32[6]{0:T(128)} %and_select_fusion.low_ref, s32[1,1536]{1,0:T(1,128)} %get-tuple-element.55.start_ref, s32[1,1536]{1,0:T(1,128)} %order_row.3, s32[1536,1]{1,0:T(8,128)} %get-tuple-element.60.order_col, f32[8,1536]{1,0:T(8,128)} %get-tuple-element.68.lse_ref, ...), custom_call_target="tpu_custom_call" | custom-call | flops 6039797760 | bytes 6291456 | tf_op jit(solution)/shard_map/attn_bwd/pallas_call | solution.py:182
  279.5 6.6 %reduce-scatter.7.cloned.1.call-done = bf16[1,256,1024]{2,1,0:T(8,128)(2,1)} async-done(((bf16[4,256,1024]{2,1,0:T(8,128)(2,1)}), bf16[1,256,1024]{2,1,0:T(8,128)(2,1)}) %reduce-scatter.7.cloned.1.call-update) | async-done | bytes 524304
  286.1 62.4 %tail.1 = (f32[384,1024]{1,0:T(8,128)}, bf16[1024,768]{1,0:T(8,128)(2,1)}, f32[1,256]{1,0:T(1,128)}, f32[128,1024]{1,0:T(8,128)}) custom-call(bf16[1536,768]{1,0:T(8,128)(2,1)} %attn_bwd.1.grad_ref, bf16[1536,512]{1,0:T(8,128)(2,1)} %get-tuple-element.71.raw_ref, f32[1536,128]{1,0:T(8,128)} %get-tuple-element.58.cos_ref, ...), custom_call_target="tpu_custom_call" | custom-call | flops 60000002048 | bytes 10000000 | tf_op jit(solution)/shard_map/tail/pallas_call | solution.py:1158
  348.5 0.0 reduce-scatter.9.cloned.1.call-done
  348.6 41.3 %settle.1 = (f32[128,256]{1,0:T(8,128)}, f32[128,256]{1,0:T(8,128)}, f32[128,256]{1,0:T(8,128)}, f32[128,256]{1,0:T(8,128)}, f32[128,1024]{1,0:T(8,128)}, /*inde...) custom-call(bf16[4,2,128,768]{3,2,1,0:T(8,128)(2,1)} %bitcast.12, ...), custom_call_target="tpu_custom_call" | custom-call | flops 1000000000 | bytes 10000000 | tf_op jit(solution)/shard_map/settle/pallas_call | solution.py:1391
  389.9 5.0 %deliver.1 = (bf16[384,1024]{1,0:T(8,128)(2,1)}, f32[384,1024]{1,0:T(8,128)}, f32[128,256]{1,0:T(8,128)}, f32[128,256]{1,0:T(8,128)}, f32[128,256]{1,0:T(8,128)}...) custom-call(bf16[384,1024]{1,0:T(8,128)(2,1)} %get-tuple-element.67., ...), custom_call_target="tpu_custom_call" | custom-call | tf_op jit(solution)/shard_map/deliver/pallas_call | solution.py:1453
Async XLA Ops:
  7.2 121.7 %all-gather.3.cloned.1.call-start = ((), (), s32[]{:S(2)}) async-start(), calls=%async_computation.2 | async-start | bytes 7864320 | tf_op jit(solution)/shard_map/all_gather | solution.py:1492
  55.3 230.9 %reduce-scatter.7.cloned.1.call-start = ((), (), s32[]{:S(2)}) async-start(), calls=%async_computation.3 | async-start | bytes 2621440
  253.6 95.0 %reduce-scatter.9.cloned.1.call-start = ((), (), s32[]{:S(2)}) async-start(), calls=%async_computation.4 | async-start | bytes 5242880
Sparse Core Ops, SparseCore 0:
  55.4 71.6 all-gather.2
  253.7 32.3 reduce-scatter.6
  289.1 52.5 reduce-scatter.8

commit v8 on v7

--- a/solution.py
+++ b/solution.py
@@ -226,11 +226,11 @@
 
 
 def middle_body(
-    att_ref, wo_hbm, w_hbm, tok_hbm, cot_hbm, aa_ref, am_ref, su_all, sg_all,
-    out_ref, datt_ref, gwu_hbm, gwd_hbm, gwo_hbm, dh1_ref, gaa_ref, gam_ref, gsu_ref, gsg_ref,
+    count, att_ref, wo_hbm, w_hbm, down_hbm, tok_hbm, cot_hbm, aa_ref, am_ref, su_all, sg_all,
+    out_ref, datt_ref, gw_hbm, down_ref, gwo_hbm, dh1_ref, gaa_ref, gam_ref, gsu_ref, gsg_ref,
     wo, wall, tok, cot, parts, mids, dbms, mid_t, dbm_t, ups, gates, mixed,
     middle, branch, dh2, own_part, send_a, recv_a, send_d, recv_d, send_z, recv_z,
-    gw, gwo, dparts, su_ref, sg_ref, load_sems, store_sems, hop_send, hop_recv, a2a_send, a2a_recv, d2a_send, d2a_recv, part_send, part_recv,
+    gw, gwo, dparts, su_ref, sg_ref, got_down, gather_send, gather_recv, scatter_send, scatter_recv, load_sems, store_sems, hop_send, hop_recv, a2a_send, a2a_recv, d2a_send, d2a_recv, part_send, part_recv,
 ):
     d = lax.axis_index("dp")
     t = lax.axis_index("tensor")
@@ -246,9 +246,18 @@
     line = [t, flip1(t), flip2(t), 3 - t]
 
     barrier = pltpu.get_barrier_semaphore()
+    half, chip, core = count // 2, d // 2, lax.rem(d, 2)
+
+    def chip_peer(i):
+        return lax.rem(chip + 1 + i, half)
+
     for peer in [core_peer] + [(d, line[k]) for k in (1, 2, 3)]:
         pl.semaphore_signal(barrier, inc=1, device_id=peer, device_id_type=MESH_ID)
-    pl.semaphore_wait(barrier, 4)
+    over(
+        half - 1,
+        lambda i: pl.semaphore_signal(barrier, inc=1, device_id=(2 * chip_peer(i) + core, t), device_id_type=MESH_ID),
+    )
+    pl.semaphore_wait(barrier, half + 3)
 
     def remote(src, dst, ssem, rsem, peer):
         return pltpu.make_async_remote_copy(
@@ -261,6 +270,23 @@
     ]
     for copy in a2a:
         copy.start()
+
+    chip_rows = tile_at(chip, qrows)
+
+    def gather(i):
+        return remote(
+            down_hbm, wall.at[2, chip_rows, :], gather_send.at[i], gather_recv.at[i], (2 * chip_peer(i) + core, t)
+        )
+
+    def scatter(i):
+        return remote(
+            gw.at[2, tile_at(chip_peer(i), qrows), :], got_down.at[chip], scatter_send.at[i], scatter_recv.at[i],
+            (2 * chip_peer(i) + core, t),
+        )
+
+    over(half - 1, lambda i: gather(i).start())
+    keep_down = pltpu.make_async_copy(down_hbm, wall.at[2, chip_rows, :], load_sems.at[3 + 2 * nq])
+    keep_down.start()
     loads = [
         pltpu.make_async_copy(wo_hbm, wo, load_sems.at[0]),
         pltpu.make_async_copy(tok_hbm, tok, load_sems.at[1]),
@@ -271,9 +297,9 @@
             pltpu.make_async_copy(w_hbm.at[q, m], wall.at[m, pl.ds(q * qrows, qrows), :], load_sems.at[3 + m * nq + q])
             for q in range(nq)
         ]
-        for m in range(3)
+        for m in range(2)
     ]
-    for copy in loads + wloads[0] + wloads[1] + wloads[2]:
+    for copy in loads + wloads[0] + wloads[1]:
         copy.start()
 
     shard = lax.rem(t, 2) + 2 * lax.rem(d, 2)
@@ -327,9 +353,13 @@
         hop(mids, 0, ch, 0).start()
         hop(mids, 0, ch, 1).start()
 
-    for m in range(3):
+    for m in range(2):
         for copy in wloads[m]:
             copy.wait()
+
+    def down_arrived():
+        keep_down.wait()
+        over(half - 1, lambda i: gather(i).wait_recv())
 
     def within(slot, at):
         return pl.ds(pl.multiple_of(slot * rows + at.start, STRIP), at.size)
@@ -405,7 +435,7 @@
         def to_z(at, cols, value):
             send_z[at, cols] = (value + recv_d[at, cols].astype(jnp.float32)).astype(jnp.bfloat16)
 
-        rows_fn(0, tile_at(0, rows), keep_own, nothing)
+        rows_fn(0, tile_at(0, rows), keep_own, nothing if phase else down_arrived)
         for ch in range(chunks):
             hop(buf, phase, ch, 1).wait_recv()
         if phase == 1:
@@ -477,8 +507,7 @@
         hop(dbms, 1, ch, 1).start()
 
     def grad_store(m, q):
-        dst = gwd_hbm.at[q] if m == 2 else gwu_hbm.at[q, m]
-        return pltpu.make_async_copy(gw.at[m, pl.ds(q * qrows, qrows), :], dst, store_sems.at[m * nq + q])
+        return pltpu.make_async_copy(gw.at[m, pl.ds(q * qrows, qrows), :], gw_hbm.at[q, m], store_sems.at[m * nq + q])
 
     def weight_grad(m):
         lhs, rhs = ((mid_t, ups), (mid_t, gates), (dbm_t, mixed))[m]
@@ -490,12 +519,12 @@
             gw[m, tile_at(q, TILE), cols] = value.astype(jnp.bfloat16)
 
         over((width // TILE) * (hid // TILE), block)
-        for q in range(nq):
-            grad_store(m, q).start()
 
     def down_grad():
         transpose_into(dbm_t, dbms, (2, 3))
         weight_grad(2)
+        over(half - 1, lambda i: scatter(i).start())
+        got_down[chip] = gw[2, chip_rows, :]
 
     tensor_pass(1, dbms, backward_rows, [lambda: transpose_into(dbm_t, dbms, (0, 1)), down_grad])
 
@@ -527,8 +556,10 @@
         else:
             datt_ref[tile_at(t, rows), :] = value
 
-    weight_grad(0)
-    weight_grad(1)
+    for m in range(2):
+        weight_grad(m)
+        for q in range(nq):
+            grad_store(m, q).start()
     transpose_into(dbm_t, mids, (0,))
 
     def out_grad(n):
@@ -539,8 +570,20 @@
             gwo[at, tile_at(line[k], heads_w)] = dot_ab(lhs, parts[k - 1]).astype(jnp.bfloat16)
 
     over(width // TILE, out_grad)
-    wo_store = pltpu.make_async_copy(gwo, gwo_hbm, store_sems.at[3 * nq])
+    wo_store = pltpu.make_async_copy(gwo, gwo_hbm, store_sems.at[2 * nq])
     wo_store.start()
+
+    over(half - 1, lambda i: scatter(i).wait_recv())
+
+    def down_sum(i):
+        at = tile_at(i, qrows // 2)
+        total = got_down[0, at, :].astype(jnp.float32)
+        total = lax.fori_loop(1, half, lambda e, value: value + got_down[e, at, :].astype(jnp.float32), total)
+        down_ref[at, :] = total.astype(jnp.bfloat16)
+
+    over(2, down_sum)
+    over(half - 1, lambda i: gather(i).wait_send())
+    over(half - 1, lambda i: scatter(i).wait_send())
 
     for k in (1, 2, 3):
         remote(
@@ -553,13 +596,13 @@
         for kind in range(3):
             hop(dbms, 1, ch, kind).wait_send()
             part_copy(1, kind, ch).wait_send()
-    for m in range(3):
+    for m in range(2):
         for q in range(nq):
             grad_store(m, q).wait()
     wo_store.wait()
 
 
-def middle_call(chunks, attended, wo, w_parts, tokens, cotangent, alpha_a, alpha_m, su, sg):
+def middle_call(count, chunks, attended, wo, w_parts, down, tokens, cotangent, alpha_a, alpha_m, su, sg):
     rows, width = tokens.shape
     group, heads_w = attended.shape
     nq, _, qrows, hid = w_parts.shape
@@ -567,12 +610,12 @@
     anywhere = pl.BlockSpec(memory_space=pl.ANY)
     dma = pltpu.SemaphoreType.DMA
     return pl.pallas_call(
-        middle_body,
+        functools.partial(middle_body, count),
         out_shape=(
             jax.ShapeDtypeStruct((rows, width), bf),
             jax.ShapeDtypeStruct((group, heads_w), bf),
             jax.ShapeDtypeStruct((nq, 2, qrows, hid), bf),
-            jax.ShapeDtypeStruct((nq, qrows, hid), bf),
+            jax.ShapeDtypeStruct((qrows, hid), bf),
             jax.ShapeDtypeStruct((width, width), bf),
             jax.ShapeDtypeStruct((rows, width), f32),
             jax.ShapeDtypeStruct((1, width), f32),
@@ -580,8 +623,8 @@
             jax.ShapeDtypeStruct((1, hid), f32),
             jax.ShapeDtypeStruct((1, hid), f32),
         ),
-        in_specs=[vmem(), anywhere, anywhere, anywhere, anywhere] + [vmem()] * 4,
-        out_specs=(vmem(), vmem(), anywhere, anywhere, anywhere) + (vmem(),) * 5,
+        in_specs=[vmem()] + [anywhere] * 5 + [vmem()] * 4,
+        out_specs=(vmem(), vmem(), anywhere, vmem(), anywhere) + (vmem(),) * 5,
         scratch_shapes=[
             pltpu.VMEM((width, width), bf),
             pltpu.VMEM((3, width, hid), bf),
@@ -607,8 +650,10 @@
             pltpu.VMEM((4, rows, heads_w), bf),
             pltpu.VMEM((1, hid), f32),
             pltpu.VMEM((1, hid), f32),
-            dma((3 + 3 * nq,)),
-            dma((3 * nq + 1,)),
+            pltpu.VMEM((count // 2, qrows, hid), bf),
+            dma((count // 2 - 1,)), dma((count // 2 - 1,)), dma((count // 2 - 1,)), dma((count // 2 - 1,)),
+            dma((4 + 2 * nq,)),
+            dma((2 * nq + 1,)),
             dma((6 * chunks,)),
             dma((6 * chunks,)),
             dma((3,)),
@@ -621,7 +666,7 @@
         compiler_params=pltpu.CompilerParams(vmem_limit_bytes=67000000, collective_id=1, has_side_effects=True),
         cost_estimate=pl.CostEstimate(flops=10**11, bytes_accessed=10**8, transcendentals=10**6),
         name="middle",
-    )(attended, wo, w_parts, tokens, cotangent, alpha_a, alpha_m, su, sg)
+    )(attended, wo, w_parts, down, tokens, cotangent, alpha_a, alpha_m, su, sg)
 
 
 def remote_copy(src, dst, send_sem, recv_sem, peer):
@@ -668,7 +713,7 @@
 
 def spread_body(
     count, tok, w_up, w_gate, w_down, wq, wk, wv, wo, order_ref, length_ref,
-    pair, tok2, wqkv, wo_all, cos_out, sin_out, col_out, start_out,
+    pair, pair_down, tok2, wqkv, wo_all, cos_out, sin_out, col_out, start_out,
     own_mlp, own_att, wo_rows, load_sem, keep_sem, a_send, a_recv, b_send, b_recv, tok_send, tok_recv,
     qkv_send, qkv_recv, oz_send, oz_recv, oq_send, oq_recv, oc_send, oc_recv,
 ):
@@ -699,11 +744,14 @@
     pl.semaphore_signal(barrier, inc=1, device_id=(flip1(d), flip2(t)), device_id_type=MESH_ID)
     pl.semaphore_wait(barrier, count + 3)
 
+    def pair_at(m, rows):
+        return pair_down.at[rows, :] if m == 2 else pair.at[m, rows, :]
+
     def b_copy(m):
-        return remote_copy(mlp[m], pair.at[m, side, :], b_send.at[m], b_recv.at[core * 3 + m], far)
+        return remote_copy(mlp[m], pair_at(m, side), b_send.at[m], b_recv.at[core * 3 + m], far)
 
     def a_copy(m):
-        return remote_copy(mlp[m], pair.at[m, side, :], a_send.at[m], a_recv.at[m], (flip1(d), t))
+        return remote_copy(mlp[m], pair_at(m, side), a_send.at[m], a_recv.at[m], (flip1(d), t))
 
     tok_copy = remote_copy(tok, tok2, tok_send, tok_recv, (d, flip1(t)))
     def oz_copy(k):
@@ -744,7 +792,7 @@
     ]
     for copy in keeps:
         copy.start()
-    pair_keeps = [pltpu.make_async_copy(own_mlp.at[m], pair.at[m, side, :], keep_sem.at[3 + m]) for m in range(3)]
+    pair_keeps = [pltpu.make_async_copy(own_mlp.at[m], pair_at(m, side), keep_sem.at[3 + m]) for m in range(3)]
 
     @pl.when(home)
     def _():
@@ -798,7 +846,7 @@
     def _():
         for m in range(3):
             pair_keeps[m].wait()
-            remote_copy(mlp[m], pair.at[m, other_side, :], a_send.at[m], a_recv.at[m], (flip1(d), t)).wait_recv()
+            remote_copy(mlp[m], pair_at(m, other_side), a_send.at[m], a_recv.at[m], (flip1(d), t)).wait_recv()
 
     @pl.when(jnp.logical_not(home))
     def _():
@@ -806,7 +854,7 @@
             a_copy(m).wait_send()
             for c in range(2):
                 remote_copy(
-                    mlp[m], pair.at[m, pl.ds(c * wrows, wrows), :], b_send.at[m], b_recv.at[c * 3 + m], far
+                    mlp[m], pair_at(m, pl.ds(c * wrows, wrows)), b_send.at[m], b_recv.at[c * 3 + m], far
                 ).wait_recv()
 
 
@@ -821,7 +869,8 @@
     return pl.pallas_call(
         functools.partial(spread_body, count),
         out_shape=(
-            jax.ShapeDtypeStruct((3, 2 * wrows, hid), bf),
+            jax.ShapeDtypeStruct((2, 2 * wrows, hid), bf),
+            jax.ShapeDtypeStruct((2 * wrows, hid), bf),
             jax.ShapeDtypeStruct((rows, width), bf),
             jax.ShapeDtypeStruct((width, 3 * wcols), bf),
             jax.ShapeDtypeStruct((width, width), bf),
@@ -831,7 +880,7 @@
             jax.ShapeDtypeStruct((1, group), jnp.int32),
         ),
         in_specs=[anywhere] * 8 + [vmem(), pl.BlockSpec(memory_space=pltpu.SMEM)],
-        out_specs=(anywhere,) * 4 + (vmem(),) * 4,
+        out_specs=(anywhere,) * 5 + (vmem(),) * 4,
         scratch_shapes=[
             pltpu.VMEM((3, wrows, hid), bf),
             pltpu.VMEM((3, wrows, wcols), bf),
@@ -874,21 +923,22 @@
     across = 3 - t
     inner = (t + 1) // 2 == 1
     arrive = (2 - t // 2, 3 - 3 * (t // 2))
-    part = rows // 2
+    pieces = mid_send.shape[0] // 2
+    part = rows // pieces
     greet([(d, near), (d, across)])
 
     def mid_copy(k):
-        src = (tok, tok2)[k // 2].at[pl.ds((k % 2) * part, part), :]
-        dst = xs.at[(t, near)[k // 2], pl.ds((k % 2) * part, part), :]
-        return remote_copy(src, dst, mid_send.at[k], recv.at[k], (d, across))
+        rows_of = pl.ds((k % pieces) * part, part)
+        src = (tok, tok2)[k // pieces].at[rows_of, :]
+        return remote_copy(src, xs.at[(t, near)[k // pieces], rows_of, :], mid_send.at[k], recv.at[k], (d, across))
 
     def on_copy(k):
-        ref = xs.at[arrive[k // 2], pl.ds((k % 2) * part, part), :]
+        ref = xs.at[arrive[k // pieces], pl.ds((k % pieces) * part, part), :]
         return remote_copy(ref, ref, on_send.at[k], recv.at[k], (d, near))
 
     @pl.when(inner)
     def _():
-        for k in range(4):
+        for k in range(2 * pieces):
             mid_copy(k).start()
 
     loads = [
@@ -901,53 +951,63 @@
     def keep(index, slot):
         return pltpu.make_async_copy(xs.at[slot], x_hbm.at[tile_at(slot, rows), :], keep_sem.at[index])
 
-    def work(index, slot):
-        keep(index, slot).start()
-
-        def strip(i):
-            at = tile_at(slot * (rows // WIDE_STRIP) + i, WIDE_STRIP)
-            x = xs[slot, tile_at(i, WIDE_STRIP), :]
-            cos = jnp.concatenate([cos_ref[at, :]] * (cols // cos_ref.shape[1]), axis=1)
-            sin = jnp.concatenate([sin_ref[at, :]] * (cols // sin_ref.shape[1]), axis=1)
-            for m in range(2):
-                raw = dot_ab(x, wqkv[:, m * cols : (m + 1) * cols])
-                raw_ref[at, m * cols : (m + 1) * cols] = raw.astype(jnp.bfloat16)
-                normed = raw * lax.rsqrt(head_sums(raw * raw) + EPS) * gain_ref[:, tile_at(t, cols)]
-                plain[at, m * cols : (m + 1) * cols] = (normed * cos + swap_halves(normed) * sin).astype(jnp.bfloat16)
-            plain[at, 2 * cols : 3 * cols] = dot_ab(x, wqkv[:, 2 * cols : 3 * cols]).astype(jnp.bfloat16)
-
-        over(rows // WIDE_STRIP, strip)
+    def strip(slot, i):
+        at = tile_at(slot * (rows // WIDE_STRIP) + i, WIDE_STRIP)
+        x = xs[slot, tile_at(i, WIDE_STRIP), :]
+        cos = jnp.concatenate([cos_ref[at, :]] * (cols // cos_ref.shape[1]), axis=1)
+        sin = jnp.concatenate([sin_ref[at, :]] * (cols // sin_ref.shape[1]), axis=1)
+        for m in range(2):
+            raw = dot_ab(x, wqkv[:, m * cols : (m + 1) * cols])
+            raw_ref[at, m * cols : (m + 1) * cols] = raw.astype(jnp.bfloat16)
+            normed = raw * lax.rsqrt(head_sums(raw * raw) + EPS) * gain_ref[:, tile_at(t, cols)]
+            plain[at, m * cols : (m + 1) * cols] = (normed * cos + swap_halves(normed) * sin).astype(jnp.bfloat16)
+        plain[at, 2 * cols : 3 * cols] = dot_ab(x, wqkv[:, 2 * cols : 3 * cols]).astype(jnp.bfloat16)
+
+    def permute(index, size, first):
+        base = tile_at(index, size)
+
+        def one(b):
+            at = tile_at(b, BLK)
+            token = lax.broadcasted_iota(jnp.int32, (BLK, size), 1) + index * size
+            hot = (token == order_col[at, :]).astype(jnp.float32)
+            value = dot_ab(hot.astype(jnp.bfloat16), plain[base, :])
+            for m, ref in enumerate((q_ref, k_ref, v_ref)):
+                piece = value[:, m * cols : (m + 1) * cols]
+                if not first:
+                    piece += ref[at, :].astype(jnp.float32)
+                ref[at, :] = piece.astype(jnp.bfloat16)
+
+        over(group // BLK, one)
 
     loads[0].wait()
-    work(0, t)
+    keep(0, t).start()
+    over(rows // WIDE_STRIP, lambda i: strip(t, i))
     loads[1].wait()
-    work(1, near)
-    for k in range(4):
-        slot = arrive[k // 2]
-        ref = xs.at[slot, pl.ds((k % 2) * part, part), :]
+    keep(1, near).start()
+    over(rows // WIDE_STRIP, lambda i: strip(near, i))
+    permute(t // 2, 2 * rows, True)
+    per_strip = WIDE_STRIP // part
+    for k in range(2 * pieces):
+        slot = arrive[k // pieces]
+        ref = xs.at[slot, pl.ds((k % pieces) * part, part), :]
         remote_copy(ref, ref, on_send.at[k], recv.at[k], (d, near)).wait_recv()
 
         @pl.when(inner)
         def _():
             on_copy(k).start()
 
-        if k % 2:
-            work(2 + k // 2, slot)
-
-    def permute(b):
-        at = tile_at(b, BLK)
-        hot = (lax.broadcasted_iota(jnp.int32, (BLK, group), 1) == order_col[at, :]).astype(jnp.float32)
-        value = dot_ab(hot.astype(jnp.bfloat16), plain[...])
-        for m, ref in enumerate((q_ref, k_ref, v_ref)):
-            ref[at, :] = value[:, m * cols : (m + 1) * cols].astype(jnp.bfloat16)
-
-    over(group // BLK, permute)
+        if k % per_strip == per_strip - 1:
+            strip(slot, (k % pieces) // per_strip)
+        if k % pieces == pieces - 1:
+            keep(2 + k // pieces, slot).start()
+            permute(slot, rows, False)
+
     for index, slot in enumerate((t, near, *arrive)):
         keep(index, slot).wait()
 
     @pl.when(inner)
     def _():
-        for k in range(4):
+        for k in range(2 * pieces):
             mid_copy(k).wait_send()
             on_copy(k).wait_send()
 
@@ -968,7 +1028,7 @@
         scratch_shapes=[
             pltpu.VMEM((group // rows, rows, width), bf),
             pltpu.VMEM((group, 3 * cols), bf),
-            dma((2,)), dma((4,)), dma((4,)), dma((4,)), dma((4,)),
+            dma((2,)), dma((4,)), dma((8,)), dma((8,)), dma((8,)),
         ],
         compiler_params=pltpu.CompilerParams(vmem_limit_bytes=VMEM_LIMIT, collective_id=3, has_side_effects=True),
         cost_estimate=pl.CostEstimate(flops=6 * 10**10, bytes_accessed=10**7, transcendentals=10**6),
@@ -1485,7 +1545,7 @@
     cotangent,
 ):
     dp_count = lax.axis_size("dp")
-    pair, near_tokens, wqkv, wo_every, cos_table, sin_table, order_col, start = spread_call(
+    pair, pair_down, near_tokens, wqkv, wo_every, cos_table, sin_table, order_col, start = spread_call(
         dp_count, tokens, w_up, w_gate, w_down_t, w_query, w_key, w_value, w_out_t, order, lengths
     )
     low = lax.slice(start[0], (0,), (start.shape[1],), (BLK,)) // BLK
@@ -1496,11 +1556,13 @@
         tokens, near_tokens, wqkv, cos_table, sin_table, order_col, scale_qk[None, :]
     )
     attended, log_totals, attended_plain = attn_fwd(low, start, order, queries, key_rows, value_rows)
-    out_rows, grad_att_rows, up_gate_grads, down_grads, wo_grads, grad_h1_kept, grad_alpha_a, grad_alpha_m, grad_su, grad_sv = middle_call(
+    out_rows, grad_att_rows, up_gate_grads, down_sums, wo_grads, grad_h1_kept, grad_alpha_a, grad_alpha_m, grad_su, grad_sv = middle_call(
+        dp_count,
         2,
         attended_plain,
         wo_every,
         mlp_parts,
+        pair_down,
         tokens,
         cotangent,
         alpha_attn[None, :],
@@ -1511,9 +1573,9 @@
     grad_qkv = attn_bwd(
         low, start, order, order_col, log_totals, queries, key_rows, value_rows, attended, grad_att_rows
     )
-    groups = same_core_groups(dp_count)
-    down_sums = lax.psum_scatter(down_grads, "dp", scatter_dimension=0, tiled=False, axis_index_groups=groups)
-    up_gate_sums = lax.psum_scatter(up_gate_grads, "dp", scatter_dimension=0, tiled=False, axis_index_groups=groups)
+    up_gate_sums = lax.psum_scatter(
+        up_gate_grads, "dp", scatter_dimension=0, tiled=False, axis_index_groups=same_core_groups(dp_count)
+    )
     grad_tokens, grad_q, gain_sum, grad_down = tail_call(
         dp_count, grad_qkv, raw, cos_table, sin_table, wqkv, all_tokens, down_sums, grad_h1_kept, scale_qk[None, :]
     )

time: 403 us -> 394 us (0.978)
  waiting for transfers between devices: 7.36 us -> 0.06 us
    unnamed x5 -> x3, waiting for transfers between devices: 7.36 us -> 0.05 us
    pallas_call x1, Pallas kernels: 58.7 us -> 54 us  [project_call(): pl.pallas_call(project_body, out_shape=(jax.ShapeDtypeStruct((group, cols...]
  transfers between devices with their start and end apart: 3 -> 2, of which waited for: 1 -> 0; matrix products, arithmetic and copies ran while one was open for 0% -> 0% of each run, Pallas kernels for 40% -> 41%
where the time goes in v8:
time: 394 us
  Pallas kernels  379 us (96%)
  between operations  14.1 us (4%)
    pallas_call x1, Pallas kernels, middle_call(): pl.pallas_call(functools.partial(middle_body, count), out_shape=(jax.Shap...  123 us
    pallas_call x1, Pallas kernels, tail_call(): pl.pallas_call(tail_body, out_shape=(shape((rows, width), f32), shape((wi...  62 us
    pallas_call x1, Pallas kernels, project_call(): pl.pallas_call(project_body, out_shape=(jax.ShapeDtypeStruct((group, cols...  54 us
    pallas_call x1, Pallas kernels, spread_call(): pl.pallas_call(functools.partial(spread_body, count), out_shape=(jax.Shap...  47.9 us
    pallas_call x1, Pallas kernels, settle_call(): pl.pallas_call(functools.partial(settle_body, count), out_shape=(shape((w...  42 us
    pallas_call x1, Pallas kernels, attn_bwd(): pl.pallas_call(attn_bwd_body, out_shape=jax.ShapeDtypeStruct((rows, 3 * c...  28.7 us
    pallas_call x1, Pallas kernels, attn_fwd(): pl.pallas_call(attn_fwd_body, out_shape=(jax.ShapeDtypeStruct((rows, cols...  15.8 us
  transfers between devices with their start and end apart: 2, of which 0 were waited for; matrix products, arithmetic and copies ran while one was open for 0% of the time, Pallas kernels for 41%

profile of v8, /device:TPU:0, one launch (start us, length us, event | category | flops | bytes accessed | tf_op | source)
XLA Modules:
  0.0 394.4 jit_solution(15658161694200283968)
XLA Ops:
  7.2 0.0 all-gather.3.cloned.1.call-start
  7.2 47.9 %spread.1 = (bf16[2,256,1024]{2,1,0:T(8,128)(2,1)}, bf16[256,1024]{1,0:T(8,128)(2,1)}, bf16[384,1024]{1,0:T(8,128)(2,1)}, bf16[1024,768]{1,0:T(8,128)(2,1)}, bf1...) custom-call(bf16[384,1024]{1,0:T(8,128)(2,1)} %tok_hbm.1, ...), custom_call_target="tpu_custom_call" | custom-call | tf_op jit(solution)/shard_map/spread/pallas_call | solution.py:869
  55.1 0.0 all-gather.3.cloned.1.call-update
  55.2 0.0 reduce-scatter.4.cloned.1.call-start
  55.2 0.7 reduce
  55.9 0.1 slice.3
  56.0 0.5 and_select_fusion.low_ref
  56.5 54.0 %project.1 = (bf16[1536,256]{1,0:T(8,128)(2,1)}, bf16[1536,256]{1,0:T(8,128)(2,1)}, bf16[1536,256]{1,0:T(8,128)(2,1)}, bf16[1536,512]{1,0:T(8,128)(2,1)}, bf16[1536,1024]{1,0:T(8,128)(2,1)}) custom-call(bf16[384,1024]{1,0:T(8,128)(2,1)} %tok_hbm.1, bf16[384,1024]{1,0:T(8,128)(2,1)} %get-tuple-element.57.tok2, bf16[1024,768]{1,0:T(8,128)(2,1)} %get-tuple-element.58.wqkv, ...), custom_call_target="tpu_custom_call" | custom-call | flops 60000002048 | bytes 10000000 | tf_op jit(solution)/shard_map/project/pallas_call | solution.py:1022
  110.6 15.8 %attn_fwd.1 = (bf16[1536,256]{1,0:T(8,128)(2,1)}, f32[8,1536]{1,0:T(8,128)}, bf16[1536,256]{1,0:T(8,128)(2,1)}) custom-call(s32[6]{0:T(128)} %and_select_fusion.low_ref, s32[1,1536]{1,0:T(1,128)} %get-tuple-element.56.start_ref, s32[1,1536]{1,0:T(1,128)} %order_row.3, bf16[1536,256]{1,0:T(8,128)(2,1)} %get-tuple-element.62.q_ref, ...), custom_call_target="tpu_custom_call" | custom-call | flops 2415919104 | bytes 3145728 | tf_op jit(solution)/shard_map/attn_fwd/pallas_call | solution.py:102
  126.4 0.0 all-gather.3.cloned.1.call-done
  126.4 123.4 %middle.1 = (bf16[384,1024]{1,0:T(8,128)(2,1)}, bf16[1536,256]{1,0:T(8,128)(2,1)}, bf16[4,2,256,1024]{3,2,1,0:T(8,128)(2,1)}, bf16[256,1024]{1,0:T(8,128)(2,1)},...) custom-call(bf16[1536,256]{1,0:T(8,128)(2,1)} %get-tuple-element.65., ...), custom_call_target="tpu_custom_call" | custom-call | flops 99999997952 | bytes 100000000 | tf_op jit(solution)/shard_map/middle/pallas_call | solution.py:612
  249.8 0.0 reduce-scatter.4.cloned.1.call-update
  249.8 28.7 %attn_bwd.1.grad_ref = bf16[1536,768]{1,0:T(8,128)(2,1)} custom-call(s32[6]{0:T(128)} %and_select_fusion.low_ref, s32[1,1536]{1,0:T(1,128)} %get-tuple-element.56.start_ref, s32[1,1536]{1,0:T(1,128)} %order_row.3, s32[1536,1]{1,0:T(8,128)} %get-tuple-element.61.order_col, f32[8,1536]{1,0:T(8,128)} %get-tuple-element.70.lse_ref, ...), custom_call_target="tpu_custom_call" | custom-call | flops 6039797760 | bytes 6291456 | tf_op jit(solution)/shard_map/attn_bwd/pallas_call | solution.py:182
  278.5 62.0 %tail.1 = (f32[384,1024]{1,0:T(8,128)}, bf16[1024,768]{1,0:T(8,128)(2,1)}, f32[1,256]{1,0:T(1,128)}, f32[128,1024]{1,0:T(8,128)}) custom-call(bf16[1536,768]{1,0:T(8,128)(2,1)} %attn_bwd.1.grad_ref, bf16[1536,512]{1,0:T(8,128)(2,1)} %get-tuple-element.73.raw_ref, f32[1536,128]{1,0:T(8,128)} %get-tuple-element.59.cos_ref, ...), custom_call_target="tpu_custom_call" | custom-call | flops 60000002048 | bytes 10000000 | tf_op jit(solution)/shard_map/tail/pallas_call | solution.py:1218
  340.5 0.0 reduce-scatter.4.cloned.1.call-done
  340.5 42.0 %settle.1 = (f32[128,256]{1,0:T(8,128)}, f32[128,256]{1,0:T(8,128)}, f32[128,256]{1,0:T(8,128)}, f32[128,256]{1,0:T(8,128)}, f32[128,1024]{1,0:T(8,128)}, /*inde...) custom-call(bf16[4,2,128,768]{3,2,1,0:T(8,128)(2,1)} %bitcast.12, ...), custom_call_target="tpu_custom_call" | custom-call | flops 1000000000 | bytes 10000000 | tf_op jit(solution)/shard_map/settle/pallas_call | solution.py:1451
  382.6 5.0 %deliver.1 = (bf16[384,1024]{1,0:T(8,128)(2,1)}, f32[384,1024]{1,0:T(8,128)}, f32[128,256]{1,0:T(8,128)}, f32[128,256]{1,0:T(8,128)}, f32[128,256]{1,0:T(8,128)}...) custom-call(bf16[384,1024]{1,0:T(8,128)(2,1)} %get-tuple-element.69., ...), custom_call_target="tpu_custom_call" | custom-call | tf_op jit(solution)/shard_map/deliver/pallas_call | solution.py:1513
Async XLA Ops:
  7.2 119.2 %all-gather.3.cloned.1.call-start = ((), (), s32[]{:S(2)}) async-start(), calls=%async_computation.1 | async-start | bytes 5242880 | tf_op jit(solution)/shard_map/all_gather | solution.py:1552
  55.2 285.4 %reduce-scatter.4.cloned.1.call-start = ((), (), s32[]{:S(2)}) async-start(), calls=%async_computation.2 | async-start | bytes 5242880
Sparse Core Ops, SparseCore 0:
  55.3 54.1 all-gather.2
  249.9 52.9 reduce-scatter.3

commit v9 on v8

--- a/solution.py
+++ b/solution.py
@@ -364,7 +364,7 @@
     def within(slot, at):
         return pl.ds(pl.multiple_of(slot * rows + at.start, STRIP), at.size)
 
-    def forward_rows(slot, at, store, ready):
+    def forward_rows(slot, at):
         where = within(slot, at)
 
         def hidden(n):
@@ -378,16 +378,12 @@
             gates[where, cols] = gate_raw.astype(jnp.bfloat16)
             mixed[where, cols] = (up * su_ref[:, cols] * silu).astype(jnp.bfloat16)
 
-        over(hid // TILE, hidden)
-        ready()
-
-        def down(n):
-            cols = tile_at(n, TILE)
-            store(at, cols, dot_abt(mixed[where, :], wall[2, cols, :]))
-
-        over(width // TILE, down)
-
-    def backward_rows(slot, at, store, ready):
+        def down(cols):
+            return dot_abt(mixed[where, :], wall[2, cols, :])
+
+        return hidden, down
+
+    def backward_rows(slot, at):
         where = within(slot, at)
 
         def hidden(n):
@@ -404,14 +400,10 @@
             ups[where, cols] = (d_up * su_ref[:, cols]).astype(jnp.bfloat16)
             gates[where, cols] = (d_gate * sg_ref[:, cols]).astype(jnp.bfloat16)
 
-        over(hid // TILE, hidden)
-        ready()
-
-        def down(n):
-            cols = tile_at(n, TILE)
-            store(at, cols, dot_abt(ups[where, :], wall[0, cols, :]) + dot_abt(gates[where, :], wall[1, cols, :]))
-
-        over(width // TILE, down)
+        def down(cols):
+            return dot_abt(ups[where, :], wall[0, cols, :]) + dot_abt(gates[where, :], wall[1, cols, :])
+
+        return hidden, down
 
     def part_copy(phase, kind, ch):
         part = tile_at(ch, crow)
@@ -419,9 +411,6 @@
         src, dst, peer = ((send_a, recv_a, core_peer), (send_d, recv_d, core_peer), (send_z, recv_z, z_peer))[kind]
         return remote(src.at[part, :], dst.at[part, :], part_send.at[index], part_recv.at[index], peer)
 
-    def nothing():
-        pass
-
     def tensor_pass(phase, buf, rows_fn, fillers):
         def keep_own(at, cols, value):
             own_part[at, cols] = value
@@ -435,32 +424,54 @@
         def to_z(at, cols, value):
             send_z[at, cols] = (value + recv_d[at, cols].astype(jnp.float32)).astype(jnp.bfloat16)
 
-        rows_fn(0, tile_at(0, rows), keep_own, nothing if phase else down_arrived)
+        tiles = hid // TILE
+        all_rows = tile_at(0, rows)
+
+        def span(low, high, body):
+            over(high - low, lambda n: body(n + low))
+
+        def store_all(at, down, store):
+            def one(n):
+                cols = tile_at(n, TILE)
+                store(at, cols, down(cols))
+
+            over(width // TILE, one)
+
+        hidden, down = rows_fn(0, all_rows)
+        over(tiles, hidden)
+        if phase == 0:
+            down_arrived()
+        store_all(all_rows, down, keep_own)
         for ch in range(chunks):
             hop(buf, phase, ch, 1).wait_recv()
         if phase == 1:
             for ch in range(chunks):
                 part_copy(0, 0, ch).wait_send()
-        rows_fn(1, tile_at(0, rows), to(send_a), nothing)
+        hidden, down = rows_fn(1, all_rows)
+        over(tiles, hidden)
+        store_all(all_rows, down, to(send_a))
         for ch in range(chunks):
             part_copy(phase, 0, ch).start()
         fillers[0]()
+
         def chunk(ch):
+            at = tile_at(ch, crow)
             hop(buf, phase, ch, 0).wait_recv()
             hop(buf, phase, ch, 2).start()
-            at = tile_at(ch, crow)
+            hidden_z, down_z = rows_fn(2, at)
+            hidden_d, down_d = rows_fn(3, at)
+            span(0, tiles // 2, hidden_z)
             hop(buf, phase, ch, 2).wait_recv()
             if phase == 1:
                 part_copy(0, 1, ch).wait_send()
-            rows_fn(3, at, to(send_d), nothing)
+            over(tiles, hidden_d)
+            store_all(at, down_d, to(send_d))
             part_copy(phase, 1, ch).start()
-
-            def ready():
-                part_copy(phase, 1, ch).wait_recv()
-                if phase == 1:
-                    part_copy(0, 2, ch).wait_send()
-
-            rows_fn(2, at, to_z, ready)
+            span(tiles // 2, tiles, hidden_z)
+            part_copy(phase, 1, ch).wait_recv()
+            if phase == 1:
+                part_copy(0, 2, ch).wait_send()
+            store_all(at, down_z, to_z)
             part_copy(phase, 2, ch).start()
 
         over(chunks, chunk)
@@ -712,10 +723,10 @@
 
 
 def spread_body(
-    count, tok, w_up, w_gate, w_down, wq, wk, wv, wo, order_ref, length_ref,
-    pair, pair_down, tok2, wqkv, wo_all, cos_out, sin_out, col_out, start_out,
+    count, tok, w_up, w_gate, wq, wk, wv, wo, order_ref, length_ref,
+    pair, tok2, wqkv, wo_all, cos_out, sin_out, col_out, start_out,
     own_mlp, own_att, wo_rows, load_sem, keep_sem, a_send, a_recv, b_send, b_recv, tok_send, tok_recv,
-    qkv_send, qkv_recv, oz_send, oz_recv, oq_send, oq_recv, oc_send, oc_recv,
+    qkv_send, qkv_recv, relay_send, relay_recv, oz_send, oz_recv, oq_send, oq_recv, oc_send, oc_recv,
 ):
     d = lax.axis_index("dp")
     t = lax.axis_index("tensor")
@@ -724,7 +735,7 @@
     far = (d - core + t // 2, flip2(t))
     wrows, wcols = wq.shape
     half = count // 2
-    mlp = (w_up, w_gate, w_down)
+    mlp = (w_up, w_gate)
     att = (wq, wk, wv)
     mine = tile_at(d, wrows)
     side = tile_at(core, wrows)
@@ -745,7 +756,7 @@
     pl.semaphore_wait(barrier, count + 3)
 
     def pair_at(m, rows):
-        return pair_down.at[rows, :] if m == 2 else pair.at[m, rows, :]
+        return pair.at[m, rows, :]
 
     def b_copy(m):
         return remote_copy(mlp[m], pair_at(m, side), b_send.at[m], b_recv.at[core * 3 + m], far)
@@ -760,28 +771,40 @@
     for k in (1, 2, 3):
         oz_copy(k).start()
     tok_copy.start()
-    for m in range(3):
+    for m in range(2):
         b_copy(m).start()
     load_o = pltpu.make_async_copy(wo, wo_rows.at[:, tile_at(t, wcols)], load_sem.at[0])
     load_o.start()
 
-    def qkv_copy(i, m):
+    def qkv_to(i, m, peer):
         return remote_copy(
-            att[m], wqkv.at[mine, pl.ds(m * wcols, wcols)], qkv_send.at[i, m], qkv_recv.at[i, m], (dp_peer(i), t)
+            att[m], wqkv.at[mine, pl.ds(m * wcols, wcols)], qkv_send.at[i, m], qkv_recv.at[i, m], (peer, t)
         )
 
-    def qkv_start(i):
+    def qkv_copy(j, m):
+        return qkv_to(j, m, lax.rem(d + 2 + 2 * j, count))
+
+    def qkv_own(m):
+        return qkv_to(half - 1, m, flip1(d))
+
+    def qkv_relay(j):
+        rows = tile_at(lax.rem(d + count - 2 - 2 * j, count), wrows)
+        return remote_copy(wqkv.at[rows, :], wqkv.at[rows, :], relay_send.at[j], relay_recv.at[j], (flip1(d), t))
+
+    def qkv_start(j):
         for m in range(3):
-            qkv_copy(i, m).start()
-
-    over(count - 1, qkv_start)
+            qkv_copy(j, m).start()
+
+    over(half - 1, qkv_start)
+    for m in range(3):
+        qkv_own(m).start()
 
     @pl.when(jnp.logical_not(home))
     def _():
-        for m in range(3):
+        for m in range(2):
             a_copy(m).start()
 
-    loads = [pltpu.make_async_copy(mlp[m], own_mlp.at[m], load_sem.at[1 + m]) for m in range(3)]
+    loads = [pltpu.make_async_copy(mlp[m], own_mlp.at[m], load_sem.at[1 + m]) for m in range(2)]
     loads += [pltpu.make_async_copy(att[m], own_att.at[m], load_sem.at[4 + m]) for m in range(3)]
     for copy in loads:
         copy.start()
@@ -792,7 +815,7 @@
     ]
     for copy in keeps:
         copy.start()
-    pair_keeps = [pltpu.make_async_copy(own_mlp.at[m], pair_at(m, side), keep_sem.at[3 + m]) for m in range(3)]
+    pair_keeps = [pltpu.make_async_copy(own_mlp.at[m], pair_at(m, side), keep_sem.at[3 + m]) for m in range(2)]
 
     @pl.when(home)
     def _():
@@ -819,17 +842,27 @@
     oc_own().start()
     rope_tables(order_ref, length_ref, cos_out, sin_out, col_out, start_out)
 
+    def qkv_next(j):
+        for m in range(3):
+            qkv_copy(j, m).wait_recv()
+        qkv_relay(j).start()
+
+    over(half - 1, qkv_next)
+
     def oq_next(j):
         oq_copy(j).wait_recv()
         oc_copy(j).start()
 
     over(half - 1, oq_next)
 
-    def qkv_wait(i):
+    def qkv_wait(j):
         for m in range(3):
-            qkv_copy(i, m).wait()
-
-    over(count - 1, qkv_wait)
+            qkv_copy(j, m).wait_send()
+        qkv_relay(j).wait()
+
+    over(half - 1, qkv_wait)
+    for m in range(3):
+        qkv_own(m).wait()
     over(half - 1, lambda j: oq_copy(j).wait_send())
     over(half - 1, lambda j: oc_copy(j).wait())
     oc_own().wait()
@@ -839,18 +872,18 @@
     for copy in keeps:
         copy.wait()
     tok_copy.wait()
-    for m in range(3):
+    for m in range(2):
         b_copy(m).wait_send()
 
     @pl.when(home)
     def _():
-        for m in range(3):
+        for m in range(2):
             pair_keeps[m].wait()
             remote_copy(mlp[m], pair_at(m, other_side), a_send.at[m], a_recv.at[m], (flip1(d), t)).wait_recv()
 
     @pl.when(jnp.logical_not(home))
     def _():
-        for m in range(3):
+        for m in range(2):
             a_copy(m).wait_send()
             for c in range(2):
                 remote_copy(
@@ -858,7 +891,7 @@
                 ).wait_recv()
 
 
-def spread_call(count, tokens, w_up, w_gate, w_down, wq, wk, wv, wo, order, lengths):
+def spread_call(count, tokens, w_up, w_gate, wq, wk, wv, wo, order, lengths):
     rows, width = tokens.shape
     group = order.shape[1]
     wrows, wcols = wq.shape
@@ -870,7 +903,6 @@
         functools.partial(spread_body, count),
         out_shape=(
             jax.ShapeDtypeStruct((2, 2 * wrows, hid), bf),
-            jax.ShapeDtypeStruct((2 * wrows, hid), bf),
             jax.ShapeDtypeStruct((rows, width), bf),
             jax.ShapeDtypeStruct((width, 3 * wcols), bf),
             jax.ShapeDtypeStruct((width, width), bf),
@@ -879,19 +911,19 @@
             jax.ShapeDtypeStruct((group, 1), jnp.int32),
             jax.ShapeDtypeStruct((1, group), jnp.int32),
         ),
-        in_specs=[anywhere] * 8 + [vmem(), pl.BlockSpec(memory_space=pltpu.SMEM)],
-        out_specs=(anywhere,) * 5 + (vmem(),) * 4,
+        in_specs=[anywhere] * 7 + [vmem(), pl.BlockSpec(memory_space=pltpu.SMEM)],
+        out_specs=(anywhere,) * 4 + (vmem(),) * 4,
         scratch_shapes=[
-            pltpu.VMEM((3, wrows, hid), bf),
+            pltpu.VMEM((2, wrows, hid), bf),
             pltpu.VMEM((3, wrows, wcols), bf),
             pltpu.VMEM((wrows, width), bf),
             dma((7,)), dma((7,)), dma((3,)), dma((3,)), dma((3,)), dma((6,)), dma, dma,
-            dma((count - 1, 3)), dma((count - 1, 3)), dma((3,)), dma((3,)),
+            dma((count // 2, 3)), dma((count // 2, 3)), dma((count // 2 - 1,)), dma((count // 2 - 1,)), dma((3,)), dma((3,)),
             dma((count // 2,)), dma((count // 2,)), dma((count // 2,)), dma((count // 2,)),
         ],
         compiler_params=pltpu.CompilerParams(vmem_limit_bytes=VMEM_LIMIT, collective_id=2, has_side_effects=True),
         name="spread",
-    )(tokens, w_up, w_gate, w_down, wq, wk, wv, wo, order, lengths)
+    )(tokens, w_up, w_gate, wq, wk, wv, wo, order, lengths)
 
 
 def head_sums(value):
@@ -912,8 +944,8 @@
 
 
 def project_body(
-    tok, tok2, wqkv, cos_ref, sin_ref, order_col, gain_ref, q_ref, k_ref, v_ref, raw_ref, x_hbm,
-    xs, plain, load_sem, keep_sem, mid_send, recv, on_send,
+    tok, tok2, w_down, wqkv, cos_ref, sin_ref, order_col, gain_ref, q_ref, k_ref, v_ref, raw_ref, x_hbm, pair_down,
+    xs, plain, own_down, load_sem, keep_sem, mid_send, recv, on_send, down_load, down_keep, a_send, a_recv, b_send, b_recv,
 ):
     t = lax.axis_index("tensor")
     d = lax.axis_index("dp")
@@ -925,7 +957,19 @@
     arrive = (2 - t // 2, 3 - 3 * (t // 2))
     pieces = mid_send.shape[0] // 2
     part = rows // pieces
-    greet([(d, near), (d, across)])
+    greet([(d, near), (d, across), (d, flip2(t)), (flip1(d), t), (flip1(d), flip2(t))])
+
+    core = lax.rem(d, 2)
+    home = core == t // 2
+    wrows = own_down.shape[0]
+
+    def down_at(c):
+        return pair_down.at[tile_at(c, wrows), :]
+
+    b_copy = remote_copy(w_down, down_at(core), b_send, b_recv.at[core], (d - core + t // 2, flip2(t)))
+    a_copy = remote_copy(w_down, down_at(core), a_send, a_recv, (flip1(d), t))
+    load_down = pltpu.make_async_copy(w_down, own_down, down_load)
+    keep_down = pltpu.make_async_copy(own_down, down_at(core), down_keep)
 
     def mid_copy(k):
         rows_of = pl.ds((k % pieces) * part, part)
@@ -940,6 +984,13 @@
     def _():
         for k in range(2 * pieces):
             mid_copy(k).start()
+        b_copy.start()
+
+    load_down.start()
+
+    @pl.when(jnp.logical_not(home))
+    def _():
+        a_copy.start()
 
     loads = [
         pltpu.make_async_copy(tok, xs.at[t], load_sem.at[0]),
@@ -986,6 +1037,12 @@
     keep(1, near).start()
     over(rows // WIDE_STRIP, lambda i: strip(near, i))
     permute(t // 2, 2 * rows, True)
+    load_down.wait()
+
+    @pl.when(home)
+    def _():
+        keep_down.start()
+
     per_strip = WIDE_STRIP // part
     for k in range(2 * pieces):
         slot = arrive[k // pieces]
@@ -996,6 +1053,12 @@
         def _():
             on_copy(k).start()
 
+        if k == 2 * pieces - 3:
+
+            @pl.when(jnp.logical_not(inner))
+            def _():
+                b_copy.start()
+
         if k % per_strip == per_strip - 1:
             strip(slot, (k % pieces) // per_strip)
         if k % pieces == pieces - 1:
@@ -1011,35 +1074,71 @@
             mid_copy(k).wait_send()
             on_copy(k).wait_send()
 
-
-def project_call(tokens, tok2, wqkv, cos, sin, order_col, gains):
+    b_copy.wait_send()
+
+    @pl.when(home)
+    def _():
+        keep_down.wait()
+        remote_copy(w_down, down_at(1 - core), a_send, a_recv, (flip1(d), t)).wait_recv()
+
+    @pl.when(jnp.logical_not(home))
+    def _():
+        a_copy.wait_send()
+        for c in range(2):
+            remote_copy(w_down, down_at(c), b_send, b_recv.at[c], (d - core + t // 2, flip2(t))).wait_recv()
+
+
+def project_call(tokens, tok2, w_down, wqkv, cos, sin, order_col, gains):
     rows, width = tokens.shape
     group = order_col.shape[0]
     cols = wqkv.shape[1] // 3
+    wrows, hid = w_down.shape
     bf = jnp.bfloat16
     anywhere = pl.BlockSpec(memory_space=pl.ANY)
     dma = pltpu.SemaphoreType.DMA
     return pl.pallas_call(
         project_body,
         out_shape=(jax.ShapeDtypeStruct((group, cols), bf),) * 3
-        + (jax.ShapeDtypeStruct((group, 2 * cols), bf), jax.ShapeDtypeStruct((group, width), bf)),
-        in_specs=[anywhere, anywhere] + [vmem()] * 5,
-        out_specs=(vmem(),) * 4 + (anywhere,),
+        + (
+            jax.ShapeDtypeStruct((group, 2 * cols), bf),
+            jax.ShapeDtypeStruct((group, width), bf),
+            jax.ShapeDtypeStruct((2 * wrows, hid), bf),
+        ),
+        in_specs=[anywhere] * 3 + [vmem()] * 5,
+        out_specs=(vmem(),) * 4 + (anywhere,) * 2,
         scratch_shapes=[
             pltpu.VMEM((group // rows, rows, width), bf),
             pltpu.VMEM((group, 3 * cols), bf),
+            pltpu.VMEM((wrows, hid), bf),
             dma((2,)), dma((4,)), dma((8,)), dma((8,)), dma((8,)),
+            dma, dma, dma, dma, dma, dma((2,)),
         ],
         compiler_params=pltpu.CompilerParams(vmem_limit_bytes=VMEM_LIMIT, collective_id=3, has_side_effects=True),
         cost_estimate=pl.CostEstimate(flops=6 * 10**10, bytes_accessed=10**7, transcendentals=10**6),
         name="project",
-    )(tokens, tok2, wqkv, cos, sin, order_col, gains)
+    )(tokens, tok2, w_down, wqkv, cos, sin, order_col, gains)
+
+
+def join(own, other, got, chip):
+    def one(e):
+        own[e] = (own[e].astype(jnp.float32) + other[e].astype(jnp.float32)).astype(own.dtype)
+
+    over(own.shape[0], one)
+    got[chip] = own[chip]
+
+
+def total_of(got):
+    return lax.fori_loop(
+        1, got.shape[0], lambda i, total: total + got[i].astype(jnp.float32), got[0].astype(jnp.float32)
+    )
 
 
 def tail_body(
-    grad_ref, raw_ref, cos_ref, sin_ref, wqkv, x_hbm, down_hbm, kept_ref, gain_ref, tok_out, gq, gain_sum, down_out,
+    count, grad_ref, raw_ref, cos_ref, sin_ref, wqkv, x_hbm, down_hbm, gwo_hbm, kept_ref, gain_ref,
+    tok_out, gq, gain_sum, down_out, wo_mid,
     xs, x_t, draw, part_far, part_mid, part_near, own_part, from_a, from_b, from_c, from_d, from_e, from_f,
-    near_mlp, far_mlp, load_sem, hop_send, hop_recv, keep_sem, near_send, near_recv, far_send, far_recv,
+    near_mlp, far_mlp, own_w, core_w, got_w, load_sem, hop_send, hop_recv, keep_sem, near_send, near_recv, far_send, far_recv,
+    load_w_sem, core_send, core_recv, w_send, w_recv,
 ):
     d = lax.axis_index("dp")
     t = lax.axis_index("tensor")
@@ -1051,9 +1150,20 @@
     outer = jnp.logical_not(inner)
     far, mid = 3 - 3 * (t // 2), 2 - t // 2
     chunk = rows // 2
-    greet([(d, near), (d, 3 - t), (d, flip2(t)), (flip1(d), t), (flip1(d), flip2(t))])
-
-    core = lax.rem(d, 2)
+    half, chip, core = count // 2, d // 2, lax.rem(d, 2)
+
+    def chip_peer(i):
+        return lax.rem(chip + 1 + i, half)
+
+    barrier = pltpu.get_barrier_semaphore()
+    for peer in [(d, near), (d, 3 - t), (d, flip2(t)), (flip1(d), t), (flip1(d), flip2(t))]:
+        pl.semaphore_signal(barrier, inc=1, device_id=peer, device_id_type=MESH_ID)
+    over(
+        half - 1,
+        lambda i: pl.semaphore_signal(barrier, inc=1, device_id=(2 * chip_peer(i) + core, t), device_id_type=MESH_ID),
+    )
+    pl.semaphore_wait(barrier, half + 4)
+
     home = core == t // 2
     away = jnp.logical_not(home)
     near_copy = remote_copy(down_hbm.at[1 - core], near_mlp, near_send, near_recv, (flip1(d), t))
@@ -1073,6 +1183,16 @@
 
     load_x = pltpu.make_async_copy(x_hbm, xs, load_sem)
     load_x.start()
+
+    core_w_copy = remote_copy(gwo_hbm.at[:, 1 - core], core_w, core_send, core_recv, (flip1(d), t))
+    load_w = pltpu.make_async_copy(gwo_hbm.at[:, core], own_w, load_w_sem)
+    core_w_copy.start()
+    load_w.start()
+
+    def w_copy(i):
+        return remote_copy(
+            own_w.at[chip_peer(i)], got_w.at[chip], w_send.at[i], w_recv.at[i], (2 * chip_peer(i) + core, t)
+        )
 
     def hop(kind, ch):
         src, dst, to = (
@@ -1139,6 +1259,10 @@
     pass_on(0, 0, part_far, from_a, 3)
     pass_on(0, 1, part_far, from_a, 3)
 
+    load_w.wait()
+    core_w_copy.wait_recv()
+    join(own_w, core_w, got_w, chip)
+    over(half - 1, lambda i: w_copy(i).start())
     load_x.wait()
 
     def flip_block(b):
@@ -1167,6 +1291,10 @@
     def _():
         near_copy.wait_recv()
 
+    over(half - 1, lambda i: w_copy(i).wait_recv())
+    wo_mid[...] = total_of(got_w).astype(jnp.bfloat16)
+    core_w_copy.wait_send()
+    over(half - 1, lambda i: w_copy(i).wait_send())
     far_same.wait_recv()
     down_out[...] = near_mlp[...].astype(jnp.float32) + far_mlp[...].astype(jnp.float32)
 
@@ -1207,7 +1335,7 @@
                 hop(kind, ch).wait_send()
 
 
-def tail_call(count, grad_qkv, raw, cos, sin, wqkv, all_tokens, down, kept, gains):
+def tail_call(count, grad_qkv, raw, cos, sin, wqkv, all_tokens, down, gwo, kept, gains):
     rows, width = kept.shape
     wrows, hid = width // count, down.shape[1]
     group, three = grad_qkv.shape
@@ -1216,15 +1344,16 @@
     dma = pltpu.SemaphoreType.DMA
     shape = jax.ShapeDtypeStruct
     return pl.pallas_call(
-        tail_body,
+        functools.partial(tail_body, count),
         out_shape=(
             shape((rows, width), f32),
             shape((width, three), bf),
             shape((1, three // 3), f32),
             shape((wrows, hid), f32),
+            shape((wrows, width), bf),
         ),
-        in_specs=[vmem()] * 5 + [anywhere] * 2 + [vmem()] * 2,
-        out_specs=(vmem(),) * 4,
+        in_specs=[vmem()] * 5 + [anywhere] * 3 + [vmem()] * 2,
+        out_specs=(vmem(),) * 5,
         scratch_shapes=[
             pltpu.VMEM((group, width), bf),
             pltpu.VMEM((width, group), bf),
@@ -1236,18 +1365,23 @@
         ]
         + [pltpu.VMEM((rows, width), bf)] * 6
         + [pltpu.VMEM((wrows, hid), bf)] * 2
-        + [dma, dma((6, 2)), dma((6, 2)), dma, dma, dma, dma((2,)), dma],
+        + [pltpu.VMEM((count // 2, wrows, width), bf)] * 3
+        + [dma, dma((6, 2)), dma((6, 2)), dma, dma, dma, dma((2,)), dma]
+        + [dma, dma, dma, dma((count // 2 - 1,)), dma((count // 2 - 1,))],
         compiler_params=pltpu.CompilerParams(vmem_limit_bytes=VMEM_LIMIT, collective_id=4, has_side_effects=True),
         cost_estimate=pl.CostEstimate(flops=6 * 10**10, bytes_accessed=10**7, transcendentals=10**6),
         name="tail",
-    )(grad_qkv, raw, cos, sin, wqkv, all_tokens, down.reshape(2, wrows, hid), kept, gains)
+    )(
+        grad_qkv, raw, cos, sin, wqkv, all_tokens, down.reshape(2, wrows, hid),
+        gwo.reshape(count // 2, 2, wrows, width), kept, gains,
+    )
 
 
 def settle_body(
-    count, gq_hbm, gwo_hbm, mlp_hbm, gain_ref, gaa_ref, gam_ref, gsu_ref, gsg_ref,
+    count, gq_hbm, mlp_hbm, wo_mid, gain_ref, gaa_ref, gam_ref, gsu_ref, gsg_ref,
     q_out, k_out, v_out, wo_out, up_out, gate_out, gain_out, aa_out, su_out, sg_out, am_out,
-    own_q, core_q, got_q, own_w, core_w, got_w, wo_mid, got_z, near_mlp, far_mlp, vec, got_v, vec_mid, got_s,
-    load_sem, core_send, core_recv, q_send, q_recv, w_send, w_recv, z_send, z_recv, v_send, v_recv, s_send, s_recv,
+    own_q, core_q, got_q, got_z, near_mlp, far_mlp, vec, got_v, vec_mid, got_s,
+    load_sem, core_send, core_recv, q_send, q_recv, z_send, z_recv, v_send, v_recv, s_send, s_recv,
     near_send, near_recv, mlp_send, mlp_recv,
 ):
     d = lax.axis_index("dp")
@@ -1279,6 +1413,15 @@
     pl.semaphore_signal(barrier, inc=1, device_id=(flip1(d), flip2(t)), device_id_type=MESH_ID)
     pl.semaphore_wait(barrier, count + 3)
 
+    def z_copy(k):
+        return remote_copy(
+            wo_mid.at[:, tile_at(line_peer(k), cols)], got_z.at[t], z_send.at[k - 1], z_recv.at[k - 1], (d, line_peer(k))
+        )
+
+    for k in (1, 2, 3):
+        z_copy(k).start()
+    got_z[t] = wo_mid[:, tile_at(t, cols)]
+
     near_copy = remote_copy(mlp_hbm.at[:, 1 - core], near_mlp, near_send, near_recv, (flip1(d), t))
     keep_mlp = pltpu.make_async_copy(mlp_hbm.at[:, core], near_mlp, load_sem.at[0])
 
@@ -1311,13 +1454,9 @@
     for u in range(3):
         far_start(u)
 
-    core_w_copy = remote_copy(gwo_hbm.at[:, 1 - core], core_w, core_send.at[0], core_recv.at[0], (flip1(d), t))
-    core_q_copy = remote_copy(gq_hbm.at[:, 1 - core], core_q, core_send.at[1], core_recv.at[1], (flip1(d), t))
-    load_w = pltpu.make_async_copy(gwo_hbm.at[:, core], own_w, load_sem.at[1])
-    load_q = pltpu.make_async_copy(gq_hbm.at[:, core], own_q, load_sem.at[2])
-    core_w_copy.start()
+    core_q_copy = remote_copy(gq_hbm.at[:, 1 - core], core_q, core_send, core_recv, (flip1(d), t))
+    load_q = pltpu.make_async_copy(gq_hbm.at[:, core], own_q, load_sem.at[1])
     core_q_copy.start()
-    load_w.start()
     load_q.start()
 
     vec[...] = jnp.zeros_like(vec)
@@ -1331,45 +1470,15 @@
 
     over(count - 1, lambda i: v_copy(i).start())
 
-    def chip_copy(own, got, sends, recvs, i):
-        return remote_copy(own.at[chip_peer(i)], got.at[chip], sends.at[i], recvs.at[i], (2 * chip_peer(i) + core, t))
-
-    def w_copy(i):
-        return chip_copy(own_w, got_w, w_send, w_recv, i)
-
     def q_copy(i):
-        return chip_copy(own_q, got_q, q_send, q_recv, i)
-
-    def join(own, other, got):
-        def one(e):
-            own[e] = (own[e].astype(f32) + other[e].astype(f32)).astype(bf)
-
-        over(half, one)
-        got[chip] = own[chip]
-
-    load_w.wait()
-    core_w_copy.wait_recv()
-    join(own_w, core_w, got_w)
-    over(half - 1, lambda i: w_copy(i).start())
+        return remote_copy(
+            own_q.at[chip_peer(i)], got_q.at[chip], q_send.at[i], q_recv.at[i], (2 * chip_peer(i) + core, t)
+        )
+
     load_q.wait()
     core_q_copy.wait_recv()
-    join(own_q, core_q, got_q)
+    join(own_q, core_q, got_q, chip)
     over(half - 1, lambda i: q_copy(i).start())
-
-    def total_of(got):
-        return lax.fori_loop(1, half, lambda i, total: total + got[i].astype(f32), got[0].astype(f32))
-
-    over(half - 1, lambda i: w_copy(i).wait_recv())
-    wo_mid[...] = total_of(got_w).astype(bf)
-
-    def z_copy(k):
-        return remote_copy(
-            wo_mid.at[:, tile_at(line_peer(k), cols)], got_z.at[t], z_send.at[k - 1], z_recv.at[k - 1], (d, line_peer(k))
-        )
-
-    for k in (1, 2, 3):
-        z_copy(k).start()
-    got_z[t] = wo_mid[:, tile_at(t, cols)]
 
     over(count - 1, lambda i: v_copy(i).wait_recv())
     even, odd = lax.fori_loop(
@@ -1424,21 +1533,15 @@
             far_same(u).wait_send()
             far_cross(u).wait_send()
 
-    core_w_copy.wait_send()
     core_q_copy.wait_send()
     over(count - 1, lambda i: v_copy(i).wait_send())
-
-    def drain(i):
-        w_copy(i).wait_send()
-        q_copy(i).wait_send()
-
-    over(half - 1, drain)
+    over(half - 1, lambda i: q_copy(i).wait_send())
     for k in (1, 2, 3):
         z_copy(k).wait_send()
         s_copy(k).wait_send()
 
 
-def settle_call(count, gq, gwo, mlp, gain_sum, gaa, gam, gsu, gsg):
+def settle_call(count, gq, mlp, wo_mid, gain_sum, gaa, gam, gsu, gsg):
     width, three = gq.shape
     half = count // 2
     cols = three // 3
@@ -1459,12 +1562,10 @@
             shape((1, 4 * hid), f32),
             shape((1, width), f32),
         ),
-        in_specs=[anywhere] * 3 + [vmem()] * 5,
+        in_specs=[anywhere] * 2 + [vmem()] * 6,
         out_specs=(vmem(),) * 11,
         scratch_shapes=[pltpu.VMEM((half, wrows, three), bf)] * 3
-        + [pltpu.VMEM((half, wrows, width), bf)] * 3
         + [
-            pltpu.VMEM((wrows, width), bf),
             pltpu.VMEM((4, wrows, cols), bf),
             pltpu.VMEM((2, wrows, hid), bf),
             pltpu.VMEM((2, wrows, hid), bf),
@@ -1472,9 +1573,9 @@
             pltpu.VMEM((count, 8, width), f32),
             pltpu.VMEM((8, width), f32),
             pltpu.VMEM((4, 8, width), f32),
-            dma((3,)),
-            dma((2,)), dma((2,)),
-            dma((half - 1,)), dma((half - 1,)), dma((half - 1,)), dma((half - 1,)),
+            dma((2,)),
+            dma, dma,
+            dma((half - 1,)), dma((half - 1,)),
             dma((3,)), dma((3,)),
             dma((count - 1,)), dma((count - 1,)),
             dma((3,)), dma((3,)),
@@ -1485,9 +1586,8 @@
         name="settle",
     )(
         gq.reshape(half, 2, wrows, three),
-        gwo.reshape(half, 2, wrows, width),
         mlp.reshape(2, 2, wrows, hid),
-        gain_sum, gaa, gam, gsu, gsg,
+        wo_mid, gain_sum, gaa, gam, gsu, gsg,
     )
 
 
@@ -1545,15 +1645,15 @@
     cotangent,
 ):
     dp_count = lax.axis_size("dp")
-    pair, pair_down, near_tokens, wqkv, wo_every, cos_table, sin_table, order_col, start = spread_call(
-        dp_count, tokens, w_up, w_gate, w_down_t, w_query, w_key, w_value, w_out_t, order, lengths
+    pair, near_tokens, wqkv, wo_every, cos_table, sin_table, order_col, start = spread_call(
+        dp_count, tokens, w_up, w_gate, w_query, w_key, w_value, w_out_t, order, lengths
     )
     low = lax.slice(start[0], (0,), (start.shape[1],), (BLK,)) // BLK
     mlp_parts = lax.all_gather(
         pair, "dp", axis=0, tiled=False, axis_index_groups=same_core_groups(dp_count)
     )
-    queries, key_rows, value_rows, raw, all_tokens = project_call(
-        tokens, near_tokens, wqkv, cos_table, sin_table, order_col, scale_qk[None, :]
+    queries, key_rows, value_rows, raw, all_tokens, pair_down = project_call(
+        tokens, near_tokens, w_down_t, wqkv, cos_table, sin_table, order_col, scale_qk[None, :]
     )
     attended, log_totals, attended_plain = attn_fwd(low, start, order, queries, key_rows, value_rows)
     out_rows, grad_att_rows, up_gate_grads, down_sums, wo_grads, grad_h1_kept, grad_alpha_a, grad_alpha_m, grad_su, grad_sv = middle_call(
@@ -1576,11 +1676,11 @@
     up_gate_sums = lax.psum_scatter(
         up_gate_grads, "dp", scatter_dimension=0, tiled=False, axis_index_groups=same_core_groups(dp_count)
     )
-    grad_tokens, grad_q, gain_sum, grad_down = tail_call(
-        dp_count, grad_qkv, raw, cos_table, sin_table, wqkv, all_tokens, down_sums, grad_h1_kept, scale_qk[None, :]
+    grad_tokens, grad_q, gain_sum, grad_down, wo_sums = tail_call(
+        dp_count, grad_qkv, raw, cos_table, sin_table, wqkv, all_tokens, down_sums, wo_grads, grad_h1_kept, scale_qk[None, :]
     )
     settled = settle_call(
-        dp_count, grad_q, wo_grads, up_gate_sums, gain_sum, grad_alpha_a, grad_alpha_m, grad_su, grad_sv
+        dp_count, grad_q, up_gate_sums, wo_sums, gain_sum, grad_alpha_a, grad_alpha_m, grad_su, grad_sv
     )
     return deliver_call([out_rows, grad_tokens, *settled[:6], grad_down], settled[6:])
 

time: 394 us -> 391 us (level); the launches traced: 394 us -> 387 us
  Pallas kernels: 379 us -> 372 us
    pallas_call x1, Pallas kernels: 47.9 us -> 42.4 us  [spread_call(): pl.pallas_call(functools.partial(spread_body, count), out_shape=(jax.Shap...]
    pallas_call x1, Pallas kernels: 54 us -> 59.3 us  [project_call(): pl.pallas_call(project_body, out_shape=(jax.ShapeDtypeStruct((group, cols...]
where the time goes in v9:
time: 391 us; the launch traced here: 387 us
  Pallas kernels  372 us (95%)
  between operations  14.1 us (4%)
    pallas_call x1, Pallas kernels, middle_call(): pl.pallas_call(functools.partial(middle_body, count), out_shape=(jax.Shap...  124 us
    pallas_call x1, Pallas kernels, tail_call(): pl.pallas_call(functools.partial(tail_body, count), out_shape=(shape((row...  60.9 us
    pallas_call x1, Pallas kernels, project_call(): pl.pallas_call(project_body, out_shape=(jax.ShapeDtypeStruct((group, cols...  59.3 us
    pallas_call x1, Pallas kernels, spread_call(): pl.pallas_call(functools.partial(spread_body, count), out_shape=(jax.Shap...  42.4 us
    pallas_call x1, Pallas kernels, settle_call(): pl.pallas_call(functools.partial(settle_body, count), out_shape=(shape((w...  41.1 us
    pallas_call x1, Pallas kernels, attn_bwd(): pl.pallas_call(attn_bwd_body, out_shape=jax.ShapeDtypeStruct((rows, 3 * c...  25.2 us
    pallas_call x1, Pallas kernels, attn_fwd(): pl.pallas_call(attn_fwd_body, out_shape=(jax.ShapeDtypeStruct((rows, cols...  13.6 us
  transfers between devices with their start and end apart: 2, of which 0 were waited for; matrix products, arithmetic and copies ran while one was open for 0% of the time, Pallas kernels for 41%

profile of v9, /device:TPU:0, one launch (start us, length us, event | category | flops | bytes accessed | tf_op | source)
XLA Modules:
  0.0 387.1 jit_solution(9677765964530091947)
XLA Ops:
  7.2 0.0 all-gather.3.cloned.1.call-start
  7.2 42.4 %spread.1 = (bf16[2,256,1024]{2,1,0:T(8,128)(2,1)}, bf16[384,1024]{1,0:T(8,128)(2,1)}, bf16[1024,768]{1,0:T(8,128)(2,1)}, bf16[1024,1024]{1,0:T(8,128)(2,1)}, f3...) custom-call(bf16[384,1024]{1,0:T(8,128)(2,1)} %tok_hbm.1, ...), custom_call_target="tpu_custom_call" | custom-call | tf_op jit(solution)/shard_map/spread/pallas_call | solution.py:902
  49.7 0.0 all-gather.3.cloned.1.call-update
  49.7 0.0 reduce-scatter.4.cloned.1.call-start
  49.7 0.7 reduce
  50.5 0.1 slice.3
  50.6 0.5 and_select_fusion.low_ref
  51.1 59.3 %project.1 = (bf16[1536,256]{1,0:T(8,128)(2,1)}, bf16[1536,256]{1,0:T(8,128)(2,1)}, bf16[1536,256]{1,0:T(8,128)(2,1)}, bf16[1536,512]{1,0:T(8,128)(2,1)}, bf16[1...) custom-call(bf16[384,1024]{1,0:T(8,128)(2,1)} %tok_hbm.1, bf16[384,1024]{1,0:T(8,128)(2,1)} %get-tuple-element.58.tok2, ...), custom_call_target="tpu_custom_call" | custom-call | flops 60000002048 | bytes 10000000 | tf_op jit(solution)/shard_map/project/pallas_call | solution.py:1099
  110.4 13.6 %attn_fwd.1 = (bf16[1536,256]{1,0:T(8,128)(2,1)}, f32[8,1536]{1,0:T(8,128)}, bf16[1536,256]{1,0:T(8,128)(2,1)}) custom-call(s32[6]{0:T(128)} %and_select_fusion.low_ref, s32[1,1536]{1,0:T(1,128)} %get-tuple-element.57.start_ref, s32[1,1536]{1,0:T(1,128)} %order_row.3, bf16[1536,256]{1,0:T(8,128)(2,1)} %get-tuple-element.63.q_ref, ...), custom_call_target="tpu_custom_call" | custom-call | flops 2415919104 | bytes 3145728 | tf_op jit(solution)/shard_map/attn_fwd/pallas_call | solution.py:102
  123.9 0.0 all-gather.3.cloned.1.call-done
  123.9 124.0 %middle.1 = (bf16[384,1024]{1,0:T(8,128)(2,1)}, bf16[1536,256]{1,0:T(8,128)(2,1)}, bf16[4,2,256,1024]{3,2,1,0:T(8,128)(2,1)}, bf16[256,1024]{1,0:T(8,128)(2,1)},...) custom-call(bf16[1536,256]{1,0:T(8,128)(2,1)} %get-tuple-element.66., ...), custom_call_target="tpu_custom_call" | custom-call | flops 99999997952 | bytes 100000000 | tf_op jit(solution)/shard_map/middle/pallas_call | solution.py:623
  247.9 0.0 reduce-scatter.4.cloned.1.call-update
  247.9 25.2 %attn_bwd.1.grad_ref = bf16[1536,768]{1,0:T(8,128)(2,1)} custom-call(s32[6]{0:T(128)} %and_select_fusion.low_ref, s32[1,1536]{1,0:T(1,128)} %get-tuple-element.57.start_ref, s32[1,1536]{1,0:T(1,128)} %order_row.3, s32[1536,1]{1,0:T(8,128)} %get-tuple-element.62.order_col, f32[8,1536]{1,0:T(8,128)} %get-tuple-element.71.lse_ref, ...), custom_call_target="tpu_custom_call" | custom-call | flops 6039797760 | bytes 6291456 | tf_op jit(solution)/shard_map/attn_bwd/pallas_call | solution.py:182
  273.2 60.9 %tail.1 = (f32[384,1024]{1,0:T(8,128)}, bf16[1024,768]{1,0:T(8,128)(2,1)}, f32[1,256]{1,0:T(1,128)}, f32[128,1024]{1,0:T(8,128)}, bf16[128,1024]{1,0:T(8,128)(2,1)}) custom-call(bf16[1536,768]{1,0:T(8,128)(2,1)} %attn_bwd.1.grad_ref, bf16[1536,512]{1,0:T(8,128)(2,1)} %get-tuple-element.74.raw_ref, f32[1536,128]{1,0:T(8,128)} %get-tuple-element.60.cos_ref, ...), custom_call_target="tpu_custom_call" | custom-call | flops 60000002048 | bytes 10000000 | tf_op jit(solution)/shard_map/tail/pallas_call | solution.py:1346
  334.1 0.0 reduce-scatter.4.cloned.1.call-done
  334.1 41.1 %settle.1 = (f32[128,256]{1,0:T(8,128)}, f32[128,256]{1,0:T(8,128)}, f32[128,256]{1,0:T(8,128)}, f32[128,256]{1,0:T(8,128)}, f32[128,1024]{1,0:T(8,128)}, /*inde...) custom-call(bf16[4,2,128,768]{3,2,1,0:T(8,128)(2,1)} %bitcast.20, ...), custom_call_target="tpu_custom_call" | custom-call | flops 1000000000 | bytes 10000000 | tf_op jit(solution)/shard_map/settle/pallas_call | solution.py:1554
  375.2 5.0 %deliver.1 = (bf16[384,1024]{1,0:T(8,128)(2,1)}, f32[384,1024]{1,0:T(8,128)}, f32[128,256]{1,0:T(8,128)}, f32[128,256]{1,0:T(8,128)}, f32[128,256]{1,0:T(8,128)}...) custom-call(bf16[384,1024]{1,0:T(8,128)(2,1)} %get-tuple-element.70., ...), custom_call_target="tpu_custom_call" | custom-call | tf_op jit(solution)/shard_map/deliver/pallas_call | solution.py:1613
Async XLA Ops:
  7.2 116.7 %all-gather.3.cloned.1.call-start = ((), (), s32[]{:S(2)}) async-start(), calls=%async_computation.1 | async-start | bytes 5242880 | tf_op jit(solution)/shard_map/all_gather | solution.py:1652
  49.7 284.4 %reduce-scatter.4.cloned.1.call-start = ((), (), s32[]{:S(2)}) async-start(), calls=%async_computation.2 | async-start | bytes 5242880
Sparse Core Ops, SparseCore 0:
  49.8 51.9 all-gather.2
  248.1 60.2 reduce-scatter.3

commit v10 on v9

--- a/solution.py
+++ b/solution.py
@@ -1053,7 +1053,7 @@
         def _():
             on_copy(k).start()
 
-        if k == 2 * pieces - 3:
+        if k == 2 * pieces - 5:
 
             @pl.when(jnp.logical_not(inner))
             def _():

time: 391 us -> 396 us (1.013)
  Pallas kernels: 372 us -> 379 us
  transfers between devices with their start and end apart: 2 -> 2, of which waited for: 0 -> 0; matrix products, arithmetic and copies ran while one was open for 0% -> 0% of each run, Pallas kernels for 41% -> 42%
where the time goes in v10:
time: 396 us; the launch traced here: 395 us
  Pallas kernels  379 us (96%)
  between operations  14.1 us (4%)
    pallas_call x1, Pallas kernels, middle_call(): pl.pallas_call(functools.partial(middle_body, count), out_shape=(jax.Shap...  125 us
    pallas_call x1, Pallas kernels, tail_call(): pl.pallas_call(functools.partial(tail_body, count), out_shape=(shape((row...  64.2 us
    pallas_call x1, Pallas kernels, project_call(): pl.pallas_call(project_body, out_shape=(jax.ShapeDtypeStruct((group, cols...  62.7 us
    pallas_call x1, Pallas kernels, spread_call(): pl.pallas_call(functools.partial(spread_body, count), out_shape=(jax.Shap...  42.4 us
    pallas_call x1, Pallas kernels, settle_call(): pl.pallas_call(functools.partial(settle_body, count), out_shape=(shape((w...  41.7 us
    pallas_call x1, Pallas kernels, attn_bwd(): pl.pallas_call(attn_bwd_body, out_shape=jax.ShapeDtypeStruct((rows, 3 * c...  25.2 us
    pallas_call x1, Pallas kernels, attn_fwd(): pl.pallas_call(attn_fwd_body, out_shape=(jax.ShapeDtypeStruct((rows, cols...  13.6 us
  transfers between devices with their start and end apart: 2, of which 0 were waited for; matrix products, arithmetic and copies ran while one was open for 0% of the time, Pallas kernels for 42%

profile of v10, /device:TPU:0, one launch (start us, length us, event | category | flops | bytes accessed | tf_op | source)
XLA Modules:
  0.0 395.1 jit_solution(1995899889585122873)
XLA Ops:
  7.2 0.0 all-gather.3.cloned.1.call-start
  7.2 42.4 %spread.1 = (bf16[2,256,1024]{2,1,0:T(8,128)(2,1)}, bf16[384,1024]{1,0:T(8,128)(2,1)}, bf16[1024,768]{1,0:T(8,128)(2,1)}, bf16[1024,1024]{1,0:T(8,128)(2,1)}, f3...) custom-call(bf16[384,1024]{1,0:T(8,128)(2,1)} %tok_hbm.1, ...), custom_call_target="tpu_custom_call" | custom-call | tf_op jit(solution)/shard_map/spread/pallas_call | solution.py:902
  49.7 0.0 all-gather.3.cloned.1.call-update
  49.7 0.0 reduce-scatter.4.cloned.1.call-start
  49.7 0.7 reduce
  50.5 0.1 slice.3
  50.6 0.5 and_select_fusion.low_ref
  51.1 62.7 %project.1 = (bf16[1536,256]{1,0:T(8,128)(2,1)}, bf16[1536,256]{1,0:T(8,128)(2,1)}, bf16[1536,256]{1,0:T(8,128)(2,1)}, bf16[1536,512]{1,0:T(8,128)(2,1)}, bf16[1...) custom-call(bf16[384,1024]{1,0:T(8,128)(2,1)} %tok_hbm.1, bf16[384,1024]{1,0:T(8,128)(2,1)} %get-tuple-element.58.tok2, ...), custom_call_target="tpu_custom_call" | custom-call | flops 60000002048 | bytes 10000000 | tf_op jit(solution)/shard_map/project/pallas_call | solution.py:1099
  113.7 13.6 %attn_fwd.1 = (bf16[1536,256]{1,0:T(8,128)(2,1)}, f32[8,1536]{1,0:T(8,128)}, bf16[1536,256]{1,0:T(8,128)(2,1)}) custom-call(s32[6]{0:T(128)} %and_select_fusion.low_ref, s32[1,1536]{1,0:T(1,128)} %get-tuple-element.57.start_ref, s32[1,1536]{1,0:T(1,128)} %order_row.3, bf16[1536,256]{1,0:T(8,128)(2,1)} %get-tuple-element.63.q_ref, ...), custom_call_target="tpu_custom_call" | custom-call | flops 2415919104 | bytes 3145728 | tf_op jit(solution)/shard_map/attn_fwd/pallas_call | solution.py:102
  127.3 0.0 all-gather.3.cloned.1.call-done
  127.3 124.6 %middle.1 = (bf16[384,1024]{1,0:T(8,128)(2,1)}, bf16[1536,256]{1,0:T(8,128)(2,1)}, bf16[4,2,256,1024]{3,2,1,0:T(8,128)(2,1)}, bf16[256,1024]{1,0:T(8,128)(2,1)},...) custom-call(bf16[1536,256]{1,0:T(8,128)(2,1)} %get-tuple-element.66., ...), custom_call_target="tpu_custom_call" | custom-call | flops 99999997952 | bytes 100000000 | tf_op jit(solution)/shard_map/middle/pallas_call | solution.py:623
  252.0 0.0 reduce-scatter.4.cloned.1.call-update
  252.0 25.2 %attn_bwd.1.grad_ref = bf16[1536,768]{1,0:T(8,128)(2,1)} custom-call(s32[6]{0:T(128)} %and_select_fusion.low_ref, s32[1,1536]{1,0:T(1,128)} %get-tuple-element.57.start_ref, s32[1,1536]{1,0:T(1,128)} %order_row.3, s32[1536,1]{1,0:T(8,128)} %get-tuple-element.62.order_col, f32[8,1536]{1,0:T(8,128)} %get-tuple-element.71.lse_ref, ...), custom_call_target="tpu_custom_call" | custom-call | flops 6039797760 | bytes 6291456 | tf_op jit(solution)/shard_map/attn_bwd/pallas_call | solution.py:182
  277.2 64.2 %tail.1 = (f32[384,1024]{1,0:T(8,128)}, bf16[1024,768]{1,0:T(8,128)(2,1)}, f32[1,256]{1,0:T(1,128)}, f32[128,1024]{1,0:T(8,128)}, bf16[128,1024]{1,0:T(8,128)(2,1)}) custom-call(bf16[1536,768]{1,0:T(8,128)(2,1)} %attn_bwd.1.grad_ref, bf16[1536,512]{1,0:T(8,128)(2,1)} %get-tuple-element.74.raw_ref, f32[1536,128]{1,0:T(8,128)} %get-tuple-element.60.cos_ref, ...), custom_call_target="tpu_custom_call" | custom-call | flops 60000002048 | bytes 10000000 | tf_op jit(solution)/shard_map/tail/pallas_call | solution.py:1346
  341.5 0.0 reduce-scatter.4.cloned.1.call-done
  341.5 41.7 %settle.1 = (f32[128,256]{1,0:T(8,128)}, f32[128,256]{1,0:T(8,128)}, f32[128,256]{1,0:T(8,128)}, f32[128,256]{1,0:T(8,128)}, f32[128,1024]{1,0:T(8,128)}, /*inde...) custom-call(bf16[4,2,128,768]{3,2,1,0:T(8,128)(2,1)} %bitcast.20, ...), custom_call_target="tpu_custom_call" | custom-call | flops 1000000000 | bytes 10000000 | tf_op jit(solution)/shard_map/settle/pallas_call | solution.py:1554
  383.2 5.0 %deliver.1 = (bf16[384,1024]{1,0:T(8,128)(2,1)}, f32[384,1024]{1,0:T(8,128)}, f32[128,256]{1,0:T(8,128)}, f32[128,256]{1,0:T(8,128)}, f32[128,256]{1,0:T(8,128)}...) custom-call(bf16[384,1024]{1,0:T(8,128)(2,1)} %get-tuple-element.70., ...), custom_call_target="tpu_custom_call" | custom-call | tf_op jit(solution)/shard_map/deliver/pallas_call | solution.py:1613
Async XLA Ops:
  7.2 120.1 %all-gather.3.cloned.1.call-start = ((), (), s32[]{:S(2)}) async-start(), calls=%async_computation.1 | async-start | bytes 5242880 | tf_op jit(solution)/shard_map/all_gather | solution.py:1652
  49.7 291.8 %reduce-scatter.4.cloned.1.call-start = ((), (), s32[]{:S(2)}) async-start(), calls=%async_computation.2 | async-start | bytes 5242880
Sparse Core Ops, SparseCore 0:
  49.8 51.9 all-gather.2
  252.1 52.2 reduce-scatter.3
